TPU v7x, 256 devices: a whole 4x4x8 slice. The times are simulated.
256 devices in a mesh: seq: 128 (over y, x_lo, z, core), tp: 2 (over x_hi).
Axes of the slice: x: 4 (x_hi: 2, x_lo: 2; x = x_hi * 2 + x_lo), y: 4, z: 8, core: 2. Of those that a mesh axis runs over, the one named last changes fastest.
Arguments:
- series: bfloat16 [32768, 2048], P(('seq', 'tp')), may hold values from -4 to 4
- norm_gain: float32 [2048], replicated, may hold values from 0.1 to 1.9
- w_query: bfloat16 [2048, 1024], P(None, 'tp'), may hold values from -0.5 to 0.5
- w_key: bfloat16 [2048, 1024], P(None, 'tp'), may hold values from -0.5 to 0.5
- w_value: bfloat16 [2048, 1024], P(None, 'tp'), may hold values from -0.125 to 0.125
- w_out: bfloat16 [1024, 2048], P('tp'), may hold values from -0.1875 to 0.1875
- out_grad: bfloat16 [32768, 2048], P(('seq', 'tp')), may hold values from -6 to 6
Outputs:
- layer_out: bfloat16 [32768, 2048], P(('seq', 'tp'))
- series_grad: bfloat16 [32768, 2048], P(('seq', 'tp'))
All inputs are finite; a program needn't handle non-finite values.
Results may differ from a plain program's by a relative error of at most 0.019.
Values may be sent and summed in bfloat16 or wider, within the bound.
No kernel may reach another device: no remote copies, remote signals or barrier semaphores. Data moves between devices by JAX's collectives and lax.ppermute only.
A program may use at most 128 MiB of HBM per device.

v0:
```python
import jax
import jax.numpy as jnp
from jax import lax
from jax.sharding import PartitionSpec as P

HD = 128
BLOCK = 64


NEG = -1e30
EPS = 1e-06


def shifted(value, axis, by):
    size = lax.axis_size(axis)
    pairs = [(i, i + by) for i in range(size) if 0 <= i + by < size]
    return lax.ppermute(value, axis, pairs)


def project_back(grads, weight):
    return jnp.einsum("tf,df->td", grads, weight, preferred_element_type=jnp.float32)


def per_device(series, norm_gain, w_query, w_key, w_value, w_out, out_grad):
    series_f = series.astype(jnp.float32)
    inv_rms = lax.rsqrt(jnp.mean(series_f * series_f, axis=-1, keepdims=True) + EPS)
    unit_rows = series_f * inv_rms
    normed_rows = (unit_rows * norm_gain).astype(jnp.bfloat16)
    gathered, out_grads = (
        lax.all_gather(normed_rows, "tp", axis=0, tiled=True),
        lax.all_gather(out_grad, "tp", axis=0, tiled=True),
    )
    tokens = gathered.shape[0]
    feat_width = w_query.shape[1]
    head_count = feat_width // HD
    blocks = tokens // BLOCK
    seq_devices = lax.axis_size("seq")
    levels = seq_devices.bit_length() - 1
    first_block = lax.axis_index("seq") * blocks
    factor = HD ** (-0.5)
    query_rows = jnp.dot(gathered, w_query, preferred_element_type=jnp.float32).astype(jnp.bfloat16)
    key_rows = jnp.dot(gathered, w_key, preferred_element_type=jnp.float32).astype(jnp.bfloat16)
    value_rows = jnp.dot(gathered, w_value, preferred_element_type=jnp.float32).astype(jnp.bfloat16)
    key_value = jnp.stack([key_rows, value_rows])
    fetched = [shifted(key_value, "seq", 2**section) for section in range(levels)]
    near_steps = [2**section for section in range(blocks.bit_length())]
    distances = near_steps + [blocks * 2**section for section in range(1, levels)]
    own_blocks = key_value.reshape(2, blocks, BLOCK, feat_width)
    extended = jnp.concatenate([fetched[0], key_value], axis=1).reshape(
        2, 2 * blocks, BLOCK, feat_width
    )
    pieces = [own_blocks] + [
        extended[:, blocks - distance : 2 * blocks - distance] for distance in near_steps
    ]
    pieces = pieces + [
        fetched[section].reshape(2, blocks, BLOCK, feat_width) for section in range(1, levels)
    ]
    keys_all = jnp.concatenate(pieces, axis=2)
    global_block = first_block + jnp.arange(blocks, dtype=jnp.int32)
    causal = lax.broadcasted_iota(jnp.int32, (BLOCK, BLOCK), 0) >= lax.broadcasted_iota(
        jnp.int32, (BLOCK, BLOCK), 1
    )
    mask_list = [jnp.broadcast_to(causal, (blocks, BLOCK, BLOCK))]
    mask_list = mask_list + [
        jnp.broadcast_to((global_block >= distance)[:, None, None], (blocks, BLOCK, BLOCK))
        for distance in distances
    ]
    key_mask = jnp.concatenate(mask_list, axis=2)[:, None]
    query_blocks = query_rows.reshape(blocks, BLOCK, head_count, HD)
    key_blocks = keys_all[0].reshape(blocks, -1, head_count, HD)
    value_blocks = keys_all[1].reshape(blocks, -1, head_count, HD)
    scores = (
        jnp.einsum("bqhe,bkhe->bhqk", query_blocks, key_blocks, preferred_element_type=jnp.float32)
        * factor
    )
    scores = jnp.where(key_mask, scores, NEG)
    peak_score = jnp.max(scores, axis=-1, keepdims=True)
    log_total = peak_score + jnp.log(jnp.sum(jnp.exp(scores - peak_score), axis=-1, keepdims=True))
    attn_prob = jnp.exp(scores - log_total)
    attn_weight = attn_prob.astype(jnp.bfloat16)
    mixed = jnp.einsum(
        "bhqk,bkhe->bqhe", attn_weight, value_blocks, preferred_element_type=jnp.float32
    ).astype(jnp.bfloat16)
    mixed_rows = mixed.reshape(tokens, feat_width)
    attn_rows = lax.psum_scatter(
        jnp.dot(mixed_rows, w_out, preferred_element_type=jnp.float32).astype(jnp.bfloat16),
        "tp",
        scatter_dimension=0,
        tiled=True,
    ).astype(jnp.float32)
    layer_out = (series_f + attn_rows).astype(jnp.bfloat16)
    grad_mixed = jnp.einsum(
        "td,fd->tf", out_grads, w_out, preferred_element_type=jnp.float32
    ).astype(jnp.bfloat16)
    grad_blocks = grad_mixed.reshape(blocks, BLOCK, head_count, HD)
    row_inner = jnp.einsum("bqhe,bqhe->bhq", grad_blocks, mixed, preferred_element_type=jnp.float32)
    grad_probs = jnp.einsum(
        "bqhe,bkhe->bhqk", grad_blocks, value_blocks, preferred_element_type=jnp.float32
    )
    grad_scores = (attn_prob * (grad_probs - row_inner[..., None])).astype(jnp.bfloat16)
    grad_query = (
        jnp.einsum("bhqk,bkhe->bqhe", grad_scores, key_blocks, preferred_element_type=jnp.float32)
        * factor
    ).astype(jnp.bfloat16)
    grad_query = grad_query.reshape(tokens, feat_width)
    grad_keys = (
        jnp.einsum("bhqk,bqhe->bkhe", grad_scores, query_blocks, preferred_element_type=jnp.float32)
        * factor
    )
    grad_values = jnp.einsum(
        "bhqk,bqhe->bkhe", attn_weight, grad_blocks, preferred_element_type=jnp.float32
    )
    grad_pairs = jnp.stack([grad_keys, grad_values]).reshape(2, blocks, -1, BLOCK, feat_width)
    spill_grads = jnp.zeros((2, 2 * blocks, BLOCK, feat_width), jnp.float32)
    for position, distance in enumerate(near_steps):
        spill_grads = spill_grads.at[:, blocks - distance : 2 * blocks - distance].add(
            grad_pairs[:, :, 1 + position]
        )
    own_grads = grad_pairs[:, :, 0] + spill_grads[:, blocks:]
    for section in range(levels):
        if section == 0:
            return_part = spill_grads[:, :blocks]
        else:
            return_part = grad_pairs[:, :, len(near_steps) + section]
        own_grads = own_grads + shifted(return_part, "seq", -(2**section))
    grad_key_rows = own_grads[0].reshape(tokens, feat_width).astype(jnp.bfloat16)
    grad_value_rows = own_grads[1].reshape(tokens, feat_width).astype(jnp.bfloat16)
    grad_normed = (
        project_back(grad_query, w_query)
        + project_back(grad_key_rows, w_key)
        + project_back(grad_value_rows, w_value)
    )
    grad_own = lax.psum_scatter(
        grad_normed.astype(jnp.bfloat16), "tp", scatter_dimension=0, tiled=True
    ).astype(jnp.float32)
    scaled = grad_own * norm_gain
    series_grad = out_grad.astype(jnp.float32) + inv_rms * (
        scaled - unit_rows * jnp.mean(scaled * unit_rows, axis=-1, keepdims=True)
    )
    return (layer_out, series_grad.astype(jnp.bfloat16))


def solution(mesh):
    in_specs = (
        P(("seq", "tp"), None),
        P(),
        P(None, "tp"),
        P(None, "tp"),
        P(None, "tp"),
        P("tp", None),
        P(("seq", "tp"), None),
    )
    out_specs = (P(("seq", "tp"), None), P(("seq", "tp"), None))
    return jax.shard_map(
        per_device, mesh=mesh, in_specs=in_specs, out_specs=out_specs, check_vma=False
    )
```

profile of v0, /device:TPU:24, one launch (start us, length us, event | category | flops | bytes accessed | tf_op | source)
XLA Modules:
  0.0 415.8 jit_solution(14355555327161746175)
XLA Ops:
  7.2 1.4 fusion.13
  8.6 2.0 fusion.7
  12.3 1.0 concatenate.19
  13.3 28.1 %all-gather.3.cloned.1.call-done = bf16[256,2048]{1,0:T(8,128)(2,1)} async-done(((bf16[128,2048]{1,0:T(8,128)(2,1)}), bf16[256,2048]{1,0:T(8,128)(2,1)}) %all-gather.3.cloned.1.call-update) | async-done | bytes 1048592 | tf_op jit(solution)/shard_map/all_gather | solution.py:30
  41.4 2.8 convolution_convert_fusion.4
  44.9 0.9 pad_maximum_fusion.1
  45.8 1.9 collective-permute-start
  47.7 3.5 collective-permute-start.1
  51.2 4.5 %collective-permute-start.2 = (bf16[2,256,512]{2,1,0:T(8,128)(2,1)}, bf16[2,256,512]{2,1,0:T(8,128)(2,1)}, u32[]{:S(2)}, u32[]{:S(2)}) collective-permute-start(bf16[2,256,512]{2,1,0:T(8,128)(2,1)} %pad_maximum_fusion.1), channel_id=1, source_target_pairs={{0,8},{2,10},{4,12},{6,14},{8,16},{10,18},{12,20},{14,22},{16,24},... | collective-permute-start | bytes 1572872 | tf_op jit(solution)/shard_map/ppermute | solution.py:17
  55.6 4.9 %collective-permute-start.3 = (bf16[2,256,512]{2,1,0:T(8,128)(2,1)}, bf16[2,256,512]{2,1,0:T(8,128)(2,1)}, u32[]{:S(2)}, u32[]{:S(2)}) collective-permute-start(bf16[2,256,512]{2,1,0:T(8,128)(2,1)} %pad_maximum_fusion.1), channel_id=1, source_target_pairs={{0,16},{2,18},{4,20},{6,22},{8,24},{10,26},{12,28},{14,30},{16,32}... | collective-permute-start | bytes 1572872 | tf_op jit(solution)/shard_map/ppermute | solution.py:17
  60.6 2.5 collective-permute-start.4
  63.1 1.0 copy.23
  64.1 1.0 copy.22
  65.1 1.9 convolution_convert_fusion.3
  67.8 47.7 %all-gather.5.cloned.1.call-done = bf16[256,2048]{1,0:T(8,128)(2,1)} async-done(((bf16[128,2048]{1,0:T(8,128)(2,1)}), bf16[256,2048]{1,0:T(8,128)(2,1)}) %all-gather.5.cloned.1.call-update) | async-done | bytes 1048592 | tf_op jit(solution)/shard_map/all_gather | solution.py:31
  115.5 2.7 convolution_convert_fusion.2
  118.3 0.8 bitcast_convert_fusion
  119.1 1.3 collective-permute-start.5
  121.2 1.3 collective-permute-start.6
  122.5 1.4 pad_maximum_fusion
  124.0 1.1 maximum_maximum_fusion
  125.1 1.2 fusion.47
  126.3 2.4 copy.64
  128.7 2.3 copy.65
  131.0 2.5 copy.66
  133.5 2.4 copy.27
  135.9 2.4 copy.28
  138.3 2.4 copy.29
  140.6 2.4 copy.30
  143.0 2.4 copy.31
  145.4 2.4 copy.32
  147.8 12.3 %concatenate.18 = bf16[2,4,640,512]{2,3,1,0:T(8,128)(2,1)} concatenate(bf16[2,4,64,512]{2,3,1,0:T(8,128)(2,1)S(1)} %pad_maximum_fusion, bf16[2,4,64,512]{2,3,1,0:T(8,128)(2,1)} %copy.64, bf16[2,4,64,512]{2,3,1,0:T(8,128)(2,1)} %copy.65, bf16[2,4,64,512]{2,3,1,0:T(8,128)(2,1)} %copy.66, bf16[2,4,64,512]{2,3,1,0:T(8,128)(2,1)} %copy.27, bf16[2,4,64,512]{2,3,1,0:T(8,128)(2,1)} %copy.28, ...), dimensions={2} | concatenate | bytes 10485760 | tf_op jit(solution)/shard_map/concatenate | solution.py:58
  160.1 3.0 fusion.46
  163.2 0.8 fusion.49
  165.5 3.2 convolution_bitcast_fusion
  168.7 2.0 multiply_reduce_fusion
  171.5 3.3 multiply_bitcast_fusion
  174.8 7.2 %copy.42 = f32[4,640,4,128]{3,2,1,0:T(4,128)} copy(f32[4,640,4,128]{1,3,2,0:T(8,128)} %multiply_bitcast_fusion) | data formatting | bytes 10485760 | tf_op jit(solution)/shard_map/mul | solution.py:107
  182.0 7.4 %stack.30 = f32[1,4,10,64,512]{4,3,2,1,0:T(8,128)} reshape(f32[4,640,4,128]{3,2,1,0:T(4,128)} %copy.42) | data formatting | bytes 10485760 | tf_op jit(solution)/shard_map/stack | solution.py:113
  189.4 5.8 %constant_dynamic-update-slice_fusion.1 = f32[2,4,10,64,512]{4,3,2,1,0:T(8,128)} fusion(f32[1,4,10,64,512]{4,3,2,1,0:T(8,128)} %stack.30), kind=kLoop, calls=%fused_computation.73 | loop fusion | bytes 10485760
  195.2 7.2 %copy.44 = f32[4,640,4,128]{3,2,1,0:T(4,128)} copy(f32[4,640,4,128]{1,3,2,0:T(8,128)} %convolution_bitcast_fusion) | data formatting | bytes 10485760 | tf_op jit(solution)/shard_map/bhqk,bqhe->bkhe/transpose | solution.py:110
  202.4 7.4 %stack.31 = f32[1,4,10,64,512]{4,3,2,1,0:T(8,128)} reshape(f32[4,640,4,128]{3,2,1,0:T(4,128)} %copy.44) | data formatting | bytes 10485760 | tf_op jit(solution)/shard_map/stack | solution.py:113
  209.8 5.9 %constant_dynamic-update-slice_fusion = f32[2,4,10,64,512]{4,3,2,1,0:T(8,128)} fusion(f32[2,4,10,64,512]{4,3,2,1,0:T(8,128)} %constant_dynamic-update-slice_fusion.1, f32[1,4,10,64,512]{4,3,2,1,0:T(8,128)} %stack.31), kind=kLoop, calls=%fused_computation.72 | loop fusion | bytes 10485760 | tf_op jit(solution)/shard_map/stack | solution.py:113
  215.7 4.6 %slice_bitcast_fusion.8 = (f32[2,4,64,512]{3,2,1,0:T(8,128)S(1)}, f32[2,4,64,512]{3,2,1,0:T(8,128)S(1)}, f32[2,4,64,512]{3,2,1,0:T(8,128)S(1)}, f32[2,4,64,512]{...) fusion(f32[2,4,10,64,512]{4,3,2,1,0:T(8,128)} %constant_dynamic, ...), kind=kLoop, calls=%fused_computation.53 | loop fusion | bytes 14680064 | tf_op jit(solution)/shard_map/add | solution.py:116
  220.3 6.9 %collective-permute-start.13 = (f32[2,4,64,512]{3,2,1,0:T(8,128)S(1)}, f32[2,4,64,512]{3,2,1,0:T(8,128)S(1)}, u32[]{:S(2)}, u32[]{:S(2)}) collective-permute-start(f32[2,4,64,512]{3,2,1,0:T(8,128)S(1)} %get-tuple-element.43), channel_id=1, source_target_pairs={{128,0},{130,2},{132,4},{134,6},{136,8},{138,10},{140,12},{142,14}... | collective-permute-start | bytes 3145736 | tf_op jit(solution)/shard_map/ppermute | solution.py:17
  227.3 4.6 %collective-permute-start.12 = (f32[2,4,64,512]{3,2,1,0:T(8,128)S(1)}, f32[2,4,64,512]{3,2,1,0:T(8,128)S(1)}, u32[]{:S(2)}, u32[]{:S(2)}) collective-permute-start(f32[2,4,64,512]{3,2,1,0:T(8,128)S(1)} %get-tuple-element.44), channel_id=1, source_target_pairs={{64,0},{66,2},{68,4},{70,6},{72,8},{74,10},{76,12},{78,14},{80,16}... | collective-permute-start | bytes 3145736 | tf_op jit(solution)/shard_map/ppermute | solution.py:17
  231.9 1.9 collective-permute-start.11
  233.8 1.9 collective-permute-start.10
  235.8 1.9 collective-permute-start.9
  238.0 1.7 fusion.25
  239.6 1.4 fusion.15
  241.1 9.8 %collective-permute-done.13 = f32[2,4,64,512]{3,2,1,0:T(8,128)S(1)} collective-permute-done((f32[2,4,64,512]{3,2,1,0:T(8,128)S(1)}, f32[2,4,64,512]{3,2,1,0:T(8,128)S(1)}, u32[]{:S(2)}, u32[]{:S(2)}) %collective-permute-start.13) | collective-permute-done | bytes 1048608 | tf_op jit(solution)/shard_map/ppermute | solution.py:17
  250.8 1.9 collective-permute-start.8
  252.7 19.3 %collective-permute-done.12 = f32[2,4,64,512]{3,2,1,0:T(8,128)S(1)} collective-permute-done((f32[2,4,64,512]{3,2,1,0:T(8,128)S(1)}, f32[2,4,64,512]{3,2,1,0:T(8,128)S(1)}, u32[]{:S(2)}, u32[]{:S(2)}) %collective-permute-start.12) | collective-permute-done | bytes 1048608 | tf_op jit(solution)/shard_map/ppermute | solution.py:17
  272.1 62.4 %collective-permute-start.7 = (f32[2,4,64,512]{3,2,1,0:T(8,128)S(1)}, f32[2,4,64,512]{3,2,1,0:T(8,128)S(1)}, u32[]{:S(2)}, u32[]{:S(2)}) collective-permute-start(f32[2,4,64,512]{3,2,1,0:T(8,128)S(1)} %fusion.15), channel_id=1, source_target_pairs={{2,0},{4,2},{6,4},{8,6},{10,8},{12,10},{14,12},{16,14},{18,16},{20... | collective-permute-start | bytes 3145736 | tf_op jit(solution)/shard_map/ppermute | solution.py:17
  334.4 1.2 fusion.6
  336.7 9.8 %collective-permute-done.7 = f32[2,4,64,512]{3,2,1,0:T(8,128)S(1)} collective-permute-done((f32[2,4,64,512]{3,2,1,0:T(8,128)S(1)}, f32[2,4,64,512]{3,2,1,0:T(8,128)S(1)}, u32[]{:S(2)}, u32[]{:S(2)}) %collective-permute-start.7) | collective-permute-done | bytes 1048608 | tf_op jit(solution)/shard_map/ppermute | solution.py:17
  346.5 2.2 fusion.23
  350.4 1.7 fusion
  352.4 3.3 convolution_convert_fusion
  355.8 21.9 %reduce-scatter.5.cloned.1.call-done = bf16[128,2048]{1,0:T(8,128)(2,1)} async-done(((bf16[256,2048]{1,0:T(8,128)(2,1)}), bf16[128,2048]{1,0:T(8,128)(2,1)}) %reduce-scatter.5.cloned.1.call-update) | async-done | bytes 524304 | tf_op jit(solution)/shard_map/reduce_scatter | solution.py:133
  377.7 1.4 fusion.8
  379.1 27.5 %reduce-scatter.3.cloned.1.call-done = bf16[128,2048]{1,0:T(8,128)(2,1)} async-done(((bf16[256,2048]{1,0:T(8,128)(2,1)}), bf16[128,2048]{1,0:T(8,128)(2,1)}) %reduce-scatter.3.cloned.1.call-update) | async-done | bytes 524304 | tf_op jit(solution)/shard_map/reduce_scatter | solution.py:85
  406.6 2.7 fusion.12
  (91 shorter events, 9.4 us)
Async XLA Ops:
  7.2 57.9 %copy-start = (bf16[2048,512]{1,0:T(8,128)(2,1)S(1)}, bf16[2048,512]{1,0:T(8,128)(2,1)}, u32[]{:S(2)}) copy-start(bf16[2048,512]{1,0:T(8,128)(2,1)} %param.15) | copy-start | bytes 6291460
  7.2 34.2 %all-gather.3.cloned.1.call-start = ((), (), s32[]{:S(2)}) async-start(), calls=%async_computation.2 | async-start | bytes 1572864 | tf_op jit(solution)/shard_map/all_gather | solution.py:30
  10.7 104.9 %all-gather.5.cloned.1.call-start = ((), (), s32[]{:S(2)}) async-start(), calls=%async_computation.4 | async-start | bytes 1572864 | tf_op jit(solution)/shard_map/all_gather | solution.py:31
  11.4 366.3 %reduce-scatter.5.cloned.1.call-start = ((), (), s32[]{:S(2)}) async-start(), calls=%async_computation.5 | async-start | bytes 1572864 | tf_op jit(solution)/shard_map/reduce_scatter | solution.py:133
  41.4 2.8 copy-start.11
  41.4 2.8 copy-start.20
  44.2 19.9 %copy-start.7 = (bf16[256,512]{1,0:T(8,128)(2,1)}, bf16[256,512]{1,0:T(8,128)(2,1)S(1)}, u32[]{:S(2)}) copy-start(bf16[256,512]{1,0:T(8,128)(2,1)S(1)} %convolution_convert_fusion.4) | copy-start | bytes 786436
  44.9 22.1 %copy-start.9 = (bf16[256,512]{1,0:T(8,128)(2,1)}, bf16[256,512]{1,0:T(8,128)(2,1)S(1)}, u32[]{:S(2)}) copy-start(bf16[256,512]{1,0:T(8,128)(2,1)S(1)} %convolution_convert_fusion.5) | copy-start | bytes 786436
  45.8 73.4 %collective-permute-start = (bf16[2,256,512]{2,1,0:T(8,128)(2,1)}, bf16[2,256,512]{2,1,0:T(8,128)(2,1)}, u32[]{:S(2)}, u32[]{:S(2)}) collective-permute-start(bf16[2,256,512]{2,1,0:T(8,128)(2,1)} %pad_maximum_fusion.1), channel_id=1, source_target_pairs={{0,2},{2,4},{4,6},{6,8},{8,10},{10,12},{12,14},{14,16},{16,18},{18... | collective-permute-start | bytes 1572872 | tf_op jit(solution)/shard_map/ppermute | solution.py:17
  47.7 72.7 %collective-permute-start.1 = (bf16[2,256,512]{2,1,0:T(8,128)(2,1)}, bf16[2,256,512]{2,1,0:T(8,128)(2,1)S(1)}, u32[]{:S(2)}, u32[]{:S(2)}) collective-permute-start(bf16[2,256,512]{2,1,0:T(8,128)(2,1)} %pad_maximum_fusion.1), channel_id=1, source_target_pairs={{0,4},{2,6},{4,8},{6,10},{8,12},{10,14},{12,16},{14,18},{16,20},{1... | collective-permute-start | bytes 1572872 | tf_op jit(solution)/shard_map/ppermute | solution.py:17
  51.2 84.7 %collective-permute-start.2 = (bf16[2,256,512]{2,1,0:T(8,128)(2,1)}, bf16[2,256,512]{2,1,0:T(8,128)(2,1)}, u32[]{:S(2)}, u32[]{:S(2)}) collective-permute-start(bf16[2,256,512]{2,1,0:T(8,128)(2,1)} %pad_maximum_fusion.1), channel_id=1, source_target_pairs={{0,8},{2,10},{4,12},{6,14},{8,16},{10,18},{12,20},{14,22},{16,24},... | collective-permute-start | bytes 1572872 | tf_op jit(solution)/shard_map/ppermute | solution.py:17
  55.6 82.6 %collective-permute-start.3 = (bf16[2,256,512]{2,1,0:T(8,128)(2,1)}, bf16[2,256,512]{2,1,0:T(8,128)(2,1)}, u32[]{:S(2)}, u32[]{:S(2)}) collective-permute-start(bf16[2,256,512]{2,1,0:T(8,128)(2,1)} %pad_maximum_fusion.1), channel_id=1, source_target_pairs={{0,16},{2,18},{4,20},{6,22},{8,24},{10,26},{12,28},{14,30},{16,32}... | collective-permute-start | bytes 1572872 | tf_op jit(solution)/shard_map/ppermute | solution.py:17
  60.6 80.0 %collective-permute-start.4 = (bf16[2,256,512]{2,1,0:T(8,128)(2,1)}, bf16[2,256,512]{2,1,0:T(8,128)(2,1)}, u32[]{:S(2)}, u32[]{:S(2)}) collective-permute-start(bf16[2,256,512]{2,1,0:T(8,128)(2,1)} %pad_maximum_fusion.1), channel_id=1, source_target_pairs={{0,32},{2,34},{4,36},{6,38},{8,40},{10,42},{12,44},{14,46},{16,48}... | collective-permute-start | bytes 1572872 | tf_op jit(solution)/shard_map/ppermute | solution.py:17
  118.3 47.2 %copy-start.4 = (bf16[4,64,4,128]{3,2,1,0:T(4,128)(2,1)}, bf16[4,64,4,128]{3,2,1,0:T(4,128)(2,1)S(1)}, u32[]{:S(2)}) copy-start(bf16[4,64,4,128]{3,2,1,0:T(4,128)(2,1)S(1)} %reshape.218) | copy-start | bytes 786436
  118.3 5.7 %copy-start.8 = (bf16[256,512]{1,0:T(8,128)(2,1)S(1)}, bf16[256,512]{1,0:T(8,128)(2,1)}, u32[]{:S(2)}) copy-start(bf16[256,512]{1,0:T(8,128)(2,1)} %copy-done.7) | copy-start | bytes 786436
  118.3 5.7 %copy-start.10 = (bf16[256,512]{1,0:T(8,128)(2,1)S(1)}, bf16[256,512]{1,0:T(8,128)(2,1)}, u32[]{:S(2)}) copy-start(bf16[256,512]{1,0:T(8,128)(2,1)} %copy-done.9) | copy-start | bytes 786436
  119.1 23.9 %collective-permute-start.5 = (bf16[2,256,512]{2,1,0:T(8,128)(2,1)}, bf16[2,256,512]{2,1,0:T(8,128)(2,1)}, u32[]{:S(2)}, u32[]{:S(2)}) collective-permute-start(bf16[2,256,512]{2,1,0:T(8,128)(2,1)} %pad_maximum_fusion.1), channel_id=1, source_target_pairs={{0,64},{2,66},{4,68},{6,70},{8,72},{10,74},{12,76},{14,78},{16,80}... | collective-permute-start | bytes 1572872 | tf_op jit(solution)/shard_map/ppermute | solution.py:17
  120.4 0.8 copy-start.18
  121.2 24.2 %collective-permute-start.6 = (bf16[2,256,512]{2,1,0:T(8,128)(2,1)}, bf16[2,256,512]{2,1,0:T(8,128)(2,1)}, u32[]{:S(2)}, u32[]{:S(2)}) collective-permute-start(bf16[2,256,512]{2,1,0:T(8,128)(2,1)} %pad_maximum_fusion.1), channel_id=1, source_target_pairs={{0,128},{2,130},{4,132},{6,134},{8,136},{10,138},{12,140},{14,142}... | collective-permute-start | bytes 1572872 | tf_op jit(solution)/shard_map/ppermute | solution.py:17
  160.1 3.1 copy-start.6
  160.1 3.1 copy-start.17
  163.1 1.5 copy-start.1
  165.5 3.3 copy-start.13
  168.7 2.0 copy-start.5
  220.3 30.5 %collective-permute-start.13 = (f32[2,4,64,512]{3,2,1,0:T(8,128)S(1)}, f32[2,4,64,512]{3,2,1,0:T(8,128)S(1)}, u32[]{:S(2)}, u32[]{:S(2)}) collective-permute-start(f32[2,4,64,512]{3,2,1,0:T(8,128)S(1)} %get-tuple-element.43), channel_id=1, source_target_pairs={{128,0},{130,2},{132,4},{134,6},{136,8},{138,10},{140,12},{142,14}... | collective-permute-start | bytes 3145736 | tf_op jit(solution)/shard_map/ppermute | solution.py:17
  227.3 44.8 %collective-permute-start.12 = (f32[2,4,64,512]{3,2,1,0:T(8,128)S(1)}, f32[2,4,64,512]{3,2,1,0:T(8,128)S(1)}, u32[]{:S(2)}, u32[]{:S(2)}) collective-permute-start(f32[2,4,64,512]{3,2,1,0:T(8,128)S(1)} %get-tuple-element.44), channel_id=1, source_target_pairs={{64,0},{66,2},{68,4},{70,6},{72,8},{74,10},{76,12},{78,14},{80,16}... | collective-permute-start | bytes 3145736 | tf_op jit(solution)/shard_map/ppermute | solution.py:17
  231.9 104.7 %collective-permute-start.11 = (f32[2,4,64,512]{3,2,1,0:T(8,128)S(1)}, f32[2,4,64,512]{3,2,1,0:T(8,128)S(1)}, u32[]{:S(2)}, u32[]{:S(2)}) collective-permute-start(f32[2,4,64,512]{3,2,1,0:T(8,128)S(1)} %get-tuple-element.39), channel_id=1, source_target_pairs={{32,0},{34,2},{36,4},{38,6},{40,8},{42,10},{44,12},{46,14},{48,16}... | collective-permute-start | bytes 3145736 | tf_op jit(solution)/shard_map/ppermute | solution.py:17
  233.8 102.8 %collective-permute-start.10 = (f32[2,4,64,512]{3,2,1,0:T(8,128)S(1)}, f32[2,4,64,512]{3,2,1,0:T(8,128)S(1)}, u32[]{:S(2)}, u32[]{:S(2)}) collective-permute-start(f32[2,4,64,512]{3,2,1,0:T(8,128)S(1)} %get-tuple-element.40), channel_id=1, source_target_pairs={{16,0},{18,2},{20,4},{22,6},{24,8},{26,10},{28,12},{30,14},{32,16}... | collective-permute-start | bytes 3145736 | tf_op jit(solution)/shard_map/ppermute | solution.py:17
  235.8 100.9 %collective-permute-start.9 = (f32[2,4,64,512]{3,2,1,0:T(8,128)S(1)}, f32[2,4,64,512]{3,2,1,0:T(8,128)S(1)}, u32[]{:S(2)}, u32[]{:S(2)}) collective-permute-start(f32[2,4,64,512]{3,2,1,0:T(8,128)S(1)} %get-tuple-element.41), channel_id=1, source_target_pairs={{8,0},{10,2},{12,4},{14,6},{16,8},{18,10},{20,12},{22,14},{24,16},... | collective-permute-start | bytes 3145736 | tf_op jit(solution)/shard_map/ppermute | solution.py:17
  237.9 96.5 %copy-start.2 = (bf16[1,4,640,512]{2,3,1,0:T(8,128)(2,1)S(1)}, bf16[1,4,640,512]{2,3,1,0:T(8,128)(2,1)}, u32[]{:S(2)}) copy-start(bf16[1,4,640,512]{2,3,1,0:T(8,128)(2,1)} %copy-done.1) | copy-start | bytes 7864324
  250.8 85.8 %collective-permute-start.8 = (f32[2,4,64,512]{3,2,1,0:T(8,128)S(1)}, f32[2,4,64,512]{3,2,1,0:T(8,128)S(1)}, u32[]{:S(2)}, u32[]{:S(2)}) collective-permute-start(f32[2,4,64,512]{3,2,1,0:T(8,128)S(1)} %get-tuple-element.42), channel_id=1, source_target_pairs={{4,0},{6,2},{8,4},{10,6},{12,8},{14,10},{16,12},{18,14},{20,16},{2... | collective-permute-start | bytes 3145736 | tf_op jit(solution)/shard_map/ppermute | solution.py:17
  272.1 74.4 %collective-permute-start.7 = (f32[2,4,64,512]{3,2,1,0:T(8,128)S(1)}, f32[2,4,64,512]{3,2,1,0:T(8,128)S(1)}, u32[]{:S(2)}, u32[]{:S(2)}) collective-permute-start(f32[2,4,64,512]{3,2,1,0:T(8,128)S(1)} %fusion.15), channel_id=1, source_target_pairs={{2,0},{4,2},{6,4},{8,6},{10,8},{12,10},{14,12},{16,14},{18,16},{20... | collective-permute-start | bytes 3145736 | tf_op jit(solution)/shard_map/ppermute | solution.py:17
  336.6 12.2 %copy-start.12 = (bf16[2048,512]{1,0:T(8,128)(2,1)S(1)}, bf16[2048,512]{1,0:T(8,128)(2,1)}, u32[]{:S(2)}) copy-start(bf16[2048,512]{1,0:T(8,128)(2,1)} %param.16) | copy-start | bytes 6291460
  348.8 1.6 copy-start.14
  350.4 1.8 copy-start.16
  352.1 25.6 %copy-start.3 = (bf16[128,2048]{1,0:T(8,128)(2,1)S(1)}, bf16[128,2048]{1,0:T(8,128)(2,1)}, u32[]{:S(2)}) copy-start(bf16[128,2048]{1,0:T(8,128)(2,1)} %param.13) | copy-start | bytes 1572868
  352.1 25.6 %copy-start.19 = (f32[2048]{0:T(1024)S(1)}, f32[2048]{0:T(1024)}, u32[]{:S(2)}) copy-start(f32[2048]{0:T(1024)} %param.14) | copy-start | bytes 24580
  352.2 54.4 %reduce-scatter.3.cloned.1.call-start = ((), (), s32[]{:S(2)}) async-start(), calls=%async_computation.3 | async-start | bytes 1572864 | tf_op jit(solution)/shard_map/reduce_scatter | solution.py:85
  352.4 54.2 %copy-start.15 = (bf16[128,2048]{1,0:T(8,128)(2,1)S(1)}, bf16[128,2048]{1,0:T(8,128)(2,1)}, u32[]{:S(2)}) copy-start(bf16[128,2048]{1,0:T(8,128)(2,1)} %param.19) | copy-start | bytes 1572868
Sparse Core Ops, SparseCore 0:
  10.8 30.5 all-gather.2
  43.2 72.2 all-gather.4
  352.2 25.4 reduce-scatter.4
  380.2 26.3 reduce-scatter.2
where the time goes:
time: 420 us; the launch traced here: 416 us
  waiting for transfers between devices  165 us (39%)
  starting transfers between devices  102 us (24%)
  local copies, waits for them, and re-layouts  91.2 us (22%)
  matrix products  25.9 us (6%)
  other arithmetic  17.9 us (4%)
  between operations  14.4 us (3%)
    ppermute x14, starting transfers between devices, shifted(): return lax.ppermute(value, axis, pairs)  101 us
    all_gather x1, waiting for transfers between devices, per_device(): lax.all_gather(out_grad, 'tp', axis=0, tiled=True)  47.7 us
    ppermute x14, waiting for transfers between devices, shifted(): return lax.ppermute(value, axis, pairs)  39 us
    all_gather x1, waiting for transfers between devices, per_device(): lax.all_gather(normed_rows, 'tp', axis=0, tiled=True)  28.1 us
    reduce_scatter x1, waiting for transfers between devices, per_device(): lax.psum_scatter(jnp.dot(mixed_rows, w_out, preferred_element_type=jnp.fl...  27.5 us
    reduce_scatter x1, waiting for transfers between devices, per_device(): lax.psum_scatter(grad_normed.astype(jnp.bfloat16), 'tp', scatter_dimensio...  21.9 us
    another operation x3, local copies, waits for them, and re-layouts, per_device(): jnp.stack([grad_keys, grad_values])  20.7 us
    unnamed x46, local copies, waits for them, and re-layouts  15.4 us
  transfers between devices with their start and end apart: 18, of which 7 were waited for; matrix products, arithmetic and copies ran while one was open for 11% of the time, Pallas kernels for 0%

commit v1 on v0

v1 whole, which is shorter than its diff:
```python
import functools

import jax
import jax.numpy as jnp
from jax import lax
from jax.experimental import pallas as pl
from jax.experimental.pallas import tpu as pltpu
from jax.sharding import PartitionSpec as P

HD = 128
BLOCK = 64
NEG = -1e30
EPS = 1e-06
F32 = jnp.float32
BF16 = jnp.bfloat16


def shifted(value, by):
    size = lax.axis_size("seq")
    pairs = [(i, i + by) for i in range(size) if 0 <= i + by < size]
    return lax.ppermute(value, "seq", pairs)


def swap_tp(value):
    return lax.ppermute(value, "tp", [(0, 1), (1, 0)])


def attn_kernel(n_far, groups, tp_ref, bias_ref, *refs):
    refs = list(refs)
    q_refs = [refs.pop(0) for _ in range(2)]
    g_refs = [refs.pop(0) for _ in range(2)]
    kv_refs = [refs.pop(0) for _ in range(2)]
    fetched = [[refs.pop(0) for _ in range(n)] for n in groups]
    mixed_ref, dq_ref, own_ref, near_ref = [refs.pop(0) for _ in range(4)]
    far_refs = [refs.pop(0) for _ in range(n_far)]
    ext, acc = refs
    turn = 2 * tp_ref[0]
    factor = HD ** (-0.5)

    def piece(pieces, which, slot):
        per = 4 // len(pieces)
        return pieces[slot // per][which, (slot % per) * BLOCK : (slot % per + 1) * BLOCK, :]

    blocks = [(slot + turn) % 4 for slot in range(4)]
    for slot in range(4):
        for which in range(2):
            ext[which, blocks[slot]] = piece(fetched[0], which, slot)
            ext[which, 4 + blocks[slot]] = piece(kv_refs, which, slot)
    acc[...] = jnp.zeros_like(acc)
    causal = lax.broadcasted_iota(jnp.int32, (BLOCK, BLOCK), 0) >= lax.broadcasted_iota(
        jnp.int32, (BLOCK, BLOCK), 1
    )
    causal_bias = jnp.where(causal, 0.0, NEG).astype(F32)
    nn = (((1,), (0,)), ((), ()))
    nt = (((1,), (1,)), ((), ()))
    tn = (((0,), (0,)), ((), ()))

    def dot(a, b, dims):
        return lax.dot_general(a, b, dims, preferred_element_type=F32)

    for slot in range(4):
        half, rows = slot // 2, slice((slot % 2) * BLOCK, (slot % 2 + 1) * BLOCK)
        out_rows = slice(slot * BLOCK, (slot + 1) * BLOCK)
        base = 4 + blocks[slot]
        keys, values = [
            jnp.concatenate(
                [piece(kv_refs, which, slot)]
                + [ext[which, base - d] for d in (1, 2, 4)]
                + [piece(fetched[s], which, slot) for s in range(1, n_far + 1)],
                axis=0,
            )
            for which in range(2)
        ]
        query = q_refs[half][rows, :]
        grad = g_refs[half][rows, :]
        score = dot(query, keys, nt) * factor + bias_ref[slot]
        score = jnp.concatenate([score[:, :BLOCK] + causal_bias, score[:, BLOCK:]], axis=1)
        peak = jnp.max(score, axis=-1, keepdims=True)
        weight = jnp.exp(score - peak)
        total = jnp.sum(weight, axis=-1, keepdims=True)
        prob = weight * (1.0 / total)
        prob_b = prob.astype(BF16)
        mixed = dot(prob_b, values, nn).astype(BF16)
        mixed_ref[out_rows, :] = mixed
        inner = jnp.sum(mixed.astype(F32) * grad.astype(F32), axis=-1, keepdims=True)
        grad_prob = dot(grad, values, nt)
        grad_score = (prob * (grad_prob - inner)).astype(BF16)
        dq_ref[out_rows, :] = (dot(grad_score, keys, nn) * factor).astype(BF16)
        grads = [dot(grad_score, query, tn) * factor, dot(prob_b, grad, tn)]
        for which in range(2):
            for at, d in enumerate((0, 1, 2, 4)):
                acc[which, base - d] += grads[which][at * BLOCK : (at + 1) * BLOCK]
            for s in range(n_far):
                far_refs[s][which, out_rows, :] = grads[which][
                    (4 + s) * BLOCK : (5 + s) * BLOCK
                ].astype(BF16)
    for slot in range(4):
        out_rows = slice(slot * BLOCK, (slot + 1) * BLOCK)
        for which in range(2):
            own_ref[which, out_rows, :] = acc[which, 4 + blocks[slot]]
            near_ref[which, out_rows, :] = acc[which, blocks[slot]].astype(BF16)


def attention(turn, bias, queries, grads, key_values, fetched):
    width = queries[0].shape[1]
    heads = width // HD
    n_far = len(fetched) - 1
    groups = tuple(len(f) for f in fetched)
    rows = 2 * queries[0].shape[0]
    flat = [a for f in fetched for a in f]

    def spec(a):
        if a.ndim == 2:
            return pl.BlockSpec((a.shape[0], HD), lambda h, t: (0, h))
        return pl.BlockSpec((a.shape[0], a.shape[1], HD), lambda h, t: (0, 0, h))

    row_out = jax.ShapeDtypeStruct((rows, width), BF16)
    pair_out = jax.ShapeDtypeStruct((2, rows, width), BF16)
    outs = [row_out, row_out, jax.ShapeDtypeStruct((2, rows, width), F32)] + [pair_out] * (1 + n_far)
    operands = [*queries, *grads, *key_values, *flat]
    return pl.pallas_call(
        functools.partial(attn_kernel, n_far, groups),
        out_shape=outs,
        grid_spec=pltpu.PrefetchScalarGridSpec(
            num_scalar_prefetch=1,
            grid=(heads,),
            in_specs=[pl.BlockSpec(bias.shape, lambda h, t: (0, 0, 0))] + [spec(a) for a in operands],
            out_specs=[spec(a) for a in outs],
            scratch_shapes=[
                pltpu.VMEM((2, 8, BLOCK, HD), BF16),
                pltpu.VMEM((2, 8, BLOCK, HD), F32),
            ],
        ),
        compiler_params=pltpu.CompilerParams(vmem_limit_bytes=32 * 2**20),
        cost_estimate=pl.CostEstimate(
            flops=6 * 2 * rows * bias.shape[2] * width,
            bytes_accessed=10 * 2**20,
            transcendentals=rows * bias.shape[2] * heads,
        ),
        name="attention",
    )(turn, bias, *operands)


def matmul(a, b):
    return jnp.dot(a, b, preferred_element_type=F32)


def matmul_t(a, b):
    return lax.dot_general(a, b, (((1,), (1,)), ((), ())), preferred_element_type=F32)


def per_device(series, norm_gain, w_query, w_key, w_value, w_out, out_grad):
    levels = lax.axis_size("seq").bit_length() - 1
    half = series.shape[0]
    blocks = 2 * half // BLOCK
    tp_index = lax.axis_index("tp")
    slots = jnp.arange(blocks, dtype=jnp.int32)
    global_block = lax.axis_index("seq") * blocks + (slots + 2 * tp_index) % blocks
    distances = [1, 2, 4] + [blocks * 2**s for s in range(1, levels)]
    reach = jnp.repeat(jnp.array([0] + distances, jnp.int32), BLOCK)
    bias = jnp.where(global_block[:, None] >= reach[None], 0.0, NEG).astype(F32)[:, None, :]

    series_f = series.astype(F32)
    inv_rms = lax.rsqrt(jnp.mean(series_f * series_f, axis=-1, keepdims=True) + EPS)
    unit_rows = series_f * inv_rms
    normed = (unit_rows * norm_gain).astype(BF16)
    normed_other = swap_tp(normed)
    out_grad_other = swap_tp(out_grad)

    def project(rows):
        query = matmul(rows, w_query).astype(BF16)
        pair = jnp.stack([matmul(rows, w_key).astype(BF16), matmul(rows, w_value).astype(BF16)])
        return query, pair

    query_own, kv_own = project(normed)
    early = (3, 2, 1)
    first = {s: shifted(kv_own, 2**s) for s in early}
    query_other, kv_other = project(normed_other)
    second = {s: shifted(kv_other, 2**s) for s in early}
    kv_all = jnp.concatenate([kv_own, kv_other], axis=1)
    fetched = [
        (first[s], second[s]) if s in early else (shifted(kv_all, 2**s),) for s in range(levels)
    ]
    grad_own = matmul_t(out_grad, w_out).astype(BF16)
    grad_other = matmul_t(out_grad_other, w_out).astype(BF16)
    mixed, grad_query, own_grads, *returns = attention(
        tp_index.astype(jnp.int32)[None],
        bias,
        (query_own, query_other),
        (grad_own, grad_other),
        (kv_own, kv_other),
        fetched,
    )
    returned = [shifted(returns[s], -(2**s)) for s in range(levels)]
    attn_other = swap_tp(matmul(mixed[half:], w_out).astype(BF16))
    attn_rows = matmul(mixed[:half], w_out) + attn_other.astype(F32)
    layer_out = (series_f + attn_rows).astype(BF16)

    for part in returned:
        own_grads = own_grads + part.astype(F32)
    grad_kv = own_grads.astype(BF16)

    def back(rows):
        return (
            matmul_t(grad_query[rows], w_query)
            + matmul_t(grad_kv[0, rows], w_key)
            + matmul_t(grad_kv[1, rows], w_value)
        )

    normed_grad_other = swap_tp(back(slice(half, None)).astype(BF16))
    normed_grad = back(slice(0, half)) + normed_grad_other.astype(F32)
    scaled = normed_grad * norm_gain
    series_grad = out_grad.astype(F32) + inv_rms * (
        scaled - unit_rows * jnp.mean(scaled * unit_rows, axis=-1, keepdims=True)
    )
    return (layer_out, series_grad.astype(BF16))


def solution(mesh):
    rows = P(("seq", "tp"), None)
    columns = P(None, "tp")
    in_specs = (rows, P(), columns, columns, columns, P("tp", None), rows)
    return jax.shard_map(
        per_device, mesh=mesh, in_specs=in_specs, out_specs=(rows, rows), check_vma=False
    )
```

time: 420 us -> 229 us (0.55)
  the two profiles are of different devices: /device:TPU:24 before, /device:TPU:238 now
where the time goes in v1:
time: 229 us; the launch traced here: 228 us
  starting transfers between devices  99.5 us (43%)
  waiting for transfers between devices  85.1 us (37%)
  matrix products  21.2 us (9%)
  Pallas kernels  14.6 us (6%)
  other arithmetic  6.39 us (3%)
    ppermute x17, starting transfers between devices, shifted(): return lax.ppermute(value, 'seq', pairs)  95.4 us
    ppermute x17, waiting for transfers between devices, shifted(): return lax.ppermute(value, 'seq', pairs)  64.5 us
    ppermute x4, waiting for transfers between devices, swap_tp(): return lax.ppermute(value, 'tp', [(0, 1), (1, 0)])  20.6 us
    pallas_call x1, Pallas kernels, attention(): pl.pallas_call(functools.partial(attn_kernel, n_far, groups), out_shape=o...  14.6 us
    dot_general x8, matrix products, matmul(): return jnp.dot(a, b, preferred_element_type=F32)  11.6 us
    dot_general x8, matrix products, matmul_t(): lax.dot_general(a, b, (((1,), (1,)), ((), ())), preferred_element_type=F32)  9.58 us
  transfers between devices with their start and end apart: 21, of which 6 were waited for; matrix products, arithmetic and copies ran while one was open for 8% of the time, Pallas kernels for 0%

profile of v1, /device:TPU:238, one launch (start us, length us, event | category | flops | bytes accessed | tf_op | source)
XLA Modules:
  0.0 228.2 jit_solution(13740617295601996177)
XLA Ops:
  0.6 0.0 copy-start
  0.6 0.0 copy-start.2
  0.7 1.4 fusion.20
  2.1 2.0 fusion.14
  4.1 2.2 fusion.11
  6.3 0.0 copy-start.7
  6.3 1.5 fusion.10
  7.9 4.6 %collective-permute-start.7 = (bf16[2,128,512]{2,1,0:T(8,128)(2,1)S(1)}, bf16[2,128,512]{2,1,0:T(8,128)(2,1)S(1)}, u32[]{:S(2)}, u32[]{:S(2)}) collective-permute-start(bf16[2,128,512]{2,1,0:T(8,128)(2,1)S(1)} %pad_maximum_fusion.refs_4_), channel_id=1, source_target_pairs={{0,16},{2,18},{4,20},{6,22},{8,24},{10,26},{12,28},{14,30},{16,32}... | collective-permute-start | bytes 786440 | tf_op jit(solution)/shard_map/ppermute | solution.py:21
  12.5 5.5 %collective-permute-start.5 = (bf16[2,128,512]{2,1,0:T(8,128)(2,1)S(1)}, bf16[2,128,512]{2,1,0:T(8,128)(2,1)S(1)}, u32[]{:S(2)}, u32[]{:S(2)}) collective-permute-start(bf16[2,128,512]{2,1,0:T(8,128)(2,1)S(1)} %pad_maximum_fusion.refs_4_), channel_id=1, source_target_pairs={{0,8},{2,10},{4,12},{6,14},{8,16},{10,18},{12,20},{14,22},{16,24},... | collective-permute-start | bytes 786440 | tf_op jit(solution)/shard_map/ppermute | solution.py:21
  18.0 2.9 %collective-permute-start.3 = (bf16[2,128,512]{2,1,0:T(8,128)(2,1)S(1)}, bf16[2,128,512]{2,1,0:T(8,128)(2,1)S(1)}, u32[]{:S(2)}, u32[]{:S(2)}) collective-permute-start(bf16[2,128,512]{2,1,0:T(8,128)(2,1)S(1)} %pad_maximum_fusion.refs_4_), channel_id=1, source_target_pairs={{0,4},{2,6},{4,8},{6,10},{8,12},{10,14},{12,16},{14,18},{16,20},{1... | collective-permute-start | bytes 786440 | tf_op jit(solution)/shard_map/ppermute | solution.py:21
  20.9 1.2 collective-permute-start
  22.1 2.4 %collective-permute-start.1 = (bf16[128,2048]{1,0:T(8,128)(2,1)}, bf16[128,2048]{1,0:T(8,128)(2,1)}, u32[]{:S(2)}, u32[]{:S(2)}) collective-permute-start(bf16[128,2048]{1,0:T(8,128)(2,1)} %param.14), channel_id=1, source_target_pairs={{0,1},{1,0},{2,3},{3,2},{4,5},{5,4},{6,7},{7,6},{8,9},{9,8},{10,11... | collective-permute-start | bytes 1572872 | tf_op jit(solution)/shard_map/ppermute | solution.py:25
  24.6 0.1 broadcast_in_dim.21
  24.6 0.1 ge.23
  24.7 2.7 %convolution_convert_fusion.6.refs_2_ = bf16[128,512]{1,0:T(8,128)(2,1)S(1)} fusion(bf16[128,2048]{1,0:T(8,128)(2,1)} %param.14, bf16[512,2048]{1,0:T(8,128)(2,1)} %param.13), kind=kOutput, calls=%fused_computation.21 | convolution fusion | flops 268500992 | bytes 2752512 | tf_op jit(solution)/shard_map/dot_general | solution.py:149
  27.5 0.0 copy-start.3
  27.5 1.6 convolution_convert_fusion.8.refs_0_
  29.1 8.6 %collective-permute-done = bf16[128,2048]{1,0:T(8,128)(2,1)} collective-permute-done((bf16[128,2048]{1,0:T(8,128)(2,1)}, bf16[128,2048]{1,0:T(8,128)(2,1)}, u32[]{:S(2)}, u32[]{:S(2)}) %collective-permute-start) | collective-permute-done | bytes 524320 | tf_op jit(solution)/shard_map/ppermute | solution.py:25
  37.7 1.5 fusion.13
  39.2 1.5 fusion.12
  40.7 0.0 copy-start.4
  40.8 4.3 %collective-permute-start.8 = (bf16[2,128,512]{2,1,0:T(8,128)(2,1)S(1)}, bf16[2,128,512]{2,1,0:T(8,128)(2,1)S(1)}, u32[]{:S(2)}, u32[]{:S(2)}) collective-permute-start(bf16[2,128,512]{2,1,0:T(8,128)(2,1)S(1)} %pad_maximum_fusion.1.refs_5_), channel_id=1, source_target_pairs={{0,16},{2,18},{4,20},{6,22},{8,24},{10,26},{12,28},{14,30},{16,32}... | collective-permute-start | bytes 786440 | tf_op jit(solution)/shard_map/ppermute | solution.py:21
  45.1 0.1 compare_select_fusion.bias_ref
  45.2 5.7 %collective-permute-start.6 = (bf16[2,128,512]{2,1,0:T(8,128)(2,1)S(1)}, bf16[2,128,512]{2,1,0:T(8,128)(2,1)S(1)}, u32[]{:S(2)}, u32[]{:S(2)}) collective-permute-start(bf16[2,128,512]{2,1,0:T(8,128)(2,1)S(1)} %pad_maximum_fusion.1.refs_5_), channel_id=1, source_target_pairs={{0,8},{2,10},{4,12},{6,14},{8,16},{10,18},{12,20},{14,22},{16,24},... | collective-permute-start | bytes 786440 | tf_op jit(solution)/shard_map/ppermute | solution.py:21
  50.8 0.0 collective-permute-done.5.refs_9_
  50.9 1.3 collective-permute-start.11
  52.2 0.0 collective-permute-done.3.refs_7_
  52.2 3.2 %collective-permute-start.10 = (bf16[2,256,512]{2,1,0:T(8,128)(2,1)S(1)}, bf16[2,256,512]{2,1,0:T(8,128)(2,1)S(1)}, u32[]{:S(2)}, u32[]{:S(2)}) collective-permute-start(bf16[2,256,512]{2,1,0:T(8,128)(2,1)S(1)} %maximum_maximum_fusion), channel_id=1, source_target_pairs={{0,64},{2,66},{4,68},{6,70},{8,72},{10,74},{12,76},{14,78},{16,80}... | collective-permute-start | bytes 1572872 | tf_op jit(solution)/shard_map/ppermute | solution.py:21
  55.4 0.0 collective-permute-done.1
  55.4 2.0 collective-permute-start.9
  57.4 0.0 collective-permute-done.8.refs_12_
  57.4 1.9 collective-permute-start.2
  59.4 1.5 convolution_convert_fusion.7.refs_1_
  60.9 16.5 %collective-permute-start.4 = (bf16[2,128,512]{2,1,0:T(8,128)(2,1)S(1)}, bf16[2,128,512]{2,1,0:T(8,128)(2,1)S(1)}, u32[]{:S(2)}, u32[]{:S(2)}) collective-permute-start(bf16[2,128,512]{2,1,0:T(8,128)(2,1)S(1)} %pad_maximum_fusion.1.refs_5_), channel_id=1, source_target_pairs={{0,4},{2,6},{4,8},{6,10},{8,12},{10,14},{12,16},{14,18},{16,20},{1... | collective-permute-start | bytes 786440 | tf_op jit(solution)/shard_map/ppermute | solution.py:21
  77.3 1.9 convolution_convert_fusion.5.refs_3_
  79.2 4.9 %collective-permute-done.4.refs_8_ = bf16[2,128,512]{2,1,0:T(8,128)(2,1)S(1)} collective-permute-done((bf16[2,128,512]{2,1,0:T(8,128)(2,1)S(1)}, bf16[2,128,512]{2,1,0:T(8,128)(2,1)S(1)}, u32[]{:S(2)}, u32[]{:S(2)}) %collective-permute-start.4) | collective-permute-done | bytes 262176 | tf_op jit(solution)/shard_map/ppermute | solution.py:21
  84.1 0.0 collective-permute-done.11.refs_15_
  84.1 0.0 collective-permute-done.10.refs_14_
  84.1 14.6 %attention.1 = (bf16[256,512]{1,0:T(8,128)(2,1)S(1)}, bf16[256,512]{1,0:T(8,128)(2,1)S(1)}, f32[2,256,512]{2,1,0:T(8,128)S(1)}, bf16[2,256,512]{2,1,0:T(8,128)(2...) custom-call(s32[1]{0:T(128)} %bitcast.tp_ref, ...), custom_call_target="tpu_custom_call" | custom-call | flops 1006632960 | bytes 10485760 | tf_op jit(solution)/shard_map/attention/pallas_call | solution.py:121
  98.7 1.9 collective-permute-start.13
  100.6 1.9 collective-permute-start.14
  102.5 5.4 %collective-permute-start.15 = (bf16[2,256,512]{2,1,0:T(8,128)(2,1)S(1)}, bf16[2,256,512]{2,1,0:T(8,128)(2,1)S(1)}, u32[]{:S(2)}, u32[]{:S(2)}) collective-permute-start(bf16[2,256,512]{2,1,0:T(8,128)(2,1)S(1)} %get-tuple-element.17), channel_id=1, source_target_pairs={{8,0},{10,2},{12,4},{14,6},{16,8},{18,10},{20,12},{22,14},{24,16},... | collective-permute-start | bytes 1572872 | tf_op jit(solution)/shard_map/ppermute | solution.py:21
  107.9 14.6 %collective-permute-start.16 = (bf16[2,256,512]{2,1,0:T(8,128)(2,1)S(1)}, bf16[2,256,512]{2,1,0:T(8,128)(2,1)S(1)}, u32[]{:S(2)}, u32[]{:S(2)}) collective-permute-start(bf16[2,256,512]{2,1,0:T(8,128)(2,1)S(1)} %get-tuple-element.18), channel_id=1, source_target_pairs={{16,0},{18,2},{20,4},{22,6},{24,8},{26,10},{28,12},{30,14},{32,16}... | collective-permute-start | bytes 1572872 | tf_op jit(solution)/shard_map/ppermute | solution.py:21
  122.5 20.6 %collective-permute-start.17 = (bf16[2,256,512]{2,1,0:T(8,128)(2,1)S(1)}, bf16[2,256,512]{2,1,0:T(8,128)(2,1)S(1)}, u32[]{:S(2)}, u32[]{:S(2)}) collective-permute-start(bf16[2,256,512]{2,1,0:T(8,128)(2,1)S(1)} %get-tuple-element.19), channel_id=1, source_target_pairs={{32,0},{34,2},{36,4},{38,6},{40,8},{42,10},{44,12},{46,14},{48,16}... | collective-permute-start | bytes 1572872 | tf_op jit(solution)/shard_map/ppermute | solution.py:21
  143.1 1.9 collective-permute-start.18
  145.0 18.1 %collective-permute-done.14 = bf16[2,256,512]{2,1,0:T(8,128)(2,1)S(1)} collective-permute-done((bf16[2,256,512]{2,1,0:T(8,128)(2,1)S(1)}, bf16[2,256,512]{2,1,0:T(8,128)(2,1)S(1)}, u32[]{:S(2)}, u32[]{:S(2)}) %collective-permute-start.14) | collective-permute-done | bytes 524320 | tf_op jit(solution)/shard_map/ppermute | solution.py:21
  163.1 1.3 collective-permute-start.19
  164.4 0.4 convolution_convert_fusion
  164.8 24.1 %collective-permute-done.15 = bf16[2,256,512]{2,1,0:T(8,128)(2,1)S(1)} collective-permute-done((bf16[2,256,512]{2,1,0:T(8,128)(2,1)S(1)}, bf16[2,256,512]{2,1,0:T(8,128)(2,1)S(1)}, u32[]{:S(2)}, u32[]{:S(2)}) %collective-permute-start.15) | collective-permute-done | bytes 524320 | tf_op jit(solution)/shard_map/ppermute | solution.py:21
  189.0 17.4 %collective-permute-done.18 = bf16[2,256,512]{2,1,0:T(8,128)(2,1)S(1)} collective-permute-done((bf16[2,256,512]{2,1,0:T(8,128)(2,1)S(1)}, bf16[2,256,512]{2,1,0:T(8,128)(2,1)S(1)}, u32[]{:S(2)}, u32[]{:S(2)}) %collective-permute-start.18) | collective-permute-done | bytes 524320 | tf_op jit(solution)/shard_map/ppermute | solution.py:21
  206.4 0.6 add_convert_fusion
  206.9 0.8 fusion.21
  207.8 0.8 fusion.22
  208.6 0.8 fusion.6
  209.4 0.5 collective-permute-start.20
  209.8 0.8 fusion.23
  210.6 0.0 copy-start.5
  210.7 0.8 fusion.24
  211.5 0.0 copy-start.6
  211.5 0.2 copy-done.5
  211.7 1.3 fusion.5
  213.0 12.0 %collective-permute-done.20 = bf16[128,2048]{1,0:T(8,128)(2,1)S(1)} collective-permute-done((bf16[128,2048]{1,0:T(8,128)(2,1)S(1)}, bf16[128,2048]{1,0:T(8,128)(2,1)S(1)}, u32[]{:S(2)}, u32[]{:S(2)}) %collective-permute-start.20) | collective-permute-done | bytes 524320 | tf_op jit(solution)/shard_map/ppermute | solution.py:25
  225.0 1.0 fusion.15
  226.0 2.2 fusion.19
  (24 shorter events, 0.2 us)
Async XLA Ops:
  0.6 26.8 %copy-start = (bf16[2048,512]{1,0:T(8,128)(2,1)S(1)}, bf16[2048,512]{1,0:T(8,128)(2,1)}, u32[]{:S(2)}) copy-start(bf16[2048,512]{1,0:T(8,128)(2,1)} %param.10) | copy-start | bytes 6291460
  0.6 5.7 %copy-start.2 = (bf16[2048,512]{1,0:T(8,128)(2,1)S(1)}, bf16[2048,512]{1,0:T(8,128)(2,1)}, u32[]{:S(2)}) copy-start(bf16[2048,512]{1,0:T(8,128)(2,1)} %param.11) | copy-start | bytes 6291460
  6.3 18.2 %copy-start.7 = (s32[10]{0:T(128)S(1)}, s32[10]{0:T(128)}, u32[]{:S(2)}) copy-start(s32[10]{0:T(128)} %constant.37.clone) | copy-start | bytes 124
  7.9 37.3 %collective-permute-start.7 = (bf16[2,128,512]{2,1,0:T(8,128)(2,1)S(1)}, bf16[2,128,512]{2,1,0:T(8,128)(2,1)S(1)}, u32[]{:S(2)}, u32[]{:S(2)}) collective-permute-start(bf16[2,128,512]{2,1,0:T(8,128)(2,1)S(1)} %pad_maximum_fusion.refs_4_), channel_id=1, source_target_pairs={{0,16},{2,18},{4,20},{6,22},{8,24},{10,26},{12,28},{14,30},{16,32}... | collective-permute-start | bytes 786440 | tf_op jit(solution)/shard_map/ppermute | solution.py:21
  12.5 38.4 %collective-permute-start.5 = (bf16[2,128,512]{2,1,0:T(8,128)(2,1)S(1)}, bf16[2,128,512]{2,1,0:T(8,128)(2,1)S(1)}, u32[]{:S(2)}, u32[]{:S(2)}) collective-permute-start(bf16[2,128,512]{2,1,0:T(8,128)(2,1)S(1)} %pad_maximum_fusion.refs_4_), channel_id=1, source_target_pairs={{0,8},{2,10},{4,12},{6,14},{8,16},{10,18},{12,20},{14,22},{16,24},... | collective-permute-start | bytes 786440 | tf_op jit(solution)/shard_map/ppermute | solution.py:21
  18.0 34.2 %collective-permute-start.3 = (bf16[2,128,512]{2,1,0:T(8,128)(2,1)S(1)}, bf16[2,128,512]{2,1,0:T(8,128)(2,1)S(1)}, u32[]{:S(2)}, u32[]{:S(2)}) collective-permute-start(bf16[2,128,512]{2,1,0:T(8,128)(2,1)S(1)} %pad_maximum_fusion.refs_4_), channel_id=1, source_target_pairs={{0,4},{2,6},{4,8},{6,10},{8,12},{10,14},{12,16},{14,18},{16,20},{1... | collective-permute-start | bytes 786440 | tf_op jit(solution)/shard_map/ppermute | solution.py:21
  20.9 16.8 %collective-permute-start = (bf16[128,2048]{1,0:T(8,128)(2,1)}, bf16[128,2048]{1,0:T(8,128)(2,1)}, u32[]{:S(2)}, u32[]{:S(2)}) collective-permute-start(bf16[128,2048]{1,0:T(8,128)(2,1)} %fusion.14), channel_id=1, source_target_pairs={{0,1},{1,0},{2,3},{3,2},{4,5},{5,4},{6,7},{7,6},{8,9},{9,8},{10,11... | collective-permute-start | bytes 1572872 | tf_op jit(solution)/shard_map/ppermute | solution.py:25
  22.1 33.2 %collective-permute-start.1 = (bf16[128,2048]{1,0:T(8,128)(2,1)}, bf16[128,2048]{1,0:T(8,128)(2,1)}, u32[]{:S(2)}, u32[]{:S(2)}) collective-permute-start(bf16[128,2048]{1,0:T(8,128)(2,1)} %param.14), channel_id=1, source_target_pairs={{0,1},{1,0},{2,3},{3,2},{4,5},{5,4},{6,7},{7,6},{8,9},{9,8},{10,11... | collective-permute-start | bytes 1572872 | tf_op jit(solution)/shard_map/ppermute | solution.py:25
  24.7 13.0 %copy-start.1 = (bf16[2048,512]{1,0:T(8,128)(2,1)S(1)}, bf16[2048,512]{1,0:T(8,128)(2,1)}, u32[]{:S(2)}) copy-start(bf16[2048,512]{1,0:T(8,128)(2,1)} %param.12) | copy-start | bytes 6291460
  27.5 11.7 %copy-start.3 = (bf16[2048,512]{1,0:T(8,128)(2,1)S(1)}, bf16[2048,512]{1,0:T(8,128)(2,1)}, u32[]{:S(2)}) copy-start(bf16[2048,512]{1,0:T(8,128)(2,1)} %param.11) | copy-start | bytes 6291460
  40.7 36.6 %copy-start.4 = (bf16[512,2048]{1,0:T(8,128)(2,1)S(1)}, bf16[512,2048]{1,0:T(8,128)(2,1)}, u32[]{:S(2)}) copy-start(bf16[512,2048]{1,0:T(8,128)(2,1)} %param.13) | copy-start | bytes 6291460
  40.8 16.7 %collective-permute-start.8 = (bf16[2,128,512]{2,1,0:T(8,128)(2,1)S(1)}, bf16[2,128,512]{2,1,0:T(8,128)(2,1)S(1)}, u32[]{:S(2)}, u32[]{:S(2)}) collective-permute-start(bf16[2,128,512]{2,1,0:T(8,128)(2,1)S(1)} %pad_maximum_fusion.1.refs_5_), channel_id=1, source_target_pairs={{0,16},{2,18},{4,20},{6,22},{8,24},{10,26},{12,28},{14,30},{16,32}... | collective-permute-start | bytes 786440 | tf_op jit(solution)/shard_map/ppermute | solution.py:21
  45.2 15.7 %collective-permute-start.6 = (bf16[2,128,512]{2,1,0:T(8,128)(2,1)S(1)}, bf16[2,128,512]{2,1,0:T(8,128)(2,1)S(1)}, u32[]{:S(2)}, u32[]{:S(2)}) collective-permute-start(bf16[2,128,512]{2,1,0:T(8,128)(2,1)S(1)} %pad_maximum_fusion.1.refs_5_), channel_id=1, source_target_pairs={{0,8},{2,10},{4,12},{6,14},{8,16},{10,18},{12,20},{14,22},{16,24},... | collective-permute-start | bytes 786440 | tf_op jit(solution)/shard_map/ppermute | solution.py:21
  50.9 33.2 %collective-permute-start.11 = (bf16[2,256,512]{2,1,0:T(8,128)(2,1)S(1)}, bf16[2,256,512]{2,1,0:T(8,128)(2,1)S(1)}, u32[]{:S(2)}, u32[]{:S(2)}) collective-permute-start(bf16[2,256,512]{2,1,0:T(8,128)(2,1)S(1)} %maximum_maximum_fusion), channel_id=1, source_target_pairs={{0,128},{2,130},{4,132},{6,134},{8,136},{10,138},{12,140},{14,142}... | collective-permute-start | bytes 1572872 | tf_op jit(solution)/shard_map/ppermute | solution.py:21
  52.2 31.9 %collective-permute-start.10 = (bf16[2,256,512]{2,1,0:T(8,128)(2,1)S(1)}, bf16[2,256,512]{2,1,0:T(8,128)(2,1)S(1)}, u32[]{:S(2)}, u32[]{:S(2)}) collective-permute-start(bf16[2,256,512]{2,1,0:T(8,128)(2,1)S(1)} %maximum_maximum_fusion), channel_id=1, source_target_pairs={{0,64},{2,66},{4,68},{6,70},{8,72},{10,74},{12,76},{14,78},{16,80}... | collective-permute-start | bytes 1572872 | tf_op jit(solution)/shard_map/ppermute | solution.py:21
  55.4 28.7 %collective-permute-start.9 = (bf16[2,256,512]{2,1,0:T(8,128)(2,1)S(1)}, bf16[2,256,512]{2,1,0:T(8,128)(2,1)S(1)}, u32[]{:S(2)}, u32[]{:S(2)}) collective-permute-start(bf16[2,256,512]{2,1,0:T(8,128)(2,1)S(1)} %maximum_maximum_fusion), channel_id=1, source_target_pairs={{0,32},{2,34},{4,36},{6,38},{8,40},{10,42},{12,44},{14,46},{16,48}... | collective-permute-start | bytes 1572872 | tf_op jit(solution)/shard_map/ppermute | solution.py:21
  57.4 26.7 %collective-permute-start.2 = (bf16[2,256,512]{2,1,0:T(8,128)(2,1)S(1)}, bf16[2,256,512]{2,1,0:T(8,128)(2,1)S(1)}, u32[]{:S(2)}, u32[]{:S(2)}) collective-permute-start(bf16[2,256,512]{2,1,0:T(8,128)(2,1)S(1)} %maximum_maximum_fusion), channel_id=1, source_target_pairs={{0,2},{2,4},{4,6},{6,8},{8,10},{10,12},{12,14},{14,16},{16,18},{18... | collective-permute-start | bytes 1572872 | tf_op jit(solution)/shard_map/ppermute | solution.py:21
  60.9 23.2 %collective-permute-start.4 = (bf16[2,128,512]{2,1,0:T(8,128)(2,1)S(1)}, bf16[2,128,512]{2,1,0:T(8,128)(2,1)S(1)}, u32[]{:S(2)}, u32[]{:S(2)}) collective-permute-start(bf16[2,128,512]{2,1,0:T(8,128)(2,1)S(1)} %pad_maximum_fusion.1.refs_5_), channel_id=1, source_target_pairs={{0,4},{2,6},{4,8},{6,10},{8,12},{10,14},{12,16},{14,18},{16,20},{1... | collective-permute-start | bytes 786440 | tf_op jit(solution)/shard_map/ppermute | solution.py:21
  98.7 44.4 %collective-permute-start.13 = (bf16[2,256,512]{2,1,0:T(8,128)(2,1)S(1)}, bf16[2,256,512]{2,1,0:T(8,128)(2,1)S(1)}, u32[]{:S(2)}, u32[]{:S(2)}) collective-permute-start(bf16[2,256,512]{2,1,0:T(8,128)(2,1)S(1)} %get-tuple-element.15), channel_id=1, source_target_pairs={{2,0},{4,2},{6,4},{8,6},{10,8},{12,10},{14,12},{16,14},{18,16},{20... | collective-permute-start | bytes 1572872 | tf_op jit(solution)/shard_map/ppermute | solution.py:21
  100.6 62.5 %collective-permute-start.14 = (bf16[2,256,512]{2,1,0:T(8,128)(2,1)S(1)}, bf16[2,256,512]{2,1,0:T(8,128)(2,1)S(1)}, u32[]{:S(2)}, u32[]{:S(2)}) collective-permute-start(bf16[2,256,512]{2,1,0:T(8,128)(2,1)S(1)} %get-tuple-element.16), channel_id=1, source_target_pairs={{4,0},{6,2},{8,4},{10,6},{12,8},{14,10},{16,12},{18,14},{20,16},{2... | collective-permute-start | bytes 1572872 | tf_op jit(solution)/shard_map/ppermute | solution.py:21
  102.5 86.4 %collective-permute-start.15 = (bf16[2,256,512]{2,1,0:T(8,128)(2,1)S(1)}, bf16[2,256,512]{2,1,0:T(8,128)(2,1)S(1)}, u32[]{:S(2)}, u32[]{:S(2)}) collective-permute-start(bf16[2,256,512]{2,1,0:T(8,128)(2,1)S(1)} %get-tuple-element.17), channel_id=1, source_target_pairs={{8,0},{10,2},{12,4},{14,6},{16,8},{18,10},{20,12},{22,14},{24,16},... | collective-permute-start | bytes 1572872 | tf_op jit(solution)/shard_map/ppermute | solution.py:21
  107.9 81.0 %collective-permute-start.16 = (bf16[2,256,512]{2,1,0:T(8,128)(2,1)S(1)}, bf16[2,256,512]{2,1,0:T(8,128)(2,1)S(1)}, u32[]{:S(2)}, u32[]{:S(2)}) collective-permute-start(bf16[2,256,512]{2,1,0:T(8,128)(2,1)S(1)} %get-tuple-element.18), channel_id=1, source_target_pairs={{16,0},{18,2},{20,4},{22,6},{24,8},{26,10},{28,12},{30,14},{32,16}... | collective-permute-start | bytes 1572872 | tf_op jit(solution)/shard_map/ppermute | solution.py:21
  122.5 66.5 %collective-permute-start.17 = (bf16[2,256,512]{2,1,0:T(8,128)(2,1)S(1)}, bf16[2,256,512]{2,1,0:T(8,128)(2,1)S(1)}, u32[]{:S(2)}, u32[]{:S(2)}) collective-permute-start(bf16[2,256,512]{2,1,0:T(8,128)(2,1)S(1)} %get-tuple-element.19), channel_id=1, source_target_pairs={{32,0},{34,2},{36,4},{38,6},{40,8},{42,10},{44,12},{46,14},{48,16}... | collective-permute-start | bytes 1572872 | tf_op jit(solution)/shard_map/ppermute | solution.py:21
  143.1 63.3 %collective-permute-start.18 = (bf16[2,256,512]{2,1,0:T(8,128)(2,1)S(1)}, bf16[2,256,512]{2,1,0:T(8,128)(2,1)S(1)}, u32[]{:S(2)}, u32[]{:S(2)}) collective-permute-start(bf16[2,256,512]{2,1,0:T(8,128)(2,1)S(1)} %get-tuple-element.20), channel_id=1, source_target_pairs={{64,0},{66,2},{68,4},{70,6},{72,8},{74,10},{76,12},{78,14},{80,16}... | collective-permute-start | bytes 1572872 | tf_op jit(solution)/shard_map/ppermute | solution.py:21
  163.1 43.3 %collective-permute-start.19 = (bf16[2,256,512]{2,1,0:T(8,128)(2,1)S(1)}, bf16[2,256,512]{2,1,0:T(8,128)(2,1)S(1)}, u32[]{:S(2)}, u32[]{:S(2)}) collective-permute-start(bf16[2,256,512]{2,1,0:T(8,128)(2,1)S(1)} %get-tuple-element.21), channel_id=1, source_target_pairs={{128,0},{130,2},{132,4},{134,6},{136,8},{138,10},{140,12},{142,14}... | collective-permute-start | bytes 1572872 | tf_op jit(solution)/shard_map/ppermute | solution.py:21
  188.9 22.5 %collective-permute-start.12 = (bf16[128,2048]{1,0:T(8,128)(2,1)S(1)}, bf16[128,2048]{1,0:T(8,128)(2,1)S(1)}, u32[]{:S(2)}, u32[]{:S(2)}) collective-permute-start(bf16[128,2048]{1,0:T(8,128)(2,1)S(1)} %convolution_convert_fusion), channel_id=1, source_target_pairs={{0,1},{1,0},{2,3},{3,2},{4,5},{5,4},{6,7},{7,6},{8,9},{9,8},{10,11... | collective-permute-start | bytes 1572872 | tf_op jit(solution)/shard_map/ppermute | solution.py:25
  209.4 15.6 %collective-permute-start.20 = (bf16[128,2048]{1,0:T(8,128)(2,1)S(1)}, bf16[128,2048]{1,0:T(8,128)(2,1)S(1)}, u32[]{:S(2)}, u32[]{:S(2)}) collective-permute-start(bf16[128,2048]{1,0:T(8,128)(2,1)S(1)} %fusion.6), channel_id=1, source_target_pairs={{0,1},{1,0},{2,3},{3,2},{4,5},{5,4},{6,7},{7,6},{8,9},{9,8},{10,11... | collective-permute-start | bytes 1572872 | tf_op jit(solution)/shard_map/ppermute | solution.py:25
  210.6 1.0 copy-start.5
  211.5 13.5 %copy-start.6 = (f32[2048]{0:T(1024)S(1)}, f32[2048]{0:T(1024)}, u32[]{:S(2)}) copy-start(f32[2048]{0:T(1024)} %param.9) | copy-start | bytes 24580

commit v2 on v1

v2 whole, which is shorter than its diff:
```python
import functools

import jax
import jax.numpy as jnp
from jax import lax
from jax.experimental import pallas as pl
from jax.experimental.pallas import tpu as pltpu
from jax.sharding import PartitionSpec as P

HD = 128
BLOCK = 64
NEG = -1e30
EPS = 1e-06
F32 = jnp.float32
BF16 = jnp.bfloat16
NN = (((1,), (0,)), ((), ()))
NT = (((1,), (1,)), ((), ()))


def shifted(value, by):
    size = lax.axis_size("seq")
    pairs = [(i, i + by) for i in range(size) if 0 <= i + by < size]
    return lax.ppermute(value, "seq", pairs)


def swap_tp(value):
    return lax.ppermute(value, "tp", [(0, 1), (1, 0)])


def dot(a, b, dims):
    return lax.dot_general(a, b, dims, preferred_element_type=F32)


def piece(pieces, which, slot):
    per = 4 // len(pieces)
    at = (slot % per) * BLOCK
    return pieces[slot // per][which, at : at + BLOCK, :]


def near_slots(step, slot):
    found = []
    for turn in (0, 2):
        block = (slot + turn) % 4 + step
        found.append((0 <= block < 4, (block + turn) % 4))
    return found


def near(is_second, own, other, which, slot, step):
    options = [
        piece(own if here else other, which, at) for here, at in near_slots(step, slot)
    ]
    return jnp.where(is_second, options[1], options[0])


def causal_bias(query_axis):
    rows = lax.broadcasted_iota(jnp.int32, (BLOCK, BLOCK), query_axis)
    keys = lax.broadcasted_iota(jnp.int32, (BLOCK, BLOCK), 1 - query_axis)
    return jnp.where(rows >= keys, 0.0, NEG).astype(F32)


def query_kernel(groups, tp_ref, bias_ref, *refs):
    refs = list(refs)
    qg = [refs.pop(0) for _ in range(2)]
    kv = [refs.pop(0) for _ in range(2)]
    fetched = [[refs.pop(0) for _ in range(n)] for n in groups]
    mixed_ref, dq_ref, stat_ref = refs
    is_second = tp_ref[0] == 1
    factor = HD ** (-0.5)
    causal = causal_bias(0)
    lane = lax.broadcasted_iota(jnp.int32, (BLOCK, HD), 1)
    for slot in range(4):
        out = slice(slot * BLOCK, (slot + 1) * BLOCK)
        keys, values = [
            jnp.concatenate(
                [piece(kv, which, slot)]
                + [near(is_second, kv, fetched[0], which, slot, -d) for d in (1, 2, 4)]
                + [piece(f, which, slot) for f in fetched[1:]],
                axis=0,
            )
            for which in range(2)
        ]
        query, grad = piece(qg, 0, slot), piece(qg, 1, slot)
        score = dot(query, keys, NT) * factor + bias_ref[slot]
        score = jnp.concatenate([score[:, :BLOCK] + causal, score[:, BLOCK:]], axis=1)
        peak = jnp.max(score, axis=-1, keepdims=True)
        weight = jnp.exp(score - peak)
        total = jnp.sum(weight, axis=-1, keepdims=True)
        prob = weight * (1.0 / total)
        mixed = dot(prob.astype(BF16), values, NN).astype(BF16)
        mixed_ref[out, :] = mixed
        inner = jnp.sum(mixed.astype(F32) * grad.astype(F32), axis=-1, keepdims=True)
        grad_score = (prob * (dot(grad, values, NT) - inner)).astype(BF16)
        dq_ref[out, :] = (dot(grad_score, keys, NN) * factor).astype(BF16)
        stat = jnp.where(lane == 0, peak + jnp.log(total), inner)
        stat_ref[0, :, out] = jnp.transpose(stat)[:2]


def key_kernel(half, groups, tp_ref, *refs):
    refs = list(refs)
    kv = refs.pop(0)
    qg = [refs.pop(0) for _ in range(2)]
    stat = refs.pop(0)
    later = [[refs.pop(0) for _ in range(n)] for n in groups]
    later_stats = [refs.pop(0) for _ in groups]
    (out_ref,) = refs
    is_second = tp_ref[0] == 1
    factor = HD ** (-0.5)
    causal = causal_bias(1)

    def stat_of(ref, slot):
        return ref[0, :, slot * BLOCK : (slot + 1) * BLOCK]

    for at in range(2):
        slot = 2 * half + at
        rows = slice(at * BLOCK, (at + 1) * BLOCK)
        queries, grads = [
            jnp.concatenate(
                [piece(qg, which, slot)]
                + [near(is_second, qg, later[0], which, slot, d) for d in (1, 2, 4)]
                + [f[0][which, rows, :] for f in later[1:]],
                axis=0,
            )
            for which in range(2)
        ]
        near_stats = []
        for d in (1, 2, 4):
            options = [
                stat_of(stat if here else later_stats[0], s) for here, s in near_slots(d, slot)
            ]
            near_stats.append(jnp.where(is_second, options[1], options[0]))
        stats = jnp.concatenate(
            [stat_of(stat, slot)] + near_stats + [stat_of(f, slot) for f in later_stats[1:]], axis=1
        )
        score = dot(kv[0, rows, :], queries, NT) * factor
        score = jnp.concatenate([score[:, :BLOCK] + causal, score[:, BLOCK:]], axis=1)
        prob = jnp.exp(score - stats[0:1])
        grad_score = (prob * (dot(kv[1, rows, :], grads, NT) - stats[1:2])).astype(BF16)
        out_ref[0, rows, :] = (dot(grad_score, queries, NN) * factor).astype(BF16)
        out_ref[1, rows, :] = dot(prob.astype(BF16), grads, NN).astype(BF16)


def head_spec(a):
    if a.ndim == 2:
        return pl.BlockSpec((a.shape[0], HD), lambda h, t: (0, h))
    return pl.BlockSpec((a.shape[0], a.shape[1], HD), lambda h, t: (0, 0, h))


def stat_spec(a):
    return pl.BlockSpec((1,) + a.shape[1:], lambda h, t: (h, 0, 0))


def call(kernel, turn, operands, in_specs, outs, out_specs, heads, keys, name):
    rows = outs[0].shape[-2]
    return pl.pallas_call(
        kernel,
        out_shape=outs,
        grid_spec=pltpu.PrefetchScalarGridSpec(
            num_scalar_prefetch=1, grid=(heads,), in_specs=in_specs, out_specs=out_specs
        ),
        compiler_params=pltpu.CompilerParams(vmem_limit_bytes=12 * 2**20),
        cost_estimate=pl.CostEstimate(
            flops=4 * 2 * rows * keys * HD * heads,
            bytes_accessed=6 * 2**20,
            transcendentals=rows * keys * heads,
        ),
        name=name,
    )(turn, *operands)


def query_side(turn, bias, qg, kv, fetched):
    rows, width = 2 * qg[0].shape[1], qg[0].shape[2]
    heads = width // HD
    operands = [*qg, *kv, *[a for f in fetched for a in f]]
    row_out = jax.ShapeDtypeStruct((rows, width), BF16)
    stat_out = jax.ShapeDtypeStruct((heads, 2, rows), F32)
    return call(
        functools.partial(query_kernel, tuple(len(f) for f in fetched)),
        turn,
        [bias, *operands],
        [pl.BlockSpec(bias.shape, lambda h, t: (0, 0, 0))] + [head_spec(a) for a in operands],
        [row_out, row_out, stat_out],
        [head_spec(row_out), head_spec(row_out), stat_spec(stat_out)],
        heads,
        bias.shape[2],
        "query_side",
    )


def key_side(half, turn, kv, qg, stat, later, later_stats):
    rows, width = kv[0].shape[1], kv[0].shape[2]
    heads = width // HD

    def half_spec(f):
        if len(f) == 2:
            return f[half], head_spec(f[half])
        return f[0], pl.BlockSpec((2, rows, HD), lambda h, t: (0, half, h))

    far = [half_spec(f) for f in later[1:]]
    operands = [kv[half], *qg, stat, *later[0], *[a for a, _ in far], *later_stats]
    in_specs = (
        [head_spec(a) for a in (kv[half], *qg)]
        + [stat_spec(stat)]
        + [head_spec(a) for a in later[0]]
        + [s for _, s in far]
        + [stat_spec(a) for a in later_stats]
    )
    out = jax.ShapeDtypeStruct((2, rows, width), BF16)
    groups = (len(later[0]),) + (1,) * len(far)
    (result,) = call(
        functools.partial(key_kernel, half, groups),
        turn,
        operands,
        in_specs,
        [out],
        [head_spec(out)],
        heads,
        (4 + len(far)) * BLOCK,
        "key_side",
    )
    return result


def matmul(a, b):
    return jnp.dot(a, b, preferred_element_type=F32)


def matmul_t(a, b):
    return lax.dot_general(a, b, NT, preferred_element_type=F32)


def exchange(own, other, sign, levels):
    whole = jnp.concatenate([own, other], axis=1)
    got = {}
    for at, rows in enumerate((own, other)):
        last, reached = rows, 0
        for s in (1, 2, 3):
            last = shifted(last, sign * (2**s - reached))
            reached = 2**s
            got[s, at] = last
    return [
        (got[s, 0], got[s, 1]) if s in (1, 2, 3) else (shifted(whole, sign * 2**s),)
        for s in range(levels)
    ]


def per_device(series, norm_gain, w_query, w_key, w_value, w_out, out_grad):
    levels = lax.axis_size("seq").bit_length() - 1
    half = series.shape[0]
    blocks = 2 * half // BLOCK
    tp_index = lax.axis_index("tp").astype(jnp.int32)
    turn = tp_index[None]
    slots = jnp.arange(blocks, dtype=jnp.int32)
    global_block = lax.axis_index("seq") * blocks + (slots + 2 * tp_index) % blocks
    distances = [1, 2, 4] + [blocks * 2**s for s in range(1, levels)]
    reach = jnp.repeat(jnp.array([0] + distances, jnp.int32), BLOCK)
    bias = jnp.where(global_block[:, None] >= reach[None], 0.0, NEG).astype(F32)[:, None, :]

    series_f = series.astype(F32)
    inv_rms = lax.rsqrt(jnp.mean(series_f * series_f, axis=-1, keepdims=True) + EPS)
    unit_rows = series_f * inv_rms
    normed = (unit_rows * norm_gain).astype(BF16)
    normed_other = swap_tp(normed)
    out_grad_other = swap_tp(out_grad)

    def key_value(rows):
        return jnp.stack([matmul(rows, w_key).astype(BF16), matmul(rows, w_value).astype(BF16)])

    def query_grad(rows, grad_rows):
        return jnp.stack(
            [matmul(rows, w_query).astype(BF16), matmul_t(grad_rows, w_out).astype(BF16)]
        )

    kv = (key_value(normed), key_value(normed_other))
    qg = (query_grad(normed, out_grad), query_grad(normed_other, out_grad_other))
    fetched = exchange(*kv, 1, levels)
    later = exchange(*qg, -1, levels)
    mixed, grad_query, stat = query_side(turn, bias, qg, kv, fetched)
    stat, later = lax.optimization_barrier((stat, later))
    later_stats = [shifted(stat, -(2**s)) for s in range(levels)]
    attn_other = swap_tp(matmul(mixed[half:], w_out).astype(BF16))
    attn_rows = matmul(mixed[:half], w_out) + attn_other.astype(F32)
    layer_out = (series_f + attn_rows).astype(BF16)

    def back(at):
        grad_kv = key_side(at, turn, kv, qg, stat, later, later_stats)
        rows = slice(at * half, (at + 1) * half)
        return (
            matmul_t(grad_query[rows], w_query)
            + matmul_t(grad_kv[0], w_key)
            + matmul_t(grad_kv[1], w_value)
        )

    normed_grad_other = swap_tp(back(1).astype(BF16))
    normed_grad = back(0) + normed_grad_other.astype(F32)
    scaled = normed_grad * norm_gain
    series_grad = out_grad.astype(F32) + inv_rms * (
        scaled - unit_rows * jnp.mean(scaled * unit_rows, axis=-1, keepdims=True)
    )
    return (layer_out, series_grad.astype(BF16))


def solution(mesh):
    rows = P(("seq", "tp"), None)
    columns = P(None, "tp")
    in_specs = (rows, P(), columns, columns, columns, P("tp", None), rows)
    return jax.shard_map(
        per_device, mesh=mesh, in_specs=in_specs, out_specs=(rows, rows), check_vma=False
    )
```

time: 229 us -> 194 us (0.85)
  the two profiles are of different devices: /device:TPU:238 before, /device:TPU:24 now
where the time goes in v2:
time: 194 us; the launch traced here: 191 us
  starting transfers between devices  110 us (57%)
  waiting for transfers between devices  25.6 us (13%)
  Pallas kernels  21 us (11%)
  local copies, waits for them, and re-layouts  15.9 us (8%)
  matrix products  12.8 us (7%)
  other arithmetic  4.88 us (3%)
    ppermute x27, starting transfers between devices, shifted(): return lax.ppermute(value, 'seq', pairs)  97.7 us
    pallas_call x3, Pallas kernels, call(): pl.pallas_call(kernel, out_shape=outs, grid_spec=pltpu.PrefetchScalarGrid...  21 us
    unnamed x72, local copies, waits for them, and re-layouts  15.8 us
    ppermute x27, waiting for transfers between devices, shifted(): return lax.ppermute(value, 'seq', pairs)  15.6 us
    ppermute x4, starting transfers between devices, swap_tp(): return lax.ppermute(value, 'tp', [(0, 1), (1, 0)])  11.9 us
    ppermute x4, waiting for transfers between devices, swap_tp(): return lax.ppermute(value, 'tp', [(0, 1), (1, 0)])  10 us
    dot_general x8, matrix products, matmul_t(): return lax.dot_general(a, b, NT, preferred_element_type=F32)  6.68 us
    dot_general x8, matrix products, matmul(): return jnp.dot(a, b, preferred_element_type=F32)  6.12 us
  transfers between devices with their start and end apart: 31, of which 7 were waited for; matrix products, arithmetic and copies ran while one was open for 7% of the time, Pallas kernels for 11%

profile of v2, /device:TPU:24, one launch (start us, length us, event | category | flops | bytes accessed | tf_op | source)
XLA Modules:
  0.0 191.3 jit_solution(9813889009836120710)
XLA Ops:
  0.7 1.4 fusion.24
  2.1 1.2 fusion.18
  3.3 3.1 %collective-permute-start = (bf16[128,2048]{1,0:T(8,128)(2,1)S(1)}, bf16[128,2048]{1,0:T(8,128)(2,1)S(1)}, u32[]{:S(2)}, u32[]{:S(2)}) collective-permute-start(bf16[128,2048]{1,0:T(8,128)(2,1)S(1)} %fusion.18), channel_id=1, source_target_pairs={{0,1},{1,0},{2,3},{3,2},{4,5},{5,4},{6,7},{7,6},{8,9},{9,8},{10,11... | collective-permute-start | bytes 1572872 | tf_op jit(solution)/shard_map/ppermute | solution.py:27
  6.4 2.1 %fusion.15 = bf16[1,128,512]{2,1,0:T(8,128)(2,1)S(1)} fusion(bf16[128,2048]{1,0:T(8,128)(2,1)S(1)} %fusion.18, bf16[2048,512]{1,0:T(8,128)(2,1)} %param.12), kind=kOutput, calls=%fused_computation.29 | convolution fusion | flops 268500992 | bytes 2752512 | tf_op jit(solution)/shard_map/dot_general | solution.py:224
  9.0 4.0 %collective-permute-start.3 = (bf16[2,128,512]{2,1,0:T(8,128)(2,1)S(1)}, bf16[2,128,512]{2,1,0:T(8,128)(2,1)S(1)}, u32[]{:S(2)}, u32[]{:S(2)}) collective-permute-start(bf16[2,128,512]{2,1,0:T(8,128)(2,1)S(1)} %pad_maximum_fusion.2.refs_2_.refs_0_), channel_id=1, source_target_pairs={{0,4},{2,6},{4,8},{6,10},{8,12},{10,14},{12,16},{14,18},{16,20},{1... | collective-permute-start | bytes 786440 | tf_op jit(solution)/shard_map/ppermute | solution.py:23
  13.5 0.8 fusion.11
  14.4 6.1 %collective-permute-start.14 = (bf16[2,128,512]{2,1,0:T(8,128)(2,1)S(1)}, bf16[2,128,512]{2,1,0:T(8,128)(2,1)S(1)}, u32[]{:S(2)}, u32[]{:S(2)}) collective-permute-start(bf16[2,128,512]{2,1,0:T(8,128)(2,1)S(1)} %pad_maximum_fusion.refs_0_.refs_1_), channel_id=1, source_target_pairs={{4,0},{6,2},{8,4},{10,6},{12,8},{14,10},{16,12},{18,14},{20,16},{2... | collective-permute-start | bytes 786440 | tf_op jit(solution)/shard_map/ppermute | solution.py:23
  20.4 2.1 %collective-permute-start.1 = (bf16[128,2048]{1,0:T(8,128)(2,1)S(1)}, bf16[128,2048]{1,0:T(8,128)(2,1)S(1)}, u32[]{:S(2)}, u32[]{:S(2)}) collective-permute-start(bf16[128,2048]{1,0:T(8,128)(2,1)S(1)} %copy-done.32), channel_id=1, source_target_pairs={{0,1},{1,0},{2,3},{3,2},{4,5},{5,4},{6,7},{7,6},{8,9},{9,8},{10,11... | collective-permute-start | bytes 1572872 | tf_op jit(solution)/shard_map/ppermute | solution.py:27
  23.2 1.9 collective-permute-start.5
  25.7 7.4 %collective-permute-start.16 = (bf16[2,128,512]{2,1,0:T(8,128)(2,1)S(1)}, bf16[2,128,512]{2,1,0:T(8,128)(2,1)S(1)}, u32[]{:S(2)}, u32[]{:S(2)}) collective-permute-start(bf16[2,128,512]{2,1,0:T(8,128)(2,1)S(1)} %collective-permute-done.14.refs_5_), channel_id=1, source_target_pairs={{4,0},{6,2},{8,4},{10,6},{12,8},{14,10},{16,12},{18,14},{20,16},{2... | collective-permute-start | bytes 786440 | tf_op jit(solution)/shard_map/ppermute | solution.py:23
  34.2 1.9 %collective-permute-start.4 = (bf16[2,128,512]{2,1,0:T(8,128)(2,1)S(1)}, bf16[2,128,512]{2,1,0:T(8,128)(2,1)S(1)}, u32[]{:S(2)}, u32[]{:S(2)}) collective-permute-start(bf16[2,128,512]{2,1,0:T(8,128)(2,1)S(1)} %pad_maximum_fusion.3.refs_3_.refs_0_), channel_id=1, source_target_pairs={{0,4},{2,6},{4,8},{6,10},{8,12},{10,14},{12,16},{14,18},{16,20},{1... | collective-permute-start | bytes 786440 | tf_op jit(solution)/shard_map/ppermute | solution.py:23
  36.1 2.0 %collective-permute-start.7 = (bf16[2,128,512]{2,1,0:T(8,128)(2,1)S(1)}, bf16[2,128,512]{2,1,0:T(8,128)(2,1)S(1)}, u32[]{:S(2)}, u32[]{:S(2)}) collective-permute-start(bf16[2,128,512]{2,1,0:T(8,128)(2,1)S(1)} %collective-permute-done.5.refs_7_), channel_id=1, source_target_pairs={{0,8},{2,10},{4,12},{6,14},{8,16},{10,18},{12,20},{14,22},{16,24},... | collective-permute-start | bytes 786440 | tf_op jit(solution)/shard_map/ppermute | solution.py:23
  38.1 7.8 %collective-permute-start.18 = (bf16[2,128,512]{2,1,0:T(8,128)(2,1)S(1)}, bf16[2,128,512]{2,1,0:T(8,128)(2,1)S(1)}, u32[]{:S(2)}, u32[]{:S(2)}) collective-permute-start(bf16[2,128,512]{2,1,0:T(8,128)(2,1)S(1)} %collective-permute-done.16.refs_6_), channel_id=1, source_target_pairs={{8,0},{10,2},{12,4},{14,6},{16,8},{18,10},{20,12},{22,14},{24,16},... | collective-permute-start | bytes 786440 | tf_op jit(solution)/shard_map/ppermute | solution.py:23
  46.4 4.9 %collective-permute-done.1 = bf16[128,2048]{1,0:T(8,128)(2,1)S(1)} collective-permute-done((bf16[128,2048]{1,0:T(8,128)(2,1)S(1)}, bf16[128,2048]{1,0:T(8,128)(2,1)S(1)}, u32[]{:S(2)}, u32[]{:S(2)}) %collective-permute-start.1) | collective-permute-done | bytes 524320 | tf_op jit(solution)/shard_map/ppermute | solution.py:27
  51.3 0.8 fusion.13
  52.2 1.9 %collective-permute-start.15 = (bf16[2,128,512]{2,1,0:T(8,128)(2,1)S(1)}, bf16[2,128,512]{2,1,0:T(8,128)(2,1)S(1)}, u32[]{:S(2)}, u32[]{:S(2)}) collective-permute-start(bf16[2,128,512]{2,1,0:T(8,128)(2,1)S(1)} %pad_maximum_fusion.1.refs_1_.refs_2_), channel_id=1, source_target_pairs={{4,0},{6,2},{8,4},{10,6},{12,8},{14,10},{16,12},{18,14},{20,16},{2... | collective-permute-start | bytes 786440 | tf_op jit(solution)/shard_map/ppermute | solution.py:23
  54.1 1.3 collective-permute-start.11
  56.1 1.3 collective-permute-start.10
  58.2 1.9 collective-permute-start.9
  60.1 1.9 %collective-permute-start.2 = (bf16[2,256,512]{2,1,0:T(8,128)(2,1)S(1)}, bf16[2,256,512]{2,1,0:T(8,128)(2,1)S(1)}, u32[]{:S(2)}, u32[]{:S(2)}) collective-permute-start(bf16[2,256,512]{2,1,0:T(8,128)(2,1)S(1)} %maximum_maximum_fusion), channel_id=1, source_target_pairs={{0,2},{2,4},{4,6},{6,8},{8,10},{10,12},{12,14},{14,16},{16,18},{18... | collective-permute-start | bytes 1572872 | tf_op jit(solution)/shard_map/ppermute | solution.py:23
  62.1 4.8 %collective-permute-start.6 = (bf16[2,128,512]{2,1,0:T(8,128)(2,1)S(1)}, bf16[2,128,512]{2,1,0:T(8,128)(2,1)}, u32[]{:S(2)}, u32[]{:S(2)}) collective-permute-start(bf16[2,128,512]{2,1,0:T(8,128)(2,1)S(1)} %collective-permute-done.4.refs_6_), channel_id=1, source_target_pairs={{0,4},{2,6},{4,8},{6,10},{8,12},{10,14},{12,16},{14,18},{16,20},{1... | collective-permute-start | bytes 786440 | tf_op jit(solution)/shard_map/ppermute | solution.py:23
  67.5 8.9 %collective-permute-done.6.refs_8_ = bf16[2,128,512]{2,1,0:T(8,128)(2,1)} collective-permute-done((bf16[2,128,512]{2,1,0:T(8,128)(2,1)S(1)}, bf16[2,128,512]{2,1,0:T(8,128)(2,1)}, u32[]{:S(2)}, u32[]{:S(2)}) %collective-permute-start.6) | collective-permute-done | bytes 262176 | tf_op jit(solution)/shard_map/ppermute | solution.py:23
  76.4 3.7 %collective-permute-start.17 = (bf16[2,128,512]{2,1,0:T(8,128)(2,1)S(1)}, bf16[2,128,512]{2,1,0:T(8,128)(2,1)S(1)}, u32[]{:S(2)}, u32[]{:S(2)}) collective-permute-start(bf16[2,128,512]{2,1,0:T(8,128)(2,1)S(1)} %collective-permute-done.15.refs_5_), channel_id=1, source_target_pairs={{4,0},{6,2},{8,4},{10,6},{12,8},{14,10},{16,12},{18,14},{20,16},{2... | collective-permute-start | bytes 786440 | tf_op jit(solution)/shard_map/ppermute | solution.py:23
  80.9 0.8 copy-done.1
  81.7 1.9 collective-permute-start.8
  83.6 0.8 maximum_maximum_fusion.1
  84.4 5.4 %collective-permute-done.10.refs_12_ = bf16[2,256,512]{2,1,0:T(8,128)(2,1)S(1)} collective-permute-done((bf16[2,256,512]{2,1,0:T(8,128)(2,1)S(1)}, bf16[2,256,512]{2,1,0:T(8,128)(2,1)S(1)}, u32[]{:S(2)}, u32[]{:S(2)}) %collective-permute-start.10) | collective-permute-done | bytes 524320 | tf_op jit(solution)/shard_map/ppermute | solution.py:23
  89.8 0.8 copy-done.3
  90.6 20.1 %collective-permute-start.22 = (bf16[2,256,512]{2,1,0:T(8,128)(2,1)}, bf16[2,256,512]{2,1,0:T(8,128)(2,1)}, u32[]{:S(2)}, u32[]{:S(2)}) collective-permute-start(bf16[2,256,512]{2,1,0:T(8,128)(2,1)} %maximum_maximum_fusion.1), channel_id=1, source_target_pairs={{128,0},{130,2},{132,4},{134,6},{136,8},{138,10},{140,12},{142,14}... | collective-permute-start | bytes 1572872 | tf_op jit(solution)/shard_map/ppermute | solution.py:23
  110.7 0.8 copy-done.5
  111.5 2.1 %collective-permute-start.21 = (bf16[2,256,512]{2,1,0:T(8,128)(2,1)}, bf16[2,256,512]{2,1,0:T(8,128)(2,1)}, u32[]{:S(2)}, u32[]{:S(2)}) collective-permute-start(bf16[2,256,512]{2,1,0:T(8,128)(2,1)} %maximum_maximum_fusion.1), channel_id=1, source_target_pairs={{64,0},{66,2},{68,4},{70,6},{72,8},{74,10},{76,12},{78,14},{80,16}... | collective-permute-start | bytes 1572872 | tf_op jit(solution)/shard_map/ppermute | solution.py:23
  113.6 0.8 copy-done.7
  114.4 1.9 collective-permute-start.20
  117.1 1.9 collective-permute-start.13
  119.2 2.1 %collective-permute-start.19 = (bf16[2,128,512]{2,1,0:T(8,128)(2,1)}, bf16[2,128,512]{2,1,0:T(8,128)(2,1)S(1)}, u32[]{:S(2)}, u32[]{:S(2)}) collective-permute-start(bf16[2,128,512]{2,1,0:T(8,128)(2,1)} %copy-done.19), channel_id=1, source_target_pairs={{8,0},{10,2},{12,4},{14,6},{16,8},{18,10},{20,12},{22,14},{24,16},... | collective-permute-start | bytes 786440 | tf_op jit(solution)/shard_map/ppermute | solution.py:23
  121.3 1.0 copy-done.2
  122.4 1.0 copy-done.4
  123.4 1.0 copy-done.6
  124.4 1.0 copy-done.8
  125.5 0.9 copy-done.16
  126.4 0.9 copy-done.18
  127.4 0.9 copy-done.22
  128.3 0.9 copy-done.24
  129.3 12.4 %query_side.1 = (bf16[256,512]{1,0:T(8,128)(2,1)S(1)}, bf16[256,512]{1,0:T(8,128)(2,1)S(1)}, f32[4,2,256]{2,1,0:T(2,128)S(1)}) custom-call(s32[1]{0:T(128)} %bitcast.tp_ref, f32[4,1,640]{2,1,0:T(1,128)S(1)} %compare_select_fusion.bias_ref, bf16[2,128,512]{2,1,0:T(8,128)(2,1)S(1)} %pad_maximum_fusion.refs_0_.refs_1_, ...), custom_call_target="tpu_custom_call" | custom-call | flops 671088640 | bytes 6291456 | tf_op jit(solution)/shard_map/query_side/pallas_call | solution.py:154
  141.7 1.4 collective-permute-start.29
  143.2 1.9 %collective-permute-start.28 = (f32[4,2,256]{2,1,0:T(2,128)S(1)}, f32[4,2,256]{2,1,0:T(2,128)S(1)}, u32[]{:S(2)}, u32[]{:S(2)}) collective-permute-start(f32[4,2,256]{2,1,0:T(2,128)S(1)} %get-tuple-element.19.refs_3_), channel_id=1, source_target_pairs={{64,0},{66,2},{68,4},{70,6},{72,8},{74,10},{76,12},{78,14},{80,16}... | collective-permute-start | bytes 24584 | tf_op jit(solution)/shard_map/ppermute | solution.py:23
  145.1 3.4 %collective-permute-start.27 = (f32[4,2,256]{2,1,0:T(2,128)S(1)}, f32[4,2,256]{2,1,0:T(2,128)S(1)}, u32[]{:S(2)}, u32[]{:S(2)}) collective-permute-start(f32[4,2,256]{2,1,0:T(2,128)S(1)} %get-tuple-element.19.refs_3_), channel_id=1, source_target_pairs={{32,0},{34,2},{36,4},{38,6},{40,8},{42,10},{44,12},{46,14},{48,16}... | collective-permute-start | bytes 24584 | tf_op jit(solution)/shard_map/ppermute | solution.py:23
  148.5 1.9 %collective-permute-start.26 = (f32[4,2,256]{2,1,0:T(2,128)S(1)}, f32[4,2,256]{2,1,0:T(2,128)S(1)}, u32[]{:S(2)}, u32[]{:S(2)}) collective-permute-start(f32[4,2,256]{2,1,0:T(2,128)S(1)} %get-tuple-element.19.refs_3_), channel_id=1, source_target_pairs={{16,0},{18,2},{20,4},{22,6},{24,8},{26,10},{28,12},{30,14},{32,16}... | collective-permute-start | bytes 24584 | tf_op jit(solution)/shard_map/ppermute | solution.py:23
  150.4 6.4 %collective-permute-start.25 = (f32[4,2,256]{2,1,0:T(2,128)S(1)}, f32[4,2,256]{2,1,0:T(2,128)S(1)}, u32[]{:S(2)}, u32[]{:S(2)}) collective-permute-start(f32[4,2,256]{2,1,0:T(2,128)S(1)} %get-tuple-element.19.refs_3_), channel_id=1, source_target_pairs={{8,0},{10,2},{12,4},{14,6},{16,8},{18,10},{20,12},{22,14},{24,16},... | collective-permute-start | bytes 24584 | tf_op jit(solution)/shard_map/ppermute | solution.py:23
  156.9 1.9 %collective-permute-start.24 = (f32[4,2,256]{2,1,0:T(2,128)S(1)}, f32[4,2,256]{2,1,0:T(2,128)S(1)}, u32[]{:S(2)}, u32[]{:S(2)}) collective-permute-start(f32[4,2,256]{2,1,0:T(2,128)S(1)} %get-tuple-element.19.refs_3_), channel_id=1, source_target_pairs={{4,0},{6,2},{8,4},{10,6},{12,8},{14,10},{16,12},{18,14},{20,16},{2... | collective-permute-start | bytes 24584 | tf_op jit(solution)/shard_map/ppermute | solution.py:23
  158.8 2.8 %collective-permute-start.23 = (f32[4,2,256]{2,1,0:T(2,128)S(1)}, f32[4,2,256]{2,1,0:T(2,128)S(1)}, u32[]{:S(2)}, u32[]{:S(2)}) collective-permute-start(f32[4,2,256]{2,1,0:T(2,128)S(1)} %get-tuple-element.19.refs_3_), channel_id=1, source_target_pairs={{2,0},{4,2},{6,4},{8,6},{10,8},{12,10},{14,12},{16,14},{18,16},{20... | collective-permute-start | bytes 24584 | tf_op jit(solution)/shard_map/ppermute | solution.py:23
  162.1 5.7 %collective-permute-start.12 = (bf16[128,2048]{1,0:T(8,128)(2,1)S(1)}, bf16[128,2048]{1,0:T(8,128)(2,1)S(1)}, u32[]{:S(2)}, u32[]{:S(2)}) collective-permute-start(bf16[128,2048]{1,0:T(8,128)(2,1)S(1)} %convolution_convert_fusion), channel_id=1, source_target_pairs={{0,1},{1,0},{2,3},{3,2},{4,5},{5,4},{6,7},{7,6},{8,9},{9,8},{10,11... | collective-permute-start | bytes 1572872 | tf_op jit(solution)/shard_map/ppermute | solution.py:27
  167.8 4.3 %key_side.3 = bf16[2,128,512]{2,1,0:T(8,128)(2,1)S(1)} custom-call(s32[1]{0:T(128)} %bitcast.tp_ref, bf16[2,128,512]{2,1,0:T(8,128)(2,1)S(1)} %pad_maximum_fusion.3.refs_3_.refs_0_, bf16[2,128,512]{2,1,0:T(8,128)(2,1)S(1)} %pad_maximum_fusion.refs_0_.refs_1_, bf16[2,128,512]{2,1,0:T(8,128)(2,1)S(1)} %pad_maximum_fusion.1.refs_1_.refs_2_, ...), custom_call_target="tpu_custom_call" | custom-call | flops 335544320 | bytes 6291456 | tf_op jit(solution)/shard_map/key_side/pallas_call | solution.py:154
  172.2 0.8 fusion.25
  173.8 0.8 fusion.26
  174.6 0.8 fusion.6
  175.4 1.0 collective-permute-start.30
  176.4 4.3 %key_side.2 = bf16[2,128,512]{2,1,0:T(8,128)(2,1)S(1)} custom-call(s32[1]{0:T(128)} %bitcast.tp_ref, bf16[2,128,512]{2,1,0:T(8,128)(2,1)S(1)} %pad_maximum_fusion.2.refs_2_.refs_0_, bf16[2,128,512]{2,1,0:T(8,128)(2,1)S(1)} %pad_maximum_fusion.refs_0_.refs_1_, bf16[2,128,512]{2,1,0:T(8,128)(2,1)S(1)} %pad_maximum_fusion.1.refs_1_.refs_2_, ...), custom_call_target="tpu_custom_call" | custom-call | flops 335544320 | bytes 6291456 | tf_op jit(solution)/shard_map/key_side/pallas_call | solution.py:154
  180.7 0.8 fusion.27
  181.6 0.8 fusion.28
  182.6 1.3 fusion.5
  183.9 5.2 %collective-permute-done.30 = bf16[128,2048]{1,0:T(8,128)(2,1)S(1)} collective-permute-done((bf16[128,2048]{1,0:T(8,128)(2,1)S(1)}, bf16[128,2048]{1,0:T(8,128)(2,1)S(1)}, u32[]{:S(2)}, u32[]{:S(2)}) %collective-permute-start.30) | collective-permute-done | bytes 524320 | tf_op jit(solution)/shard_map/ppermute | solution.py:27
  189.1 1.0 fusion.19
  190.1 1.2 fusion.23
  (104 shorter events, 9.2 us)
Async XLA Ops:
  0.6 12.3 %copy-start = (bf16[2048,512]{1,0:T(8,128)(2,1)S(1)}, bf16[2048,512]{1,0:T(8,128)(2,1)}, u32[]{:S(2)}) copy-start(bf16[2048,512]{1,0:T(8,128)(2,1)} %param.10) | copy-start | bytes 6291460
  0.6 7.8 %copy-start.27 = (bf16[2048,512]{1,0:T(8,128)(2,1)S(1)}, bf16[2048,512]{1,0:T(8,128)(2,1)}, u32[]{:S(2)}) copy-start(bf16[2048,512]{1,0:T(8,128)(2,1)} %param.11) | copy-start | bytes 6291460
  3.3 29.9 %collective-permute-start = (bf16[128,2048]{1,0:T(8,128)(2,1)S(1)}, bf16[128,2048]{1,0:T(8,128)(2,1)S(1)}, u32[]{:S(2)}, u32[]{:S(2)}) collective-permute-start(bf16[128,2048]{1,0:T(8,128)(2,1)S(1)} %fusion.18), channel_id=1, source_target_pairs={{0,1},{1,0},{2,3},{3,2},{4,5},{5,4},{6,7},{7,6},{8,9},{9,8},{10,11... | collective-permute-start | bytes 1572872 | tf_op jit(solution)/shard_map/ppermute | solution.py:27
  8.9 4.5 %copy-start.29 = (bf16[512,2048]{1,0:T(8,128)(2,1)S(1)}, bf16[512,2048]{1,0:T(8,128)(2,1)}, u32[]{:S(2)}) copy-start(bf16[512,2048]{1,0:T(8,128)(2,1)} %param.13) | copy-start | bytes 6291460
  8.9 4.5 %copy-start.32 = (bf16[128,2048]{1,0:T(8,128)(2,1)S(1)}, bf16[128,2048]{1,0:T(8,128)(2,1)}, u32[]{:S(2)}) copy-start(bf16[128,2048]{1,0:T(8,128)(2,1)} %param.14) | copy-start | bytes 1572868
  9.0 14.2 %collective-permute-start.3 = (bf16[2,128,512]{2,1,0:T(8,128)(2,1)S(1)}, bf16[2,128,512]{2,1,0:T(8,128)(2,1)S(1)}, u32[]{:S(2)}, u32[]{:S(2)}) collective-permute-start(bf16[2,128,512]{2,1,0:T(8,128)(2,1)S(1)} %pad_maximum_fusion.2.refs_2_.refs_0_), channel_id=1, source_target_pairs={{0,4},{2,6},{4,8},{6,10},{8,12},{10,14},{12,16},{14,18},{16,20},{1... | collective-permute-start | bytes 786440 | tf_op jit(solution)/shard_map/ppermute | solution.py:23
  13.5 19.7 %copy-start.25 = (bf16[2048,512]{1,0:T(8,128)(2,1)S(1)}, bf16[2048,512]{1,0:T(8,128)(2,1)}, u32[]{:S(2)}) copy-start(bf16[2048,512]{1,0:T(8,128)(2,1)} %param.12) | copy-start | bytes 6291460
  14.4 11.4 %collective-permute-start.14 = (bf16[2,128,512]{2,1,0:T(8,128)(2,1)S(1)}, bf16[2,128,512]{2,1,0:T(8,128)(2,1)S(1)}, u32[]{:S(2)}, u32[]{:S(2)}) collective-permute-start(bf16[2,128,512]{2,1,0:T(8,128)(2,1)S(1)} %pad_maximum_fusion.refs_0_.refs_1_), channel_id=1, source_target_pairs={{4,0},{6,2},{8,4},{10,6},{12,8},{14,10},{16,12},{18,14},{20,16},{2... | collective-permute-start | bytes 786440 | tf_op jit(solution)/shard_map/ppermute | solution.py:23
  20.4 30.8 %collective-permute-start.1 = (bf16[128,2048]{1,0:T(8,128)(2,1)S(1)}, bf16[128,2048]{1,0:T(8,128)(2,1)S(1)}, u32[]{:S(2)}, u32[]{:S(2)}) collective-permute-start(bf16[128,2048]{1,0:T(8,128)(2,1)S(1)} %copy-done.32), channel_id=1, source_target_pairs={{0,1},{1,0},{2,3},{3,2},{4,5},{5,4},{6,7},{7,6},{8,9},{9,8},{10,11... | collective-permute-start | bytes 1572872 | tf_op jit(solution)/shard_map/ppermute | solution.py:27
  23.2 10.9 %copy-start.15 = (bf16[2,128,512]{2,1,0:T(8,128)(2,1)}, bf16[2,128,512]{2,1,0:T(8,128)(2,1)S(1)}, u32[]{:S(2)}) copy-start(bf16[2,128,512]{2,1,0:T(8,128)(2,1)S(1)} %collective-permute-done.3.refs_5_) | copy-start | bytes 786436
  23.2 12.9 %collective-permute-start.5 = (bf16[2,128,512]{2,1,0:T(8,128)(2,1)S(1)}, bf16[2,128,512]{2,1,0:T(8,128)(2,1)S(1)}, u32[]{:S(2)}, u32[]{:S(2)}) collective-permute-start(bf16[2,128,512]{2,1,0:T(8,128)(2,1)S(1)} %collective-permute-done.3.refs_5_), channel_id=1, source_target_pairs={{0,4},{2,6},{4,8},{6,10},{8,12},{10,14},{12,16},{14,18},{16,20},{1... | collective-permute-start | bytes 786440 | tf_op jit(solution)/shard_map/ppermute | solution.py:23
  25.7 12.4 %collective-permute-start.16 = (bf16[2,128,512]{2,1,0:T(8,128)(2,1)S(1)}, bf16[2,128,512]{2,1,0:T(8,128)(2,1)S(1)}, u32[]{:S(2)}, u32[]{:S(2)}) collective-permute-start(bf16[2,128,512]{2,1,0:T(8,128)(2,1)S(1)} %collective-permute-done.14.refs_5_), channel_id=1, source_target_pairs={{4,0},{6,2},{8,4},{10,6},{12,8},{14,10},{16,12},{18,14},{20,16},{2... | collective-permute-start | bytes 786440 | tf_op jit(solution)/shard_map/ppermute | solution.py:23
  34.2 26.0 %collective-permute-start.4 = (bf16[2,128,512]{2,1,0:T(8,128)(2,1)S(1)}, bf16[2,128,512]{2,1,0:T(8,128)(2,1)S(1)}, u32[]{:S(2)}, u32[]{:S(2)}) collective-permute-start(bf16[2,128,512]{2,1,0:T(8,128)(2,1)S(1)} %pad_maximum_fusion.3.refs_3_.refs_0_), channel_id=1, source_target_pairs={{0,4},{2,6},{4,8},{6,10},{8,12},{10,14},{12,16},{14,18},{16,20},{1... | collective-permute-start | bytes 786440 | tf_op jit(solution)/shard_map/ppermute | solution.py:23
  36.1 16.0 %copy-start.17 = (bf16[2,128,512]{2,1,0:T(8,128)(2,1)}, bf16[2,128,512]{2,1,0:T(8,128)(2,1)S(1)}, u32[]{:S(2)}) copy-start(bf16[2,128,512]{2,1,0:T(8,128)(2,1)S(1)} %collective-permute-done.5.refs_7_) | copy-start | bytes 786436
  36.1 19.3 %collective-permute-start.7 = (bf16[2,128,512]{2,1,0:T(8,128)(2,1)S(1)}, bf16[2,128,512]{2,1,0:T(8,128)(2,1)S(1)}, u32[]{:S(2)}, u32[]{:S(2)}) collective-permute-start(bf16[2,128,512]{2,1,0:T(8,128)(2,1)S(1)} %collective-permute-done.5.refs_7_), channel_id=1, source_target_pairs={{0,8},{2,10},{4,12},{6,14},{8,16},{10,18},{12,20},{14,22},{16,24},... | collective-permute-start | bytes 786440 | tf_op jit(solution)/shard_map/ppermute | solution.py:23
  38.1 14.0 %copy-start.9 = (bf16[2,128,512]{2,1,0:T(8,128)(2,1)}, bf16[2,128,512]{2,1,0:T(8,128)(2,1)S(1)}, u32[]{:S(2)}) copy-start(bf16[2,128,512]{2,1,0:T(8,128)(2,1)S(1)} %collective-permute-done.16.refs_6_) | copy-start | bytes 786436
  38.1 19.4 %collective-permute-start.18 = (bf16[2,128,512]{2,1,0:T(8,128)(2,1)S(1)}, bf16[2,128,512]{2,1,0:T(8,128)(2,1)S(1)}, u32[]{:S(2)}, u32[]{:S(2)}) collective-permute-start(bf16[2,128,512]{2,1,0:T(8,128)(2,1)S(1)} %collective-permute-done.16.refs_6_), channel_id=1, source_target_pairs={{8,0},{10,2},{12,4},{14,6},{16,8},{18,10},{20,12},{22,14},{24,16},... | collective-permute-start | bytes 786440 | tf_op jit(solution)/shard_map/ppermute | solution.py:23
  46.4 72.6 %copy-start.35 = (s32[10]{0:T(128)S(1)}, s32[10]{0:T(128)}, u32[]{:S(2)}) copy-start(s32[10]{0:T(128)} %constant.37.clone) | copy-start | bytes 124
  52.2 9.9 %collective-permute-start.15 = (bf16[2,128,512]{2,1,0:T(8,128)(2,1)S(1)}, bf16[2,128,512]{2,1,0:T(8,128)(2,1)S(1)}, u32[]{:S(2)}, u32[]{:S(2)}) collective-permute-start(bf16[2,128,512]{2,1,0:T(8,128)(2,1)S(1)} %pad_maximum_fusion.1.refs_1_.refs_2_), channel_id=1, source_target_pairs={{4,0},{6,2},{8,4},{10,6},{12,8},{14,10},{16,12},{18,14},{20,16},{2... | collective-permute-start | bytes 786440 | tf_op jit(solution)/shard_map/ppermute | solution.py:23
  54.1 26.8 %collective-permute-start.11 = (bf16[2,256,512]{2,1,0:T(8,128)(2,1)S(1)}, bf16[2,256,512]{2,1,0:T(8,128)(2,1)S(1)}, u32[]{:S(2)}, u32[]{:S(2)}) collective-permute-start(bf16[2,256,512]{2,1,0:T(8,128)(2,1)S(1)} %maximum_maximum_fusion), channel_id=1, source_target_pairs={{0,128},{2,130},{4,132},{6,134},{8,136},{10,138},{12,140},{14,142}... | collective-permute-start | bytes 1572872 | tf_op jit(solution)/shard_map/ppermute | solution.py:23
  56.1 33.7 %collective-permute-start.10 = (bf16[2,256,512]{2,1,0:T(8,128)(2,1)S(1)}, bf16[2,256,512]{2,1,0:T(8,128)(2,1)S(1)}, u32[]{:S(2)}, u32[]{:S(2)}) collective-permute-start(bf16[2,256,512]{2,1,0:T(8,128)(2,1)S(1)} %maximum_maximum_fusion), channel_id=1, source_target_pairs={{0,64},{2,66},{4,68},{6,70},{8,72},{10,74},{12,76},{14,78},{16,80}... | collective-permute-start | bytes 1572872 | tf_op jit(solution)/shard_map/ppermute | solution.py:23
  57.5 0.7 copy-start.11
  58.2 52.5 %collective-permute-start.9 = (bf16[2,256,512]{2,1,0:T(8,128)(2,1)S(1)}, bf16[2,256,512]{2,1,0:T(8,128)(2,1)S(1)}, u32[]{:S(2)}, u32[]{:S(2)}) collective-permute-start(bf16[2,256,512]{2,1,0:T(8,128)(2,1)S(1)} %maximum_maximum_fusion), channel_id=1, source_target_pairs={{0,32},{2,34},{4,36},{6,38},{8,40},{10,42},{12,44},{14,46},{16,48}... | collective-permute-start | bytes 1572872 | tf_op jit(solution)/shard_map/ppermute | solution.py:23
  60.1 53.5 %collective-permute-start.2 = (bf16[2,256,512]{2,1,0:T(8,128)(2,1)S(1)}, bf16[2,256,512]{2,1,0:T(8,128)(2,1)S(1)}, u32[]{:S(2)}, u32[]{:S(2)}) collective-permute-start(bf16[2,256,512]{2,1,0:T(8,128)(2,1)S(1)} %maximum_maximum_fusion), channel_id=1, source_target_pairs={{0,2},{2,4},{4,6},{6,8},{8,10},{10,12},{12,14},{14,16},{16,18},{18... | collective-permute-start | bytes 1572872 | tf_op jit(solution)/shard_map/ppermute | solution.py:23
  62.1 14.4 %collective-permute-start.6 = (bf16[2,128,512]{2,1,0:T(8,128)(2,1)S(1)}, bf16[2,128,512]{2,1,0:T(8,128)(2,1)}, u32[]{:S(2)}, u32[]{:S(2)}) collective-permute-start(bf16[2,128,512]{2,1,0:T(8,128)(2,1)S(1)} %collective-permute-done.4.refs_6_), channel_id=1, source_target_pairs={{0,4},{2,6},{4,8},{6,10},{8,12},{10,14},{12,16},{14,18},{16,20},{1... | collective-permute-start | bytes 786440 | tf_op jit(solution)/shard_map/ppermute | solution.py:23
  76.4 39.9 %collective-permute-start.17 = (bf16[2,128,512]{2,1,0:T(8,128)(2,1)S(1)}, bf16[2,128,512]{2,1,0:T(8,128)(2,1)S(1)}, u32[]{:S(2)}, u32[]{:S(2)}) collective-permute-start(bf16[2,128,512]{2,1,0:T(8,128)(2,1)S(1)} %collective-permute-done.15.refs_5_), channel_id=1, source_target_pairs={{4,0},{6,2},{8,4},{10,6},{12,8},{14,10},{16,12},{18,14},{20,16},{2... | collective-permute-start | bytes 786440 | tf_op jit(solution)/shard_map/ppermute | solution.py:23
  80.9 0.8 copy-start.1
  81.7 37.5 %collective-permute-start.8 = (bf16[2,128,512]{2,1,0:T(8,128)(2,1)}, bf16[2,128,512]{2,1,0:T(8,128)(2,1)}, u32[]{:S(2)}, u32[]{:S(2)}) collective-permute-start(bf16[2,128,512]{2,1,0:T(8,128)(2,1)} %collective-permute-done.6.refs_8_), channel_id=1, source_target_pairs={{0,8},{2,10},{4,12},{6,14},{8,16},{10,18},{12,20},{14,22},{16,24},... | collective-permute-start | bytes 786440 | tf_op jit(solution)/shard_map/ppermute | solution.py:23
  89.8 0.8 copy-start.3
  90.6 51.1 %collective-permute-start.22 = (bf16[2,256,512]{2,1,0:T(8,128)(2,1)}, bf16[2,256,512]{2,1,0:T(8,128)(2,1)}, u32[]{:S(2)}, u32[]{:S(2)}) collective-permute-start(bf16[2,256,512]{2,1,0:T(8,128)(2,1)} %maximum_maximum_fusion.1), channel_id=1, source_target_pairs={{128,0},{130,2},{132,4},{134,6},{136,8},{138,10},{140,12},{142,14}... | collective-permute-start | bytes 1572872 | tf_op jit(solution)/shard_map/ppermute | solution.py:23
  110.7 0.8 copy-start.5
  111.5 30.2 %collective-permute-start.21 = (bf16[2,256,512]{2,1,0:T(8,128)(2,1)}, bf16[2,256,512]{2,1,0:T(8,128)(2,1)}, u32[]{:S(2)}, u32[]{:S(2)}) collective-permute-start(bf16[2,256,512]{2,1,0:T(8,128)(2,1)} %maximum_maximum_fusion.1), channel_id=1, source_target_pairs={{64,0},{66,2},{68,4},{70,6},{72,8},{74,10},{76,12},{78,14},{80,16}... | collective-permute-start | bytes 1572872 | tf_op jit(solution)/shard_map/ppermute | solution.py:23
  113.6 0.8 copy-start.7
  114.4 27.3 %collective-permute-start.20 = (bf16[2,256,512]{2,1,0:T(8,128)(2,1)}, bf16[2,256,512]{2,1,0:T(8,128)(2,1)}, u32[]{:S(2)}, u32[]{:S(2)}) collective-permute-start(bf16[2,256,512]{2,1,0:T(8,128)(2,1)} %maximum_maximum_fusion.1), channel_id=1, source_target_pairs={{32,0},{34,2},{36,4},{38,6},{40,8},{42,10},{44,12},{46,14},{48,16}... | collective-permute-start | bytes 1572872 | tf_op jit(solution)/shard_map/ppermute | solution.py:23
  116.4 0.7 copy-start.19
  117.1 24.6 %collective-permute-start.13 = (bf16[2,256,512]{2,1,0:T(8,128)(2,1)}, bf16[2,256,512]{2,1,0:T(8,128)(2,1)}, u32[]{:S(2)}, u32[]{:S(2)}) collective-permute-start(bf16[2,256,512]{2,1,0:T(8,128)(2,1)} %maximum_maximum_fusion.1), channel_id=1, source_target_pairs={{2,0},{4,2},{6,4},{8,6},{10,8},{12,10},{14,12},{16,14},{18,16},{20... | collective-permute-start | bytes 1572872 | tf_op jit(solution)/shard_map/ppermute | solution.py:23
  119.2 22.6 %collective-permute-start.19 = (bf16[2,128,512]{2,1,0:T(8,128)(2,1)}, bf16[2,128,512]{2,1,0:T(8,128)(2,1)S(1)}, u32[]{:S(2)}, u32[]{:S(2)}) collective-permute-start(bf16[2,128,512]{2,1,0:T(8,128)(2,1)} %copy-done.19), channel_id=1, source_target_pairs={{8,0},{10,2},{12,4},{14,6},{16,8},{18,10},{20,12},{22,14},{24,16},... | collective-permute-start | bytes 786440 | tf_op jit(solution)/shard_map/ppermute | solution.py:23
  121.3 1.0 copy-start.2
  122.4 1.0 copy-start.4
  123.4 1.0 copy-start.6
  124.4 1.0 copy-start.8
  125.5 0.9 copy-start.16
  126.4 0.9 copy-start.18
  127.4 0.9 copy-start.22
  128.3 0.9 copy-start.24
  129.3 32.4 %copy-start.30 = (bf16[512,2048]{1,0:T(8,128)(2,1)S(1)}, bf16[512,2048]{1,0:T(8,128)(2,1)}, u32[]{:S(2)}) copy-start(bf16[512,2048]{1,0:T(8,128)(2,1)} %param.13) | copy-start | bytes 6291460
  141.7 26.2 %copy-start.14 = (bf16[2,128,512]{2,1,0:T(8,128)(2,1)S(1)}, bf16[2,128,512]{2,1,0:T(8,128)(2,1)}, u32[]{:S(2)}) copy-start(bf16[2,128,512]{2,1,0:T(8,128)(2,1)} %copy-done.13) | copy-start | bytes 786436
  141.7 26.2 %copy-start.20 = (bf16[2,128,512]{2,1,0:T(8,128)(2,1)S(1)}, bf16[2,128,512]{2,1,0:T(8,128)(2,1)}, u32[]{:S(2)}) copy-start(bf16[2,128,512]{2,1,0:T(8,128)(2,1)} %copy-done.19) | copy-start | bytes 786436
  141.7 15.1 %collective-permute-start.29 = (f32[4,2,256]{2,1,0:T(2,128)S(1)}, f32[4,2,256]{2,1,0:T(2,128)S(1)}, u32[]{:S(2)}, u32[]{:S(2)}) collective-permute-start(f32[4,2,256]{2,1,0:T(2,128)S(1)} %get-tuple-element.19.refs_3_), channel_id=1, source_target_pairs={{128,0},{130,2},{132,4},{134,6},{136,8},{138,10},{140,12},{142,14}... | collective-permute-start | bytes 24584 | tf_op jit(solution)/shard_map/ppermute | solution.py:23
  143.2 15.6 %collective-permute-start.28 = (f32[4,2,256]{2,1,0:T(2,128)S(1)}, f32[4,2,256]{2,1,0:T(2,128)S(1)}, u32[]{:S(2)}, u32[]{:S(2)}) collective-permute-start(f32[4,2,256]{2,1,0:T(2,128)S(1)} %get-tuple-element.19.refs_3_), channel_id=1, source_target_pairs={{64,0},{66,2},{68,4},{70,6},{72,8},{74,10},{76,12},{78,14},{80,16}... | collective-permute-start | bytes 24584 | tf_op jit(solution)/shard_map/ppermute | solution.py:23
  145.1 17.0 %collective-permute-start.27 = (f32[4,2,256]{2,1,0:T(2,128)S(1)}, f32[4,2,256]{2,1,0:T(2,128)S(1)}, u32[]{:S(2)}, u32[]{:S(2)}) collective-permute-start(f32[4,2,256]{2,1,0:T(2,128)S(1)} %get-tuple-element.19.refs_3_), channel_id=1, source_target_pairs={{32,0},{34,2},{36,4},{38,6},{40,8},{42,10},{44,12},{46,14},{48,16}... | collective-permute-start | bytes 24584 | tf_op jit(solution)/shard_map/ppermute | solution.py:23
  148.5 19.3 %collective-permute-start.26 = (f32[4,2,256]{2,1,0:T(2,128)S(1)}, f32[4,2,256]{2,1,0:T(2,128)S(1)}, u32[]{:S(2)}, u32[]{:S(2)}) collective-permute-start(f32[4,2,256]{2,1,0:T(2,128)S(1)} %get-tuple-element.19.refs_3_), channel_id=1, source_target_pairs={{16,0},{18,2},{20,4},{22,6},{24,8},{26,10},{28,12},{30,14},{32,16}... | collective-permute-start | bytes 24584 | tf_op jit(solution)/shard_map/ppermute | solution.py:23
  150.4 17.4 %collective-permute-start.25 = (f32[4,2,256]{2,1,0:T(2,128)S(1)}, f32[4,2,256]{2,1,0:T(2,128)S(1)}, u32[]{:S(2)}, u32[]{:S(2)}) collective-permute-start(f32[4,2,256]{2,1,0:T(2,128)S(1)} %get-tuple-element.19.refs_3_), channel_id=1, source_target_pairs={{8,0},{10,2},{12,4},{14,6},{16,8},{18,10},{20,12},{22,14},{24,16},... | collective-permute-start | bytes 24584 | tf_op jit(solution)/shard_map/ppermute | solution.py:23
  156.9 10.9 %collective-permute-start.24 = (f32[4,2,256]{2,1,0:T(2,128)S(1)}, f32[4,2,256]{2,1,0:T(2,128)S(1)}, u32[]{:S(2)}, u32[]{:S(2)}) collective-permute-start(f32[4,2,256]{2,1,0:T(2,128)S(1)} %get-tuple-element.19.refs_3_), channel_id=1, source_target_pairs={{4,0},{6,2},{8,4},{10,6},{12,8},{14,10},{16,12},{18,14},{20,16},{2... | collective-permute-start | bytes 24584 | tf_op jit(solution)/shard_map/ppermute | solution.py:23
  158.8 9.0 %collective-permute-start.23 = (f32[4,2,256]{2,1,0:T(2,128)S(1)}, f32[4,2,256]{2,1,0:T(2,128)S(1)}, u32[]{:S(2)}, u32[]{:S(2)}) collective-permute-start(f32[4,2,256]{2,1,0:T(2,128)S(1)} %get-tuple-element.19.refs_3_), channel_id=1, source_target_pairs={{2,0},{4,2},{6,4},{8,6},{10,8},{12,10},{14,12},{16,14},{18,16},{20... | collective-permute-start | bytes 24584 | tf_op jit(solution)/shard_map/ppermute | solution.py:23
  162.1 10.1 %copy-start.26 = (bf16[2048,512]{1,0:T(8,128)(2,1)S(1)}, bf16[2048,512]{1,0:T(8,128)(2,1)}, u32[]{:S(2)}) copy-start(bf16[2048,512]{1,0:T(8,128)(2,1)} %param.12) | copy-start | bytes 6291460
  162.1 20.2 %collective-permute-start.12 = (bf16[128,2048]{1,0:T(8,128)(2,1)S(1)}, bf16[128,2048]{1,0:T(8,128)(2,1)S(1)}, u32[]{:S(2)}, u32[]{:S(2)}) collective-permute-start(bf16[128,2048]{1,0:T(8,128)(2,1)S(1)} %convolution_convert_fusion), channel_id=1, source_target_pairs={{0,1},{1,0},{2,3},{3,2},{4,5},{5,4},{6,7},{7,6},{8,9},{9,8},{10,11... | collective-permute-start | bytes 1572872 | tf_op jit(solution)/shard_map/ppermute | solution.py:27
  172.2 1.6 copy-start.28
  174.6 1.8 copy-start.10
  174.6 1.8 copy-start.12
  175.4 13.6 %collective-permute-start.30 = (bf16[128,2048]{1,0:T(8,128)(2,1)S(1)}, bf16[128,2048]{1,0:T(8,128)(2,1)S(1)}, u32[]{:S(2)}, u32[]{:S(2)}) collective-permute-start(bf16[128,2048]{1,0:T(8,128)(2,1)S(1)} %fusion.6), channel_id=1, source_target_pairs={{0,1},{1,0},{2,3},{3,2},{4,5},{5,4},{6,7},{7,6},{8,9},{9,8},{10,11... | collective-permute-start | bytes 1572872 | tf_op jit(solution)/shard_map/ppermute | solution.py:27
  181.6 1.0 copy-start.31
  182.4 6.7 %copy-start.34 = (f32[2048]{0:T(1024)S(1)}, f32[2048]{0:T(1024)}, u32[]{:S(2)}) copy-start(f32[2048]{0:T(1024)} %param.9) | copy-start | bytes 24580
  183.9 6.2 %copy-start.33 = (bf16[128,2048]{1,0:T(8,128)(2,1)S(1)}, bf16[128,2048]{1,0:T(8,128)(2,1)}, u32[]{:S(2)}) copy-start(bf16[128,2048]{1,0:T(8,128)(2,1)} %param.14) | copy-start | bytes 1572868
  (3 other events, 2.1 us)

commit v3 on v2

--- a/solution.py
+++ b/solution.py
@@ -15,6 +15,8 @@
 BF16 = jnp.bfloat16
 NN = (((1,), (0,)), ((), ()))
 NT = (((1,), (1,)), ((), ()))
+TN = (((0,), (0,)), ((), ()))
+NEAR = (1, 2, 4)
 
 
 def shifted(value, by):
@@ -58,13 +60,15 @@
     return jnp.where(rows >= keys, 0.0, NEG).astype(F32)
 
 
-def query_kernel(groups, tp_ref, bias_ref, *refs):
+def query_kernel(groups, where_ref, bias_ref, *refs):
     refs = list(refs)
     qg = [refs.pop(0) for _ in range(2)]
     kv = [refs.pop(0) for _ in range(2)]
     fetched = [[refs.pop(0) for _ in range(n)] for n in groups]
-    mixed_ref, dq_ref, stat_ref = refs
-    is_second = tp_ref[0] == 1
+    one = refs.pop(0)
+    two = [refs.pop(0) for _ in range(2)]
+    mixed_ref, dq_ref, stat_ref, *back_refs = refs
+    is_second = where_ref[0] == 1
     factor = HD ** (-0.5)
     causal = causal_bias(0)
     lane = lax.broadcasted_iota(jnp.int32, (BLOCK, HD), 1)
@@ -73,8 +77,10 @@
         keys, values = [
             jnp.concatenate(
                 [piece(kv, which, slot)]
-                + [near(is_second, kv, fetched[0], which, slot, -d) for d in (1, 2, 4)]
-                + [piece(f, which, slot) for f in fetched[1:]],
+                + [near(is_second, kv, fetched[0], which, slot, -d) for d in NEAR]
+                + [piece(f, which, slot) for f in fetched[1:]]
+                + [one[which, out, :]]
+                + [t[0, which, out, :] for t in two],
                 axis=0,
             )
             for which in range(2)
@@ -86,24 +92,32 @@
         weight = jnp.exp(score - peak)
         total = jnp.sum(weight, axis=-1, keepdims=True)
         prob = weight * (1.0 / total)
-        mixed = dot(prob.astype(BF16), values, NN).astype(BF16)
+        prob_b = prob.astype(BF16)
+        mixed = dot(prob_b, values, NN).astype(BF16)
         mixed_ref[out, :] = mixed
         inner = jnp.sum(mixed.astype(F32) * grad.astype(F32), axis=-1, keepdims=True)
         grad_score = (prob * (dot(grad, values, NT) - inner)).astype(BF16)
         dq_ref[out, :] = (dot(grad_score, keys, NN) * factor).astype(BF16)
         stat = jnp.where(lane == 0, peak + jnp.log(total), inner)
         stat_ref[0, :, out] = jnp.transpose(stat)[:2]
-
-
-def key_kernel(half, groups, tp_ref, *refs):
+        first = keys.shape[0] - len(back_refs) * BLOCK
+        grad_keys = (dot(grad_score[:, first:], query, TN) * factor).astype(BF16)
+        grad_values = dot(prob_b[:, first:], grad, TN).astype(BF16)
+        for at, ref in enumerate(back_refs):
+            ref[0, out, :] = grad_keys[at * BLOCK : (at + 1) * BLOCK]
+            ref[1, out, :] = grad_values[at * BLOCK : (at + 1) * BLOCK]
+
+
+def key_kernel(half, groups, n_back, where_ref, *refs):
     refs = list(refs)
     kv = refs.pop(0)
     qg = [refs.pop(0) for _ in range(2)]
     stat = refs.pop(0)
     later = [[refs.pop(0) for _ in range(n)] for n in groups]
     later_stats = [refs.pop(0) for _ in groups]
+    back = [refs.pop(0) for _ in range(n_back)]
     (out_ref,) = refs
-    is_second = tp_ref[0] == 1
+    is_second = where_ref[0] == 1
     factor = HD ** (-0.5)
     causal = causal_bias(1)
 
@@ -116,14 +130,14 @@
         queries, grads = [
             jnp.concatenate(
                 [piece(qg, which, slot)]
-                + [near(is_second, qg, later[0], which, slot, d) for d in (1, 2, 4)]
+                + [near(is_second, qg, later[0], which, slot, d) for d in NEAR]
                 + [f[0][which, rows, :] for f in later[1:]],
                 axis=0,
             )
             for which in range(2)
         ]
         near_stats = []
-        for d in (1, 2, 4):
+        for d in NEAR:
             options = [
                 stat_of(stat if here else later_stats[0], s) for here, s in near_slots(d, slot)
             ]
@@ -135,21 +149,27 @@
         score = jnp.concatenate([score[:, :BLOCK] + causal, score[:, BLOCK:]], axis=1)
         prob = jnp.exp(score - stats[0:1])
         grad_score = (prob * (dot(kv[1, rows, :], grads, NT) - stats[1:2])).astype(BF16)
-        out_ref[0, rows, :] = (dot(grad_score, queries, NN) * factor).astype(BF16)
-        out_ref[1, rows, :] = dot(prob.astype(BF16), grads, NN).astype(BF16)
+        totals = [
+            dot(grad_score, queries, NN) * factor,
+            dot(prob.astype(BF16), grads, NN),
+        ]
+        for which in range(2):
+            for ref in back:
+                totals[which] += ref[which, rows, :].astype(F32)
+            out_ref[which, rows, :] = totals[which].astype(BF16)
 
 
 def head_spec(a):
     if a.ndim == 2:
-        return pl.BlockSpec((a.shape[0], HD), lambda h, t: (0, h))
-    return pl.BlockSpec((a.shape[0], a.shape[1], HD), lambda h, t: (0, 0, h))
+        return pl.BlockSpec((a.shape[0], HD), lambda h, w: (0, h))
+    return pl.BlockSpec((a.shape[0], a.shape[1], HD), lambda h, w: (0, 0, h))
 
 
 def stat_spec(a):
-    return pl.BlockSpec((1,) + a.shape[1:], lambda h, t: (h, 0, 0))
-
-
-def call(kernel, turn, operands, in_specs, outs, out_specs, heads, keys, name):
+    return pl.BlockSpec((1,) + a.shape[1:], lambda h, w: (h, 0, 0))
+
+
+def call(kernel, where, operands, in_specs, outs, out_specs, heads, keys, name):
     rows = outs[0].shape[-2]
     return pl.pallas_call(
         kernel,
@@ -157,58 +177,65 @@
         grid_spec=pltpu.PrefetchScalarGridSpec(
             num_scalar_prefetch=1, grid=(heads,), in_specs=in_specs, out_specs=out_specs
         ),
-        compiler_params=pltpu.CompilerParams(vmem_limit_bytes=12 * 2**20),
+        compiler_params=pltpu.CompilerParams(vmem_limit_bytes=10 * 2**20),
         cost_estimate=pl.CostEstimate(
             flops=4 * 2 * rows * keys * HD * heads,
             bytes_accessed=6 * 2**20,
             transcendentals=rows * keys * heads,
         ),
         name=name,
-    )(turn, *operands)
-
-
-def query_side(turn, bias, qg, kv, fetched):
+    )(where, *operands)
+
+
+def query_side(where, bias, qg, kv, fetched, one, column):
     rows, width = 2 * qg[0].shape[1], qg[0].shape[2]
     heads = width // HD
-    operands = [*qg, *kv, *[a for f in fetched for a in f]]
+    far = [a for f in fetched for a in f] + [one, column]
+    far = [pltpu.with_memory_space_constraint(a, pltpu.HBM) for a in far]
+    column = far.pop()
+    operands = [*qg, *kv, *far]
     row_out = jax.ShapeDtypeStruct((rows, width), BF16)
     stat_out = jax.ShapeDtypeStruct((heads, 2, rows), F32)
+    back_out = jax.ShapeDtypeStruct((2, rows, width), BF16)
+
+    def column_spec(back):
+        return pl.BlockSpec(
+            (1, 2, rows, HD), lambda h, w: (jnp.maximum(w[1] - back, 0), 0, 0, h)
+        )
+
     return call(
         functools.partial(query_kernel, tuple(len(f) for f in fetched)),
-        turn,
-        [bias, *operands],
-        [pl.BlockSpec(bias.shape, lambda h, t: (0, 0, 0))] + [head_spec(a) for a in operands],
-        [row_out, row_out, stat_out],
-        [head_spec(row_out), head_spec(row_out), stat_spec(stat_out)],
+        where,
+        [bias, *operands, column, column],
+        [pl.BlockSpec(bias.shape, lambda h, w: (0, 0, 0))]
+        + [head_spec(a) for a in operands]
+        + [column_spec(1), column_spec(2)],
+        [row_out, row_out, stat_out] + [back_out] * 3,
+        [head_spec(row_out), head_spec(row_out), stat_spec(stat_out)] + [head_spec(back_out)] * 3,
         heads,
         bias.shape[2],
         "query_side",
     )
 
 
-def key_side(half, turn, kv, qg, stat, later, later_stats):
+def key_side(half, where, kv, qg, stat, later, later_stats, returned):
     rows, width = kv[0].shape[1], kv[0].shape[2]
     heads = width // HD
-
-    def half_spec(f):
-        if len(f) == 2:
-            return f[half], head_spec(f[half])
-        return f[0], pl.BlockSpec((2, rows, HD), lambda h, t: (0, half, h))
-
-    far = [half_spec(f) for f in later[1:]]
-    operands = [kv[half], *qg, stat, *later[0], *[a for a, _ in far], *later_stats]
+    half_of_whole = pl.BlockSpec((2, rows, HD), lambda h, w: (0, half, h))
+    far = [f[half] for f in later[1:]]
+    operands = [kv[half], *qg, stat, *later[0], *far, *later_stats, *returned]
     in_specs = (
         [head_spec(a) for a in (kv[half], *qg)]
         + [stat_spec(stat)]
-        + [head_spec(a) for a in later[0]]
-        + [s for _, s in far]
+        + [head_spec(a) for a in (*later[0], *far)]
         + [stat_spec(a) for a in later_stats]
+        + [half_of_whole] * len(returned)
     )
     out = jax.ShapeDtypeStruct((2, rows, width), BF16)
     groups = (len(later[0]),) + (1,) * len(far)
     (result,) = call(
-        functools.partial(key_kernel, half, groups),
-        turn,
+        functools.partial(key_kernel, half, groups, len(returned)),
+        where,
         operands,
         in_specs,
         [out],
@@ -228,19 +255,9 @@
     return lax.dot_general(a, b, NT, preferred_element_type=F32)
 
 
-def exchange(own, other, sign, levels):
-    whole = jnp.concatenate([own, other], axis=1)
-    got = {}
-    for at, rows in enumerate((own, other)):
-        last, reached = rows, 0
-        for s in (1, 2, 3):
-            last = shifted(last, sign * (2**s - reached))
-            reached = 2**s
-            got[s, at] = last
-    return [
-        (got[s, 0], got[s, 1]) if s in (1, 2, 3) else (shifted(whole, sign * 2**s),)
-        for s in range(levels)
-    ]
+def relay(two, sign):
+    four = shifted(two, sign * 2)
+    return two, four, shifted(four, sign * 4)
 
 
 def per_device(series, norm_gain, w_query, w_key, w_value, w_out, out_grad):
@@ -248,9 +265,12 @@
     half = series.shape[0]
     blocks = 2 * half // BLOCK
     tp_index = lax.axis_index("tp").astype(jnp.int32)
-    turn = tp_index[None]
+    seq_index = lax.axis_index("seq").astype(jnp.int32)
+    seq_size = lax.axis_size("seq")
+    run = seq_size // 4
+    where = jnp.stack([tp_index, seq_index // run])
     slots = jnp.arange(blocks, dtype=jnp.int32)
-    global_block = lax.axis_index("seq") * blocks + (slots + 2 * tp_index) % blocks
+    global_block = seq_index * blocks + (slots + 2 * tp_index) % blocks
     distances = [1, 2, 4] + [blocks * 2**s for s in range(1, levels)]
     reach = jnp.repeat(jnp.array([0] + distances, jnp.int32), BLOCK)
     bias = jnp.where(global_block[:, None] >= reach[None], 0.0, NEG).astype(F32)[:, None, :]
@@ -270,19 +290,34 @@
             [matmul(rows, w_query).astype(BF16), matmul_t(grad_rows, w_out).astype(BF16)]
         )
 
-    kv = (key_value(normed), key_value(normed_other))
-    qg = (query_grad(normed, out_grad), query_grad(normed_other, out_grad_other))
-    fetched = exchange(*kv, 1, levels)
-    later = exchange(*qg, -1, levels)
-    mixed, grad_query, stat = query_side(turn, bias, qg, kv, fetched)
-    stat, later = lax.optimization_barrier((stat, later))
-    later_stats = [shifted(stat, -(2**s)) for s in range(levels)]
+    kv_own = key_value(normed)
+    qg_own = query_grad(normed, out_grad)
+    kv_two, qg_two = shifted(kv_own, 2), shifted(qg_own, -2)
+    normed_other, kv_two, qg_two = lax.optimization_barrier((normed_other, kv_two, qg_two))
+    kv = (kv_own, key_value(normed_other))
+    qg = (qg_own, query_grad(normed_other, out_grad_other))
+    kv_all = jnp.concatenate(kv, axis=1)
+    column = lax.all_gather(
+        kv_all,
+        "seq",
+        axis_index_groups=[list(range(k, seq_size, run)) for k in range(run)],
+    )
+    kv_far = [relay(kv_two, 1), relay(shifted(kv[1], 2), 1)]
+    qg_far = [relay(qg_two, -1), relay(shifted(qg[1], -2), -1)]
+    fetched = [(shifted(kv_all, 1),)] + list(zip(*kv_far))
+    later = [(shifted(jnp.concatenate(qg, axis=1), -1),)] + list(zip(*qg_far))
+    mixed, grad_query, stat, *backs = query_side(
+        where, bias, qg, kv, fetched, shifted(kv_all, 16), column
+    )
+    stat, backs, later = lax.optimization_barrier((stat, backs, later))
+    returned = [shifted(b, -by) for b, by in zip(backs, (16, run, 2 * run))]
+    later_stats = [shifted(stat, -by) for by in (1, 2, 4, 8)]
     attn_other = swap_tp(matmul(mixed[half:], w_out).astype(BF16))
     attn_rows = matmul(mixed[:half], w_out) + attn_other.astype(F32)
     layer_out = (series_f + attn_rows).astype(BF16)
 
     def back(at):
-        grad_kv = key_side(at, turn, kv, qg, stat, later, later_stats)
+        grad_kv = key_side(at, where, kv, qg, stat, later, later_stats, returned)
         rows = slice(at * half, (at + 1) * half)
         return (
             matmul_t(grad_query[rows], w_query)

time: 194 us -> 205 us (1.057)
  the two profiles are of different devices: /device:TPU:24 before, /device:TPU:46 now
where the time goes in v3:
time: 205 us; the launch traced here: 204 us
  starting transfers between devices  103 us (50%)
  waiting for transfers between devices  37.7 us (18%)
  Pallas kernels  24.8 us (12%)
  matrix products  15 us (7%)
  between operations  14.7 us (7%)
  other arithmetic  6.8 us (3%)
  local copies, waits for them, and re-layouts  2.55 us (1%)
    ppermute x22, starting transfers between devices, shifted(): return lax.ppermute(value, 'seq', pairs)  95.1 us
    ppermute x22, waiting for transfers between devices, shifted(): return lax.ppermute(value, 'seq', pairs)  30.1 us
    pallas_call x3, Pallas kernels, call(): pl.pallas_call(kernel, out_shape=outs, grid_spec=pltpu.PrefetchScalarGrid...  24.8 us
    dot_general x8, matrix products, matmul_t(): return lax.dot_general(a, b, NT, preferred_element_type=F32)  7.9 us
    ppermute x4, waiting for transfers between devices, swap_tp(): return lax.ppermute(value, 'tp', [(0, 1), (1, 0)])  7.59 us
    ppermute x4, starting transfers between devices, swap_tp(): return lax.ppermute(value, 'tp', [(0, 1), (1, 0)])  7.55 us
    dot_general x8, matrix products, matmul(): return jnp.dot(a, b, preferred_element_type=F32)  7.12 us
  transfers between devices with their start and end apart: 27, of which 7 were waited for; matrix products, arithmetic and copies ran while one was open for 7% of the time, Pallas kernels for 12%

profile of v3, /device:TPU:46, one launch (start us, length us, event | category | flops | bytes accessed | tf_op | source)
XLA Modules:
  0.0 204.3 jit_solution(369891414380438625)
XLA Ops:
  7.2 1.4 fusion.24
  8.6 1.2 fusion.18
  9.9 1.5 collective-permute-start
  11.4 2.0 fusion.12
  13.4 0.5 fusion.13
  13.9 3.9 %collective-permute-start.1 = (bf16[2,128,512]{2,1,0:T(8,128)(2,1)S(1)}, bf16[2,128,512]{2,1,0:T(8,128)(2,1)S(1)}, u32[]{:S(2)}, u32[]{:S(2)}) collective-permute-start(bf16[2,128,512]{2,1,0:T(8,128)(2,1)S(1)} %pad_maximum_fusion.1.refs_2_.refs_0_), channel_id=1, source_target_pairs={{0,4},{2,6},{4,8},{6,10},{8,12},{10,14},{12,16},{14,18},{16,20},{1... | collective-permute-start | bytes 786440 | tf_op jit(solution)/shard_map/ppermute | solution.py:25
  17.9 0.4 fusion.10
  18.4 2.0 %fusion.11 = bf16[1,128,512]{2,1,0:T(8,128)(2,1)S(1)} fusion(bf16[128,2048]{1,0:T(8,128)(2,1)} %param.14, bf16[512,2048]{1,0:T(8,128)(2,1)S(1)} %copy-done.7), kind=kOutput, calls=%fused_computation.25 | convolution fusion | flops 268500992 | bytes 2752512 | tf_op jit(solution)/shard_map/dot_general | solution.py:255
  20.5 0.6 copy-done.12
  21.1 2.0 collective-permute-start.2
  23.2 0.6 collective-permute-done.1.refs_5_
  23.7 7.0 %collective-permute-done.2.refs_5_ = bf16[2,128,512]{2,1,0:T(8,128)(2,1)S(1)} collective-permute-done((bf16[2,128,512]{2,1,0:T(8,128)(2,1)S(1)}, bf16[2,128,512]{2,1,0:T(8,128)(2,1)S(1)}, u32[]{:S(2)}, u32[]{:S(2)}) %collective-permute-start.2) | collective-permute-done | bytes 262176 | tf_op jit(solution)/shard_map/ppermute | solution.py:25
  30.7 0.5 fusion.16
  31.2 0.4 fusion.17
  31.6 0.8 maximum_maximum_fusion
  32.5 2.2 %collective-permute-start.3 = (bf16[128,2048]{1,0:T(8,128)(2,1)}, bf16[128,2048]{1,0:T(8,128)(2,1)S(1)}, u32[]{:S(2)}, u32[]{:S(2)}) collective-permute-start(bf16[128,2048]{1,0:T(8,128)(2,1)} %param.14), channel_id=1, source_target_pairs={{0,1},{1,0},{2,3},{3,2},{4,5},{5,4},{6,7},{7,6},{8,9},{9,8},{10,11... | collective-permute-start | bytes 1572872 | tf_op jit(solution)/shard_map/ppermute | solution.py:29
  34.7 3.7 %collective-permute-start.10 = (bf16[2,256,512]{2,1,0:T(8,128)(2,1)}, bf16[2,256,512]{2,1,0:T(8,128)(2,1)}, u32[]{:S(2)}, u32[]{:S(2)}) collective-permute-start(bf16[2,256,512]{2,1,0:T(8,128)(2,1)} %maximum_maximum_fusion), channel_id=1, source_target_pairs={{0,32},{2,34},{4,36},{6,38},{8,40},{10,42},{12,44},{14,46},{16,48}... | collective-permute-start | bytes 1572872 | tf_op jit(solution)/shard_map/ppermute | solution.py:25
  38.5 5.0 %collective-permute-start.5 = (bf16[2,128,512]{2,1,0:T(8,128)(2,1)S(1)}, bf16[2,128,512]{2,1,0:T(8,128)(2,1)}, u32[]{:S(2)}, u32[]{:S(2)}) collective-permute-start(bf16[2,128,512]{2,1,0:T(8,128)(2,1)S(1)} %pad_maximum_fusion.3.refs_3_.refs_0_), channel_id=1, source_target_pairs={{0,4},{2,6},{4,8},{6,10},{8,12},{10,14},{12,16},{14,18},{16,20},{1... | collective-permute-start | bytes 786440 | tf_op jit(solution)/shard_map/ppermute | solution.py:25
  43.5 4.8 %collective-permute-start.6 = (bf16[2,128,512]{2,1,0:T(8,128)(2,1)}, bf16[2,128,512]{2,1,0:T(8,128)(2,1)S(1)}, u32[]{:S(2)}, u32[]{:S(2)}) collective-permute-start(bf16[2,128,512]{2,1,0:T(8,128)(2,1)} %copy-done.14), channel_id=1, source_target_pairs={{0,4},{2,6},{4,8},{6,10},{8,12},{10,14},{12,16},{14,18},{16,20},{1... | collective-permute-start | bytes 786440 | tf_op jit(solution)/shard_map/ppermute | solution.py:25
  48.4 1.5 fusion.14
  49.9 0.8 fusion.15
  50.8 13.6 %collective-permute-start.13 = (bf16[2,128,512]{2,1,0:T(8,128)(2,1)S(1)}, bf16[2,128,512]{2,1,0:T(8,128)(2,1)}, u32[]{:S(2)}, u32[]{:S(2)}) collective-permute-start(bf16[2,128,512]{2,1,0:T(8,128)(2,1)S(1)} %pad_maximum_fusion.2.refs_1_.refs_2_), channel_id=1, source_target_pairs={{4,0},{6,2},{8,4},{10,6},{12,8},{14,10},{16,12},{18,14},{20,16},{2... | collective-permute-start | bytes 786440 | tf_op jit(solution)/shard_map/ppermute | solution.py:25
  64.4 1.9 collective-permute-start.4
  66.3 1.9 collective-permute-start.14
  68.3 3.9 %collective-permute-start.7 = (bf16[2,128,512]{2,1,0:T(8,128)(2,1)}, bf16[2,128,512]{2,1,0:T(8,128)(2,1)}, u32[]{:S(2)}, u32[]{:S(2)}) collective-permute-start(bf16[2,128,512]{2,1,0:T(8,128)(2,1)} %collective-permute-done.5.refs_6_), channel_id=1, source_target_pairs={{0,4},{2,6},{4,8},{6,10},{8,12},{10,14},{12,16},{14,18},{16,20},{1... | collective-permute-start | bytes 786440 | tf_op jit(solution)/shard_map/ppermute | solution.py:25
  72.2 1.9 collective-permute-start.15
  74.2 0.8 maximum_maximum_fusion.1
  75.0 0.7 copy-done.1
  75.7 7.0 %collective-permute-start.12 = (bf16[2,256,512]{2,1,0:T(8,128)(2,1)}, bf16[2,256,512]{2,1,0:T(8,128)(2,1)}, u32[]{:S(2)}, u32[]{:S(2)}) collective-permute-start(bf16[2,256,512]{2,1,0:T(8,128)(2,1)} %maximum_maximum_fusion.1), channel_id=1, source_target_pairs={{2,0},{4,2},{6,4},{8,6},{10,8},{12,10},{14,12},{16,14},{18,16},{20... | collective-permute-start | bytes 1572872 | tf_op jit(solution)/shard_map/ppermute | solution.py:25
  82.7 0.1 pad_add_fusion.where_ref
  82.8 1.9 collective-permute-start.8
  84.8 1.9 collective-permute-start.9
  86.7 0.1 broadcast_in_dim.10
  86.8 0.1 ge.23
  86.9 6.9 %collective-permute-start.16 = (bf16[2,128,512]{2,1,0:T(8,128)(2,1)}, bf16[2,128,512]{2,1,0:T(8,128)(2,1)}, u32[]{:S(2)}, u32[]{:S(2)}) collective-permute-start(bf16[2,128,512]{2,1,0:T(8,128)(2,1)} %copy-done.1), channel_id=1, source_target_pairs={{8,0},{10,2},{12,4},{14,6},{16,8},{18,10},{20,12},{22,14},{24,16},... | collective-permute-start | bytes 786440 | tf_op jit(solution)/shard_map/ppermute | solution.py:25
  93.8 4.8 %collective-permute-start.17 = (bf16[2,128,512]{2,1,0:T(8,128)(2,1)}, bf16[2,128,512]{2,1,0:T(8,128)(2,1)}, u32[]{:S(2)}, u32[]{:S(2)}) collective-permute-start(bf16[2,128,512]{2,1,0:T(8,128)(2,1)} %collective-permute-done.15.refs_6_), channel_id=1, source_target_pairs={{8,0},{10,2},{12,4},{14,6},{16,8},{18,10},{20,12},{22,14},{24,16},... | collective-permute-start | bytes 786440 | tf_op jit(solution)/shard_map/ppermute | solution.py:25
  98.6 0.1 compare_select_fusion.bias_ref
  98.8 15.4 %query_side.1 = (bf16[256,512]{1,0:T(8,128)(2,1)S(1)}, bf16[256,512]{1,0:T(8,128)(2,1)S(1)}, f32[4,2,256]{2,1,0:T(2,128)S(1)}, bf16[2,256,512]{2,1,0:T(8,128)(2,...) custom-call(s32[2]{0:T(128)S(1)} %pad_add_fusion.where_ref, ...), custom_call_target="tpu_custom_call" | custom-call | flops 671088640 | bytes 6291456 | tf_op jit(solution)/shard_map/query_side/pallas_call | solution.py:174
  114.2 6.4 %collective-permute-start.22 = (bf16[2,256,512]{2,1,0:T(8,128)(2,1)S(1)}, bf16[2,256,512]{2,1,0:T(8,128)(2,1)S(1)}, u32[]{:S(2)}, u32[]{:S(2)}) collective-permute-start(bf16[2,256,512]{2,1,0:T(8,128)(2,1)S(1)} %get-tuple-element.36), channel_id=1, source_target_pairs={{32,0},{34,2},{36,4},{38,6},{40,8},{42,10},{44,12},{46,14},{48,16}... | collective-permute-start | bytes 1572872 | tf_op jit(solution)/shard_map/ppermute | solution.py:25
  120.7 1.9 collective-permute-start.23
  122.6 1.3 collective-permute-start.24
  123.9 12.5 %collective-permute-start.18 = (f32[4,2,256]{2,1,0:T(2,128)S(1)}, f32[4,2,256]{2,1,0:T(2,128)S(1)}, u32[]{:S(2)}, u32[]{:S(2)}) collective-permute-start(f32[4,2,256]{2,1,0:T(2,128)S(1)} %get-tuple-element.31.refs_3_), channel_id=1, source_target_pairs={{2,0},{4,2},{6,4},{8,6},{10,8},{12,10},{14,12},{16,14},{18,16},{20... | collective-permute-start | bytes 24584 | tf_op jit(solution)/shard_map/ppermute | solution.py:25
  136.5 2.6 %collective-permute-start.19 = (f32[4,2,256]{2,1,0:T(2,128)S(1)}, f32[4,2,256]{2,1,0:T(2,128)S(1)}, u32[]{:S(2)}, u32[]{:S(2)}) collective-permute-start(f32[4,2,256]{2,1,0:T(2,128)S(1)} %get-tuple-element.31.refs_3_), channel_id=1, source_target_pairs={{4,0},{6,2},{8,4},{10,6},{12,8},{14,10},{16,12},{18,14},{20,16},{2... | collective-permute-start | bytes 24584 | tf_op jit(solution)/shard_map/ppermute | solution.py:25
  139.1 1.9 collective-permute-start.20
  141.0 1.0 collective-permute-done.19.refs_9_
  142.0 2.9 %collective-permute-start.21 = (f32[4,2,256]{2,1,0:T(2,128)S(1)}, f32[4,2,256]{2,1,0:T(2,128)S(1)}, u32[]{:S(2)}, u32[]{:S(2)}) collective-permute-start(f32[4,2,256]{2,1,0:T(2,128)S(1)} %get-tuple-element.31.refs_3_), channel_id=1, source_target_pairs={{16,0},{18,2},{20,4},{22,6},{24,8},{26,10},{28,12},{30,14},{32,16}... | collective-permute-start | bytes 24584 | tf_op jit(solution)/shard_map/ppermute | solution.py:25
  145.0 0.4 convolution_convert_fusion
  145.5 3.6 %collective-permute-start.11 = (bf16[128,2048]{1,0:T(8,128)(2,1)S(1)}, bf16[128,2048]{1,0:T(8,128)(2,1)S(1)}, u32[]{:S(2)}, u32[]{:S(2)}) collective-permute-start(bf16[128,2048]{1,0:T(8,128)(2,1)S(1)} %convolution_convert_fusion), channel_id=1, source_target_pairs={{0,1},{1,0},{2,3},{3,2},{4,5},{5,4},{6,7},{7,6},{8,9},{9,8},{10,11... | collective-permute-start | bytes 1572872 | tf_op jit(solution)/shard_map/ppermute | solution.py:29
  149.1 2.4 %collective-permute-done.21.refs_11_ = f32[4,2,256]{2,1,0:T(2,128)S(1)} collective-permute-done((f32[4,2,256]{2,1,0:T(2,128)S(1)}, f32[4,2,256]{2,1,0:T(2,128)S(1)}, u32[]{:S(2)}, u32[]{:S(2)}) %collective-permute-start.21) | collective-permute-done | bytes 8224 | tf_op jit(solution)/shard_map/ppermute | solution.py:25
  151.5 19.0 %collective-permute-done.24.refs_14_ = bf16[2,256,512]{2,1,0:T(8,128)(2,1)S(1)} collective-permute-done((bf16[2,256,512]{2,1,0:T(8,128)(2,1)S(1)}, bf16[2,256,512]{2,1,0:T(8,128)(2,1)S(1)}, u32[]{:S(2)}, u32[]{:S(2)}) %collective-permute-start.24) | collective-permute-done | bytes 524320 | tf_op jit(solution)/shard_map/ppermute | solution.py:25
  170.5 4.8 %key_side.3 = bf16[2,128,512]{2,1,0:T(8,128)(2,1)S(1)} custom-call(s32[2]{0:T(128)S(1)} %pad_add_fusion.where_ref, bf16[2,128,512]{2,1,0:T(8,128)(2,1)S(1)} %pad_maximum_fusion.3.refs_3_.refs_0_, bf16[2,128,512]{2,1,0:T(8,128)(2,1)S(1)} %pad_maximum_fusion.refs_0_.refs_1_, bf16[2,128,512]{2,1,0:T(8,128)(2,1)S(1)} %pad_maximum_fusion.2.refs_1_.refs_2_, ...), custom_call_target="tpu_custom_call" | custom-call | flops 234881024 | bytes 6291456 | tf_op jit(solution)/shard_map/key_side/pallas_call | solution.py:174
  175.3 0.8 fusion.25
  176.1 0.8 copy-done.6
  176.9 0.8 fusion.26
  177.7 0.8 fusion.6
  178.5 0.3 collective-permute-start.25
  178.8 4.7 %key_side.2 = bf16[2,128,512]{2,1,0:T(8,128)(2,1)S(1)} custom-call(s32[2]{0:T(128)S(1)} %pad_add_fusion.where_ref, bf16[2,128,512]{2,1,0:T(8,128)(2,1)S(1)} %pad_maximum_fusion.1.refs_2_.refs_0_, bf16[2,128,512]{2,1,0:T(8,128)(2,1)S(1)} %pad_maximum_fusion.refs_0_.refs_1_, bf16[2,128,512]{2,1,0:T(8,128)(2,1)S(1)} %pad_maximum_fusion.2.refs_1_.refs_2_, ...), custom_call_target="tpu_custom_call" | custom-call | flops 234881024 | bytes 6291456 | tf_op jit(solution)/shard_map/key_side/pallas_call | solution.py:174
  183.5 0.8 fusion.27
  184.3 0.8 fusion.28
  185.1 0.2 copy-done.10
  185.3 1.3 fusion.5
  186.6 7.6 %collective-permute-done.25 = bf16[128,2048]{1,0:T(8,128)(2,1)S(1)} collective-permute-done((bf16[128,2048]{1,0:T(8,128)(2,1)S(1)}, bf16[128,2048]{1,0:T(8,128)(2,1)S(1)}, u32[]{:S(2)}, u32[]{:S(2)}) %collective-permute-start.25) | collective-permute-done | bytes 524320 | tf_op jit(solution)/shard_map/ppermute | solution.py:29
  194.2 1.0 fusion.19
  195.2 2.2 %fusion.23 = bf16[128,2048]{1,0:T(8,128)(2,1)} fusion(f32[128,2048]{1,0:T(8,128)S(1)} %get-tuple-element.43, bf16[128,2048]{1,0:T(8,128)(2,1)S(1)} %copy-done.10, bf16[128,2048]{1,0:T(8,128)(2,1)} %param.14, f32[128]{0:T(128)S(1)} %broadcast_multiply_fusion, f32[128]{0:T(128)S(1)} %add_rsqrt_fusion), kind=kLoop, calls=%fused_computation.37 | loop fusion | flops 2097152 | bytes 2622464 | tf_op jit(solution)/shard_map/convert_element_type | solution.py:334
  (62 shorter events, 0.4 us)
Async XLA Ops:
  7.2 10.7 %copy-start = (bf16[2048,512]{1,0:T(8,128)(2,1)S(1)}, bf16[2048,512]{1,0:T(8,128)(2,1)}, u32[]{:S(2)}) copy-start(bf16[2048,512]{1,0:T(8,128)(2,1)} %param.10) | copy-start | bytes 6291460
  7.2 91.6 %all-gather.3.cloned.1.call-start = ((), (), s32[]{:S(2)}) async-start(), calls=%async_computation | async-start | bytes 2621440 | tf_op jit(solution)/shard_map/all_gather | solution.py:300
  7.2 6.2 %copy-start.3 = (bf16[2048,512]{1,0:T(8,128)(2,1)S(1)}, bf16[2048,512]{1,0:T(8,128)(2,1)}, u32[]{:S(2)}) copy-start(bf16[2048,512]{1,0:T(8,128)(2,1)} %param.12) | copy-start | bytes 6291460
  9.9 20.8 %collective-permute-start = (bf16[128,2048]{1,0:T(8,128)(2,1)S(1)}, bf16[128,2048]{1,0:T(8,128)(2,1)S(1)}, u32[]{:S(2)}, u32[]{:S(2)}) collective-permute-start(bf16[128,2048]{1,0:T(8,128)(2,1)S(1)} %fusion.18), channel_id=1, source_target_pairs={{0,1},{1,0},{2,3},{3,2},{4,5},{5,4},{6,7},{7,6},{8,9},{9,8},{10,11... | collective-permute-start | bytes 1572872 | tf_op jit(solution)/shard_map/ppermute | solution.py:29
  13.9 4.5 %copy-start.7 = (bf16[512,2048]{1,0:T(8,128)(2,1)S(1)}, bf16[512,2048]{1,0:T(8,128)(2,1)}, u32[]{:S(2)}) copy-start(bf16[512,2048]{1,0:T(8,128)(2,1)} %param.13) | copy-start | bytes 6291460
  13.9 9.8 %collective-permute-start.1 = (bf16[2,128,512]{2,1,0:T(8,128)(2,1)S(1)}, bf16[2,128,512]{2,1,0:T(8,128)(2,1)S(1)}, u32[]{:S(2)}, u32[]{:S(2)}) collective-permute-start(bf16[2,128,512]{2,1,0:T(8,128)(2,1)S(1)} %pad_maximum_fusion.1.refs_2_.refs_0_), channel_id=1, source_target_pairs={{0,4},{2,6},{4,8},{6,10},{8,12},{10,14},{12,16},{14,18},{16,20},{1... | collective-permute-start | bytes 786440 | tf_op jit(solution)/shard_map/ppermute | solution.py:25
  18.4 12.3 %copy-start.5 = (bf16[2048,512]{1,0:T(8,128)(2,1)S(1)}, bf16[2048,512]{1,0:T(8,128)(2,1)}, u32[]{:S(2)}) copy-start(bf16[2048,512]{1,0:T(8,128)(2,1)} %param.11) | copy-start | bytes 6291460
  20.4 0.7 copy-start.12
  21.1 9.6 %collective-permute-start.2 = (bf16[2,128,512]{2,1,0:T(8,128)(2,1)S(1)}, bf16[2,128,512]{2,1,0:T(8,128)(2,1)S(1)}, u32[]{:S(2)}, u32[]{:S(2)}) collective-permute-start(bf16[2,128,512]{2,1,0:T(8,128)(2,1)S(1)} %pad_maximum_fusion.refs_0_.refs_1_), channel_id=1, source_target_pairs={{4,0},{6,2},{8,4},{10,6},{12,8},{14,10},{16,12},{18,14},{20,16},{2... | collective-permute-start | bytes 786440 | tf_op jit(solution)/shard_map/ppermute | solution.py:25
  23.7 7.9 %copy-start.14 = (bf16[2,128,512]{2,1,0:T(8,128)(2,1)}, bf16[2,128,512]{2,1,0:T(8,128)(2,1)S(1)}, u32[]{:S(2)}) copy-start(bf16[2,128,512]{2,1,0:T(8,128)(2,1)S(1)} %collective-permute-done.1.refs_5_) | copy-start | bytes 786436
  30.7 0.9 copy-start.11
  32.5 17.4 %copy-start.8 = (bf16[512,2048]{1,0:T(8,128)(2,1)S(1)}, bf16[512,2048]{1,0:T(8,128)(2,1)}, u32[]{:S(2)}) copy-start(bf16[512,2048]{1,0:T(8,128)(2,1)} %param.13) | copy-start | bytes 6291460
  32.5 17.4 %collective-permute-start.3 = (bf16[128,2048]{1,0:T(8,128)(2,1)}, bf16[128,2048]{1,0:T(8,128)(2,1)S(1)}, u32[]{:S(2)}, u32[]{:S(2)}) collective-permute-start(bf16[128,2048]{1,0:T(8,128)(2,1)} %param.14), channel_id=1, source_target_pairs={{0,1},{1,0},{2,3},{3,2},{4,5},{5,4},{6,7},{7,6},{8,9},{9,8},{10,11... | collective-permute-start | bytes 1572872 | tf_op jit(solution)/shard_map/ppermute | solution.py:29
  34.7 48.1 %collective-permute-start.10 = (bf16[2,256,512]{2,1,0:T(8,128)(2,1)}, bf16[2,256,512]{2,1,0:T(8,128)(2,1)}, u32[]{:S(2)}, u32[]{:S(2)}) collective-permute-start(bf16[2,256,512]{2,1,0:T(8,128)(2,1)} %maximum_maximum_fusion), channel_id=1, source_target_pairs={{0,32},{2,34},{4,36},{6,38},{8,40},{10,42},{12,44},{14,46},{16,48}... | collective-permute-start | bytes 1572872 | tf_op jit(solution)/shard_map/ppermute | solution.py:25
  38.5 27.8 %collective-permute-start.5 = (bf16[2,128,512]{2,1,0:T(8,128)(2,1)S(1)}, bf16[2,128,512]{2,1,0:T(8,128)(2,1)}, u32[]{:S(2)}, u32[]{:S(2)}) collective-permute-start(bf16[2,128,512]{2,1,0:T(8,128)(2,1)S(1)} %pad_maximum_fusion.3.refs_3_.refs_0_), channel_id=1, source_target_pairs={{0,4},{2,6},{4,8},{6,10},{8,12},{10,14},{12,16},{14,18},{16,20},{1... | collective-permute-start | bytes 786440 | tf_op jit(solution)/shard_map/ppermute | solution.py:25
  43.5 24.7 %collective-permute-start.6 = (bf16[2,128,512]{2,1,0:T(8,128)(2,1)}, bf16[2,128,512]{2,1,0:T(8,128)(2,1)S(1)}, u32[]{:S(2)}, u32[]{:S(2)}) collective-permute-start(bf16[2,128,512]{2,1,0:T(8,128)(2,1)} %copy-done.14), channel_id=1, source_target_pairs={{0,4},{2,6},{4,8},{6,10},{8,12},{10,14},{12,16},{14,18},{16,20},{1... | collective-permute-start | bytes 786440 | tf_op jit(solution)/shard_map/ppermute | solution.py:25
  49.9 24.3 %copy-start.13 = (bf16[1,128,512]{2,1,0:T(8,128)(2,1)S(1)}, bf16[1,128,512]{2,1,0:T(8,128)(2,1)}, u32[]{:S(2)}) copy-start(bf16[1,128,512]{2,1,0:T(8,128)(2,1)} %copy-done.12) | copy-start | bytes 393220
  49.9 36.8 %copy-start.17 = (s32[10]{0:T(128)S(1)}, s32[10]{0:T(128)}, u32[]{:S(2)}) copy-start(s32[10]{0:T(128)} %constant.52.clone) | copy-start | bytes 124
  50.8 21.4 %collective-permute-start.13 = (bf16[2,128,512]{2,1,0:T(8,128)(2,1)S(1)}, bf16[2,128,512]{2,1,0:T(8,128)(2,1)}, u32[]{:S(2)}, u32[]{:S(2)}) collective-permute-start(bf16[2,128,512]{2,1,0:T(8,128)(2,1)S(1)} %pad_maximum_fusion.2.refs_1_.refs_2_), channel_id=1, source_target_pairs={{4,0},{6,2},{8,4},{10,6},{12,8},{14,10},{16,12},{18,14},{20,16},{2... | collective-permute-start | bytes 786440 | tf_op jit(solution)/shard_map/ppermute | solution.py:25
  64.4 22.5 %collective-permute-start.4 = (bf16[2,256,512]{2,1,0:T(8,128)(2,1)}, bf16[2,256,512]{2,1,0:T(8,128)(2,1)}, u32[]{:S(2)}, u32[]{:S(2)}) collective-permute-start(bf16[2,256,512]{2,1,0:T(8,128)(2,1)} %maximum_maximum_fusion), channel_id=1, source_target_pairs={{0,2},{2,4},{4,6},{6,8},{8,10},{10,12},{12,14},{14,16},{16,18},{18... | collective-permute-start | bytes 1572872 | tf_op jit(solution)/shard_map/ppermute | solution.py:25
  66.3 8.7 %collective-permute-start.14 = (bf16[2,128,512]{2,1,0:T(8,128)(2,1)S(1)}, bf16[2,128,512]{2,1,0:T(8,128)(2,1)S(1)}, u32[]{:S(2)}, u32[]{:S(2)}) collective-permute-start(bf16[2,128,512]{2,1,0:T(8,128)(2,1)S(1)} %collective-permute-done.2.refs_5_), channel_id=1, source_target_pairs={{4,0},{6,2},{8,4},{10,6},{12,8},{14,10},{16,12},{18,14},{20,16},{2... | collective-permute-start | bytes 786440 | tf_op jit(solution)/shard_map/ppermute | solution.py:25
  68.3 14.5 %copy-start.15 = (bf16[2,128,512]{2,1,0:T(8,128)(2,1)}, bf16[2,128,512]{2,1,0:T(8,128)(2,1)S(1)}, u32[]{:S(2)}) copy-start(bf16[2,128,512]{2,1,0:T(8,128)(2,1)S(1)} %collective-permute-done.6.refs_7_) | copy-start | bytes 786436
  68.3 16.5 %collective-permute-start.7 = (bf16[2,128,512]{2,1,0:T(8,128)(2,1)}, bf16[2,128,512]{2,1,0:T(8,128)(2,1)}, u32[]{:S(2)}, u32[]{:S(2)}) collective-permute-start(bf16[2,128,512]{2,1,0:T(8,128)(2,1)} %collective-permute-done.5.refs_6_), channel_id=1, source_target_pairs={{0,4},{2,6},{4,8},{6,10},{8,12},{10,14},{12,16},{14,18},{16,20},{1... | collective-permute-start | bytes 786440 | tf_op jit(solution)/shard_map/ppermute | solution.py:25
  72.2 21.6 %collective-permute-start.15 = (bf16[2,128,512]{2,1,0:T(8,128)(2,1)}, bf16[2,128,512]{2,1,0:T(8,128)(2,1)}, u32[]{:S(2)}, u32[]{:S(2)}) collective-permute-start(bf16[2,128,512]{2,1,0:T(8,128)(2,1)} %collective-permute-done.13.refs_5_), channel_id=1, source_target_pairs={{4,0},{6,2},{8,4},{10,6},{12,8},{14,10},{16,12},{18,14},{20,16},{2... | collective-permute-start | bytes 786440 | tf_op jit(solution)/shard_map/ppermute | solution.py:25
  75.0 0.7 copy-start.1
  75.7 38.5 %collective-permute-start.12 = (bf16[2,256,512]{2,1,0:T(8,128)(2,1)}, bf16[2,256,512]{2,1,0:T(8,128)(2,1)}, u32[]{:S(2)}, u32[]{:S(2)}) collective-permute-start(bf16[2,256,512]{2,1,0:T(8,128)(2,1)} %maximum_maximum_fusion.1), channel_id=1, source_target_pairs={{2,0},{4,2},{6,4},{8,6},{10,8},{12,10},{14,12},{16,14},{18,16},{20... | collective-permute-start | bytes 1572872 | tf_op jit(solution)/shard_map/ppermute | solution.py:25
  82.8 15.9 %collective-permute-start.8 = (bf16[2,128,512]{2,1,0:T(8,128)(2,1)}, bf16[2,128,512]{2,1,0:T(8,128)(2,1)}, u32[]{:S(2)}, u32[]{:S(2)}) collective-permute-start(bf16[2,128,512]{2,1,0:T(8,128)(2,1)} %copy-done.15), channel_id=1, source_target_pairs={{0,8},{2,10},{4,12},{6,14},{8,16},{10,18},{12,20},{14,22},{16,24},... | collective-permute-start | bytes 786440 | tf_op jit(solution)/shard_map/ppermute | solution.py:25
  84.8 14.0 %collective-permute-start.9 = (bf16[2,128,512]{2,1,0:T(8,128)(2,1)}, bf16[2,128,512]{2,1,0:T(8,128)(2,1)}, u32[]{:S(2)}, u32[]{:S(2)}) collective-permute-start(bf16[2,128,512]{2,1,0:T(8,128)(2,1)} %collective-permute-done.7.refs_8_), channel_id=1, source_target_pairs={{0,8},{2,10},{4,12},{6,14},{8,16},{10,18},{12,20},{14,22},{16,24},... | collective-permute-start | bytes 786440 | tf_op jit(solution)/shard_map/ppermute | solution.py:25
  86.9 27.4 %collective-permute-start.16 = (bf16[2,128,512]{2,1,0:T(8,128)(2,1)}, bf16[2,128,512]{2,1,0:T(8,128)(2,1)}, u32[]{:S(2)}, u32[]{:S(2)}) collective-permute-start(bf16[2,128,512]{2,1,0:T(8,128)(2,1)} %copy-done.1), channel_id=1, source_target_pairs={{8,0},{10,2},{12,4},{14,6},{16,8},{18,10},{20,12},{22,14},{24,16},... | collective-permute-start | bytes 786440 | tf_op jit(solution)/shard_map/ppermute | solution.py:25
  93.8 20.4 %collective-permute-start.17 = (bf16[2,128,512]{2,1,0:T(8,128)(2,1)}, bf16[2,128,512]{2,1,0:T(8,128)(2,1)}, u32[]{:S(2)}, u32[]{:S(2)}) collective-permute-start(bf16[2,128,512]{2,1,0:T(8,128)(2,1)} %collective-permute-done.15.refs_6_), channel_id=1, source_target_pairs={{8,0},{10,2},{12,4},{14,6},{16,8},{18,10},{20,12},{22,14},{24,16},... | collective-permute-start | bytes 786440 | tf_op jit(solution)/shard_map/ppermute | solution.py:25
  98.8 46.2 %copy-start.9 = (bf16[512,2048]{1,0:T(8,128)(2,1)S(1)}, bf16[512,2048]{1,0:T(8,128)(2,1)}, u32[]{:S(2)}) copy-start(bf16[512,2048]{1,0:T(8,128)(2,1)} %param.13) | copy-start | bytes 6291460
  114.2 37.2 %collective-permute-start.22 = (bf16[2,256,512]{2,1,0:T(8,128)(2,1)S(1)}, bf16[2,256,512]{2,1,0:T(8,128)(2,1)S(1)}, u32[]{:S(2)}, u32[]{:S(2)}) collective-permute-start(bf16[2,256,512]{2,1,0:T(8,128)(2,1)S(1)} %get-tuple-element.36), channel_id=1, source_target_pairs={{32,0},{34,2},{36,4},{38,6},{40,8},{42,10},{44,12},{46,14},{48,16}... | collective-permute-start | bytes 1572872 | tf_op jit(solution)/shard_map/ppermute | solution.py:25
  120.7 30.8 %collective-permute-start.23 = (bf16[2,256,512]{2,1,0:T(8,128)(2,1)S(1)}, bf16[2,256,512]{2,1,0:T(8,128)(2,1)S(1)}, u32[]{:S(2)}, u32[]{:S(2)}) collective-permute-start(bf16[2,256,512]{2,1,0:T(8,128)(2,1)S(1)} %get-tuple-element.37), channel_id=1, source_target_pairs={{64,0},{66,2},{68,4},{70,6},{72,8},{74,10},{76,12},{78,14},{80,16}... | collective-permute-start | bytes 1572872 | tf_op jit(solution)/shard_map/ppermute | solution.py:25
  122.6 47.9 %collective-permute-start.24 = (bf16[2,256,512]{2,1,0:T(8,128)(2,1)S(1)}, bf16[2,256,512]{2,1,0:T(8,128)(2,1)S(1)}, u32[]{:S(2)}, u32[]{:S(2)}) collective-permute-start(bf16[2,256,512]{2,1,0:T(8,128)(2,1)S(1)} %get-tuple-element.38), channel_id=1, source_target_pairs={{128,0},{130,2},{132,4},{134,6},{136,8},{138,10},{140,12},{142,14}... | collective-permute-start | bytes 1572872 | tf_op jit(solution)/shard_map/ppermute | solution.py:25
  123.9 15.1 %collective-permute-start.18 = (f32[4,2,256]{2,1,0:T(2,128)S(1)}, f32[4,2,256]{2,1,0:T(2,128)S(1)}, u32[]{:S(2)}, u32[]{:S(2)}) collective-permute-start(f32[4,2,256]{2,1,0:T(2,128)S(1)} %get-tuple-element.31.refs_3_), channel_id=1, source_target_pairs={{2,0},{4,2},{6,4},{8,6},{10,8},{12,10},{14,12},{16,14},{18,16},{20... | collective-permute-start | bytes 24584 | tf_op jit(solution)/shard_map/ppermute | solution.py:25
  136.5 5.5 %collective-permute-start.19 = (f32[4,2,256]{2,1,0:T(2,128)S(1)}, f32[4,2,256]{2,1,0:T(2,128)S(1)}, u32[]{:S(2)}, u32[]{:S(2)}) collective-permute-start(f32[4,2,256]{2,1,0:T(2,128)S(1)} %get-tuple-element.31.refs_3_), channel_id=1, source_target_pairs={{4,0},{6,2},{8,4},{10,6},{12,8},{14,10},{16,12},{18,14},{20,16},{2... | collective-permute-start | bytes 24584 | tf_op jit(solution)/shard_map/ppermute | solution.py:25
  139.1 6.4 %collective-permute-start.20 = (f32[4,2,256]{2,1,0:T(2,128)S(1)}, f32[4,2,256]{2,1,0:T(2,128)S(1)}, u32[]{:S(2)}, u32[]{:S(2)}) collective-permute-start(f32[4,2,256]{2,1,0:T(2,128)S(1)} %get-tuple-element.31.refs_3_), channel_id=1, source_target_pairs={{8,0},{10,2},{12,4},{14,6},{16,8},{18,10},{20,12},{22,14},{24,16},... | collective-permute-start | bytes 24584 | tf_op jit(solution)/shard_map/ppermute | solution.py:25
  142.0 9.4 %collective-permute-start.21 = (f32[4,2,256]{2,1,0:T(2,128)S(1)}, f32[4,2,256]{2,1,0:T(2,128)S(1)}, u32[]{:S(2)}, u32[]{:S(2)}) collective-permute-start(f32[4,2,256]{2,1,0:T(2,128)S(1)} %get-tuple-element.31.refs_3_), channel_id=1, source_target_pairs={{16,0},{18,2},{20,4},{22,6},{24,8},{26,10},{28,12},{30,14},{32,16}... | collective-permute-start | bytes 24584 | tf_op jit(solution)/shard_map/ppermute | solution.py:25
  145.4 29.8 %copy-start.4 = (bf16[2048,512]{1,0:T(8,128)(2,1)S(1)}, bf16[2048,512]{1,0:T(8,128)(2,1)}, u32[]{:S(2)}) copy-start(bf16[2048,512]{1,0:T(8,128)(2,1)} %param.12) | copy-start | bytes 6291460
  145.5 39.6 %collective-permute-start.11 = (bf16[128,2048]{1,0:T(8,128)(2,1)S(1)}, bf16[128,2048]{1,0:T(8,128)(2,1)S(1)}, u32[]{:S(2)}, u32[]{:S(2)}) collective-permute-start(bf16[128,2048]{1,0:T(8,128)(2,1)S(1)} %convolution_convert_fusion), channel_id=1, source_target_pairs={{0,1},{1,0},{2,3},{3,2},{4,5},{5,4},{6,7},{7,6},{8,9},{9,8},{10,11... | collective-permute-start | bytes 1572872 | tf_op jit(solution)/shard_map/ppermute | solution.py:29
  175.3 1.6 copy-start.6
  177.7 1.1 copy-start.2
  178.5 15.7 %collective-permute-start.25 = (bf16[128,2048]{1,0:T(8,128)(2,1)S(1)}, bf16[128,2048]{1,0:T(8,128)(2,1)S(1)}, u32[]{:S(2)}, u32[]{:S(2)}) collective-permute-start(bf16[128,2048]{1,0:T(8,128)(2,1)S(1)} %fusion.6), channel_id=1, source_target_pairs={{0,1},{1,0},{2,3},{3,2},{4,5},{5,4},{6,7},{7,6},{8,9},{9,8},{10,11... | collective-permute-start | bytes 1572872 | tf_op jit(solution)/shard_map/ppermute | solution.py:29
  184.3 1.0 copy-start.10
  185.1 9.1 %copy-start.16 = (f32[2048]{0:T(1024)S(1)}, f32[2048]{0:T(1024)}, u32[]{:S(2)}) copy-start(f32[2048]{0:T(1024)} %param.9) | copy-start | bytes 24580
Sparse Core Ops, SparseCore 0:
  32.6 34.4 all-gather.2

commit v4 on v3

--- a/solution.py
+++ b/solution.py
@@ -60,52 +60,64 @@
     return jnp.where(rows >= keys, 0.0, NEG).astype(F32)
 
 
-def query_kernel(groups, where_ref, bias_ref, *refs):
+def query_kernel(groups, n_back, where_ref, bias_ref, *refs):
     refs = list(refs)
     qg = [refs.pop(0) for _ in range(2)]
     kv = [refs.pop(0) for _ in range(2)]
     fetched = [[refs.pop(0) for _ in range(n)] for n in groups]
-    one = refs.pop(0)
-    two = [refs.pop(0) for _ in range(2)]
     mixed_ref, dq_ref, stat_ref, *back_refs = refs
     is_second = where_ref[0] == 1
     factor = HD ** (-0.5)
     causal = causal_bias(0)
     lane = lax.broadcasted_iota(jnp.int32, (BLOCK, HD), 1)
-    for slot in range(4):
-        out = slice(slot * BLOCK, (slot + 1) * BLOCK)
-        keys, values = [
-            jnp.concatenate(
-                [piece(kv, which, slot)]
-                + [near(is_second, kv, fetched[0], which, slot, -d) for d in NEAR]
-                + [piece(f, which, slot) for f in fetched[1:]]
-                + [one[which, out, :]]
-                + [t[0, which, out, :] for t in two],
-                axis=0,
-            )
-            for which in range(2)
-        ]
-        query, grad = piece(qg, 0, slot), piece(qg, 1, slot)
-        score = dot(query, keys, NT) * factor + bias_ref[slot]
-        score = jnp.concatenate([score[:, :BLOCK] + causal, score[:, BLOCK:]], axis=1)
-        peak = jnp.max(score, axis=-1, keepdims=True)
-        weight = jnp.exp(score - peak)
-        total = jnp.sum(weight, axis=-1, keepdims=True)
-        prob = weight * (1.0 / total)
-        prob_b = prob.astype(BF16)
-        mixed = dot(prob_b, values, NN).astype(BF16)
-        mixed_ref[out, :] = mixed
-        inner = jnp.sum(mixed.astype(F32) * grad.astype(F32), axis=-1, keepdims=True)
-        grad_score = (prob * (dot(grad, values, NT) - inner)).astype(BF16)
-        dq_ref[out, :] = (dot(grad_score, keys, NN) * factor).astype(BF16)
-        stat = jnp.where(lane == 0, peak + jnp.log(total), inner)
+    slots = range(4)
+
+    def gather(which, slot):
+        return jnp.concatenate(
+            [piece(kv, which, slot)]
+            + [near(is_second, kv, fetched[0], which, slot, -d) for d in NEAR]
+            + [piece(f, which, slot) for f in fetched[1:]],
+            axis=0,
+        )
+
+    def rows(slot):
+        return slice(slot * BLOCK, (slot + 1) * BLOCK)
+
+    query = [piece(qg, 0, slot) for slot in slots]
+    grad = [piece(qg, 1, slot) for slot in slots]
+    keys = [gather(0, slot) for slot in slots]
+    values = [gather(1, slot) for slot in slots]
+    score = []
+    for slot in slots:
+        s = dot(query[slot], keys[slot], NT) * factor + bias_ref[slot]
+        score.append(jnp.concatenate([s[:, :BLOCK] + causal, s[:, BLOCK:]], axis=1))
+    grad_prob = [dot(grad[slot], values[slot], NT) for slot in slots]
+    peak = [jnp.max(s, axis=-1, keepdims=True) for s in score]
+    weight = [jnp.exp(score[slot] - peak[slot]) for slot in slots]
+    total = [jnp.sum(w, axis=-1, keepdims=True) for w in weight]
+    prob = [weight[slot] * (1.0 / total[slot]) for slot in slots]
+    prob_b = [p.astype(BF16) for p in prob]
+    mixed = [dot(prob_b[slot], values[slot], NN).astype(BF16) for slot in slots]
+    inner = [
+        jnp.sum(mixed[slot].astype(F32) * grad[slot].astype(F32), axis=-1, keepdims=True)
+        for slot in slots
+    ]
+    grad_score = [
+        (prob[slot] * (grad_prob[slot] - inner[slot])).astype(BF16) for slot in slots
+    ]
+    first = keys[0].shape[0] - n_back * BLOCK
+    for slot in slots:
+        out = rows(slot)
+        mixed_ref[out, :] = mixed[slot]
+        dq_ref[out, :] = (dot(grad_score[slot], keys[slot], NN) * factor).astype(BF16)
+        stat = jnp.where(lane == 0, peak[slot] + jnp.log(total[slot]), inner[slot])
         stat_ref[0, :, out] = jnp.transpose(stat)[:2]
-        first = keys.shape[0] - len(back_refs) * BLOCK
-        grad_keys = (dot(grad_score[:, first:], query, TN) * factor).astype(BF16)
-        grad_values = dot(prob_b[:, first:], grad, TN).astype(BF16)
-        for at, ref in enumerate(back_refs):
-            ref[0, out, :] = grad_keys[at * BLOCK : (at + 1) * BLOCK]
-            ref[1, out, :] = grad_values[at * BLOCK : (at + 1) * BLOCK]
+        if n_back:
+            grad_keys = (dot(grad_score[slot][:, first:], query[slot], TN) * factor).astype(BF16)
+            grad_values = dot(prob_b[slot][:, first:], grad[slot], TN).astype(BF16)
+            for at, ref in enumerate(back_refs):
+                ref[0, out, :] = grad_keys[at * BLOCK : (at + 1) * BLOCK]
+                ref[1, out, :] = grad_values[at * BLOCK : (at + 1) * BLOCK]
 
 
 def key_kernel(half, groups, n_back, where_ref, *refs):
@@ -187,31 +199,22 @@
     )(where, *operands)
 
 
-def query_side(where, bias, qg, kv, fetched, one, column):
+def query_side(where, bias, qg, kv, fetched, n_back):
     rows, width = 2 * qg[0].shape[1], qg[0].shape[2]
     heads = width // HD
-    far = [a for f in fetched for a in f] + [one, column]
-    far = [pltpu.with_memory_space_constraint(a, pltpu.HBM) for a in far]
-    column = far.pop()
+    far = [pltpu.with_memory_space_constraint(a, pltpu.HBM) for f in fetched for a in f]
     operands = [*qg, *kv, *far]
     row_out = jax.ShapeDtypeStruct((rows, width), BF16)
     stat_out = jax.ShapeDtypeStruct((heads, 2, rows), F32)
     back_out = jax.ShapeDtypeStruct((2, rows, width), BF16)
-
-    def column_spec(back):
-        return pl.BlockSpec(
-            (1, 2, rows, HD), lambda h, w: (jnp.maximum(w[1] - back, 0), 0, 0, h)
-        )
-
+    outs = [row_out, row_out, stat_out] + [back_out] * n_back
     return call(
-        functools.partial(query_kernel, tuple(len(f) for f in fetched)),
+        functools.partial(query_kernel, tuple(len(f) for f in fetched), n_back),
         where,
-        [bias, *operands, column, column],
-        [pl.BlockSpec(bias.shape, lambda h, w: (0, 0, 0))]
-        + [head_spec(a) for a in operands]
-        + [column_spec(1), column_spec(2)],
-        [row_out, row_out, stat_out] + [back_out] * 3,
-        [head_spec(row_out), head_spec(row_out), stat_spec(stat_out)] + [head_spec(back_out)] * 3,
+        [bias, *operands],
+        [pl.BlockSpec(bias.shape, lambda h, w: (0, 0, 0))] + [head_spec(a) for a in operands],
+        outs,
+        [head_spec(row_out), head_spec(row_out), stat_spec(stat_out)] + [head_spec(back_out)] * n_back,
         heads,
         bias.shape[2],
         "query_side",
@@ -222,12 +225,13 @@
     rows, width = kv[0].shape[1], kv[0].shape[2]
     heads = width // HD
     half_of_whole = pl.BlockSpec((2, rows, HD), lambda h, w: (0, half, h))
-    far = [f[half] for f in later[1:]]
+    far = [f[-1] if len(f) == 1 else f[half] for f in later[1:]]
     operands = [kv[half], *qg, stat, *later[0], *far, *later_stats, *returned]
     in_specs = (
         [head_spec(a) for a in (kv[half], *qg)]
         + [stat_spec(stat)]
-        + [head_spec(a) for a in (*later[0], *far)]
+        + [head_spec(a) for a in later[0]]
+        + [half_of_whole if len(f) == 1 else head_spec(f[half]) for f in later[1:]]
         + [stat_spec(a) for a in later_stats]
         + [half_of_whole] * len(returned)
     )
@@ -255,9 +259,10 @@
     return lax.dot_general(a, b, NT, preferred_element_type=F32)
 
 
-def relay(two, sign):
+def relay(rows, sign):
+    two = shifted(rows, sign * 2)
     four = shifted(two, sign * 2)
-    return two, four, shifted(four, sign * 4)
+    return [(two,), (four,), (shifted(four, sign * 4),)]
 
 
 def per_device(series, norm_gain, w_query, w_key, w_value, w_out, out_grad):
@@ -266,9 +271,7 @@
     blocks = 2 * half // BLOCK
     tp_index = lax.axis_index("tp").astype(jnp.int32)
     seq_index = lax.axis_index("seq").astype(jnp.int32)
-    seq_size = lax.axis_size("seq")
-    run = seq_size // 4
-    where = jnp.stack([tp_index, seq_index // run])
+    where = tp_index[None]
     slots = jnp.arange(blocks, dtype=jnp.int32)
     global_block = seq_index * blocks + (slots + 2 * tp_index) % blocks
     distances = [1, 2, 4] + [blocks * 2**s for s in range(1, levels)]
@@ -290,27 +293,15 @@
             [matmul(rows, w_query).astype(BF16), matmul_t(grad_rows, w_out).astype(BF16)]
         )
 
-    kv_own = key_value(normed)
-    qg_own = query_grad(normed, out_grad)
-    kv_two, qg_two = shifted(kv_own, 2), shifted(qg_own, -2)
-    normed_other, kv_two, qg_two = lax.optimization_barrier((normed_other, kv_two, qg_two))
-    kv = (kv_own, key_value(normed_other))
-    qg = (qg_own, query_grad(normed_other, out_grad_other))
+    kv = (key_value(normed), key_value(normed_other))
+    qg = (query_grad(normed, out_grad), query_grad(normed_other, out_grad_other))
     kv_all = jnp.concatenate(kv, axis=1)
-    column = lax.all_gather(
-        kv_all,
-        "seq",
-        axis_index_groups=[list(range(k, seq_size, run)) for k in range(run)],
-    )
-    kv_far = [relay(kv_two, 1), relay(shifted(kv[1], 2), 1)]
-    qg_far = [relay(qg_two, -1), relay(shifted(qg[1], -2), -1)]
-    fetched = [(shifted(kv_all, 1),)] + list(zip(*kv_far))
-    later = [(shifted(jnp.concatenate(qg, axis=1), -1),)] + list(zip(*qg_far))
-    mixed, grad_query, stat, *backs = query_side(
-        where, bias, qg, kv, fetched, shifted(kv_all, 16), column
-    )
+    qg_all = jnp.concatenate(qg, axis=1)
+    fetched = [(shifted(kv_all, 1),)] + relay(kv_all, 1) + [(shifted(kv_all, by),) for by in (16, 32, 64)]
+    later = [(shifted(qg_all, -1),)] + relay(qg_all, -1)
+    mixed, grad_query, stat, *backs = query_side(where, bias, qg, kv, fetched, 3)
     stat, backs, later = lax.optimization_barrier((stat, backs, later))
-    returned = [shifted(b, -by) for b, by in zip(backs, (16, run, 2 * run))]
+    returned = [shifted(b, -by) for b, by in zip(backs, (16, 32, 64))]
     later_stats = [shifted(stat, -by) for by in (1, 2, 4, 8)]
     attn_other = swap_tp(matmul(mixed[half:], w_out).astype(BF16))
     attn_rows = matmul(mixed[:half], w_out) + attn_other.astype(F32)

time: 205 us -> 201 us (0.980)
  the two profiles are of different devices: /device:TPU:46 before, /device:TPU:206 now
where the time goes in v4:
time: 201 us
  starting transfers between devices  97.1 us (48%)
  waiting for transfers between devices  65.8 us (33%)
  Pallas kernels  13.9 us (7%)
  matrix products  13 us (6%)
  other arithmetic  6.89 us (3%)
  local copies, waits for them, and re-layouts  2.62 us (1%)
    ppermute x18, starting transfers between devices, shifted(): return lax.ppermute(value, 'seq', pairs)  92.9 us
    ppermute x18, waiting for transfers between devices, shifted(): return lax.ppermute(value, 'seq', pairs)  44.5 us
    ppermute x4, waiting for transfers between devices, swap_tp(): return lax.ppermute(value, 'tp', [(0, 1), (1, 0)])  21.4 us
    pallas_call x3, Pallas kernels, call(): pl.pallas_call(kernel, out_shape=outs, grid_spec=pltpu.PrefetchScalarGrid...  13.9 us
    dot_general x8, matrix products, matmul_t(): return lax.dot_general(a, b, NT, preferred_element_type=F32)  8.44 us
    dot_general x8, matrix products, matmul(): return jnp.dot(a, b, preferred_element_type=F32)  4.55 us
    ppermute x4, starting transfers between devices, swap_tp(): return lax.ppermute(value, 'tp', [(0, 1), (1, 0)])  4.19 us
  transfers between devices with their start and end apart: 22, of which 10 were waited for; matrix products, arithmetic and copies ran while one was open for 8% of the time, Pallas kernels for 7%

profile of v4, /device:TPU:206, one launch (start us, length us, event | category | flops | bytes accessed | tf_op | source)
XLA Modules:
  0.0 200.6 jit_solution(10608379440218946824)
XLA Ops:
  0.6 0.0 copy-start
  0.7 1.4 fusion.24
  2.1 1.2 fusion.18
  3.3 1.5 collective-permute-start
  4.8 2.1 %collective-permute-start.1 = (bf16[128,2048]{1,0:T(8,128)(2,1)}, bf16[128,2048]{1,0:T(8,128)(2,1)S(1)}, u32[]{:S(2)}, u32[]{:S(2)}) collective-permute-start(bf16[128,2048]{1,0:T(8,128)(2,1)} %param.14), channel_id=1, source_target_pairs={{0,1},{1,0},{2,3},{3,2},{4,5},{5,4},{6,7},{7,6},{8,9},{9,8},{10,11... | collective-permute-start | bytes 1572872 | tf_op jit(solution)/shard_map/ppermute | solution.py:29
  6.9 2.6 %fusion.11 = bf16[1,128,512]{2,1,0:T(8,128)(2,1)S(1)} fusion(bf16[128,2048]{1,0:T(8,128)(2,1)} %param.14, bf16[512,2048]{1,0:T(8,128)(2,1)} %param.13), kind=kOutput, calls=%fused_computation.25 | convolution fusion | flops 268500992 | bytes 2752512 | tf_op jit(solution)/shard_map/dot_general | solution.py:259
  9.5 0.4 fusion.15
  10.0 0.4 fusion.14
  10.5 0.5 fusion.10
  11.0 8.7 %collective-permute-done = bf16[128,2048]{1,0:T(8,128)(2,1)S(1)} collective-permute-done((bf16[128,2048]{1,0:T(8,128)(2,1)S(1)}, bf16[128,2048]{1,0:T(8,128)(2,1)S(1)}, u32[]{:S(2)}, u32[]{:S(2)}) %collective-permute-start) | collective-permute-done | bytes 524320 | tf_op jit(solution)/shard_map/ppermute | solution.py:29
  19.7 0.5 fusion.17
  20.2 0.5 fusion.16
  20.7 0.8 maximum_maximum_fusion
  21.5 2.9 %collective-permute-start.3 = (bf16[2,256,512]{2,1,0:T(8,128)(2,1)}, bf16[2,256,512]{2,1,0:T(8,128)(2,1)}, u32[]{:S(2)}, u32[]{:S(2)}) collective-permute-start(bf16[2,256,512]{2,1,0:T(8,128)(2,1)} %maximum_maximum_fusion), channel_id=1, source_target_pairs={{0,4},{2,6},{4,8},{6,10},{8,12},{10,14},{12,16},{14,18},{16,20},{1... | collective-permute-start | bytes 1572872 | tf_op jit(solution)/shard_map/ppermute | solution.py:25
  24.4 0.5 fusion.12
  24.9 4.9 %collective-permute-done.1 = bf16[128,2048]{1,0:T(8,128)(2,1)S(1)} collective-permute-done((bf16[128,2048]{1,0:T(8,128)(2,1)}, bf16[128,2048]{1,0:T(8,128)(2,1)S(1)}, u32[]{:S(2)}, u32[]{:S(2)}) %collective-permute-start.1) | collective-permute-done | bytes 524320 | tf_op jit(solution)/shard_map/ppermute | solution.py:29
  29.8 0.8 fusion.13
  30.7 0.6 copy-done.9
  31.3 2.9 %collective-permute-start.11 = (bf16[2,256,512]{2,1,0:T(8,128)(2,1)S(1)}, bf16[2,256,512]{2,1,0:T(8,128)(2,1)S(1)}, u32[]{:S(2)}, u32[]{:S(2)}) collective-permute-start(bf16[2,256,512]{2,1,0:T(8,128)(2,1)S(1)} %maximum_maximum_fusion.1), channel_id=1, source_target_pairs={{4,0},{6,2},{8,4},{10,6},{12,8},{14,10},{16,12},{18,14},{20,16},{2... | collective-permute-start | bytes 1572872 | tf_op jit(solution)/shard_map/ppermute | solution.py:25
  34.3 5.0 %collective-permute-start.8 = (bf16[2,256,512]{2,1,0:T(8,128)(2,1)}, bf16[2,256,512]{2,1,0:T(8,128)(2,1)}, u32[]{:S(2)}, u32[]{:S(2)}) collective-permute-start(bf16[2,256,512]{2,1,0:T(8,128)(2,1)} %maximum_maximum_fusion), channel_id=1, source_target_pairs={{0,128},{2,130},{4,132},{6,134},{8,136},{10,138},{12,140},{14,142}... | collective-permute-start | bytes 1572872 | tf_op jit(solution)/shard_map/ppermute | solution.py:25
  39.3 2.9 %collective-permute-start.4 = (bf16[2,256,512]{2,1,0:T(8,128)(2,1)}, bf16[2,256,512]{2,1,0:T(8,128)(2,1)}, u32[]{:S(2)}, u32[]{:S(2)}) collective-permute-start(bf16[2,256,512]{2,1,0:T(8,128)(2,1)} %collective-permute-done.3.refs_5_), channel_id=1, source_target_pairs={{0,4},{2,6},{4,8},{6,10},{8,12},{10,14},{12,16},{14,18},{16,20},{1... | collective-permute-start | bytes 1572872 | tf_op jit(solution)/shard_map/ppermute | solution.py:25
  42.2 1.9 collective-permute-start.7
  44.2 1.9 collective-permute-done.11.refs_5_
  46.0 2.9 %collective-permute-start.12 = (bf16[2,256,512]{2,1,0:T(8,128)(2,1)S(1)}, bf16[2,256,512]{2,1,0:T(8,128)(2,1)S(1)}, u32[]{:S(2)}, u32[]{:S(2)}) collective-permute-start(bf16[2,256,512]{2,1,0:T(8,128)(2,1)S(1)} %collective-permute-done.11.refs_5_), channel_id=1, source_target_pairs={{4,0},{6,2},{8,4},{10,6},{12,8},{14,10},{16,12},{18,14},{20,16},{2... | collective-permute-start | bytes 1572872 | tf_op jit(solution)/shard_map/ppermute | solution.py:25
  49.0 0.1 broadcast_in_dim.21
  49.0 0.1 ge.23
  49.1 1.1 pad_maximum_fusion
  50.2 3.7 %collective-permute-start.6 = (bf16[2,256,512]{2,1,0:T(8,128)(2,1)}, bf16[2,256,512]{2,1,0:T(8,128)(2,1)S(1)}, u32[]{:S(2)}, u32[]{:S(2)}) collective-permute-start(bf16[2,256,512]{2,1,0:T(8,128)(2,1)} %maximum_maximum_fusion), channel_id=1, source_target_pairs={{0,32},{2,34},{4,36},{6,38},{8,40},{10,42},{12,44},{14,46},{16,48}... | collective-permute-start | bytes 1572872 | tf_op jit(solution)/shard_map/ppermute | solution.py:25
  54.0 1.9 collective-permute-start.2
  55.9 50.6 %collective-permute-start.5 = (bf16[2,256,512]{2,1,0:T(8,128)(2,1)}, bf16[2,256,512]{2,1,0:T(8,128)(2,1)S(1)}, u32[]{:S(2)}, u32[]{:S(2)}) collective-permute-start(bf16[2,256,512]{2,1,0:T(8,128)(2,1)} %collective-permute-done.4.refs_6_), channel_id=1, source_target_pairs={{0,8},{2,10},{4,12},{6,14},{8,16},{10,18},{12,20},{14,22},{16,24},... | collective-permute-start | bytes 1572872 | tf_op jit(solution)/shard_map/ppermute | solution.py:25
  106.6 3.4 %collective-permute-start.10 = (bf16[2,256,512]{2,1,0:T(8,128)(2,1)}, bf16[2,256,512]{2,1,0:T(8,128)(2,1)S(1)}, u32[]{:S(2)}, u32[]{:S(2)}) collective-permute-start(bf16[2,256,512]{2,1,0:T(8,128)(2,1)} %copy-done.17), channel_id=1, source_target_pairs={{2,0},{4,2},{6,4},{8,6},{10,8},{12,10},{14,12},{16,14},{18,16},{20... | collective-permute-start | bytes 1572872 | tf_op jit(solution)/shard_map/ppermute | solution.py:25
  109.9 1.9 collective-permute-start.13
  111.9 0.1 compare_select_fusion.bias_ref
  112.0 0.9 pad_maximum_fusion.1.refs_1_.refs_2_
  113.0 7.1 %collective-permute-done.5.refs_7_ = bf16[2,256,512]{2,1,0:T(8,128)(2,1)S(1)} collective-permute-done((bf16[2,256,512]{2,1,0:T(8,128)(2,1)}, bf16[2,256,512]{2,1,0:T(8,128)(2,1)S(1)}, u32[]{:S(2)}, u32[]{:S(2)}) %collective-permute-start.5) | collective-permute-done | bytes 524320 | tf_op jit(solution)/shard_map/ppermute | solution.py:25
  120.1 0.8 copy-done.16
  120.9 7.3 %query_side.1 = (bf16[256,512]{1,0:T(8,128)(2,1)S(1)}, bf16[256,512]{1,0:T(8,128)(2,1)S(1)}, f32[4,2,256]{2,1,0:T(2,128)S(1)}, bf16[2,256,512]{2,1,0:T(8,128)(2,...) custom-call(s32[1]{0:T(128)} %bitcast.where_ref, ...), custom_call_target="tpu_custom_call" | custom-call | flops 671088640 | bytes 6291456 | tf_op jit(solution)/shard_map/query_side/pallas_call | solution.py:186
  128.1 5.6 %collective-permute-done.10.refs_4_ = bf16[2,256,512]{2,1,0:T(8,128)(2,1)S(1)} collective-permute-done((bf16[2,256,512]{2,1,0:T(8,128)(2,1)}, bf16[2,256,512]{2,1,0:T(8,128)(2,1)S(1)}, u32[]{:S(2)}, u32[]{:S(2)}) %collective-permute-start.10) | collective-permute-done | bytes 524320 | tf_op jit(solution)/shard_map/ppermute | solution.py:25
  133.8 9.1 %collective-permute-done.13.refs_7_ = bf16[2,256,512]{2,1,0:T(8,128)(2,1)S(1)} collective-permute-done((bf16[2,256,512]{2,1,0:T(8,128)(2,1)S(1)}, bf16[2,256,512]{2,1,0:T(8,128)(2,1)S(1)}, u32[]{:S(2)}, u32[]{:S(2)}) %collective-permute-start.13) | collective-permute-done | bytes 524320 | tf_op jit(solution)/shard_map/ppermute | solution.py:25
  142.9 1.9 collective-permute-start.18
  144.8 1.9 collective-permute-start.19
  146.8 1.3 collective-permute-start.20
  148.1 1.9 collective-permute-start.17
  150.0 1.9 collective-permute-start.16
  151.9 8.4 %collective-permute-done.17.refs_11_ = f32[4,2,256]{2,1,0:T(2,128)S(1)} collective-permute-done((f32[4,2,256]{2,1,0:T(2,128)S(1)}, f32[4,2,256]{2,1,0:T(2,128)S(1)}, u32[]{:S(2)}, u32[]{:S(2)}) %collective-permute-start.17) | collective-permute-done | bytes 8224 | tf_op jit(solution)/shard_map/ppermute | solution.py:25
  160.3 1.9 collective-permute-start.15
  162.2 1.9 collective-permute-start.14
  164.2 0.4 convolution_convert_fusion
  164.6 1.2 collective-permute-done.15.refs_9_
  165.8 11.1 %collective-permute-done.19.refs_13_ = bf16[2,256,512]{2,1,0:T(8,128)(2,1)S(1)} collective-permute-done((bf16[2,256,512]{2,1,0:T(8,128)(2,1)S(1)}, bf16[2,256,512]{2,1,0:T(8,128)(2,1)S(1)}, u32[]{:S(2)}, u32[]{:S(2)}) %collective-permute-start.19) | collective-permute-done | bytes 524320 | tf_op jit(solution)/shard_map/ppermute | solution.py:25
  177.0 3.3 %key_side.3 = bf16[2,128,512]{2,1,0:T(8,128)(2,1)S(1)} custom-call(s32[1]{0:T(128)} %bitcast.where_ref, bf16[2,128,512]{2,1,0:T(8,128)(2,1)S(1)} %pad_maximum_fusion.3.refs_3_.refs_0_, bf16[2,128,512]{2,1,0:T(8,128)(2,1)S(1)} %get-tuple-element.32.refs_0_.refs_1_, bf16[2,128,512]{2,1,0:T(8,128)(2,1)S(1)} %pad_maximum_fusion.1.refs_1_.refs_2_, ...), custom_call_target="tpu_custom_call" | custom-call | flops 234881024 | bytes 6291456 | tf_op jit(solution)/shard_map/key_side/pallas_call | solution.py:186
  180.3 0.8 fusion.25
  181.1 0.8 copy-done.4
  181.9 0.8 fusion.26
  182.7 0.8 fusion.6
  183.5 0.6 collective-permute-start.21
  184.1 3.3 %key_side.2 = bf16[2,128,512]{2,1,0:T(8,128)(2,1)S(1)} custom-call(s32[1]{0:T(128)} %bitcast.where_ref, bf16[2,128,512]{2,1,0:T(8,128)(2,1)S(1)} %get-tuple-element.33.refs_2_.refs_0_, bf16[2,128,512]{2,1,0:T(8,128)(2,1)S(1)} %get-tuple-element.32.refs_0_.refs_1_, bf16[2,128,512]{2,1,0:T(8,128)(2,1)S(1)} %pad_maximum_fusion.1.refs_1_.refs_2_, ...), custom_call_target="tpu_custom_call" | custom-call | flops 234881024 | bytes 6291456 | tf_op jit(solution)/shard_map/key_side/pallas_call | solution.py:186
  187.4 0.8 fusion.27
  188.2 0.8 fusion.28
  189.1 0.2 copy-done.7
  189.3 1.3 fusion.5
  190.6 7.8 %collective-permute-done.21 = bf16[128,2048]{1,0:T(8,128)(2,1)S(1)} collective-permute-done((bf16[128,2048]{1,0:T(8,128)(2,1)S(1)}, bf16[128,2048]{1,0:T(8,128)(2,1)S(1)}, u32[]{:S(2)}, u32[]{:S(2)}) %collective-permute-start.21) | collective-permute-done | bytes 524320 | tf_op jit(solution)/shard_map/ppermute | solution.py:29
  198.4 1.0 fusion.19
  199.4 1.2 fusion.23
  (53 shorter events, 0.2 us)
Async XLA Ops:
  0.6 9.8 %copy-start = (bf16[2048,512]{1,0:T(8,128)(2,1)S(1)}, bf16[2048,512]{1,0:T(8,128)(2,1)}, u32[]{:S(2)}) copy-start(bf16[2048,512]{1,0:T(8,128)(2,1)} %param.10) | copy-start | bytes 6291460
  0.6 8.9 %copy-start.1 = (bf16[2048,512]{1,0:T(8,128)(2,1)S(1)}, bf16[2048,512]{1,0:T(8,128)(2,1)}, u32[]{:S(2)}) copy-start(bf16[2048,512]{1,0:T(8,128)(2,1)} %param.12) | copy-start | bytes 6291460
  3.3 6.7 %copy-start.3 = (bf16[2048,512]{1,0:T(8,128)(2,1)S(1)}, bf16[2048,512]{1,0:T(8,128)(2,1)}, u32[]{:S(2)}) copy-start(bf16[2048,512]{1,0:T(8,128)(2,1)} %param.11) | copy-start | bytes 6291460
  3.3 16.4 %collective-permute-start = (bf16[128,2048]{1,0:T(8,128)(2,1)S(1)}, bf16[128,2048]{1,0:T(8,128)(2,1)S(1)}, u32[]{:S(2)}, u32[]{:S(2)}) collective-permute-start(bf16[128,2048]{1,0:T(8,128)(2,1)S(1)} %fusion.18), channel_id=1, source_target_pairs={{0,1},{1,0},{2,3},{3,2},{4,5},{5,4},{6,7},{7,6},{8,9},{9,8},{10,11... | collective-permute-start | bytes 1572872 | tf_op jit(solution)/shard_map/ppermute | solution.py:29
  4.8 25.0 %collective-permute-start.1 = (bf16[128,2048]{1,0:T(8,128)(2,1)}, bf16[128,2048]{1,0:T(8,128)(2,1)S(1)}, u32[]{:S(2)}, u32[]{:S(2)}) collective-permute-start(bf16[128,2048]{1,0:T(8,128)(2,1)} %param.14), channel_id=1, source_target_pairs={{0,1},{1,0},{2,3},{3,2},{4,5},{5,4},{6,7},{7,6},{8,9},{9,8},{10,11... | collective-permute-start | bytes 1572872 | tf_op jit(solution)/shard_map/ppermute | solution.py:29
  9.5 21.1 %copy-start.10 = (bf16[1,128,512]{2,1,0:T(8,128)(2,1)}, bf16[1,128,512]{2,1,0:T(8,128)(2,1)S(1)}, u32[]{:S(2)}) copy-start(bf16[1,128,512]{2,1,0:T(8,128)(2,1)S(1)} %fusion.11) | copy-start | bytes 393220
  10.0 10.7 %copy-start.11 = (bf16[1,128,512]{2,1,0:T(8,128)(2,1)}, bf16[1,128,512]{2,1,0:T(8,128)(2,1)S(1)}, u32[]{:S(2)}) copy-start(bf16[1,128,512]{2,1,0:T(8,128)(2,1)S(1)} %fusion.15) | copy-start | bytes 393220
  10.5 10.2 %copy-start.12 = (bf16[1,128,512]{2,1,0:T(8,128)(2,1)}, bf16[1,128,512]{2,1,0:T(8,128)(2,1)S(1)}, u32[]{:S(2)}) copy-start(bf16[1,128,512]{2,1,0:T(8,128)(2,1)S(1)} %fusion.14) | copy-start | bytes 393220
  11.0 19.7 %copy-start.13 = (bf16[1,128,512]{2,1,0:T(8,128)(2,1)}, bf16[1,128,512]{2,1,0:T(8,128)(2,1)S(1)}, u32[]{:S(2)}) copy-start(bf16[1,128,512]{2,1,0:T(8,128)(2,1)S(1)} %fusion.10) | copy-start | bytes 393220
  20.7 9.1 %copy-start.5 = (bf16[512,2048]{1,0:T(8,128)(2,1)S(1)}, bf16[512,2048]{1,0:T(8,128)(2,1)}, u32[]{:S(2)}) copy-start(bf16[512,2048]{1,0:T(8,128)(2,1)} %param.13) | copy-start | bytes 6291460
  21.5 17.7 %collective-permute-start.3 = (bf16[2,256,512]{2,1,0:T(8,128)(2,1)}, bf16[2,256,512]{2,1,0:T(8,128)(2,1)}, u32[]{:S(2)}, u32[]{:S(2)}) collective-permute-start(bf16[2,256,512]{2,1,0:T(8,128)(2,1)} %maximum_maximum_fusion), channel_id=1, source_target_pairs={{0,4},{2,6},{4,8},{6,10},{8,12},{10,14},{12,16},{14,18},{16,20},{1... | collective-permute-start | bytes 1572872 | tf_op jit(solution)/shard_map/ppermute | solution.py:25
  24.9 24.0 %copy-start.19 = (s32[10]{0:T(128)S(1)}, s32[10]{0:T(128)}, u32[]{:S(2)}) copy-start(s32[10]{0:T(128)} %constant.37.clone) | copy-start | bytes 124
  30.7 0.6 copy-start.9
  31.3 14.7 %copy-start.17 = (bf16[2,256,512]{2,1,0:T(8,128)(2,1)}, bf16[2,256,512]{2,1,0:T(8,128)(2,1)S(1)}, u32[]{:S(2)}) copy-start(bf16[2,256,512]{2,1,0:T(8,128)(2,1)S(1)} %maximum_maximum_fusion.1) | copy-start | bytes 1572868
  31.3 14.7 %collective-permute-start.11 = (bf16[2,256,512]{2,1,0:T(8,128)(2,1)S(1)}, bf16[2,256,512]{2,1,0:T(8,128)(2,1)S(1)}, u32[]{:S(2)}, u32[]{:S(2)}) collective-permute-start(bf16[2,256,512]{2,1,0:T(8,128)(2,1)S(1)} %maximum_maximum_fusion.1), channel_id=1, source_target_pairs={{4,0},{6,2},{8,4},{10,6},{12,8},{14,10},{16,12},{18,14},{20,16},{2... | collective-permute-start | bytes 1572872 | tf_op jit(solution)/shard_map/ppermute | solution.py:25
  34.3 19.7 %collective-permute-start.8 = (bf16[2,256,512]{2,1,0:T(8,128)(2,1)}, bf16[2,256,512]{2,1,0:T(8,128)(2,1)}, u32[]{:S(2)}, u32[]{:S(2)}) collective-permute-start(bf16[2,256,512]{2,1,0:T(8,128)(2,1)} %maximum_maximum_fusion), channel_id=1, source_target_pairs={{0,128},{2,130},{4,132},{6,134},{8,136},{10,138},{12,140},{14,142}... | collective-permute-start | bytes 1572872 | tf_op jit(solution)/shard_map/ppermute | solution.py:25
  39.3 16.7 %collective-permute-start.4 = (bf16[2,256,512]{2,1,0:T(8,128)(2,1)}, bf16[2,256,512]{2,1,0:T(8,128)(2,1)}, u32[]{:S(2)}, u32[]{:S(2)}) collective-permute-start(bf16[2,256,512]{2,1,0:T(8,128)(2,1)} %collective-permute-done.3.refs_5_), channel_id=1, source_target_pairs={{0,4},{2,6},{4,8},{6,10},{8,12},{10,14},{12,16},{14,18},{16,20},{1... | collective-permute-start | bytes 1572872 | tf_op jit(solution)/shard_map/ppermute | solution.py:25
  42.2 64.3 %collective-permute-start.7 = (bf16[2,256,512]{2,1,0:T(8,128)(2,1)}, bf16[2,256,512]{2,1,0:T(8,128)(2,1)}, u32[]{:S(2)}, u32[]{:S(2)}) collective-permute-start(bf16[2,256,512]{2,1,0:T(8,128)(2,1)} %maximum_maximum_fusion), channel_id=1, source_target_pairs={{0,64},{2,66},{4,68},{6,70},{8,72},{10,74},{12,76},{14,78},{16,80}... | collective-permute-start | bytes 1572872 | tf_op jit(solution)/shard_map/ppermute | solution.py:25
  46.0 63.9 %collective-permute-start.12 = (bf16[2,256,512]{2,1,0:T(8,128)(2,1)S(1)}, bf16[2,256,512]{2,1,0:T(8,128)(2,1)S(1)}, u32[]{:S(2)}, u32[]{:S(2)}) collective-permute-start(bf16[2,256,512]{2,1,0:T(8,128)(2,1)S(1)} %collective-permute-done.11.refs_5_), channel_id=1, source_target_pairs={{4,0},{6,2},{8,4},{10,6},{12,8},{14,10},{16,12},{18,14},{20,16},{2... | collective-permute-start | bytes 1572872 | tf_op jit(solution)/shard_map/ppermute | solution.py:25
  50.2 62.7 %collective-permute-start.6 = (bf16[2,256,512]{2,1,0:T(8,128)(2,1)}, bf16[2,256,512]{2,1,0:T(8,128)(2,1)S(1)}, u32[]{:S(2)}, u32[]{:S(2)}) collective-permute-start(bf16[2,256,512]{2,1,0:T(8,128)(2,1)} %maximum_maximum_fusion), channel_id=1, source_target_pairs={{0,32},{2,34},{4,36},{6,38},{8,40},{10,42},{12,44},{14,46},{16,48}... | collective-permute-start | bytes 1572872 | tf_op jit(solution)/shard_map/ppermute | solution.py:25
  54.0 58.9 %collective-permute-start.2 = (bf16[2,256,512]{2,1,0:T(8,128)(2,1)}, bf16[2,256,512]{2,1,0:T(8,128)(2,1)S(1)}, u32[]{:S(2)}, u32[]{:S(2)}) collective-permute-start(bf16[2,256,512]{2,1,0:T(8,128)(2,1)} %maximum_maximum_fusion), channel_id=1, source_target_pairs={{0,2},{2,4},{4,6},{6,8},{8,10},{10,12},{12,14},{14,16},{16,18},{18... | collective-permute-start | bytes 1572872 | tf_op jit(solution)/shard_map/ppermute | solution.py:25
  55.9 64.1 %collective-permute-start.5 = (bf16[2,256,512]{2,1,0:T(8,128)(2,1)}, bf16[2,256,512]{2,1,0:T(8,128)(2,1)S(1)}, u32[]{:S(2)}, u32[]{:S(2)}) collective-permute-start(bf16[2,256,512]{2,1,0:T(8,128)(2,1)} %collective-permute-done.4.refs_6_), channel_id=1, source_target_pairs={{0,8},{2,10},{4,12},{6,14},{8,16},{10,18},{12,20},{14,22},{16,24},... | collective-permute-start | bytes 1572872 | tf_op jit(solution)/shard_map/ppermute | solution.py:25
  106.6 27.2 %collective-permute-start.10 = (bf16[2,256,512]{2,1,0:T(8,128)(2,1)}, bf16[2,256,512]{2,1,0:T(8,128)(2,1)S(1)}, u32[]{:S(2)}, u32[]{:S(2)}) collective-permute-start(bf16[2,256,512]{2,1,0:T(8,128)(2,1)} %copy-done.17), channel_id=1, source_target_pairs={{2,0},{4,2},{6,4},{8,6},{10,8},{12,10},{14,12},{16,14},{18,16},{20... | collective-permute-start | bytes 1572872 | tf_op jit(solution)/shard_map/ppermute | solution.py:25
  109.9 33.0 %collective-permute-start.13 = (bf16[2,256,512]{2,1,0:T(8,128)(2,1)S(1)}, bf16[2,256,512]{2,1,0:T(8,128)(2,1)S(1)}, u32[]{:S(2)}, u32[]{:S(2)}) collective-permute-start(bf16[2,256,512]{2,1,0:T(8,128)(2,1)S(1)} %collective-permute-done.12.refs_6_), channel_id=1, source_target_pairs={{8,0},{10,2},{12,4},{14,6},{16,8},{18,10},{20,12},{22,14},{24,16},... | collective-permute-start | bytes 1572872 | tf_op jit(solution)/shard_map/ppermute | solution.py:25
  112.9 7.1 %copy-start.14 = (bf16[2,256,512]{2,1,0:T(8,128)(2,1)}, bf16[2,256,512]{2,1,0:T(8,128)(2,1)S(1)}, u32[]{:S(2)}) copy-start(bf16[2,256,512]{2,1,0:T(8,128)(2,1)S(1)} %collective-permute-done.6.refs_8_) | copy-start | bytes 1572868
  112.9 7.1 %copy-start.15 = (bf16[2,256,512]{2,1,0:T(8,128)(2,1)}, bf16[2,256,512]{2,1,0:T(8,128)(2,1)S(1)}, u32[]{:S(2)}) copy-start(bf16[2,256,512]{2,1,0:T(8,128)(2,1)S(1)} %collective-permute-done.2.refs_4_) | copy-start | bytes 1572868
  120.1 0.8 copy-start.16
  120.9 43.3 %copy-start.6 = (bf16[512,2048]{1,0:T(8,128)(2,1)S(1)}, bf16[512,2048]{1,0:T(8,128)(2,1)}, u32[]{:S(2)}) copy-start(bf16[512,2048]{1,0:T(8,128)(2,1)} %param.13) | copy-start | bytes 6291460
  142.9 22.9 %collective-permute-start.18 = (bf16[2,256,512]{2,1,0:T(8,128)(2,1)S(1)}, bf16[2,256,512]{2,1,0:T(8,128)(2,1)S(1)}, u32[]{:S(2)}, u32[]{:S(2)}) collective-permute-start(bf16[2,256,512]{2,1,0:T(8,128)(2,1)S(1)} %get-tuple-element.27), channel_id=1, source_target_pairs={{32,0},{34,2},{36,4},{38,6},{40,8},{42,10},{44,12},{46,14},{48,16}... | collective-permute-start | bytes 1572872 | tf_op jit(solution)/shard_map/ppermute | solution.py:25
  144.8 32.1 %collective-permute-start.19 = (bf16[2,256,512]{2,1,0:T(8,128)(2,1)S(1)}, bf16[2,256,512]{2,1,0:T(8,128)(2,1)S(1)}, u32[]{:S(2)}, u32[]{:S(2)}) collective-permute-start(bf16[2,256,512]{2,1,0:T(8,128)(2,1)S(1)} %get-tuple-element.28), channel_id=1, source_target_pairs={{64,0},{66,2},{68,4},{70,6},{72,8},{74,10},{76,12},{78,14},{80,16}... | collective-permute-start | bytes 1572872 | tf_op jit(solution)/shard_map/ppermute | solution.py:25
  146.8 30.2 %collective-permute-start.20 = (bf16[2,256,512]{2,1,0:T(8,128)(2,1)S(1)}, bf16[2,256,512]{2,1,0:T(8,128)(2,1)S(1)}, u32[]{:S(2)}, u32[]{:S(2)}) collective-permute-start(bf16[2,256,512]{2,1,0:T(8,128)(2,1)S(1)} %get-tuple-element.29), channel_id=1, source_target_pairs={{128,0},{130,2},{132,4},{134,6},{136,8},{138,10},{140,12},{142,14}... | collective-permute-start | bytes 1572872 | tf_op jit(solution)/shard_map/ppermute | solution.py:25
  148.1 12.2 %collective-permute-start.17 = (f32[4,2,256]{2,1,0:T(2,128)S(1)}, f32[4,2,256]{2,1,0:T(2,128)S(1)}, u32[]{:S(2)}, u32[]{:S(2)}) collective-permute-start(f32[4,2,256]{2,1,0:T(2,128)S(1)} %get-tuple-element.22.refs_3_), channel_id=1, source_target_pairs={{16,0},{18,2},{20,4},{22,6},{24,8},{26,10},{28,12},{30,14},{32,16}... | collective-permute-start | bytes 24584 | tf_op jit(solution)/shard_map/ppermute | solution.py:25
  150.0 12.2 %collective-permute-start.16 = (f32[4,2,256]{2,1,0:T(2,128)S(1)}, f32[4,2,256]{2,1,0:T(2,128)S(1)}, u32[]{:S(2)}, u32[]{:S(2)}) collective-permute-start(f32[4,2,256]{2,1,0:T(2,128)S(1)} %get-tuple-element.22.refs_3_), channel_id=1, source_target_pairs={{8,0},{10,2},{12,4},{14,6},{16,8},{18,10},{20,12},{22,14},{24,16},... | collective-permute-start | bytes 24584 | tf_op jit(solution)/shard_map/ppermute | solution.py:25
  160.3 5.5 %collective-permute-start.15 = (f32[4,2,256]{2,1,0:T(2,128)S(1)}, f32[4,2,256]{2,1,0:T(2,128)S(1)}, u32[]{:S(2)}, u32[]{:S(2)}) collective-permute-start(f32[4,2,256]{2,1,0:T(2,128)S(1)} %get-tuple-element.22.refs_3_), channel_id=1, source_target_pairs={{4,0},{6,2},{8,4},{10,6},{12,8},{14,10},{16,12},{18,14},{20,16},{2... | collective-permute-start | bytes 24584 | tf_op jit(solution)/shard_map/ppermute | solution.py:25
  162.2 3.6 %collective-permute-start.14 = (f32[4,2,256]{2,1,0:T(2,128)S(1)}, f32[4,2,256]{2,1,0:T(2,128)S(1)}, u32[]{:S(2)}, u32[]{:S(2)}) collective-permute-start(f32[4,2,256]{2,1,0:T(2,128)S(1)} %get-tuple-element.22.refs_3_), channel_id=1, source_target_pairs={{2,0},{4,2},{6,4},{8,6},{10,8},{12,10},{14,12},{16,14},{18,16},{20... | collective-permute-start | bytes 24584 | tf_op jit(solution)/shard_map/ppermute | solution.py:25
  164.6 15.7 %copy-start.2 = (bf16[2048,512]{1,0:T(8,128)(2,1)S(1)}, bf16[2048,512]{1,0:T(8,128)(2,1)}, u32[]{:S(2)}) copy-start(bf16[2048,512]{1,0:T(8,128)(2,1)} %param.12) | copy-start | bytes 6291460
  165.8 23.2 %collective-permute-start.9 = (bf16[128,2048]{1,0:T(8,128)(2,1)S(1)}, bf16[128,2048]{1,0:T(8,128)(2,1)S(1)}, u32[]{:S(2)}, u32[]{:S(2)}) collective-permute-start(bf16[128,2048]{1,0:T(8,128)(2,1)S(1)} %convolution_convert_fusion), channel_id=1, source_target_pairs={{0,1},{1,0},{2,3},{3,2},{4,5},{5,4},{6,7},{7,6},{8,9},{9,8},{10,11... | collective-permute-start | bytes 1572872 | tf_op jit(solution)/shard_map/ppermute | solution.py:29
  180.3 1.6 copy-start.4
  183.5 14.8 %collective-permute-start.21 = (bf16[128,2048]{1,0:T(8,128)(2,1)S(1)}, bf16[128,2048]{1,0:T(8,128)(2,1)S(1)}, u32[]{:S(2)}, u32[]{:S(2)}) collective-permute-start(bf16[128,2048]{1,0:T(8,128)(2,1)S(1)} %fusion.6), channel_id=1, source_target_pairs={{0,1},{1,0},{2,3},{3,2},{4,5},{5,4},{6,7},{7,6},{8,9},{9,8},{10,11... | collective-permute-start | bytes 1572872 | tf_op jit(solution)/shard_map/ppermute | solution.py:29
  188.2 1.0 copy-start.7
  189.1 9.3 %copy-start.18 = (f32[2048]{0:T(1024)S(1)}, f32[2048]{0:T(1024)}, u32[]{:S(2)}) copy-start(f32[2048]{0:T(1024)} %param.9) | copy-start | bytes 24580
  190.6 8.8 %copy-start.8 = (bf16[128,2048]{1,0:T(8,128)(2,1)S(1)}, bf16[128,2048]{1,0:T(8,128)(2,1)}, u32[]{:S(2)}) copy-start(bf16[128,2048]{1,0:T(8,128)(2,1)} %param.14) | copy-start | bytes 1572868

commit v5 on v4

--- a/solution.py
+++ b/solution.py
@@ -259,10 +259,20 @@
     return lax.dot_general(a, b, NT, preferred_element_type=F32)
 
 
-def relay(rows, sign):
+def swapped(own, passed, bit, sign):
+    size = lax.axis_size("seq")
+    high = (lax.axis_index("seq") // bit) % 2 == 1
+    sent = jnp.where(high, passed, own) if sign > 0 else jnp.where(high, own, passed)
+    return lax.ppermute(sent, "seq", [(i, i ^ bit) for i in range(size)])
+
+
+def exchange(rows, sign):
     two = shifted(rows, sign * 2)
+    far = shifted(rows, sign * 32)
     four = shifted(two, sign * 2)
-    return [(two,), (four,), (shifted(four, sign * 4),)]
+    one = swapped(rows, two, 1, sign)
+    sixteen = swapped(rows, far, 16, sign)
+    return [one, two, four, shifted(four, sign * 4), sixteen, far, shifted(far, sign * 32)]
 
 
 def per_device(series, norm_gain, w_query, w_key, w_value, w_out, out_grad):
@@ -283,7 +293,8 @@
     unit_rows = series_f * inv_rms
     normed = (unit_rows * norm_gain).astype(BF16)
     normed_other = swap_tp(normed)
-    out_grad_other = swap_tp(out_grad)
+    out_grad_later, normed_other = lax.optimization_barrier((out_grad, normed_other))
+    out_grad_other = swap_tp(out_grad_later)
 
     def key_value(rows):
         return jnp.stack([matmul(rows, w_key).astype(BF16), matmul(rows, w_value).astype(BF16)])
@@ -297,18 +308,20 @@
     qg = (query_grad(normed, out_grad), query_grad(normed_other, out_grad_other))
     kv_all = jnp.concatenate(kv, axis=1)
     qg_all = jnp.concatenate(qg, axis=1)
-    fetched = [(shifted(kv_all, 1),)] + relay(kv_all, 1) + [(shifted(kv_all, by),) for by in (16, 32, 64)]
-    later = [(shifted(qg_all, -1),)] + relay(qg_all, -1)
-    mixed, grad_query, stat, *backs = query_side(where, bias, qg, kv, fetched, 3)
-    stat, backs, later = lax.optimization_barrier((stat, backs, later))
-    returned = [shifted(b, -by) for b, by in zip(backs, (16, 32, 64))]
-    later_stats = [shifted(stat, -by) for by in (1, 2, 4, 8)]
+    fetched = exchange(kv_all, 1)
+    later = exchange(qg_all, -1)
+    mixed, grad_query, stat = query_side(where, bias, qg, kv, [(f,) for f in fetched], 0)
+    last = later.pop(3)
+    stat, later = lax.optimization_barrier((stat, later))
+    later.insert(3, last)
+    later = [(f,) for f in later]
+    later_stats = [shifted(stat, -(2**s)) for s in range(levels)]
     attn_other = swap_tp(matmul(mixed[half:], w_out).astype(BF16))
     attn_rows = matmul(mixed[:half], w_out) + attn_other.astype(F32)
     layer_out = (series_f + attn_rows).astype(BF16)
 
     def back(at):
-        grad_kv = key_side(at, where, kv, qg, stat, later, later_stats, returned)
+        grad_kv = key_side(at, where, kv, qg, stat, later, later_stats, [])
         rows = slice(at * half, (at + 1) * half)
         return (
             matmul_t(grad_query[rows], w_query)

time: 201 us -> 171 us (0.85)
  the two profiles are of different devices: /device:TPU:206 before, /device:TPU:24 now
where the time goes in v5:
time: 171 us; the launch traced here: 170 us
  waiting for transfers between devices  64.6 us (38%)
  starting transfers between devices  62.5 us (37%)
  Pallas kernels  14.3 us (8%)
  matrix products  12.8 us (7%)
  other arithmetic  11.5 us (7%)
  local copies, waits for them, and re-layouts  2.66 us (2%)
    ppermute x17, starting transfers between devices, shifted(): return lax.ppermute(value, 'seq', pairs)  50.6 us
    ppermute x4, waiting for transfers between devices, swap_tp(): return lax.ppermute(value, 'tp', [(0, 1), (1, 0)])  36.3 us
    ppermute x17, waiting for transfers between devices, shifted(): return lax.ppermute(value, 'seq', pairs)  28.3 us
    pallas_call x3, Pallas kernels, call(): pl.pallas_call(kernel, out_shape=outs, grid_spec=pltpu.PrefetchScalarGrid...  14.3 us
    ppermute x4, starting transfers between devices, swap_tp(): return lax.ppermute(value, 'tp', [(0, 1), (1, 0)])  10.1 us
    dot_general x8, matrix products, matmul_t(): return lax.dot_general(a, b, NT, preferred_element_type=F32)  6.68 us
    dot_general x8, matrix products, matmul(): return jnp.dot(a, b, preferred_element_type=F32)  6.12 us
  transfers between devices with their start and end apart: 25, of which 7 were waited for; matrix products, arithmetic and copies ran while one was open for 11% of the time, Pallas kernels for 8%

profile of v5, /device:TPU:24, one launch (start us, length us, event | category | flops | bytes accessed | tf_op | source)
XLA Modules:
  0.0 169.7 jit_solution(16414833666905468897)
XLA Ops:
  0.7 1.4 fusion.24
  2.1 1.2 fusion.18
  3.3 3.1 %collective-permute-start = (bf16[128,2048]{1,0:T(8,128)(2,1)S(1)}, bf16[128,2048]{1,0:T(8,128)(2,1)S(1)}, u32[]{:S(2)}, u32[]{:S(2)}) collective-permute-start(bf16[128,2048]{1,0:T(8,128)(2,1)S(1)} %fusion.18), channel_id=1, source_target_pairs={{0,1},{1,0},{2,3},{3,2},{4,5},{5,4},{6,7},{7,6},{8,9},{9,8},{10,11... | collective-permute-start | bytes 1572872 | tf_op jit(solution)/shard_map/ppermute | solution.py:29
  6.4 2.1 %fusion.15 = bf16[1,128,512]{2,1,0:T(8,128)(2,1)S(1)} fusion(bf16[128,2048]{1,0:T(8,128)(2,1)S(1)} %fusion.18, bf16[2048,512]{1,0:T(8,128)(2,1)} %param.12), kind=kOutput, calls=%fused_computation.29 | convolution fusion | flops 268500992 | bytes 2752512 | tf_op jit(solution)/shard_map/dot_general | solution.py:255
  8.5 0.5 fusion.14
  9.0 9.6 %collective-permute-done = bf16[128,2048]{1,0:T(8,128)(2,1)S(1)} collective-permute-done((bf16[128,2048]{1,0:T(8,128)(2,1)S(1)}, bf16[128,2048]{1,0:T(8,128)(2,1)S(1)}, u32[]{:S(2)}, u32[]{:S(2)}) %collective-permute-start) | collective-permute-done | bytes 524320 | tf_op jit(solution)/shard_map/ppermute | solution.py:29
  18.6 0.4 fusion.17
  19.0 0.4 fusion.16
  19.5 0.8 maximum_maximum_fusion
  20.3 3.8 %collective-permute-start.2 = (bf16[2,256,512]{2,1,0:T(8,128)(2,1)}, bf16[2,256,512]{2,1,0:T(8,128)(2,1)}, u32[]{:S(2)}, u32[]{:S(2)}) collective-permute-start(bf16[2,256,512]{2,1,0:T(8,128)(2,1)} %maximum_maximum_fusion), channel_id=1, source_target_pairs={{0,4},{2,6},{4,8},{6,10},{8,12},{10,14},{12,16},{14,18},{16,20},{1... | collective-permute-start | bytes 1572872 | tf_op jit(solution)/shard_map/ppermute | solution.py:25
  24.2 3.1 %collective-permute-start.1 = (bf16[128,2048]{1,0:T(8,128)(2,1)S(1)}, bf16[128,2048]{1,0:T(8,128)(2,1)S(1)}, u32[]{:S(2)}, u32[]{:S(2)}) collective-permute-start(bf16[128,2048]{1,0:T(8,128)(2,1)S(1)} %copy-done.9), channel_id=1, source_target_pairs={{0,1},{1,0},{2,3},{3,2},{4,5},{5,4},{6,7},{7,6},{8,9},{9,8},{10,11... | collective-permute-start | bytes 1572872 | tf_op jit(solution)/shard_map/ppermute | solution.py:29
  27.3 0.8 fusion.11
  28.2 0.5 fusion.10
  28.6 1.3 collective-permute-start.6
  29.9 0.4 fusion.12
  30.4 10.4 %collective-permute-done.2.refs_5_ = bf16[2,256,512]{2,1,0:T(8,128)(2,1)} collective-permute-done((bf16[2,256,512]{2,1,0:T(8,128)(2,1)}, bf16[2,256,512]{2,1,0:T(8,128)(2,1)}, u32[]{:S(2)}, u32[]{:S(2)}) %collective-permute-start.2) | collective-permute-done | bytes 524320 | tf_op jit(solution)/shard_map/ppermute | solution.py:25
  40.8 1.9 %collective-permute-start.4 = (bf16[2,256,512]{2,1,0:T(8,128)(2,1)}, bf16[2,256,512]{2,1,0:T(8,128)(2,1)}, u32[]{:S(2)}, u32[]{:S(2)}) collective-permute-start(bf16[2,256,512]{2,1,0:T(8,128)(2,1)} %collective-permute-done.2.refs_5_), channel_id=1, source_target_pairs={{0,4},{2,6},{4,8},{6,10},{8,12},{10,14},{12,16},{14,18},{16,20},{1... | collective-permute-start | bytes 1572872 | tf_op jit(solution)/shard_map/ppermute | solution.py:25
  42.7 18.1 %collective-permute-done.1 = bf16[128,2048]{1,0:T(8,128)(2,1)S(1)} collective-permute-done((bf16[128,2048]{1,0:T(8,128)(2,1)S(1)}, bf16[128,2048]{1,0:T(8,128)(2,1)S(1)}, u32[]{:S(2)}, u32[]{:S(2)}) %collective-permute-start.1) | collective-permute-done | bytes 524320 | tf_op jit(solution)/shard_map/ppermute | solution.py:29
  60.8 0.8 fusion.13
  61.6 0.6 copy-done.15
  62.3 0.8 maximum_maximum_fusion.1
  63.1 2.0 %collective-permute-start.10 = (bf16[2,256,512]{2,1,0:T(8,128)(2,1)}, bf16[2,256,512]{2,1,0:T(8,128)(2,1)S(1)}, u32[]{:S(2)}, u32[]{:S(2)}) collective-permute-start(bf16[2,256,512]{2,1,0:T(8,128)(2,1)} %maximum_maximum_fusion.1), channel_id=1, source_target_pairs={{4,0},{6,2},{8,4},{10,6},{12,8},{14,10},{16,12},{18,14},{20,16},{2... | collective-permute-start | bytes 1572872 | tf_op jit(solution)/shard_map/ppermute | solution.py:25
  65.2 2.7 %collective-permute-start.13 = (bf16[2,256,512]{2,1,0:T(8,128)(2,1)}, bf16[2,256,512]{2,1,0:T(8,128)(2,1)S(1)}, u32[]{:S(2)}, u32[]{:S(2)}) collective-permute-start(bf16[2,256,512]{2,1,0:T(8,128)(2,1)} %maximum_maximum_fusion.1), channel_id=1, source_target_pairs={{64,0},{66,2},{68,4},{70,6},{72,8},{74,10},{76,12},{78,14},{80,16}... | collective-permute-start | bytes 1572872 | tf_op jit(solution)/shard_map/ppermute | solution.py:25
  67.9 1.3 collective-permute-start.8
  69.2 2.1 %broadcast_select_fusion.1 = (bf16[2,256,512]{2,1,0:T(8,128)(2,1)}, bf16[2,256,512]{2,1,0:T(8,128)(2,1)}) fusion(bf16[2,256,512]{2,1,0:T(8,128)(2,1)} %collective-permute-done.6.refs_9_, pred[]{:T(512)S(6)} %eq.16, bf16[1,128,512]{2,1,0:T(8,128)(2,1)S(1)} %fusion.17, bf16[1,128,512]{2,1,0:T(8,128)(2,1)S(1)} %fusion.16, bf16[1,128,512]{2,1,0:T(8,128)(2,1)S(1)} %fusion.15, ...), kind=kLoop, calls=%fused_computation.42 | loop fusion | flops 2621440 | bytes 2621442 | tf_op jit(solution)/shard_map/jit(_where)/select_n | solution.py:265
  71.3 1.6 collective-permute-start.7
  73.0 1.8 %pad_maximum_fusion = (bf16[2,128,512]{2,1,0:T(8,128)(2,1)S(1)}, bf16[2,128,512]{2,1,0:T(8,128)(2,1)}) fusion(bf16[1,128,512]{2,1,0:T(8,128)(2,1)} %copy-done.17, bf16[1,128,512]{2,1,0:T(8,128)(2,1)} %copy-done.18, bf16[1,128,512]{2,1,0:T(8,128)(2,1)} %copy-done.19, bf16[1,128,512]{2,1,0:T(8,128)(2,1)} %copy-done.20), kind=kLoop, calls=%fused_computation.45 | loop fusion | flops 262144 | bytes 1048576 | tf_op jit(solution)/shard_map/stack | solution.py:303
  74.8 2.3 %collective-permute-done.10.refs_5_ = bf16[2,256,512]{2,1,0:T(8,128)(2,1)S(1)} collective-permute-done((bf16[2,256,512]{2,1,0:T(8,128)(2,1)}, bf16[2,256,512]{2,1,0:T(8,128)(2,1)S(1)}, u32[]{:S(2)}, u32[]{:S(2)}) %collective-permute-start.10) | collective-permute-done | bytes 524320 | tf_op jit(solution)/shard_map/ppermute | solution.py:25
  77.1 5.3 %collective-permute-start.12 = (bf16[2,256,512]{2,1,0:T(8,128)(2,1)S(1)}, bf16[2,256,512]{2,1,0:T(8,128)(2,1)}, u32[]{:S(2)}, u32[]{:S(2)}) collective-permute-start(bf16[2,256,512]{2,1,0:T(8,128)(2,1)S(1)} %collective-permute-done.10.refs_5_), channel_id=1, source_target_pairs={{4,0},{6,2},{8,4},{10,6},{12,8},{14,10},{16,12},{18,14},{20,16},{2... | collective-permute-start | bytes 1572872 | tf_op jit(solution)/shard_map/ppermute | solution.py:25
  82.5 0.6 fusion.33
  83.2 2.1 %collective-permute-start.5 = (bf16[2,256,512]{2,1,0:T(8,128)(2,1)}, bf16[2,256,512]{2,1,0:T(8,128)(2,1)S(1)}, u32[]{:S(2)}, u32[]{:S(2)}) collective-permute-start(bf16[2,256,512]{2,1,0:T(8,128)(2,1)} %collective-permute-done.4.refs_6_), channel_id=1, source_target_pairs={{0,8},{2,10},{4,12},{6,14},{8,16},{10,18},{12,20},{14,22},{16,24},... | collective-permute-start | bytes 1572872 | tf_op jit(solution)/shard_map/ppermute | solution.py:25
  85.2 1.3 broadcast_select_fusion
  86.6 0.1 collective-permute-start.14
  86.7 0.1 collective-permute-start.11
  86.8 2.7 %collective-permute-start.15 = (bf16[2,256,512]{2,1,0:T(8,128)(2,1)S(1)}, bf16[2,256,512]{2,1,0:T(8,128)(2,1)S(1)}, u32[]{:S(2)}, u32[]{:S(2)}) collective-permute-start(bf16[2,256,512]{2,1,0:T(8,128)(2,1)S(1)} %collective-permute-done.13.refs_9_), channel_id=1, source_target_pairs={{64,0},{66,2},{68,4},{70,6},{72,8},{74,10},{76,12},{78,14},{80,16}... | collective-permute-start | bytes 1572872 | tf_op jit(solution)/shard_map/ppermute | solution.py:25
  89.5 0.1 compare_select_fusion.bias_ref
  89.6 1.9 %collective-permute-done.12.refs_6_ = bf16[2,256,512]{2,1,0:T(8,128)(2,1)} collective-permute-done((bf16[2,256,512]{2,1,0:T(8,128)(2,1)S(1)}, bf16[2,256,512]{2,1,0:T(8,128)(2,1)}, u32[]{:S(2)}, u32[]{:S(2)}) %collective-permute-start.12) | collective-permute-done | bytes 524320 | tf_op jit(solution)/shard_map/ppermute | solution.py:25
  91.4 5.9 %collective-permute-start.16 = (bf16[2,256,512]{2,1,0:T(8,128)(2,1)}, bf16[2,256,512]{2,1,0:T(8,128)(2,1)S(1)}, u32[]{:S(2)}, u32[]{:S(2)}) collective-permute-start(bf16[2,256,512]{2,1,0:T(8,128)(2,1)} %collective-permute-done.12.refs_6_), channel_id=1, source_target_pairs={{8,0},{10,2},{12,4},{14,6},{16,8},{18,10},{20,12},{22,14},{24,16},... | collective-permute-start | bytes 1572872 | tf_op jit(solution)/shard_map/ppermute | solution.py:25
  97.5 13.7 %collective-permute-done.5.refs_7_ = bf16[2,256,512]{2,1,0:T(8,128)(2,1)S(1)} collective-permute-done((bf16[2,256,512]{2,1,0:T(8,128)(2,1)}, bf16[2,256,512]{2,1,0:T(8,128)(2,1)S(1)}, u32[]{:S(2)}, u32[]{:S(2)}) %collective-permute-start.5) | collective-permute-done | bytes 524320 | tf_op jit(solution)/shard_map/ppermute | solution.py:25
  111.2 0.8 copy-done.21
  112.0 5.9 %query_side.1 = (bf16[256,512]{1,0:T(8,128)(2,1)S(1)}, bf16[256,512]{1,0:T(8,128)(2,1)S(1)}, f32[4,2,256]{2,1,0:T(2,128)S(1)}) custom-call(s32[1]{0:T(128)} %bitcast.where_ref, f32[4,1,640]{2,1,0:T(1,128)S(1)} %compare_select_fusion.bias_ref, bf16[2,128,512]{2,1,0:T(8,128)(2,1)S(1)} %get-tuple-element.32.refs_0_.refs_1_, ...), custom_call_target="tpu_custom_call" | custom-call | flops 671088640 | bytes 6291456 | tf_op jit(solution)/shard_map/query_side/pallas_call | solution.py:186
  118.0 2.7 %collective-permute-start.23 = (f32[4,2,256]{2,1,0:T(2,128)S(1)}, f32[4,2,256]{2,1,0:T(2,128)S(1)}, u32[]{:S(2)}, u32[]{:S(2)}) collective-permute-start(f32[4,2,256]{2,1,0:T(2,128)S(1)} %get-tuple-element.19.refs_3_), channel_id=1, source_target_pairs={{128,0},{130,2},{132,4},{134,6},{136,8},{138,10},{140,12},{142,14}... | collective-permute-start | bytes 24584 | tf_op jit(solution)/shard_map/ppermute | solution.py:25
  120.7 1.5 collective-permute-start.22
  122.2 1.9 %collective-permute-start.21 = (f32[4,2,256]{2,1,0:T(2,128)S(1)}, f32[4,2,256]{2,1,0:T(2,128)S(1)}, u32[]{:S(2)}, u32[]{:S(2)}) collective-permute-start(f32[4,2,256]{2,1,0:T(2,128)S(1)} %get-tuple-element.19.refs_3_), channel_id=1, source_target_pairs={{32,0},{34,2},{36,4},{38,6},{40,8},{42,10},{44,12},{46,14},{48,16}... | collective-permute-start | bytes 24584 | tf_op jit(solution)/shard_map/ppermute | solution.py:25
  124.1 4.0 %collective-permute-start.20 = (f32[4,2,256]{2,1,0:T(2,128)S(1)}, f32[4,2,256]{2,1,0:T(2,128)S(1)}, u32[]{:S(2)}, u32[]{:S(2)}) collective-permute-start(f32[4,2,256]{2,1,0:T(2,128)S(1)} %get-tuple-element.19.refs_3_), channel_id=1, source_target_pairs={{16,0},{18,2},{20,4},{22,6},{24,8},{26,10},{28,12},{30,14},{32,16}... | collective-permute-start | bytes 24584 | tf_op jit(solution)/shard_map/ppermute | solution.py:25
  128.2 4.1 %collective-permute-start.19 = (f32[4,2,256]{2,1,0:T(2,128)S(1)}, f32[4,2,256]{2,1,0:T(2,128)S(1)}, u32[]{:S(2)}, u32[]{:S(2)}) collective-permute-start(f32[4,2,256]{2,1,0:T(2,128)S(1)} %get-tuple-element.19.refs_3_), channel_id=1, source_target_pairs={{8,0},{10,2},{12,4},{14,6},{16,8},{18,10},{20,12},{22,14},{24,16},... | collective-permute-start | bytes 24584 | tf_op jit(solution)/shard_map/ppermute | solution.py:25
  132.3 5.4 %collective-permute-start.18 = (f32[4,2,256]{2,1,0:T(2,128)S(1)}, f32[4,2,256]{2,1,0:T(2,128)S(1)}, u32[]{:S(2)}, u32[]{:S(2)}) collective-permute-start(f32[4,2,256]{2,1,0:T(2,128)S(1)} %get-tuple-element.19.refs_3_), channel_id=1, source_target_pairs={{4,0},{6,2},{8,4},{10,6},{12,8},{14,10},{16,12},{18,14},{20,16},{2... | collective-permute-start | bytes 24584 | tf_op jit(solution)/shard_map/ppermute | solution.py:25
  137.7 1.9 %collective-permute-start.17 = (f32[4,2,256]{2,1,0:T(2,128)S(1)}, f32[4,2,256]{2,1,0:T(2,128)S(1)}, u32[]{:S(2)}, u32[]{:S(2)}) collective-permute-start(f32[4,2,256]{2,1,0:T(2,128)S(1)} %get-tuple-element.19.refs_3_), channel_id=1, source_target_pairs={{2,0},{4,2},{6,4},{8,6},{10,8},{12,10},{14,12},{16,14},{18,16},{20... | collective-permute-start | bytes 24584 | tf_op jit(solution)/shard_map/ppermute | solution.py:25
  139.7 0.4 convolution_convert_fusion
  140.1 1.8 %collective-permute-start.9 = (bf16[128,2048]{1,0:T(8,128)(2,1)S(1)}, bf16[128,2048]{1,0:T(8,128)(2,1)S(1)}, u32[]{:S(2)}, u32[]{:S(2)}) collective-permute-start(bf16[128,2048]{1,0:T(8,128)(2,1)S(1)} %convolution_convert_fusion), channel_id=1, source_target_pairs={{0,1},{1,0},{2,3},{3,2},{4,5},{5,4},{6,7},{7,6},{8,9},{9,8},{10,11... | collective-permute-start | bytes 1572872 | tf_op jit(solution)/shard_map/ppermute | solution.py:29
  141.9 4.2 %key_side.3 = bf16[2,128,512]{2,1,0:T(8,128)(2,1)S(1)} custom-call(s32[1]{0:T(128)} %bitcast.where_ref, bf16[2,128,512]{2,1,0:T(8,128)(2,1)S(1)} %pad_maximum_fusion.3.refs_3_.refs_0_, bf16[2,128,512]{2,1,0:T(8,128)(2,1)S(1)} %get-tuple-element.32.refs_0_.refs_1_, bf16[2,128,512]{2,1,0:T(8,128)(2,1)S(1)} %pad_maximum_fusion.1.refs_1_.refs_2_, ...), custom_call_target="tpu_custom_call" | custom-call | flops 335544320 | bytes 6291456 | tf_op jit(solution)/shard_map/key_side/pallas_call | solution.py:186
  146.1 0.8 fusion.25
  147.0 0.8 copy-done.5
  147.7 0.8 fusion.26
  148.5 0.8 fusion.6
  149.4 2.1 %collective-permute-start.24 = (bf16[128,2048]{1,0:T(8,128)(2,1)S(1)}, bf16[128,2048]{1,0:T(8,128)(2,1)S(1)}, u32[]{:S(2)}, u32[]{:S(2)}) collective-permute-start(bf16[128,2048]{1,0:T(8,128)(2,1)S(1)} %fusion.6), channel_id=1, source_target_pairs={{0,1},{1,0},{2,3},{3,2},{4,5},{5,4},{6,7},{7,6},{8,9},{9,8},{10,11... | collective-permute-start | bytes 1572872 | tf_op jit(solution)/shard_map/ppermute | solution.py:29
  151.5 4.2 %key_side.2 = bf16[2,128,512]{2,1,0:T(8,128)(2,1)S(1)} custom-call(s32[1]{0:T(128)} %bitcast.where_ref, bf16[2,128,512]{2,1,0:T(8,128)(2,1)S(1)} %copy-done.1, bf16[2,128,512]{2,1,0:T(8,128)(2,1)S(1)} %get-tuple-element.32.refs_0_.refs_1_, bf16[2,128,512]{2,1,0:T(8,128)(2,1)S(1)} %pad_maximum_fusion.1.refs_1_.refs_2_, ...), custom_call_target="tpu_custom_call" | custom-call | flops 335544320 | bytes 6291456 | tf_op jit(solution)/shard_map/key_side/pallas_call | solution.py:186
  155.6 0.8 fusion.27
  156.5 0.8 fusion.28
  157.3 0.2 copy-done.8
  157.5 1.3 fusion.5
  158.8 8.7 %collective-permute-done.24 = bf16[128,2048]{1,0:T(8,128)(2,1)S(1)} collective-permute-done((bf16[128,2048]{1,0:T(8,128)(2,1)S(1)}, bf16[128,2048]{1,0:T(8,128)(2,1)S(1)}, u32[]{:S(2)}, u32[]{:S(2)}) %collective-permute-start.24) | collective-permute-done | bytes 524320 | tf_op jit(solution)/shard_map/ppermute | solution.py:29
  167.5 1.0 fusion.19
  168.5 1.2 fusion.23
  (71 shorter events, 0.4 us)
Async XLA Ops:
  0.6 27.5 %copy-start = (bf16[2048,512]{1,0:T(8,128)(2,1)S(1)}, bf16[2048,512]{1,0:T(8,128)(2,1)}, u32[]{:S(2)}) copy-start(bf16[2048,512]{1,0:T(8,128)(2,1)} %param.10) | copy-start | bytes 6291460
  0.6 7.8 %copy-start.4 = (bf16[2048,512]{1,0:T(8,128)(2,1)S(1)}, bf16[2048,512]{1,0:T(8,128)(2,1)}, u32[]{:S(2)}) copy-start(bf16[2048,512]{1,0:T(8,128)(2,1)} %param.11) | copy-start | bytes 6291460
  3.3 15.3 %copy-start.2 = (bf16[2048,512]{1,0:T(8,128)(2,1)S(1)}, bf16[2048,512]{1,0:T(8,128)(2,1)}, u32[]{:S(2)}) copy-start(bf16[2048,512]{1,0:T(8,128)(2,1)} %param.12) | copy-start | bytes 6291460
  3.3 15.3 %collective-permute-start = (bf16[128,2048]{1,0:T(8,128)(2,1)S(1)}, bf16[128,2048]{1,0:T(8,128)(2,1)S(1)}, u32[]{:S(2)}, u32[]{:S(2)}) collective-permute-start(bf16[128,2048]{1,0:T(8,128)(2,1)S(1)} %fusion.18), channel_id=1, source_target_pairs={{0,1},{1,0},{2,3},{3,2},{4,5},{5,4},{6,7},{7,6},{8,9},{9,8},{10,11... | collective-permute-start | bytes 1572872 | tf_op jit(solution)/shard_map/ppermute | solution.py:29
  8.5 60.7 %copy-start.19 = (bf16[1,128,512]{2,1,0:T(8,128)(2,1)}, bf16[1,128,512]{2,1,0:T(8,128)(2,1)S(1)}, u32[]{:S(2)}) copy-start(bf16[1,128,512]{2,1,0:T(8,128)(2,1)S(1)} %fusion.15) | copy-start | bytes 393220
  9.0 10.5 %copy-start.20 = (bf16[1,128,512]{2,1,0:T(8,128)(2,1)}, bf16[1,128,512]{2,1,0:T(8,128)(2,1)S(1)}, u32[]{:S(2)}) copy-start(bf16[1,128,512]{2,1,0:T(8,128)(2,1)S(1)} %fusion.14) | copy-start | bytes 393220
  19.0 5.2 %copy-start.9 = (bf16[128,2048]{1,0:T(8,128)(2,1)S(1)}, bf16[128,2048]{1,0:T(8,128)(2,1)}, u32[]{:S(2)}) copy-start(bf16[128,2048]{1,0:T(8,128)(2,1)} %param.14) | copy-start | bytes 1572868
  19.0 8.3 %copy-start.6 = (bf16[512,2048]{1,0:T(8,128)(2,1)S(1)}, bf16[512,2048]{1,0:T(8,128)(2,1)}, u32[]{:S(2)}) copy-start(bf16[512,2048]{1,0:T(8,128)(2,1)} %param.13) | copy-start | bytes 6291460
  19.5 49.7 %copy-start.11 = (bf16[1,128,512]{2,1,0:T(8,128)(2,1)}, bf16[1,128,512]{2,1,0:T(8,128)(2,1)S(1)}, u32[]{:S(2)}) copy-start(bf16[1,128,512]{2,1,0:T(8,128)(2,1)S(1)} %fusion.16) | copy-start | bytes 393220
  20.3 20.4 %collective-permute-start.2 = (bf16[2,256,512]{2,1,0:T(8,128)(2,1)}, bf16[2,256,512]{2,1,0:T(8,128)(2,1)}, u32[]{:S(2)}, u32[]{:S(2)}) collective-permute-start(bf16[2,256,512]{2,1,0:T(8,128)(2,1)} %maximum_maximum_fusion), channel_id=1, source_target_pairs={{0,4},{2,6},{4,8},{6,10},{8,12},{10,14},{12,16},{14,18},{16,20},{1... | collective-permute-start | bytes 1572872 | tf_op jit(solution)/shard_map/ppermute | solution.py:25
  24.2 36.6 %collective-permute-start.1 = (bf16[128,2048]{1,0:T(8,128)(2,1)S(1)}, bf16[128,2048]{1,0:T(8,128)(2,1)S(1)}, u32[]{:S(2)}, u32[]{:S(2)}) collective-permute-start(bf16[128,2048]{1,0:T(8,128)(2,1)S(1)} %copy-done.9), channel_id=1, source_target_pairs={{0,1},{1,0},{2,3},{3,2},{4,5},{5,4},{6,7},{7,6},{8,9},{9,8},{10,11... | collective-permute-start | bytes 1572872 | tf_op jit(solution)/shard_map/ppermute | solution.py:29
  28.1 33.5 %copy-start.17 = (bf16[1,128,512]{2,1,0:T(8,128)(2,1)}, bf16[1,128,512]{2,1,0:T(8,128)(2,1)S(1)}, u32[]{:S(2)}) copy-start(bf16[1,128,512]{2,1,0:T(8,128)(2,1)S(1)} %fusion.11) | copy-start | bytes 393220
  28.6 33.0 %copy-start.18 = (bf16[1,128,512]{2,1,0:T(8,128)(2,1)}, bf16[1,128,512]{2,1,0:T(8,128)(2,1)S(1)}, u32[]{:S(2)}) copy-start(bf16[1,128,512]{2,1,0:T(8,128)(2,1)S(1)} %fusion.10) | copy-start | bytes 393220
  28.6 39.3 %collective-permute-start.6 = (bf16[2,256,512]{2,1,0:T(8,128)(2,1)}, bf16[2,256,512]{2,1,0:T(8,128)(2,1)}, u32[]{:S(2)}, u32[]{:S(2)}) collective-permute-start(bf16[2,256,512]{2,1,0:T(8,128)(2,1)} %maximum_maximum_fusion), channel_id=1, source_target_pairs={{0,64},{2,66},{4,68},{6,70},{8,72},{10,74},{12,76},{14,78},{16,80}... | collective-permute-start | bytes 1572872 | tf_op jit(solution)/shard_map/ppermute | solution.py:25
  30.4 31.2 %copy-start.13 = (bf16[1,128,512]{2,1,0:T(8,128)(2,1)}, bf16[1,128,512]{2,1,0:T(8,128)(2,1)S(1)}, u32[]{:S(2)}) copy-start(bf16[1,128,512]{2,1,0:T(8,128)(2,1)S(1)} %fusion.12) | copy-start | bytes 393220
  40.8 32.2 %collective-permute-start.4 = (bf16[2,256,512]{2,1,0:T(8,128)(2,1)}, bf16[2,256,512]{2,1,0:T(8,128)(2,1)}, u32[]{:S(2)}, u32[]{:S(2)}) collective-permute-start(bf16[2,256,512]{2,1,0:T(8,128)(2,1)} %collective-permute-done.2.refs_5_), channel_id=1, source_target_pairs={{0,4},{2,6},{4,8},{6,10},{8,12},{10,14},{12,16},{14,18},{16,20},{1... | collective-permute-start | bytes 1572872 | tf_op jit(solution)/shard_map/ppermute | solution.py:25
  61.6 0.7 copy-start.15
  63.1 19.9 %copy-start.23 = (s32[10]{0:T(128)S(1)}, s32[10]{0:T(128)}, u32[]{:S(2)}) copy-start(s32[10]{0:T(128)} %constant.81.clone) | copy-start | bytes 124
  63.1 14.0 %collective-permute-start.10 = (bf16[2,256,512]{2,1,0:T(8,128)(2,1)}, bf16[2,256,512]{2,1,0:T(8,128)(2,1)S(1)}, u32[]{:S(2)}, u32[]{:S(2)}) collective-permute-start(bf16[2,256,512]{2,1,0:T(8,128)(2,1)} %maximum_maximum_fusion.1), channel_id=1, source_target_pairs={{4,0},{6,2},{8,4},{10,6},{12,8},{14,10},{16,12},{18,14},{20,16},{2... | collective-permute-start | bytes 1572872 | tf_op jit(solution)/shard_map/ppermute | solution.py:25
  65.2 18.0 %collective-permute-start.13 = (bf16[2,256,512]{2,1,0:T(8,128)(2,1)}, bf16[2,256,512]{2,1,0:T(8,128)(2,1)S(1)}, u32[]{:S(2)}, u32[]{:S(2)}) collective-permute-start(bf16[2,256,512]{2,1,0:T(8,128)(2,1)} %maximum_maximum_fusion.1), channel_id=1, source_target_pairs={{64,0},{66,2},{68,4},{70,6},{72,8},{74,10},{76,12},{78,14},{80,16}... | collective-permute-start | bytes 1572872 | tf_op jit(solution)/shard_map/ppermute | solution.py:25
  67.9 18.7 %collective-permute-start.8 = (bf16[2,256,512]{2,1,0:T(8,128)(2,1)}, bf16[2,256,512]{2,1,0:T(8,128)(2,1)}, u32[]{:S(2)}, u32[]{:S(2)}) collective-permute-start(bf16[2,256,512]{2,1,0:T(8,128)(2,1)} %collective-permute-done.6.refs_9_), channel_id=1, source_target_pairs={{0,64},{2,66},{4,68},{6,70},{8,72},{10,74},{12,76},{14,78},{16,80}... | collective-permute-start | bytes 1572872 | tf_op jit(solution)/shard_map/ppermute | solution.py:25
  71.3 15.3 %collective-permute-start.7 = (bf16[2,256,512]{2,1,0:T(8,128)(2,1)}, bf16[2,256,512]{2,1,0:T(8,128)(2,1)}, u32[]{:S(2)}, u32[]{:S(2)}) collective-permute-start(bf16[2,256,512]{2,1,0:T(8,128)(2,1)} %get-tuple-element.28), channel_id=1, source_target_pairs={{0,32},{2,34},{4,36},{6,38},{8,40},{10,42},{12,44},{14,46},{16,48}... | collective-permute-start | bytes 1572872 | tf_op jit(solution)/shard_map/ppermute | solution.py:266
  73.0 13.8 %collective-permute-start.3 = (bf16[2,256,512]{2,1,0:T(8,128)(2,1)}, bf16[2,256,512]{2,1,0:T(8,128)(2,1)}, u32[]{:S(2)}, u32[]{:S(2)}) collective-permute-start(bf16[2,256,512]{2,1,0:T(8,128)(2,1)} %get-tuple-element.29), channel_id=1, source_target_pairs={{0,2},{2,0},{4,6},{6,4},{8,10},{10,8},{12,14},{14,12},{16,18},{18,... | collective-permute-start | bytes 1572872 | tf_op jit(solution)/shard_map/ppermute | solution.py:266
  77.1 14.3 %collective-permute-start.12 = (bf16[2,256,512]{2,1,0:T(8,128)(2,1)S(1)}, bf16[2,256,512]{2,1,0:T(8,128)(2,1)}, u32[]{:S(2)}, u32[]{:S(2)}) collective-permute-start(bf16[2,256,512]{2,1,0:T(8,128)(2,1)S(1)} %collective-permute-done.10.refs_5_), channel_id=1, source_target_pairs={{4,0},{6,2},{8,4},{10,6},{12,8},{14,10},{16,12},{18,14},{20,16},{2... | collective-permute-start | bytes 1572872 | tf_op jit(solution)/shard_map/ppermute | solution.py:25
  83.2 6.3 %copy-start.24 = (s32[4]{0:T(128)S(1)}, s32[4]{0:T(128)}, u32[]{:S(2)}) copy-start(s32[4]{0:T(128)} %fusion.33) | copy-start | bytes 52
  83.2 14.2 %copy-start.12 = (bf16[1,128,512]{2,1,0:T(8,128)(2,1)S(1)}, bf16[1,128,512]{2,1,0:T(8,128)(2,1)}, u32[]{:S(2)}) copy-start(bf16[1,128,512]{2,1,0:T(8,128)(2,1)} %copy-done.11) | copy-start | bytes 393220
  83.2 14.3 %copy-start.14 = (bf16[1,128,512]{2,1,0:T(8,128)(2,1)S(1)}, bf16[1,128,512]{2,1,0:T(8,128)(2,1)}, u32[]{:S(2)}) copy-start(bf16[1,128,512]{2,1,0:T(8,128)(2,1)} %copy-done.13) | copy-start | bytes 393220
  83.2 14.3 %copy-start.16 = (bf16[1,128,512]{2,1,0:T(8,128)(2,1)S(1)}, bf16[1,128,512]{2,1,0:T(8,128)(2,1)}, u32[]{:S(2)}) copy-start(bf16[1,128,512]{2,1,0:T(8,128)(2,1)} %copy-done.15) | copy-start | bytes 393220
  83.2 28.8 %copy-start.1 = (bf16[2,128,512]{2,1,0:T(8,128)(2,1)S(1)}, bf16[2,128,512]{2,1,0:T(8,128)(2,1)}, u32[]{:S(2)}) copy-start(bf16[2,128,512]{2,1,0:T(8,128)(2,1)} %get-tuple-element.33.refs_2_.refs_0_) | copy-start | bytes 786436
  83.2 28.0 %collective-permute-start.5 = (bf16[2,256,512]{2,1,0:T(8,128)(2,1)}, bf16[2,256,512]{2,1,0:T(8,128)(2,1)S(1)}, u32[]{:S(2)}, u32[]{:S(2)}) collective-permute-start(bf16[2,256,512]{2,1,0:T(8,128)(2,1)} %collective-permute-done.4.refs_6_), channel_id=1, source_target_pairs={{0,8},{2,10},{4,12},{6,14},{8,16},{10,18},{12,20},{14,22},{16,24},... | collective-permute-start | bytes 1572872 | tf_op jit(solution)/shard_map/ppermute | solution.py:25
  86.6 31.4 %collective-permute-start.14 = (bf16[2,256,512]{2,1,0:T(8,128)(2,1)S(1)}, bf16[2,256,512]{2,1,0:T(8,128)(2,1)S(1)}, u32[]{:S(2)}, u32[]{:S(2)}) collective-permute-start(bf16[2,256,512]{2,1,0:T(8,128)(2,1)S(1)} %get-tuple-element.26), channel_id=1, source_target_pairs={{0,32},{2,34},{4,36},{6,38},{8,40},{10,42},{12,44},{14,46},{16,48}... | collective-permute-start | bytes 1572872 | tf_op jit(solution)/shard_map/ppermute | solution.py:266
  86.7 31.3 %collective-permute-start.11 = (bf16[2,256,512]{2,1,0:T(8,128)(2,1)S(1)}, bf16[2,256,512]{2,1,0:T(8,128)(2,1)S(1)}, u32[]{:S(2)}, u32[]{:S(2)}) collective-permute-start(bf16[2,256,512]{2,1,0:T(8,128)(2,1)S(1)} %get-tuple-element.27), channel_id=1, source_target_pairs={{0,2},{2,0},{4,6},{6,4},{8,10},{10,8},{12,14},{14,12},{16,18},{18,... | collective-permute-start | bytes 1572872 | tf_op jit(solution)/shard_map/ppermute | solution.py:266
  86.8 31.2 %collective-permute-start.15 = (bf16[2,256,512]{2,1,0:T(8,128)(2,1)S(1)}, bf16[2,256,512]{2,1,0:T(8,128)(2,1)S(1)}, u32[]{:S(2)}, u32[]{:S(2)}) collective-permute-start(bf16[2,256,512]{2,1,0:T(8,128)(2,1)S(1)} %collective-permute-done.13.refs_9_), channel_id=1, source_target_pairs={{64,0},{66,2},{68,4},{70,6},{72,8},{74,10},{76,12},{78,14},{80,16}... | collective-permute-start | bytes 1572872 | tf_op jit(solution)/shard_map/ppermute | solution.py:25
  91.4 50.5 %collective-permute-start.16 = (bf16[2,256,512]{2,1,0:T(8,128)(2,1)}, bf16[2,256,512]{2,1,0:T(8,128)(2,1)S(1)}, u32[]{:S(2)}, u32[]{:S(2)}) collective-permute-start(bf16[2,256,512]{2,1,0:T(8,128)(2,1)} %collective-permute-done.12.refs_6_), channel_id=1, source_target_pairs={{8,0},{10,2},{12,4},{14,6},{16,8},{18,10},{20,12},{22,14},{24,16},... | collective-permute-start | bytes 1572872 | tf_op jit(solution)/shard_map/ppermute | solution.py:25
  111.2 0.8 copy-start.21
  112.0 27.7 %copy-start.7 = (bf16[512,2048]{1,0:T(8,128)(2,1)S(1)}, bf16[512,2048]{1,0:T(8,128)(2,1)}, u32[]{:S(2)}) copy-start(bf16[512,2048]{1,0:T(8,128)(2,1)} %param.13) | copy-start | bytes 6291460
  118.0 10.2 %collective-permute-start.23 = (f32[4,2,256]{2,1,0:T(2,128)S(1)}, f32[4,2,256]{2,1,0:T(2,128)S(1)}, u32[]{:S(2)}, u32[]{:S(2)}) collective-permute-start(f32[4,2,256]{2,1,0:T(2,128)S(1)} %get-tuple-element.19.refs_3_), channel_id=1, source_target_pairs={{128,0},{130,2},{132,4},{134,6},{136,8},{138,10},{140,12},{142,14}... | collective-permute-start | bytes 24584 | tf_op jit(solution)/shard_map/ppermute | solution.py:25
  120.7 11.6 %collective-permute-start.22 = (f32[4,2,256]{2,1,0:T(2,128)S(1)}, f32[4,2,256]{2,1,0:T(2,128)S(1)}, u32[]{:S(2)}, u32[]{:S(2)}) collective-permute-start(f32[4,2,256]{2,1,0:T(2,128)S(1)} %get-tuple-element.19.refs_3_), channel_id=1, source_target_pairs={{64,0},{66,2},{68,4},{70,6},{72,8},{74,10},{76,12},{78,14},{80,16}... | collective-permute-start | bytes 24584 | tf_op jit(solution)/shard_map/ppermute | solution.py:25
  122.2 15.5 %collective-permute-start.21 = (f32[4,2,256]{2,1,0:T(2,128)S(1)}, f32[4,2,256]{2,1,0:T(2,128)S(1)}, u32[]{:S(2)}, u32[]{:S(2)}) collective-permute-start(f32[4,2,256]{2,1,0:T(2,128)S(1)} %get-tuple-element.19.refs_3_), channel_id=1, source_target_pairs={{32,0},{34,2},{36,4},{38,6},{40,8},{42,10},{44,12},{46,14},{48,16}... | collective-permute-start | bytes 24584 | tf_op jit(solution)/shard_map/ppermute | solution.py:25
  124.1 16.0 %collective-permute-start.20 = (f32[4,2,256]{2,1,0:T(2,128)S(1)}, f32[4,2,256]{2,1,0:T(2,128)S(1)}, u32[]{:S(2)}, u32[]{:S(2)}) collective-permute-start(f32[4,2,256]{2,1,0:T(2,128)S(1)} %get-tuple-element.19.refs_3_), channel_id=1, source_target_pairs={{16,0},{18,2},{20,4},{22,6},{24,8},{26,10},{28,12},{30,14},{32,16}... | collective-permute-start | bytes 24584 | tf_op jit(solution)/shard_map/ppermute | solution.py:25
  128.2 13.7 %collective-permute-start.19 = (f32[4,2,256]{2,1,0:T(2,128)S(1)}, f32[4,2,256]{2,1,0:T(2,128)S(1)}, u32[]{:S(2)}, u32[]{:S(2)}) collective-permute-start(f32[4,2,256]{2,1,0:T(2,128)S(1)} %get-tuple-element.19.refs_3_), channel_id=1, source_target_pairs={{8,0},{10,2},{12,4},{14,6},{16,8},{18,10},{20,12},{22,14},{24,16},... | collective-permute-start | bytes 24584 | tf_op jit(solution)/shard_map/ppermute | solution.py:25
  132.3 9.6 %collective-permute-start.18 = (f32[4,2,256]{2,1,0:T(2,128)S(1)}, f32[4,2,256]{2,1,0:T(2,128)S(1)}, u32[]{:S(2)}, u32[]{:S(2)}) collective-permute-start(f32[4,2,256]{2,1,0:T(2,128)S(1)} %get-tuple-element.19.refs_3_), channel_id=1, source_target_pairs={{4,0},{6,2},{8,4},{10,6},{12,8},{14,10},{16,12},{18,14},{20,16},{2... | collective-permute-start | bytes 24584 | tf_op jit(solution)/shard_map/ppermute | solution.py:25
  137.7 4.2 %collective-permute-start.17 = (f32[4,2,256]{2,1,0:T(2,128)S(1)}, f32[4,2,256]{2,1,0:T(2,128)S(1)}, u32[]{:S(2)}, u32[]{:S(2)}) collective-permute-start(f32[4,2,256]{2,1,0:T(2,128)S(1)} %get-tuple-element.19.refs_3_), channel_id=1, source_target_pairs={{2,0},{4,2},{6,4},{8,6},{10,8},{12,10},{14,12},{16,14},{18,16},{20... | collective-permute-start | bytes 24584 | tf_op jit(solution)/shard_map/ppermute | solution.py:25
  140.1 6.0 %copy-start.3 = (bf16[2048,512]{1,0:T(8,128)(2,1)S(1)}, bf16[2048,512]{1,0:T(8,128)(2,1)}, u32[]{:S(2)}) copy-start(bf16[2048,512]{1,0:T(8,128)(2,1)} %param.12) | copy-start | bytes 6291460
  140.1 17.1 %collective-permute-start.9 = (bf16[128,2048]{1,0:T(8,128)(2,1)S(1)}, bf16[128,2048]{1,0:T(8,128)(2,1)S(1)}, u32[]{:S(2)}, u32[]{:S(2)}) collective-permute-start(bf16[128,2048]{1,0:T(8,128)(2,1)S(1)} %convolution_convert_fusion), channel_id=1, source_target_pairs={{0,1},{1,0},{2,3},{3,2},{4,5},{5,4},{6,7},{7,6},{8,9},{9,8},{10,11... | collective-permute-start | bytes 1572872 | tf_op jit(solution)/shard_map/ppermute | solution.py:29
  146.1 1.6 copy-start.5
  149.4 18.1 %collective-permute-start.24 = (bf16[128,2048]{1,0:T(8,128)(2,1)S(1)}, bf16[128,2048]{1,0:T(8,128)(2,1)S(1)}, u32[]{:S(2)}, u32[]{:S(2)}) collective-permute-start(bf16[128,2048]{1,0:T(8,128)(2,1)S(1)} %fusion.6), channel_id=1, source_target_pairs={{0,1},{1,0},{2,3},{3,2},{4,5},{5,4},{6,7},{7,6},{8,9},{9,8},{10,11... | collective-permute-start | bytes 1572872 | tf_op jit(solution)/shard_map/ppermute | solution.py:29
  156.4 1.0 copy-start.8
  157.3 10.2 %copy-start.22 = (f32[2048]{0:T(1024)S(1)}, f32[2048]{0:T(1024)}, u32[]{:S(2)}) copy-start(f32[2048]{0:T(1024)} %param.9) | copy-start | bytes 24580
  158.8 9.7 %copy-start.10 = (bf16[128,2048]{1,0:T(8,128)(2,1)S(1)}, bf16[128,2048]{1,0:T(8,128)(2,1)}, u32[]{:S(2)}) copy-start(bf16[128,2048]{1,0:T(8,128)(2,1)} %param.14) | copy-start | bytes 1572868

commit v6 on v5

--- a/solution.py
+++ b/solution.py
@@ -266,15 +266,6 @@
     return lax.ppermute(sent, "seq", [(i, i ^ bit) for i in range(size)])
 
 
-def exchange(rows, sign):
-    two = shifted(rows, sign * 2)
-    far = shifted(rows, sign * 32)
-    four = shifted(two, sign * 2)
-    one = swapped(rows, two, 1, sign)
-    sixteen = swapped(rows, far, 16, sign)
-    return [one, two, four, shifted(four, sign * 4), sixteen, far, shifted(far, sign * 32)]
-
-
 def per_device(series, norm_gain, w_query, w_key, w_value, w_out, out_grad):
     levels = lax.axis_size("seq").bit_length() - 1
     half = series.shape[0]
@@ -293,8 +284,6 @@
     unit_rows = series_f * inv_rms
     normed = (unit_rows * norm_gain).astype(BF16)
     normed_other = swap_tp(normed)
-    out_grad_later, normed_other = lax.optimization_barrier((out_grad, normed_other))
-    out_grad_other = swap_tp(out_grad_later)
 
     def key_value(rows):
         return jnp.stack([matmul(rows, w_key).astype(BF16), matmul(rows, w_value).astype(BF16)])
@@ -304,27 +293,51 @@
             [matmul(rows, w_query).astype(BF16), matmul_t(grad_rows, w_out).astype(BF16)]
         )
 
-    kv = (key_value(normed), key_value(normed_other))
+    kv_own = key_value(normed)
+    early = {by: shifted(kv_own, by) for by in (32, 2, 8)}
+    normed_other, early[32], early[2] = lax.optimization_barrier((normed_other, early[32], early[2]))
+    out_grad_late, normed_other = lax.optimization_barrier((out_grad, normed_other))
+    out_grad_other = swap_tp(out_grad_late)
+    kv = (kv_own, key_value(normed_other))
+    pairs = {by: (early[by], shifted(kv[1], by)) for by in (2, 32, 8)}
+    two, far = [jnp.concatenate(pairs[by], axis=1) for by in (2, 32)]
+    four = shifted(two, 2)
+    kv_all = jnp.concatenate(kv, axis=1)
+    far_kv, early[8] = lax.optimization_barrier((far, pairs[8][0]))
+    two_kv, late_eight, four = lax.optimization_barrier((two, pairs[8][1], four))
+    fetched = [
+        (swapped(kv_all, two_kv, 1, 1),),
+        pairs[2],
+        (four,),
+        (early[8], late_eight),
+        (swapped(kv_all, far_kv, 16, 1),),
+        pairs[32],
+        (shifted(far, 32),),
+    ]
+
     qg = (query_grad(normed, out_grad), query_grad(normed_other, out_grad_other))
-    kv_all = jnp.concatenate(kv, axis=1)
     qg_all = jnp.concatenate(qg, axis=1)
-    fetched = exchange(kv_all, 1)
-    later = exchange(qg_all, -1)
-    mixed, grad_query, stat = query_side(where, bias, qg, kv, [(f,) for f in fetched], 0)
-    last = later.pop(3)
+    two = shifted(qg_all, -2)
+    qg_late, _ = lax.optimization_barrier((qg_all, four))
+    far = shifted(qg_late, -32)
+    four = shifted(two, -2)
+    later = [swapped(qg_all, two, 1, -1), two, four, swapped(qg_all, far, 16, -1), far]
+    mixed, grad_query, stat = query_side(where, bias, qg, kv, fetched, 0)
     stat, later = lax.optimization_barrier((stat, later))
-    later.insert(3, last)
+    later = later[:3] + [shifted(four, -4)] + later[3:] + [shifted(far, -32)]
     later = [(f,) for f in later]
     later_stats = [shifted(stat, -(2**s)) for s in range(levels)]
     attn_other = swap_tp(matmul(mixed[half:], w_out).astype(BF16))
     attn_rows = matmul(mixed[:half], w_out) + attn_other.astype(F32)
     layer_out = (series_f + attn_rows).astype(BF16)
 
+    grad_queries = lax.optimization_barrier(matmul_t(grad_query, w_query))
+
     def back(at):
         grad_kv = key_side(at, where, kv, qg, stat, later, later_stats, [])
         rows = slice(at * half, (at + 1) * half)
         return (
-            matmul_t(grad_query[rows], w_query)
+            grad_queries[rows]
             + matmul_t(grad_kv[0], w_key)
             + matmul_t(grad_kv[1], w_value)
         )

time: 171 us -> 187 us (1.094)
  starting transfers between devices: 62.5 us -> 86.6 us
  waiting for transfers between devices: 64.6 us -> 55.3 us
  other arithmetic: 11.5 us -> 8.55 us
  matrix products: 12.8 us -> 15.3 us
    ppermute x17 -> x20, starting transfers between devices: 50.6 us -> 79.3 us  [shifted(): return lax.ppermute(value, 'seq', pairs)]
    ppermute x4, waiting for transfers between devices: 36.3 us -> 17.5 us  [swap_tp(): return lax.ppermute(value, 'tp', [(0, 1), (1, 0)])]
    ppermute x17 -> x20, waiting for transfers between devices: 28.3 us -> 35.2 us  [shifted(): return lax.ppermute(value, 'seq', pairs)]
    ppermute x4, starting transfers between devices: 10.1 us -> 7.1 us  [swap_tp(): return lax.ppermute(value, 'tp', [(0, 1), (1, 0)])]
    ppermute x4, waiting for transfers between devices: 0.01 us -> 2.6 us  [swapped(): return lax.ppermute(sent, 'seq', [(i, i ^ bit) for i in range(size)])]
    dot_general x8, matrix products: 6.12 us -> 8.41 us  [matmul(): return jnp.dot(a, b, preferred_element_type=F32)]
    dot_general x8 -> x7, matrix products: 6.68 us -> 6.92 us  [matmul_t(): return lax.dot_general(a, b, NT, preferred_element_type=F32)]
  transfers between devices with their start and end apart: 25 -> 28, of which waited for: 7 -> 9; matrix products, arithmetic and copies ran while one was open for 11% -> 12% of each run, Pallas kernels for 8% -> 7%
where the time goes in v6:
time: 187 us; the launch traced here: 185 us
  starting transfers between devices  86.6 us (46%)
  waiting for transfers between devices  55.3 us (30%)
  matrix products  15.3 us (8%)
  Pallas kernels  13.4 us (7%)
  other arithmetic  8.55 us (5%)
  local copies, waits for them, and re-layouts  4.52 us (2%)
    ppermute x20, starting transfers between devices, shifted(): return lax.ppermute(value, 'seq', pairs)  79.3 us
    ppermute x20, waiting for transfers between devices, shifted(): return lax.ppermute(value, 'seq', pairs)  35.2 us
    ppermute x4, waiting for transfers between devices, swap_tp(): return lax.ppermute(value, 'tp', [(0, 1), (1, 0)])  17.5 us
    pallas_call x3, Pallas kernels, call(): pl.pallas_call(kernel, out_shape=outs, grid_spec=pltpu.PrefetchScalarGrid...  13.4 us
    dot_general x8, matrix products, matmul(): return jnp.dot(a, b, preferred_element_type=F32)  8.41 us
    ppermute x4, starting transfers between devices, swap_tp(): return lax.ppermute(value, 'tp', [(0, 1), (1, 0)])  7.1 us
    dot_general x7, matrix products, matmul_t(): return lax.dot_general(a, b, NT, preferred_element_type=F32)  6.92 us
  transfers between devices with their start and end apart: 28, of which 9 were waited for; matrix products, arithmetic and copies ran while one was open for 12% of the time, Pallas kernels for 7%

profile of v6, /device:TPU:24, one launch (start us, length us, event | category | flops | bytes accessed | tf_op | source)
XLA Modules:
  0.0 185.2 jit_solution(21597681469272415)
XLA Ops:
  0.6 1.4 fusion.24
  2.0 1.2 fusion.18
  3.3 3.1 %collective-permute-start = (bf16[128,2048]{1,0:T(8,128)(2,1)S(1)}, bf16[128,2048]{1,0:T(8,128)(2,1)S(1)}, u32[]{:S(2)}, u32[]{:S(2)}) collective-permute-start(bf16[128,2048]{1,0:T(8,128)(2,1)S(1)} %fusion.18), channel_id=1, source_target_pairs={{0,1},{1,0},{2,3},{3,2},{4,5},{5,4},{6,7},{7,6},{8,9},{9,8},{10,11... | collective-permute-start | bytes 1572872 | tf_op jit(solution)/shard_map/ppermute | solution.py:29
  6.4 2.1 %fusion.13 = bf16[1,128,512]{2,1,0:T(8,128)(2,1)S(1)} fusion(bf16[128,2048]{1,0:T(8,128)(2,1)S(1)} %fusion.18, bf16[2048,512]{1,0:T(8,128)(2,1)} %param.12), kind=kOutput, calls=%fused_computation.27 | convolution fusion | flops 268500992 | bytes 2752512 | tf_op jit(solution)/shard_map/dot_general | solution.py:255
  8.5 0.5 fusion.12
  9.0 4.1 %collective-permute-start.2 = (bf16[2,128,512]{2,1,0:T(8,128)(2,1)S(1)}, bf16[2,128,512]{2,1,0:T(8,128)(2,1)S(1)}, u32[]{:S(2)}, u32[]{:S(2)}) collective-permute-start(bf16[2,128,512]{2,1,0:T(8,128)(2,1)S(1)} %pad_maximum_fusion.1.refs_2_.refs_0_), channel_id=1, source_target_pairs={{0,4},{2,6},{4,8},{6,10},{8,12},{10,14},{12,16},{14,18},{16,20},{1... | collective-permute-start | bytes 786440 | tf_op jit(solution)/shard_map/ppermute | solution.py:25
  13.1 1.3 collective-permute-start.1
  14.4 8.2 %collective-permute-start.9 = (bf16[2,128,512]{2,1,0:T(8,128)(2,1)S(1)}, bf16[2,128,512]{2,1,0:T(8,128)(2,1)}, u32[]{:S(2)}, u32[]{:S(2)}) collective-permute-start(bf16[2,128,512]{2,1,0:T(8,128)(2,1)S(1)} %pad_maximum_fusion.1.refs_2_.refs_0_), channel_id=1, source_target_pairs={{0,16},{2,18},{4,20},{6,22},{8,24},{10,26},{12,28},{14,30},{16,32}... | collective-permute-start | bytes 786440 | tf_op jit(solution)/shard_map/ppermute | solution.py:25
  22.7 0.9 fusion.11
  23.6 10.2 %collective-permute-done.1.refs_11_ = bf16[2,128,512]{2,1,0:T(8,128)(2,1)S(1)} collective-permute-done((bf16[2,128,512]{2,1,0:T(8,128)(2,1)S(1)}, bf16[2,128,512]{2,1,0:T(8,128)(2,1)S(1)}, u32[]{:S(2)}, u32[]{:S(2)}) %collective-permute-start.1) | collective-permute-done | bytes 262176 | tf_op jit(solution)/shard_map/ppermute | solution.py:25
  33.8 0.5 fusion.17
  34.3 0.5 fusion.16
  34.8 0.7 pad_maximum_fusion.3.refs_3_.refs_0_
  35.5 1.9 %collective-permute-start.4 = (bf16[2,128,512]{2,1,0:T(8,128)(2,1)}, bf16[2,128,512]{2,1,0:T(8,128)(2,1)}, u32[]{:S(2)}, u32[]{:S(2)}) collective-permute-start(bf16[2,128,512]{2,1,0:T(8,128)(2,1)} %pad_maximum_fusion.3.refs_3_.refs_0_), channel_id=1, source_target_pairs={{0,4},{2,6},{4,8},{6,10},{8,12},{10,14},{12,16},{14,18},{16,20},{1... | collective-permute-start | bytes 786440 | tf_op jit(solution)/shard_map/ppermute | solution.py:25
  37.4 0.1 collective-permute-start.3
  37.5 1.1 fusion.10
  38.7 1.4 collective-permute-start.8
  40.1 1.9 %collective-permute-start.5 = (bf16[2,128,512]{2,1,0:T(8,128)(2,1)}, bf16[2,128,512]{2,1,0:T(8,128)(2,1)S(1)}, u32[]{:S(2)}, u32[]{:S(2)}) collective-permute-start(bf16[2,128,512]{2,1,0:T(8,128)(2,1)} %pad_maximum_fusion.3.refs_3_.refs_0_), channel_id=1, source_target_pairs={{0,16},{2,18},{4,20},{6,22},{8,24},{10,26},{12,28},{14,30},{16,32}... | collective-permute-start | bytes 786440 | tf_op jit(solution)/shard_map/ppermute | solution.py:25
  42.0 1.0 constant_dynamic-update-slice_fusion.1
  43.0 15.7 %collective-permute-done.4.refs_6_ = bf16[2,128,512]{2,1,0:T(8,128)(2,1)} collective-permute-done((bf16[2,128,512]{2,1,0:T(8,128)(2,1)}, bf16[2,128,512]{2,1,0:T(8,128)(2,1)}, u32[]{:S(2)}, u32[]{:S(2)}) %collective-permute-start.4) | collective-permute-done | bytes 262176 | tf_op jit(solution)/shard_map/ppermute | solution.py:25
  58.7 1.0 constant_dynamic-update-slice_fusion
  59.7 2.1 %collective-permute-start.6 = (bf16[2,256,512]{2,1,0:T(8,128)(2,1)S(1)}, bf16[2,256,512]{2,1,0:T(8,128)(2,1)S(1)}, u32[]{:S(2)}, u32[]{:S(2)}) collective-permute-start(bf16[2,256,512]{2,1,0:T(8,128)(2,1)S(1)} %constant_dynamic-update-slice_fusion), channel_id=1, source_target_pairs={{0,4},{2,6},{4,8},{6,10},{8,12},{10,14},{12,16},{14,18},{16,20},{1... | collective-permute-start | bytes 1572872 | tf_op jit(solution)/shard_map/ppermute | solution.py:25
  61.7 2.0 %fusion.14 = bf16[1,128,512]{2,1,0:T(8,128)(2,1)S(1)} fusion(bf16[128,2048]{1,0:T(8,128)(2,1)S(1)} %collective-permute-done, bf16[2048,512]{1,0:T(8,128)(2,1)} %param.10), kind=kOutput, calls=%fused_computation.28 | convolution fusion | flops 268500992 | bytes 2752512 | tf_op jit(solution)/shard_map/dot_general | solution.py:255
  63.8 5.4 %collective-permute-done.3 = bf16[128,2048]{1,0:T(8,128)(2,1)} collective-permute-done((bf16[128,2048]{1,0:T(8,128)(2,1)S(1)}, bf16[128,2048]{1,0:T(8,128)(2,1)}, u32[]{:S(2)}, u32[]{:S(2)}) %collective-permute-start.3) | collective-permute-done | bytes 524320 | tf_op jit(solution)/shard_map/ppermute | solution.py:29
  69.2 1.9 %fusion.15 = bf16[1,128,512]{2,1,0:T(8,128)(2,1)S(1)} fusion(bf16[128,2048]{1,0:T(8,128)(2,1)} %collective-permute-done.3, bf16[512,2048]{1,0:T(8,128)(2,1)S(1)} %copy-done.2), kind=kOutput, calls=%fused_computation.29 | convolution fusion | flops 268500992 | bytes 2752512 | tf_op jit(solution)/shard_map/dot_general | solution.py:259
  71.2 0.8 maximum_maximum_fusion.1
  72.0 2.0 %collective-permute-start.13 = (bf16[2,256,512]{2,1,0:T(8,128)(2,1)}, bf16[2,256,512]{2,1,0:T(8,128)(2,1)S(1)}, u32[]{:S(2)}, u32[]{:S(2)}) collective-permute-start(bf16[2,256,512]{2,1,0:T(8,128)(2,1)} %maximum_maximum_fusion.1), channel_id=1, source_target_pairs={{4,0},{6,2},{8,4},{10,6},{12,8},{14,10},{16,12},{18,14},{20,16},{2... | collective-permute-start | bytes 1572872 | tf_op jit(solution)/shard_map/ppermute | solution.py:25
  74.1 4.3 %collective-permute-done.6.refs_7_ = bf16[2,256,512]{2,1,0:T(8,128)(2,1)S(1)} collective-permute-done((bf16[2,256,512]{2,1,0:T(8,128)(2,1)S(1)}, bf16[2,256,512]{2,1,0:T(8,128)(2,1)S(1)}, u32[]{:S(2)}, u32[]{:S(2)}) %collective-permute-start.6) | collective-permute-done | bytes 524320 | tf_op jit(solution)/shard_map/ppermute | solution.py:25
  78.4 1.3 collective-permute-start.16
  79.8 0.7 constant_dynamic-update-slice_fusion.3
  80.5 0.8 constant_dynamic-update-slice_fusion.2
  81.2 1.3 collective-permute-start.11
  82.6 1.2 broadcast_select_fusion.1
  83.8 0.5 fusion.29
  84.6 2.5 %collective-permute-done.13.refs_5_ = bf16[2,256,512]{2,1,0:T(8,128)(2,1)S(1)} collective-permute-done((bf16[2,256,512]{2,1,0:T(8,128)(2,1)}, bf16[2,256,512]{2,1,0:T(8,128)(2,1)S(1)}, u32[]{:S(2)}, u32[]{:S(2)}) %collective-permute-start.13) | collective-permute-done | bytes 524320 | tf_op jit(solution)/shard_map/ppermute | solution.py:25
  87.1 5.4 %collective-permute-start.15 = (bf16[2,256,512]{2,1,0:T(8,128)(2,1)S(1)}, bf16[2,256,512]{2,1,0:T(8,128)(2,1)S(1)}, u32[]{:S(2)}, u32[]{:S(2)}) collective-permute-start(bf16[2,256,512]{2,1,0:T(8,128)(2,1)S(1)} %collective-permute-done.13.refs_5_), channel_id=1, source_target_pairs={{4,0},{6,2},{8,4},{10,6},{12,8},{14,10},{16,12},{18,14},{20,16},{2... | collective-permute-start | bytes 1572872 | tf_op jit(solution)/shard_map/ppermute | solution.py:25
  92.5 1.3 broadcast_select_fusion
  93.9 2.4 %collective-permute-done.11.refs_13_ = bf16[2,256,512]{2,1,0:T(8,128)(2,1)} collective-permute-done((bf16[2,256,512]{2,1,0:T(8,128)(2,1)}, bf16[2,256,512]{2,1,0:T(8,128)(2,1)}, u32[]{:S(2)}, u32[]{:S(2)}) %collective-permute-start.11) | collective-permute-done | bytes 524320 | tf_op jit(solution)/shard_map/ppermute | solution.py:25
  96.4 2.6 %collective-permute-done.10.refs_10_ = bf16[2,256,512]{2,1,0:T(8,128)(2,1)} collective-permute-done((bf16[2,256,512]{2,1,0:T(8,128)(2,1)}, bf16[2,256,512]{2,1,0:T(8,128)(2,1)}, u32[]{:S(2)}, u32[]{:S(2)}) %collective-permute-start.10) | collective-permute-done | bytes 524320 | tf_op jit(solution)/shard_map/ppermute | solution.py:266
  99.0 4.2 %collective-permute-start.19 = (bf16[2,256,512]{2,1,0:T(8,128)(2,1)S(1)}, bf16[2,256,512]{2,1,0:T(8,128)(2,1)S(1)}, u32[]{:S(2)}, u32[]{:S(2)}) collective-permute-start(bf16[2,256,512]{2,1,0:T(8,128)(2,1)S(1)} %collective-permute-done.16.refs_9_), channel_id=1, source_target_pairs={{64,0},{66,2},{68,4},{70,6},{72,8},{74,10},{76,12},{78,14},{80,16}... | collective-permute-start | bytes 1572872 | tf_op jit(solution)/shard_map/ppermute | solution.py:25
  103.4 0.8 copy-done.30
  104.1 6.0 %query_side.1 = (bf16[256,512]{1,0:T(8,128)(2,1)S(1)}, bf16[256,512]{1,0:T(8,128)(2,1)S(1)}, f32[4,2,256]{2,1,0:T(2,128)S(1)}) custom-call(s32[1]{0:T(128)} %bitcast.where_ref, f32[4,1,640]{2,1,0:T(1,128)S(1)} %compare_select_fusion.bias_ref, bf16[2,128,512]{2,1,0:T(8,128)(2,1)S(1)} %pad_maximum_fusion.refs_0_.refs_1_, ...), custom_call_target="tpu_custom_call" | custom-call | flops 671088640 | bytes 6291456 | tf_op jit(solution)/shard_map/query_side/pallas_call | solution.py:186
  110.1 1.9 %collective-permute-start.18 = (bf16[2,256,512]{2,1,0:T(8,128)(2,1)S(1)}, bf16[2,256,512]{2,1,0:T(8,128)(2,1)S(1)}, u32[]{:S(2)}, u32[]{:S(2)}) collective-permute-start(bf16[2,256,512]{2,1,0:T(8,128)(2,1)S(1)} %collective-permute-done.15.refs_6_), channel_id=1, source_target_pairs={{8,0},{10,2},{12,4},{14,6},{16,8},{18,10},{20,12},{22,14},{24,16},... | collective-permute-start | bytes 1572872 | tf_op jit(solution)/shard_map/ppermute | solution.py:25
  112.1 1.8 collective-permute-start.26
  113.9 1.4 collective-permute-start.25
  115.3 1.9 %collective-permute-start.24 = (f32[4,2,256]{2,1,0:T(2,128)S(1)}, f32[4,2,256]{2,1,0:T(2,128)S(1)}, u32[]{:S(2)}, u32[]{:S(2)}) collective-permute-start(f32[4,2,256]{2,1,0:T(2,128)S(1)} %get-tuple-element.36.refs_3_), channel_id=1, source_target_pairs={{32,0},{34,2},{36,4},{38,6},{40,8},{42,10},{44,12},{46,14},{48,16}... | collective-permute-start | bytes 24584 | tf_op jit(solution)/shard_map/ppermute | solution.py:25
  117.2 0.8 fusion.31
  118.0 1.9 %collective-permute-start.23 = (f32[4,2,256]{2,1,0:T(2,128)S(1)}, f32[4,2,256]{2,1,0:T(2,128)S(1)}, u32[]{:S(2)}, u32[]{:S(2)}) collective-permute-start(f32[4,2,256]{2,1,0:T(2,128)S(1)} %get-tuple-element.36.refs_3_), channel_id=1, source_target_pairs={{16,0},{18,2},{20,4},{22,6},{24,8},{26,10},{28,12},{30,14},{32,16}... | collective-permute-start | bytes 24584 | tf_op jit(solution)/shard_map/ppermute | solution.py:25
  119.9 9.3 %collective-permute-start.22 = (f32[4,2,256]{2,1,0:T(2,128)S(1)}, f32[4,2,256]{2,1,0:T(2,128)S(1)}, u32[]{:S(2)}, u32[]{:S(2)}) collective-permute-start(f32[4,2,256]{2,1,0:T(2,128)S(1)} %get-tuple-element.36.refs_3_), channel_id=1, source_target_pairs={{8,0},{10,2},{12,4},{14,6},{16,8},{18,10},{20,12},{22,14},{24,16},... | collective-permute-start | bytes 24584 | tf_op jit(solution)/shard_map/ppermute | solution.py:25
  129.2 24.0 %collective-permute-start.21 = (f32[4,2,256]{2,1,0:T(2,128)S(1)}, f32[4,2,256]{2,1,0:T(2,128)S(1)}, u32[]{:S(2)}, u32[]{:S(2)}) collective-permute-start(f32[4,2,256]{2,1,0:T(2,128)S(1)} %get-tuple-element.36.refs_3_), channel_id=1, source_target_pairs={{4,0},{6,2},{8,4},{10,6},{12,8},{14,10},{16,12},{18,14},{20,16},{2... | collective-permute-start | bytes 24584 | tf_op jit(solution)/shard_map/ppermute | solution.py:25
  153.2 1.9 %collective-permute-start.20 = (f32[4,2,256]{2,1,0:T(2,128)S(1)}, f32[4,2,256]{2,1,0:T(2,128)S(1)}, u32[]{:S(2)}, u32[]{:S(2)}) collective-permute-start(f32[4,2,256]{2,1,0:T(2,128)S(1)} %get-tuple-element.36.refs_3_), channel_id=1, source_target_pairs={{2,0},{4,2},{6,4},{8,6},{10,8},{12,10},{14,12},{16,14},{18,16},{20... | collective-permute-start | bytes 24584 | tf_op jit(solution)/shard_map/ppermute | solution.py:25
  155.2 0.4 convolution_convert_fusion
  155.7 1.2 collective-permute-start.12
  156.9 4.0 %key_side.3 = bf16[2,128,512]{2,1,0:T(8,128)(2,1)S(1)} custom-call(s32[1]{0:T(128)} %bitcast.where_ref, bf16[2,128,512]{2,1,0:T(8,128)(2,1)} %pad_maximum_fusion.3.refs_3_.refs_0_, bf16[2,128,512]{2,1,0:T(8,128)(2,1)S(1)} %pad_maximum_fusion.refs_0_.refs_1_, bf16[2,128,512]{2,1,0:T(8,128)(2,1)S(1)} %pad_maximum_fusion.2.refs_1_.refs_2_, ...), custom_call_target="tpu_custom_call" | custom-call | flops 335544320 | bytes 6291456 | tf_op jit(solution)/shard_map/key_side/pallas_call | solution.py:186
  160.9 0.8 fusion.25
  161.7 0.8 fusion.6
  162.5 2.7 %collective-permute-start.27 = (bf16[128,2048]{1,0:T(8,128)(2,1)S(1)}, bf16[128,2048]{1,0:T(8,128)(2,1)S(1)}, u32[]{:S(2)}, u32[]{:S(2)}) collective-permute-start(bf16[128,2048]{1,0:T(8,128)(2,1)S(1)} %fusion.6), channel_id=1, source_target_pairs={{0,1},{1,0},{2,3},{3,2},{4,5},{5,4},{6,7},{7,6},{8,9},{9,8},{10,11... | collective-permute-start | bytes 1572872 | tf_op jit(solution)/shard_map/ppermute | solution.py:29
  165.2 6.9 %collective-permute-done.12 = bf16[128,2048]{1,0:T(8,128)(2,1)S(1)} collective-permute-done((bf16[128,2048]{1,0:T(8,128)(2,1)S(1)}, bf16[128,2048]{1,0:T(8,128)(2,1)S(1)}, u32[]{:S(2)}, u32[]{:S(2)}) %collective-permute-start.12) | collective-permute-done | bytes 524320 | tf_op jit(solution)/shard_map/ppermute | solution.py:29
  172.2 1.3 fusion.5
  173.5 3.5 %key_side.2 = bf16[2,128,512]{2,1,0:T(8,128)(2,1)S(1)} custom-call(s32[1]{0:T(128)} %bitcast.where_ref, bf16[2,128,512]{2,1,0:T(8,128)(2,1)S(1)} %pad_maximum_fusion.1.refs_2_.refs_0_, bf16[2,128,512]{2,1,0:T(8,128)(2,1)S(1)} %pad_maximum_fusion.refs_0_.refs_1_, bf16[2,128,512]{2,1,0:T(8,128)(2,1)S(1)} %pad_maximum_fusion.2.refs_1_.refs_2_, ...), custom_call_target="tpu_custom_call" | custom-call | flops 335544320 | bytes 6291456 | tf_op jit(solution)/shard_map/key_side/pallas_call | solution.py:186
  177.0 0.8 fusion.26
  177.8 5.2 %collective-permute-done.27 = bf16[128,2048]{1,0:T(8,128)(2,1)S(1)} collective-permute-done((bf16[128,2048]{1,0:T(8,128)(2,1)S(1)}, bf16[128,2048]{1,0:T(8,128)(2,1)S(1)}, u32[]{:S(2)}, u32[]{:S(2)}) %collective-permute-start.27) | collective-permute-done | bytes 524320 | tf_op jit(solution)/shard_map/ppermute | solution.py:29
  183.0 1.0 fusion.19
  184.0 1.2 fusion.23
  (100 shorter events, 0.7 us)
Async XLA Ops:
  0.6 7.8 %copy-start = (bf16[2048,512]{1,0:T(8,128)(2,1)S(1)}, bf16[2048,512]{1,0:T(8,128)(2,1)}, u32[]{:S(2)}) copy-start(bf16[2048,512]{1,0:T(8,128)(2,1)} %param.11) | copy-start | bytes 6291460
  3.3 30.5 %collective-permute-start = (bf16[128,2048]{1,0:T(8,128)(2,1)S(1)}, bf16[128,2048]{1,0:T(8,128)(2,1)S(1)}, u32[]{:S(2)}, u32[]{:S(2)}) collective-permute-start(bf16[128,2048]{1,0:T(8,128)(2,1)S(1)} %fusion.18), channel_id=1, source_target_pairs={{0,1},{1,0},{2,3},{3,2},{4,5},{5,4},{6,7},{7,6},{8,9},{9,8},{10,11... | collective-permute-start | bytes 1572872 | tf_op jit(solution)/shard_map/ppermute | solution.py:29
  8.5 6.0 %copy-start.17 = (bf16[1,128,512]{2,1,0:T(8,128)(2,1)}, bf16[1,128,512]{2,1,0:T(8,128)(2,1)S(1)}, u32[]{:S(2)}) copy-start(bf16[1,128,512]{2,1,0:T(8,128)(2,1)S(1)} %fusion.13) | copy-start | bytes 393220
  8.5 14.2 %copy-start.1 = (bf16[512,2048]{1,0:T(8,128)(2,1)S(1)}, bf16[512,2048]{1,0:T(8,128)(2,1)}, u32[]{:S(2)}) copy-start(bf16[512,2048]{1,0:T(8,128)(2,1)} %param.13) | copy-start | bytes 6291460
  8.5 14.2 %copy-start.9 = (bf16[128,2048]{1,0:T(8,128)(2,1)S(1)}, bf16[128,2048]{1,0:T(8,128)(2,1)}, u32[]{:S(2)}) copy-start(bf16[128,2048]{1,0:T(8,128)(2,1)} %param.14) | copy-start | bytes 1572868
  9.0 5.5 %copy-start.19 = (bf16[1,128,512]{2,1,0:T(8,128)(2,1)}, bf16[1,128,512]{2,1,0:T(8,128)(2,1)S(1)}, u32[]{:S(2)}) copy-start(bf16[1,128,512]{2,1,0:T(8,128)(2,1)S(1)} %fusion.12) | copy-start | bytes 393220
  9.0 24.8 %copy-start.4 = (bf16[2048,512]{1,0:T(8,128)(2,1)S(1)}, bf16[2048,512]{1,0:T(8,128)(2,1)}, u32[]{:S(2)}) copy-start(bf16[2048,512]{1,0:T(8,128)(2,1)} %param.12) | copy-start | bytes 6291460
  9.0 14.5 %collective-permute-start.2 = (bf16[2,128,512]{2,1,0:T(8,128)(2,1)S(1)}, bf16[2,128,512]{2,1,0:T(8,128)(2,1)S(1)}, u32[]{:S(2)}, u32[]{:S(2)}) collective-permute-start(bf16[2,128,512]{2,1,0:T(8,128)(2,1)S(1)} %pad_maximum_fusion.1.refs_2_.refs_0_), channel_id=1, source_target_pairs={{0,4},{2,6},{4,8},{6,10},{8,12},{10,14},{12,16},{14,18},{16,20},{1... | collective-permute-start | bytes 786440 | tf_op jit(solution)/shard_map/ppermute | solution.py:25
  13.1 20.6 %collective-permute-start.1 = (bf16[2,128,512]{2,1,0:T(8,128)(2,1)S(1)}, bf16[2,128,512]{2,1,0:T(8,128)(2,1)S(1)}, u32[]{:S(2)}, u32[]{:S(2)}) collective-permute-start(bf16[2,128,512]{2,1,0:T(8,128)(2,1)S(1)} %pad_maximum_fusion.1.refs_2_.refs_0_), channel_id=1, source_target_pairs={{0,64},{2,66},{4,68},{6,70},{8,72},{10,74},{12,76},{14,78},{16,80}... | collective-permute-start | bytes 786440 | tf_op jit(solution)/shard_map/ppermute | solution.py:25
  14.4 68.1 %collective-permute-start.9 = (bf16[2,128,512]{2,1,0:T(8,128)(2,1)S(1)}, bf16[2,128,512]{2,1,0:T(8,128)(2,1)}, u32[]{:S(2)}, u32[]{:S(2)}) collective-permute-start(bf16[2,128,512]{2,1,0:T(8,128)(2,1)S(1)} %pad_maximum_fusion.1.refs_2_.refs_0_), channel_id=1, source_target_pairs={{0,16},{2,18},{4,20},{6,22},{8,24},{10,26},{12,28},{14,30},{16,32}... | collective-permute-start | bytes 786440 | tf_op jit(solution)/shard_map/ppermute | solution.py:25
  23.6 11.2 %copy-start.25 = (bf16[2,128,512]{2,1,0:T(8,128)(2,1)}, bf16[2,128,512]{2,1,0:T(8,128)(2,1)S(1)}, u32[]{:S(2)}) copy-start(bf16[2,128,512]{2,1,0:T(8,128)(2,1)S(1)} %collective-permute-done.2.refs_5_) | copy-start | bytes 786436
  33.7 1.0 copy-start.26
  34.2 4.4 %copy-start.21 = (bf16[1,128,512]{2,1,0:T(8,128)(2,1)}, bf16[1,128,512]{2,1,0:T(8,128)(2,1)S(1)}, u32[]{:S(2)}) copy-start(bf16[1,128,512]{2,1,0:T(8,128)(2,1)S(1)} %fusion.17) | copy-start | bytes 393220
  34.3 3.2 %copy-start.6 = (bf16[2048,512]{1,0:T(8,128)(2,1)S(1)}, bf16[2048,512]{1,0:T(8,128)(2,1)}, u32[]{:S(2)}) copy-start(bf16[2048,512]{1,0:T(8,128)(2,1)} %param.10) | copy-start | bytes 6291460
  34.7 3.9 %copy-start.23 = (bf16[1,128,512]{2,1,0:T(8,128)(2,1)}, bf16[1,128,512]{2,1,0:T(8,128)(2,1)S(1)}, u32[]{:S(2)}) copy-start(bf16[1,128,512]{2,1,0:T(8,128)(2,1)S(1)} %fusion.16) | copy-start | bytes 393220
  35.5 23.2 %collective-permute-start.4 = (bf16[2,128,512]{2,1,0:T(8,128)(2,1)}, bf16[2,128,512]{2,1,0:T(8,128)(2,1)}, u32[]{:S(2)}, u32[]{:S(2)}) collective-permute-start(bf16[2,128,512]{2,1,0:T(8,128)(2,1)} %pad_maximum_fusion.3.refs_3_.refs_0_), channel_id=1, source_target_pairs={{0,4},{2,6},{4,8},{6,10},{8,12},{10,14},{12,16},{14,18},{16,20},{1... | collective-permute-start | bytes 786440 | tf_op jit(solution)/shard_map/ppermute | solution.py:25
  37.4 31.8 %collective-permute-start.3 = (bf16[128,2048]{1,0:T(8,128)(2,1)S(1)}, bf16[128,2048]{1,0:T(8,128)(2,1)}, u32[]{:S(2)}, u32[]{:S(2)}) collective-permute-start(bf16[128,2048]{1,0:T(8,128)(2,1)S(1)} %copy-done.9), channel_id=1, source_target_pairs={{0,1},{1,0},{2,3},{3,2},{4,5},{5,4},{6,7},{7,6},{8,9},{9,8},{10,11... | collective-permute-start | bytes 1572872 | tf_op jit(solution)/shard_map/ppermute | solution.py:29
  38.6 30.6 %copy-start.2 = (bf16[512,2048]{1,0:T(8,128)(2,1)S(1)}, bf16[512,2048]{1,0:T(8,128)(2,1)}, u32[]{:S(2)}) copy-start(bf16[512,2048]{1,0:T(8,128)(2,1)} %param.13) | copy-start | bytes 6291460
  38.7 41.8 %collective-permute-start.8 = (bf16[2,128,512]{2,1,0:T(8,128)(2,1)}, bf16[2,128,512]{2,1,0:T(8,128)(2,1)S(1)}, u32[]{:S(2)}, u32[]{:S(2)}) collective-permute-start(bf16[2,128,512]{2,1,0:T(8,128)(2,1)} %pad_maximum_fusion.3.refs_3_.refs_0_), channel_id=1, source_target_pairs={{0,64},{2,66},{4,68},{6,70},{8,72},{10,74},{12,76},{14,78},{16,80}... | collective-permute-start | bytes 786440 | tf_op jit(solution)/shard_map/ppermute | solution.py:25
  40.1 34.0 %collective-permute-start.5 = (bf16[2,128,512]{2,1,0:T(8,128)(2,1)}, bf16[2,128,512]{2,1,0:T(8,128)(2,1)S(1)}, u32[]{:S(2)}, u32[]{:S(2)}) collective-permute-start(bf16[2,128,512]{2,1,0:T(8,128)(2,1)} %pad_maximum_fusion.3.refs_3_.refs_0_), channel_id=1, source_target_pairs={{0,16},{2,18},{4,20},{6,22},{8,24},{10,26},{12,28},{14,30},{16,32}... | collective-permute-start | bytes 786440 | tf_op jit(solution)/shard_map/ppermute | solution.py:25
  59.6 11.5 %copy-start.11 = (bf16[1,128,512]{2,1,0:T(8,128)(2,1)S(1)}, bf16[1,128,512]{2,1,0:T(8,128)(2,1)}, u32[]{:S(2)}) copy-start(bf16[1,128,512]{2,1,0:T(8,128)(2,1)} %fusion.10) | copy-start | bytes 393220
  59.7 18.8 %collective-permute-start.6 = (bf16[2,256,512]{2,1,0:T(8,128)(2,1)S(1)}, bf16[2,256,512]{2,1,0:T(8,128)(2,1)S(1)}, u32[]{:S(2)}, u32[]{:S(2)}) collective-permute-start(bf16[2,256,512]{2,1,0:T(8,128)(2,1)S(1)} %constant_dynamic-update-slice_fusion), channel_id=1, source_target_pairs={{0,4},{2,6},{4,8},{6,10},{8,12},{10,14},{12,16},{14,18},{16,20},{1... | collective-permute-start | bytes 1572872 | tf_op jit(solution)/shard_map/ppermute | solution.py:25
  63.8 16.7 %copy-start.13 = (bf16[1,128,512]{2,1,0:T(8,128)(2,1)}, bf16[1,128,512]{2,1,0:T(8,128)(2,1)S(1)}, u32[]{:S(2)}) copy-start(bf16[1,128,512]{2,1,0:T(8,128)(2,1)S(1)} %fusion.14) | copy-start | bytes 393220
  63.8 16.0 %copy-start.27 = (bf16[2,128,512]{2,1,0:T(8,128)(2,1)S(1)}, bf16[2,128,512]{2,1,0:T(8,128)(2,1)}, u32[]{:S(2)}) copy-start(bf16[2,128,512]{2,1,0:T(8,128)(2,1)} %copy-done.26) | copy-start | bytes 786436
  63.8 18.8 %copy-start.18 = (bf16[1,128,512]{2,1,0:T(8,128)(2,1)S(1)}, bf16[1,128,512]{2,1,0:T(8,128)(2,1)}, u32[]{:S(2)}) copy-start(bf16[1,128,512]{2,1,0:T(8,128)(2,1)} %copy-done.17) | copy-start | bytes 393220
  63.8 18.8 %copy-start.20 = (bf16[1,128,512]{2,1,0:T(8,128)(2,1)S(1)}, bf16[1,128,512]{2,1,0:T(8,128)(2,1)}, u32[]{:S(2)}) copy-start(bf16[1,128,512]{2,1,0:T(8,128)(2,1)} %copy-done.19) | copy-start | bytes 393220
  63.8 18.8 %copy-start.22 = (bf16[1,128,512]{2,1,0:T(8,128)(2,1)S(1)}, bf16[1,128,512]{2,1,0:T(8,128)(2,1)}, u32[]{:S(2)}) copy-start(bf16[1,128,512]{2,1,0:T(8,128)(2,1)} %copy-done.21) | copy-start | bytes 393220
  63.8 18.8 %copy-start.24 = (bf16[1,128,512]{2,1,0:T(8,128)(2,1)S(1)}, bf16[1,128,512]{2,1,0:T(8,128)(2,1)}, u32[]{:S(2)}) copy-start(bf16[1,128,512]{2,1,0:T(8,128)(2,1)} %copy-done.23) | copy-start | bytes 393220
  71.2 12.7 %copy-start.15 = (bf16[1,128,512]{2,1,0:T(8,128)(2,1)}, bf16[1,128,512]{2,1,0:T(8,128)(2,1)S(1)}, u32[]{:S(2)}) copy-start(bf16[1,128,512]{2,1,0:T(8,128)(2,1)S(1)} %fusion.15) | copy-start | bytes 393220
  72.0 12.3 %copy-start.33 = (s32[10]{0:T(128)S(1)}, s32[10]{0:T(128)}, u32[]{:S(2)}) copy-start(s32[10]{0:T(128)} %constant.81.clone) | copy-start | bytes 124
  72.0 15.1 %collective-permute-start.13 = (bf16[2,256,512]{2,1,0:T(8,128)(2,1)}, bf16[2,256,512]{2,1,0:T(8,128)(2,1)S(1)}, u32[]{:S(2)}, u32[]{:S(2)}) collective-permute-start(bf16[2,256,512]{2,1,0:T(8,128)(2,1)} %maximum_maximum_fusion.1), channel_id=1, source_target_pairs={{4,0},{6,2},{8,4},{10,6},{12,8},{14,10},{16,12},{18,14},{20,16},{2... | collective-permute-start | bytes 1572872 | tf_op jit(solution)/shard_map/ppermute | solution.py:25
  74.1 10.3 %copy-start.31 = (bf16[2,128,512]{2,1,0:T(8,128)(2,1)}, bf16[2,128,512]{2,1,0:T(8,128)(2,1)S(1)}, u32[]{:S(2)}) copy-start(bf16[2,128,512]{2,1,0:T(8,128)(2,1)S(1)} %collective-permute-done.5.refs_9_) | copy-start | bytes 786436
  78.4 5.4 %copy-start.29 = (bf16[2,256,512]{2,1,0:T(8,128)(2,1)}, bf16[2,256,512]{2,1,0:T(8,128)(2,1)S(1)}, u32[]{:S(2)}) copy-start(bf16[2,256,512]{2,1,0:T(8,128)(2,1)S(1)} %collective-permute-done.6.refs_7_) | copy-start | bytes 1572868
  78.4 14.1 %collective-permute-start.16 = (bf16[2,256,512]{2,1,0:T(8,128)(2,1)}, bf16[2,256,512]{2,1,0:T(8,128)(2,1)S(1)}, u32[]{:S(2)}, u32[]{:S(2)}) collective-permute-start(bf16[2,256,512]{2,1,0:T(8,128)(2,1)} %maximum_maximum_fusion.1), channel_id=1, source_target_pairs={{64,0},{66,2},{68,4},{70,6},{72,8},{74,10},{76,12},{78,14},{80,16}... | collective-permute-start | bytes 1572872 | tf_op jit(solution)/shard_map/ppermute | solution.py:25
  80.5 3.3 %copy-start.28 = (bf16[2,128,512]{2,1,0:T(8,128)(2,1)}, bf16[2,128,512]{2,1,0:T(8,128)(2,1)S(1)}, u32[]{:S(2)}) copy-start(bf16[2,128,512]{2,1,0:T(8,128)(2,1)S(1)} %collective-permute-done.8.refs_12_) | copy-start | bytes 786436
  81.2 15.1 %collective-permute-start.11 = (bf16[2,256,512]{2,1,0:T(8,128)(2,1)}, bf16[2,256,512]{2,1,0:T(8,128)(2,1)}, u32[]{:S(2)}, u32[]{:S(2)}) collective-permute-start(bf16[2,256,512]{2,1,0:T(8,128)(2,1)} %constant_dynamic-update-slice_fusion.2), channel_id=1, source_target_pairs={{0,64},{2,66},{4,68},{6,70},{8,72},{10,74},{12,76},{14,78},{16,80}... | collective-permute-start | bytes 1572872 | tf_op jit(solution)/shard_map/ppermute | solution.py:25
  83.8 15.2 %collective-permute-start.10 = (bf16[2,256,512]{2,1,0:T(8,128)(2,1)}, bf16[2,256,512]{2,1,0:T(8,128)(2,1)}, u32[]{:S(2)}, u32[]{:S(2)}) collective-permute-start(bf16[2,256,512]{2,1,0:T(8,128)(2,1)} %get-tuple-element.44), channel_id=1, source_target_pairs={{0,32},{2,34},{4,36},{6,38},{8,40},{10,42},{12,44},{14,46},{16,48}... | collective-permute-start | bytes 1572872 | tf_op jit(solution)/shard_map/ppermute | solution.py:266
  84.5 11.8 %copy-start.34 = (s32[4]{0:T(128)S(1)}, s32[4]{0:T(128)}, u32[]{:S(2)}) copy-start(s32[4]{0:T(128)} %fusion.29) | copy-start | bytes 52
  84.5 18.7 %copy-start.12 = (bf16[1,128,512]{2,1,0:T(8,128)(2,1)S(1)}, bf16[1,128,512]{2,1,0:T(8,128)(2,1)}, u32[]{:S(2)}) copy-start(bf16[1,128,512]{2,1,0:T(8,128)(2,1)} %fusion.10) | copy-start | bytes 393220
  84.5 18.8 %copy-start.14 = (bf16[1,128,512]{2,1,0:T(8,128)(2,1)S(1)}, bf16[1,128,512]{2,1,0:T(8,128)(2,1)}, u32[]{:S(2)}) copy-start(bf16[1,128,512]{2,1,0:T(8,128)(2,1)} %copy-done.13) | copy-start | bytes 393220
  84.5 18.8 %copy-start.16 = (bf16[1,128,512]{2,1,0:T(8,128)(2,1)S(1)}, bf16[1,128,512]{2,1,0:T(8,128)(2,1)}, u32[]{:S(2)}) copy-start(bf16[1,128,512]{2,1,0:T(8,128)(2,1)} %copy-done.15) | copy-start | bytes 393220
  84.5 18.8 %collective-permute-start.7 = (bf16[2,256,512]{2,1,0:T(8,128)(2,1)}, bf16[2,256,512]{2,1,0:T(8,128)(2,1)S(1)}, u32[]{:S(2)}, u32[]{:S(2)}) collective-permute-start(bf16[2,256,512]{2,1,0:T(8,128)(2,1)} %get-tuple-element.45), channel_id=1, source_target_pairs={{0,2},{2,0},{4,6},{6,4},{8,10},{10,8},{12,14},{14,12},{16,18},{18,... | collective-permute-start | bytes 1572872 | tf_op jit(solution)/shard_map/ppermute | solution.py:266
  87.1 23.0 %collective-permute-start.15 = (bf16[2,256,512]{2,1,0:T(8,128)(2,1)S(1)}, bf16[2,256,512]{2,1,0:T(8,128)(2,1)S(1)}, u32[]{:S(2)}, u32[]{:S(2)}) collective-permute-start(bf16[2,256,512]{2,1,0:T(8,128)(2,1)S(1)} %collective-permute-done.13.refs_5_), channel_id=1, source_target_pairs={{4,0},{6,2},{8,4},{10,6},{12,8},{14,10},{16,12},{18,14},{20,16},{2... | collective-permute-start | bytes 1572872 | tf_op jit(solution)/shard_map/ppermute | solution.py:25
  93.8 18.2 %collective-permute-start.17 = (bf16[2,256,512]{2,1,0:T(8,128)(2,1)S(1)}, bf16[2,256,512]{2,1,0:T(8,128)(2,1)S(1)}, u32[]{:S(2)}, u32[]{:S(2)}) collective-permute-start(bf16[2,256,512]{2,1,0:T(8,128)(2,1)S(1)} %get-tuple-element.42), channel_id=1, source_target_pairs={{0,32},{2,34},{4,36},{6,38},{8,40},{10,42},{12,44},{14,46},{16,48}... | collective-permute-start | bytes 1572872 | tf_op jit(solution)/shard_map/ppermute | solution.py:266
  96.3 15.7 %collective-permute-start.14 = (bf16[2,256,512]{2,1,0:T(8,128)(2,1)S(1)}, bf16[2,256,512]{2,1,0:T(8,128)(2,1)S(1)}, u32[]{:S(2)}, u32[]{:S(2)}) collective-permute-start(bf16[2,256,512]{2,1,0:T(8,128)(2,1)S(1)} %get-tuple-element.43), channel_id=1, source_target_pairs={{0,2},{2,0},{4,6},{6,4},{8,10},{10,8},{12,14},{14,12},{16,18},{18,... | collective-permute-start | bytes 1572872 | tf_op jit(solution)/shard_map/ppermute | solution.py:266
  99.0 19.0 %collective-permute-start.19 = (bf16[2,256,512]{2,1,0:T(8,128)(2,1)S(1)}, bf16[2,256,512]{2,1,0:T(8,128)(2,1)S(1)}, u32[]{:S(2)}, u32[]{:S(2)}) collective-permute-start(bf16[2,256,512]{2,1,0:T(8,128)(2,1)S(1)} %collective-permute-done.16.refs_9_), channel_id=1, source_target_pairs={{64,0},{66,2},{68,4},{70,6},{72,8},{74,10},{76,12},{78,14},{80,16}... | collective-permute-start | bytes 1572872 | tf_op jit(solution)/shard_map/ppermute | solution.py:25
  103.4 0.8 copy-start.30
  104.1 13.0 %copy-start.7 = (bf16[2048,512]{1,0:T(8,128)(2,1)S(1)}, bf16[2048,512]{1,0:T(8,128)(2,1)}, u32[]{:S(2)}) copy-start(bf16[2048,512]{1,0:T(8,128)(2,1)} %param.10) | copy-start | bytes 6291460
  110.1 46.8 %collective-permute-start.18 = (bf16[2,256,512]{2,1,0:T(8,128)(2,1)S(1)}, bf16[2,256,512]{2,1,0:T(8,128)(2,1)S(1)}, u32[]{:S(2)}, u32[]{:S(2)}) collective-permute-start(bf16[2,256,512]{2,1,0:T(8,128)(2,1)S(1)} %collective-permute-done.15.refs_6_), channel_id=1, source_target_pairs={{8,0},{10,2},{12,4},{14,6},{16,8},{18,10},{20,12},{22,14},{24,16},... | collective-permute-start | bytes 1572872 | tf_op jit(solution)/shard_map/ppermute | solution.py:25
  112.1 7.9 %collective-permute-start.26 = (f32[4,2,256]{2,1,0:T(2,128)S(1)}, f32[4,2,256]{2,1,0:T(2,128)S(1)}, u32[]{:S(2)}, u32[]{:S(2)}) collective-permute-start(f32[4,2,256]{2,1,0:T(2,128)S(1)} %get-tuple-element.36.refs_3_), channel_id=1, source_target_pairs={{128,0},{130,2},{132,4},{134,6},{136,8},{138,10},{140,12},{142,14}... | collective-permute-start | bytes 24584 | tf_op jit(solution)/shard_map/ppermute | solution.py:25
  113.9 15.3 %collective-permute-start.25 = (f32[4,2,256]{2,1,0:T(2,128)S(1)}, f32[4,2,256]{2,1,0:T(2,128)S(1)}, u32[]{:S(2)}, u32[]{:S(2)}) collective-permute-start(f32[4,2,256]{2,1,0:T(2,128)S(1)} %get-tuple-element.36.refs_3_), channel_id=1, source_target_pairs={{64,0},{66,2},{68,4},{70,6},{72,8},{74,10},{76,12},{78,14},{80,16}... | collective-permute-start | bytes 24584 | tf_op jit(solution)/shard_map/ppermute | solution.py:25
  115.3 38.0 %collective-permute-start.24 = (f32[4,2,256]{2,1,0:T(2,128)S(1)}, f32[4,2,256]{2,1,0:T(2,128)S(1)}, u32[]{:S(2)}, u32[]{:S(2)}) collective-permute-start(f32[4,2,256]{2,1,0:T(2,128)S(1)} %get-tuple-element.36.refs_3_), channel_id=1, source_target_pairs={{32,0},{34,2},{36,4},{38,6},{40,8},{42,10},{44,12},{46,14},{48,16}... | collective-permute-start | bytes 24584 | tf_op jit(solution)/shard_map/ppermute | solution.py:25
  117.2 38.0 %copy-start.3 = (bf16[512,2048]{1,0:T(8,128)(2,1)S(1)}, bf16[512,2048]{1,0:T(8,128)(2,1)}, u32[]{:S(2)}) copy-start(bf16[512,2048]{1,0:T(8,128)(2,1)} %param.13) | copy-start | bytes 6291460
  118.0 37.7 %collective-permute-start.23 = (f32[4,2,256]{2,1,0:T(2,128)S(1)}, f32[4,2,256]{2,1,0:T(2,128)S(1)}, u32[]{:S(2)}, u32[]{:S(2)}) collective-permute-start(f32[4,2,256]{2,1,0:T(2,128)S(1)} %get-tuple-element.36.refs_3_), channel_id=1, source_target_pairs={{16,0},{18,2},{20,4},{22,6},{24,8},{26,10},{28,12},{30,14},{32,16}... | collective-permute-start | bytes 24584 | tf_op jit(solution)/shard_map/ppermute | solution.py:25
  119.9 36.9 %collective-permute-start.22 = (f32[4,2,256]{2,1,0:T(2,128)S(1)}, f32[4,2,256]{2,1,0:T(2,128)S(1)}, u32[]{:S(2)}, u32[]{:S(2)}) collective-permute-start(f32[4,2,256]{2,1,0:T(2,128)S(1)} %get-tuple-element.36.refs_3_), channel_id=1, source_target_pairs={{8,0},{10,2},{12,4},{14,6},{16,8},{18,10},{20,12},{22,14},{24,16},... | collective-permute-start | bytes 24584 | tf_op jit(solution)/shard_map/ppermute | solution.py:25
  129.2 27.6 %collective-permute-start.21 = (f32[4,2,256]{2,1,0:T(2,128)S(1)}, f32[4,2,256]{2,1,0:T(2,128)S(1)}, u32[]{:S(2)}, u32[]{:S(2)}) collective-permute-start(f32[4,2,256]{2,1,0:T(2,128)S(1)} %get-tuple-element.36.refs_3_), channel_id=1, source_target_pairs={{4,0},{6,2},{8,4},{10,6},{12,8},{14,10},{16,12},{18,14},{20,16},{2... | collective-permute-start | bytes 24584 | tf_op jit(solution)/shard_map/ppermute | solution.py:25
  153.2 3.6 %collective-permute-start.20 = (f32[4,2,256]{2,1,0:T(2,128)S(1)}, f32[4,2,256]{2,1,0:T(2,128)S(1)}, u32[]{:S(2)}, u32[]{:S(2)}) collective-permute-start(f32[4,2,256]{2,1,0:T(2,128)S(1)} %get-tuple-element.36.refs_3_), channel_id=1, source_target_pairs={{2,0},{4,2},{6,4},{8,6},{10,8},{12,10},{14,12},{16,14},{18,16},{20... | collective-permute-start | bytes 24584 | tf_op jit(solution)/shard_map/ppermute | solution.py:25
  155.6 5.3 %copy-start.5 = (bf16[2048,512]{1,0:T(8,128)(2,1)S(1)}, bf16[2048,512]{1,0:T(8,128)(2,1)}, u32[]{:S(2)}) copy-start(bf16[2048,512]{1,0:T(8,128)(2,1)} %param.12) | copy-start | bytes 6291460
  155.7 16.5 %collective-permute-start.12 = (bf16[128,2048]{1,0:T(8,128)(2,1)S(1)}, bf16[128,2048]{1,0:T(8,128)(2,1)S(1)}, u32[]{:S(2)}, u32[]{:S(2)}) collective-permute-start(bf16[128,2048]{1,0:T(8,128)(2,1)S(1)} %convolution_convert_fusion), channel_id=1, source_target_pairs={{0,1},{1,0},{2,3},{3,2},{4,5},{5,4},{6,7},{7,6},{8,9},{9,8},{10,11... | collective-permute-start | bytes 1572872 | tf_op jit(solution)/shard_map/ppermute | solution.py:29
  161.7 10.4 %copy-start.8 = (bf16[128,2048]{1,0:T(8,128)(2,1)S(1)}, bf16[128,2048]{1,0:T(8,128)(2,1)}, u32[]{:S(2)}) copy-start(bf16[128,2048]{1,0:T(8,128)(2,1)} %param.8) | copy-start | bytes 1572868
  162.5 20.5 %collective-permute-start.27 = (bf16[128,2048]{1,0:T(8,128)(2,1)S(1)}, bf16[128,2048]{1,0:T(8,128)(2,1)S(1)}, u32[]{:S(2)}, u32[]{:S(2)}) collective-permute-start(bf16[128,2048]{1,0:T(8,128)(2,1)S(1)} %fusion.6), channel_id=1, source_target_pairs={{0,1},{1,0},{2,3},{3,2},{4,5},{5,4},{6,7},{7,6},{8,9},{9,8},{10,11... | collective-permute-start | bytes 1572872 | tf_op jit(solution)/shard_map/ppermute | solution.py:29
  177.0 6.0 %copy-start.32 = (f32[2048]{0:T(1024)S(1)}, f32[2048]{0:T(1024)}, u32[]{:S(2)}) copy-start(f32[2048]{0:T(1024)} %param.9) | copy-start | bytes 24580
  177.8 6.2 %copy-start.10 = (bf16[128,2048]{1,0:T(8,128)(2,1)S(1)}, bf16[128,2048]{1,0:T(8,128)(2,1)}, u32[]{:S(2)}) copy-start(bf16[128,2048]{1,0:T(8,128)(2,1)} %param.14) | copy-start | bytes 1572868

commit v7 on v5

--- a/solution.py
+++ b/solution.py
@@ -120,14 +120,13 @@
                 ref[1, out, :] = grad_values[at * BLOCK : (at + 1) * BLOCK]
 
 
-def key_kernel(half, groups, n_back, where_ref, *refs):
+def key_kernel(half, groups, where_ref, *refs):
     refs = list(refs)
     kv = refs.pop(0)
     qg = [refs.pop(0) for _ in range(2)]
     stat = refs.pop(0)
     later = [[refs.pop(0) for _ in range(n)] for n in groups]
     later_stats = [refs.pop(0) for _ in groups]
-    back = [refs.pop(0) for _ in range(n_back)]
     (out_ref,) = refs
     is_second = where_ref[0] == 1
     factor = HD ** (-0.5)
@@ -136,39 +135,40 @@
     def stat_of(ref, slot):
         return ref[0, :, slot * BLOCK : (slot + 1) * BLOCK]
 
-    for at in range(2):
-        slot = 2 * half + at
+    def gather(which, at):
         rows = slice(at * BLOCK, (at + 1) * BLOCK)
-        queries, grads = [
-            jnp.concatenate(
-                [piece(qg, which, slot)]
-                + [near(is_second, qg, later[0], which, slot, d) for d in NEAR]
-                + [f[0][which, rows, :] for f in later[1:]],
-                axis=0,
-            )
-            for which in range(2)
-        ]
-        near_stats = []
+        return jnp.concatenate(
+            [piece(qg, which, 2 * half + at)]
+            + [near(is_second, qg, later[0], which, 2 * half + at, d) for d in NEAR]
+            + [f[0][which, rows, :] for f in later[1:]],
+            axis=0,
+        )
+
+    def gather_stats(slot):
+        parts = [stat_of(stat, slot)]
         for d in NEAR:
             options = [
                 stat_of(stat if here else later_stats[0], s) for here, s in near_slots(d, slot)
             ]
-            near_stats.append(jnp.where(is_second, options[1], options[0]))
-        stats = jnp.concatenate(
-            [stat_of(stat, slot)] + near_stats + [stat_of(f, slot) for f in later_stats[1:]], axis=1
-        )
-        score = dot(kv[0, rows, :], queries, NT) * factor
-        score = jnp.concatenate([score[:, :BLOCK] + causal, score[:, BLOCK:]], axis=1)
-        prob = jnp.exp(score - stats[0:1])
-        grad_score = (prob * (dot(kv[1, rows, :], grads, NT) - stats[1:2])).astype(BF16)
-        totals = [
-            dot(grad_score, queries, NN) * factor,
-            dot(prob.astype(BF16), grads, NN),
-        ]
-        for which in range(2):
-            for ref in back:
-                totals[which] += ref[which, rows, :].astype(F32)
-            out_ref[which, rows, :] = totals[which].astype(BF16)
+            parts.append(jnp.where(is_second, options[1], options[0]))
+        return jnp.concatenate(parts + [stat_of(f, slot) for f in later_stats[1:]], axis=1)
+
+    both = range(2)
+    rows = [slice(at * BLOCK, (at + 1) * BLOCK) for at in both]
+    queries = [gather(0, at) for at in both]
+    grads = [gather(1, at) for at in both]
+    stats = [gather_stats(2 * half + at) for at in both]
+    score = [dot(kv[0, rows[at], :], queries[at], NT) * factor for at in both]
+    grad_prob = [dot(kv[1, rows[at], :], grads[at], NT) for at in both]
+    score = [jnp.concatenate([s[:, :BLOCK] + causal, s[:, BLOCK:]], axis=1) for s in score]
+    prob = [jnp.exp(score[at] - stats[at][0:1]) for at in both]
+    grad_score = [(prob[at] * (grad_prob[at] - stats[at][1:2])).astype(BF16) for at in both]
+    prob_b = [p.astype(BF16) for p in prob]
+    grad_keys = [dot(grad_score[at], queries[at], NN) * factor for at in both]
+    grad_values = [dot(prob_b[at], grads[at], NN) for at in both]
+    for at in both:
+        out_ref[0, rows[at], :] = grad_keys[at].astype(BF16)
+        out_ref[1, rows[at], :] = grad_values[at].astype(BF16)
 
 
 def head_spec(a):
@@ -221,24 +221,23 @@
     )
 
 
-def key_side(half, where, kv, qg, stat, later, later_stats, returned):
+def key_side(half, where, kv, qg, stat, later, later_stats):
     rows, width = kv[0].shape[1], kv[0].shape[2]
     heads = width // HD
     half_of_whole = pl.BlockSpec((2, rows, HD), lambda h, w: (0, half, h))
     far = [f[-1] if len(f) == 1 else f[half] for f in later[1:]]
-    operands = [kv[half], *qg, stat, *later[0], *far, *later_stats, *returned]
+    operands = [kv[half], *qg, stat, *later[0], *far, *later_stats]
     in_specs = (
         [head_spec(a) for a in (kv[half], *qg)]
         + [stat_spec(stat)]
         + [head_spec(a) for a in later[0]]
         + [half_of_whole if len(f) == 1 else head_spec(f[half]) for f in later[1:]]
         + [stat_spec(a) for a in later_stats]
-        + [half_of_whole] * len(returned)
     )
     out = jax.ShapeDtypeStruct((2, rows, width), BF16)
     groups = (len(later[0]),) + (1,) * len(far)
     (result,) = call(
-        functools.partial(key_kernel, half, groups, len(returned)),
+        functools.partial(key_kernel, half, groups),
         where,
         operands,
         in_specs,
@@ -270,9 +269,21 @@
     two = shifted(rows, sign * 2)
     far = shifted(rows, sign * 32)
     four = shifted(two, sign * 2)
-    one = swapped(rows, two, 1, sign)
+    eight = shifted(four, sign * 4)
     sixteen = swapped(rows, far, 16, sign)
-    return [one, two, four, shifted(four, sign * 4), sixteen, far, shifted(far, sign * 32)]
+    two_last = two
+    if sign > 0:
+        two_last, eight = lax.optimization_barrier((two, eight))
+    one = swapped(rows, two_last, 1, sign)
+    return [one, two, four, eight, sixteen, far, shifted(far, sign * 32)]
+
+
+def exchange_stats(stat):
+    two, far = shifted(stat, -2), shifted(stat, -32)
+    direct = [shifted(stat, -by) for by in (64, 8, 4)]
+    one = swapped(stat, two, 1, -1)
+    sixteen = swapped(stat, far, 16, -1)
+    return [one, two, direct[2], direct[1], sixteen, far, direct[0]]
 
 
 def per_device(series, norm_gain, w_query, w_key, w_value, w_out, out_grad):
@@ -293,8 +304,7 @@
     unit_rows = series_f * inv_rms
     normed = (unit_rows * norm_gain).astype(BF16)
     normed_other = swap_tp(normed)
-    out_grad_later, normed_other = lax.optimization_barrier((out_grad, normed_other))
-    out_grad_other = swap_tp(out_grad_later)
+    out_grad_other = swap_tp(out_grad)
 
     def key_value(rows):
         return jnp.stack([matmul(rows, w_key).astype(BF16), matmul(rows, w_value).astype(BF16)])
@@ -315,16 +325,18 @@
     stat, later = lax.optimization_barrier((stat, later))
     later.insert(3, last)
     later = [(f,) for f in later]
-    later_stats = [shifted(stat, -(2**s)) for s in range(levels)]
+    later_stats = exchange_stats(stat)
     attn_other = swap_tp(matmul(mixed[half:], w_out).astype(BF16))
     attn_rows = matmul(mixed[:half], w_out) + attn_other.astype(F32)
     layer_out = (series_f + attn_rows).astype(BF16)
 
+    grad_queries = lax.optimization_barrier(matmul_t(grad_query, w_query))
+
     def back(at):
-        grad_kv = key_side(at, where, kv, qg, stat, later, later_stats, [])
+        grad_kv = key_side(at, where, kv, qg, stat, later, later_stats)
         rows = slice(at * half, (at + 1) * half)
         return (
-            matmul_t(grad_query[rows], w_query)
+            grad_queries[rows]
             + matmul_t(grad_kv[0], w_key)
             + matmul_t(grad_kv[1], w_value)
         )

time: 171 us -> 174 us (1.018)
  waiting for transfers between devices: 64.6 us -> 71.2 us
  other arithmetic: 11.5 us -> 8.29 us
  starting transfers between devices: 62.5 us -> 65 us
  Pallas kernels: 14.3 us -> 12.2 us
    ppermute x4 -> x6, waiting for transfers between devices: 0.01 us -> 9.41 us  [swapped(): return lax.ppermute(sent, 'seq', [(i, i ^ bit) for i in range(size)])]
    ppermute x4, starting transfers between devices: 10.1 us -> 14.1 us  [swap_tp(): return lax.ppermute(value, 'tp', [(0, 1), (1, 0)])]
    ppermute x17 -> x15, waiting for transfers between devices: 28.3 us -> 24.4 us  [shifted(): return lax.ppermute(value, 'seq', pairs)]
    ppermute x17 -> x15, starting transfers between devices: 50.6 us -> 48.3 us  [shifted(): return lax.ppermute(value, 'seq', pairs)]
    pallas_call x3, Pallas kernels: 14.3 us -> 12.2 us  [call(): pl.pallas_call(kernel, out_shape=outs, grid_spec=pltpu.PrefetchScalarGrid...]
    dot_general x8 -> x7, matrix products: 6.68 us -> 5.84 us  [matmul_t(): return lax.dot_general(a, b, NT, preferred_element_type=F32)]
  transfers between devices with their start and end apart: 25 -> 25, of which waited for: 7 -> 8; matrix products, arithmetic and copies ran while one was open for 11% -> 8% of each run, Pallas kernels for 8% -> 7%
where the time goes in v7:
time: 174 us; the launch traced here: 172 us
  waiting for transfers between devices  71.2 us (41%)
  starting transfers between devices  65 us (37%)
  Pallas kernels  12.2 us (7%)
  matrix products  11.9 us (7%)
  other arithmetic  8.29 us (5%)
    ppermute x15, starting transfers between devices, shifted(): return lax.ppermute(value, 'seq', pairs)  48.3 us
    ppermute x4, waiting for transfers between devices, swap_tp(): return lax.ppermute(value, 'tp', [(0, 1), (1, 0)])  37.4 us
    ppermute x15, waiting for transfers between devices, shifted(): return lax.ppermute(value, 'seq', pairs)  24.4 us
    ppermute x4, starting transfers between devices, swap_tp(): return lax.ppermute(value, 'tp', [(0, 1), (1, 0)])  14.1 us
    pallas_call x3, Pallas kernels, call(): pl.pallas_call(kernel, out_shape=outs, grid_spec=pltpu.PrefetchScalarGrid...  12.2 us
    ppermute x6, waiting for transfers between devices, swapped(): return lax.ppermute(sent, 'seq', [(i, i ^ bit) for i in range(size)])  9.41 us
    dot_general x8, matrix products, matmul(): return jnp.dot(a, b, preferred_element_type=F32)  6.1 us
    dot_general x7, matrix products, matmul_t(): return lax.dot_general(a, b, NT, preferred_element_type=F32)  5.84 us
  transfers between devices with their start and end apart: 25, of which 8 were waited for; matrix products, arithmetic and copies ran while one was open for 8% of the time, Pallas kernels for 7%

profile of v7, /device:TPU:24, one launch (start us, length us, event | category | flops | bytes accessed | tf_op | source)
XLA Modules:
  0.0 171.8 jit_solution(7134540388817397845)
XLA Ops:
  0.6 1.4 fusion.24
  2.0 1.2 fusion.18
  3.3 3.1 %collective-permute-start = (bf16[128,2048]{1,0:T(8,128)(2,1)S(1)}, bf16[128,2048]{1,0:T(8,128)(2,1)S(1)}, u32[]{:S(2)}, u32[]{:S(2)}) collective-permute-start(bf16[128,2048]{1,0:T(8,128)(2,1)S(1)} %fusion.18), channel_id=1, source_target_pairs={{0,1},{1,0},{2,3},{3,2},{4,5},{5,4},{6,7},{7,6},{8,9},{9,8},{10,11... | collective-permute-start | bytes 1572872 | tf_op jit(solution)/shard_map/ppermute | solution.py:29
  6.4 2.1 %fusion.15 = bf16[1,128,512]{2,1,0:T(8,128)(2,1)S(1)} fusion(bf16[128,2048]{1,0:T(8,128)(2,1)S(1)} %fusion.18, bf16[2048,512]{1,0:T(8,128)(2,1)} %param.12), kind=kOutput, calls=%fused_computation.29 | convolution fusion | flops 268500992 | bytes 2752512 | tf_op jit(solution)/shard_map/dot_general | solution.py:254
  8.5 0.5 fusion.14
  9.0 9.6 %collective-permute-done = bf16[128,2048]{1,0:T(8,128)(2,1)S(1)} collective-permute-done((bf16[128,2048]{1,0:T(8,128)(2,1)S(1)}, bf16[128,2048]{1,0:T(8,128)(2,1)S(1)}, u32[]{:S(2)}, u32[]{:S(2)}) %collective-permute-start) | collective-permute-done | bytes 524320 | tf_op jit(solution)/shard_map/ppermute | solution.py:29
  18.5 0.4 fusion.17
  19.0 0.4 fusion.16
  19.5 0.8 maximum_maximum_fusion
  20.3 3.9 %collective-permute-start.2 = (bf16[2,256,512]{2,1,0:T(8,128)(2,1)}, bf16[2,256,512]{2,1,0:T(8,128)(2,1)S(1)}, u32[]{:S(2)}, u32[]{:S(2)}) collective-permute-start(bf16[2,256,512]{2,1,0:T(8,128)(2,1)} %maximum_maximum_fusion), channel_id=1, source_target_pairs={{0,4},{2,6},{4,8},{6,10},{8,12},{10,14},{12,16},{14,18},{16,20},{1... | collective-permute-start | bytes 1572872 | tf_op jit(solution)/shard_map/ppermute | solution.py:25
  24.3 3.1 %collective-permute-start.1 = (bf16[128,2048]{1,0:T(8,128)(2,1)S(1)}, bf16[128,2048]{1,0:T(8,128)(2,1)S(1)}, u32[]{:S(2)}, u32[]{:S(2)}) collective-permute-start(bf16[128,2048]{1,0:T(8,128)(2,1)S(1)} %copy-done.9), channel_id=1, source_target_pairs={{0,1},{1,0},{2,3},{3,2},{4,5},{5,4},{6,7},{7,6},{8,9},{9,8},{10,11... | collective-permute-start | bytes 1572872 | tf_op jit(solution)/shard_map/ppermute | solution.py:29
  27.4 0.8 fusion.11
  28.3 0.4 fusion.10
  28.8 1.3 collective-permute-start.6
  30.1 10.7 %collective-permute-done.2.refs_5_ = bf16[2,256,512]{2,1,0:T(8,128)(2,1)S(1)} collective-permute-done((bf16[2,256,512]{2,1,0:T(8,128)(2,1)}, bf16[2,256,512]{2,1,0:T(8,128)(2,1)S(1)}, u32[]{:S(2)}, u32[]{:S(2)}) %collective-permute-start.2) | collective-permute-done | bytes 524320 | tf_op jit(solution)/shard_map/ppermute | solution.py:25
  40.8 1.9 %collective-permute-start.3 = (bf16[2,256,512]{2,1,0:T(8,128)(2,1)S(1)}, bf16[2,256,512]{2,1,0:T(8,128)(2,1)}, u32[]{:S(2)}, u32[]{:S(2)}) collective-permute-start(bf16[2,256,512]{2,1,0:T(8,128)(2,1)S(1)} %collective-permute-done.2.refs_5_), channel_id=1, source_target_pairs={{0,4},{2,6},{4,8},{6,10},{8,12},{10,14},{12,16},{14,18},{16,20},{1... | collective-permute-start | bytes 1572872 | tf_op jit(solution)/shard_map/ppermute | solution.py:25
  42.7 0.5 fusion.12
  43.2 17.7 %collective-permute-done.1 = bf16[128,2048]{1,0:T(8,128)(2,1)S(1)} collective-permute-done((bf16[128,2048]{1,0:T(8,128)(2,1)S(1)}, bf16[128,2048]{1,0:T(8,128)(2,1)S(1)}, u32[]{:S(2)}, u32[]{:S(2)}) %collective-permute-start.1) | collective-permute-done | bytes 524320 | tf_op jit(solution)/shard_map/ppermute | solution.py:29
  60.9 0.8 fusion.13
  61.8 0.7 copy-done.11
  62.4 0.8 maximum_maximum_fusion.1
  63.3 1.9 %collective-permute-start.10 = (bf16[2,256,512]{2,1,0:T(8,128)(2,1)}, bf16[2,256,512]{2,1,0:T(8,128)(2,1)S(1)}, u32[]{:S(2)}, u32[]{:S(2)}) collective-permute-start(bf16[2,256,512]{2,1,0:T(8,128)(2,1)} %maximum_maximum_fusion.1), channel_id=1, source_target_pairs={{4,0},{6,2},{8,4},{10,6},{12,8},{14,10},{16,12},{18,14},{20,16},{2... | collective-permute-start | bytes 1572872 | tf_op jit(solution)/shard_map/ppermute | solution.py:25
  65.2 1.9 %collective-permute-start.4 = (bf16[2,256,512]{2,1,0:T(8,128)(2,1)}, bf16[2,256,512]{2,1,0:T(8,128)(2,1)}, u32[]{:S(2)}, u32[]{:S(2)}) collective-permute-start(bf16[2,256,512]{2,1,0:T(8,128)(2,1)} %collective-permute-done.3.refs_6_), channel_id=1, source_target_pairs={{0,8},{2,10},{4,12},{6,14},{8,16},{10,18},{12,20},{14,22},{16,24},... | collective-permute-start | bytes 1572872 | tf_op jit(solution)/shard_map/ppermute | solution.py:25
  67.1 2.7 %collective-permute-start.13 = (bf16[2,256,512]{2,1,0:T(8,128)(2,1)}, bf16[2,256,512]{2,1,0:T(8,128)(2,1)S(1)}, u32[]{:S(2)}, u32[]{:S(2)}) collective-permute-start(bf16[2,256,512]{2,1,0:T(8,128)(2,1)} %maximum_maximum_fusion.1), channel_id=1, source_target_pairs={{64,0},{66,2},{68,4},{70,6},{72,8},{74,10},{76,12},{78,14},{80,16}... | collective-permute-start | bytes 1572872 | tf_op jit(solution)/shard_map/ppermute | solution.py:25
  69.9 0.1 broadcast_in_dim.21
  69.9 0.1 ge.23
  70.0 1.2 pad_maximum_fusion
  71.2 1.3 collective-permute-start.8
  72.5 4.6 %collective-permute-done.10.refs_5_ = bf16[2,256,512]{2,1,0:T(8,128)(2,1)S(1)} collective-permute-done((bf16[2,256,512]{2,1,0:T(8,128)(2,1)}, bf16[2,256,512]{2,1,0:T(8,128)(2,1)S(1)}, u32[]{:S(2)}, u32[]{:S(2)}) %collective-permute-start.10) | collective-permute-done | bytes 524320 | tf_op jit(solution)/shard_map/ppermute | solution.py:25
  77.2 5.7 %collective-permute-start.12 = (bf16[2,256,512]{2,1,0:T(8,128)(2,1)S(1)}, bf16[2,256,512]{2,1,0:T(8,128)(2,1)S(1)}, u32[]{:S(2)}, u32[]{:S(2)}) collective-permute-start(bf16[2,256,512]{2,1,0:T(8,128)(2,1)S(1)} %collective-permute-done.10.refs_5_), channel_id=1, source_target_pairs={{4,0},{6,2},{8,4},{10,6},{12,8},{14,10},{16,12},{18,14},{20,16},{2... | collective-permute-start | bytes 1572872 | tf_op jit(solution)/shard_map/ppermute | solution.py:25
  82.8 9.0 %collective-permute-done.4.refs_7_ = bf16[2,256,512]{2,1,0:T(8,128)(2,1)} collective-permute-done((bf16[2,256,512]{2,1,0:T(8,128)(2,1)}, bf16[2,256,512]{2,1,0:T(8,128)(2,1)}, u32[]{:S(2)}, u32[]{:S(2)}) %collective-permute-start.4) | collective-permute-done | bytes 524320 | tf_op jit(solution)/shard_map/ppermute | solution.py:25
  91.8 1.2 broadcast_select_fusion.1
  93.0 0.1 collective-permute-start.7
  93.1 0.1 collective-permute-start.5
  93.3 0.2 broadcast_select_fusion
  93.5 2.0 %collective-permute-start.14 = (bf16[2,256,512]{2,1,0:T(8,128)(2,1)S(1)}, bf16[2,256,512]{2,1,0:T(8,128)(2,1)S(1)}, u32[]{:S(2)}, u32[]{:S(2)}) collective-permute-start(bf16[2,256,512]{2,1,0:T(8,128)(2,1)S(1)} %get-tuple-element.26), channel_id=1, source_target_pairs={{0,32},{2,34},{4,36},{6,38},{8,40},{10,42},{12,44},{14,46},{16,48}... | collective-permute-start | bytes 1572872 | tf_op jit(solution)/shard_map/ppermute | solution.py:265
  95.5 0.2 collective-permute-start.11
  95.7 2.7 %collective-permute-start.15 = (bf16[2,256,512]{2,1,0:T(8,128)(2,1)S(1)}, bf16[2,256,512]{2,1,0:T(8,128)(2,1)S(1)}, u32[]{:S(2)}, u32[]{:S(2)}) collective-permute-start(bf16[2,256,512]{2,1,0:T(8,128)(2,1)S(1)} %collective-permute-done.13.refs_9_), channel_id=1, source_target_pairs={{64,0},{66,2},{68,4},{70,6},{72,8},{74,10},{76,12},{78,14},{80,16}... | collective-permute-start | bytes 1572872 | tf_op jit(solution)/shard_map/ppermute | solution.py:25
  98.4 0.1 compare_select_fusion.bias_ref
  98.6 9.4 %collective-permute-done.7.refs_8_ = bf16[2,256,512]{2,1,0:T(8,128)(2,1)S(1)} collective-permute-done((bf16[2,256,512]{2,1,0:T(8,128)(2,1)S(1)}, bf16[2,256,512]{2,1,0:T(8,128)(2,1)S(1)}, u32[]{:S(2)}, u32[]{:S(2)}) %collective-permute-start.7) | collective-permute-done | bytes 524320 | tf_op jit(solution)/shard_map/ppermute | solution.py:265
  108.0 1.9 %collective-permute-start.16 = (bf16[2,256,512]{2,1,0:T(8,128)(2,1)S(1)}, bf16[2,256,512]{2,1,0:T(8,128)(2,1)S(1)}, u32[]{:S(2)}, u32[]{:S(2)}) collective-permute-start(bf16[2,256,512]{2,1,0:T(8,128)(2,1)S(1)} %collective-permute-done.12.refs_6_), channel_id=1, source_target_pairs={{8,0},{10,2},{12,4},{14,6},{16,8},{18,10},{20,12},{22,14},{24,16},... | collective-permute-start | bytes 1572872 | tf_op jit(solution)/shard_map/ppermute | solution.py:25
  109.9 0.8 copy-done.21
  110.7 5.9 %query_side.1 = (bf16[256,512]{1,0:T(8,128)(2,1)S(1)}, bf16[256,512]{1,0:T(8,128)(2,1)S(1)}, f32[4,2,256]{2,1,0:T(2,128)S(1)}) custom-call(s32[1]{0:T(128)} %bitcast.where_ref, f32[4,1,640]{2,1,0:T(1,128)S(1)} %compare_select_fusion.bias_ref, bf16[2,128,512]{2,1,0:T(8,128)(2,1)S(1)} %get-tuple-element.34.refs_0_.refs_1_, ...), custom_call_target="tpu_custom_call" | custom-call | flops 671088640 | bytes 6291456 | tf_op jit(solution)/shard_map/query_side/pallas_call | solution.py:186
  116.7 3.1 %collective-permute-start.23 = (f32[4,2,256]{2,1,0:T(2,128)S(1)}, f32[4,2,256]{2,1,0:T(2,128)S(1)}, u32[]{:S(2)}, u32[]{:S(2)}) collective-permute-start(f32[4,2,256]{2,1,0:T(2,128)S(1)} %get-tuple-element.19.refs_3_), channel_id=1, source_target_pairs={{128,0},{130,2},{132,4},{134,6},{136,8},{138,10},{140,12},{142,14}... | collective-permute-start | bytes 24584 | tf_op jit(solution)/shard_map/ppermute | solution.py:25
  119.8 1.3 collective-permute-start.21
  121.1 3.6 %collective-permute-start.20 = (f32[4,2,256]{2,1,0:T(2,128)S(1)}, f32[4,2,256]{2,1,0:T(2,128)S(1)}, u32[]{:S(2)}, u32[]{:S(2)}) collective-permute-start(f32[4,2,256]{2,1,0:T(2,128)S(1)} %get-tuple-element.19.refs_3_), channel_id=1, source_target_pairs={{16,0},{18,2},{20,4},{22,6},{24,8},{26,10},{28,12},{30,14},{32,16}... | collective-permute-start | bytes 24584 | tf_op jit(solution)/shard_map/ppermute | solution.py:25
  124.7 13.2 %collective-permute-start.17 = (f32[4,2,256]{2,1,0:T(2,128)S(1)}, f32[4,2,256]{2,1,0:T(2,128)S(1)}, u32[]{:S(2)}, u32[]{:S(2)}) collective-permute-start(f32[4,2,256]{2,1,0:T(2,128)S(1)} %get-tuple-element.19.refs_3_), channel_id=1, source_target_pairs={{4,0},{6,2},{8,4},{10,6},{12,8},{14,10},{16,12},{18,14},{20,16},{2... | collective-permute-start | bytes 24584 | tf_op jit(solution)/shard_map/ppermute | solution.py:25
  137.9 0.8 fusion.31
  138.7 1.9 %collective-permute-start.19 = (f32[4,2,256]{2,1,0:T(2,128)S(1)}, f32[4,2,256]{2,1,0:T(2,128)S(1)}, u32[]{:S(2)}, u32[]{:S(2)}) collective-permute-start(f32[4,2,256]{2,1,0:T(2,128)S(1)} %get-tuple-element.19.refs_3_), channel_id=1, source_target_pairs={{8,0},{10,2},{12,4},{14,6},{16,8},{18,10},{20,12},{22,14},{24,16},... | collective-permute-start | bytes 24584 | tf_op jit(solution)/shard_map/ppermute | solution.py:25
  140.7 0.1 collective-permute-start.22
  140.8 0.1 collective-permute-start.18
  140.9 0.4 convolution_convert_fusion
  141.4 4.4 %collective-permute-start.9 = (bf16[128,2048]{1,0:T(8,128)(2,1)S(1)}, bf16[128,2048]{1,0:T(8,128)(2,1)S(1)}, u32[]{:S(2)}, u32[]{:S(2)}) collective-permute-start(bf16[128,2048]{1,0:T(8,128)(2,1)S(1)} %convolution_convert_fusion), channel_id=1, source_target_pairs={{0,1},{1,0},{2,3},{3,2},{4,5},{5,4},{6,7},{7,6},{8,9},{9,8},{10,11... | collective-permute-start | bytes 1572872 | tf_op jit(solution)/shard_map/ppermute | solution.py:29
  145.7 3.2 %key_side.3 = bf16[2,128,512]{2,1,0:T(8,128)(2,1)S(1)} custom-call(s32[1]{0:T(128)} %bitcast.where_ref, bf16[2,128,512]{2,1,0:T(8,128)(2,1)S(1)} %pad_maximum_fusion.3.refs_3_.refs_0_, bf16[2,128,512]{2,1,0:T(8,128)(2,1)S(1)} %get-tuple-element.34.refs_0_.refs_1_, bf16[2,128,512]{2,1,0:T(8,128)(2,1)S(1)} %pad_maximum_fusion.1.refs_1_.refs_2_, ...), custom_call_target="tpu_custom_call" | custom-call | flops 335544320 | bytes 6291456 | tf_op jit(solution)/shard_map/key_side/pallas_call | solution.py:186
  148.9 0.8 fusion.25
  149.8 0.8 fusion.6
  150.6 3.5 %collective-permute-start.24 = (bf16[128,2048]{1,0:T(8,128)(2,1)S(1)}, bf16[128,2048]{1,0:T(8,128)(2,1)S(1)}, u32[]{:S(2)}, u32[]{:S(2)}) collective-permute-start(bf16[128,2048]{1,0:T(8,128)(2,1)S(1)} %fusion.6), channel_id=1, source_target_pairs={{0,1},{1,0},{2,3},{3,2},{4,5},{5,4},{6,7},{7,6},{8,9},{9,8},{10,11... | collective-permute-start | bytes 1572872 | tf_op jit(solution)/shard_map/ppermute | solution.py:29
  154.1 3.1 %key_side.2 = bf16[2,128,512]{2,1,0:T(8,128)(2,1)S(1)} custom-call(s32[1]{0:T(128)} %bitcast.where_ref, bf16[2,128,512]{2,1,0:T(8,128)(2,1)S(1)} %get-tuple-element.35.refs_2_.refs_0_, bf16[2,128,512]{2,1,0:T(8,128)(2,1)S(1)} %get-tuple-element.34.refs_0_.refs_1_, bf16[2,128,512]{2,1,0:T(8,128)(2,1)S(1)} %pad_maximum_fusion.1.refs_1_.refs_2_, ...), custom_call_target="tpu_custom_call" | custom-call | flops 335544320 | bytes 6291456 | tf_op jit(solution)/shard_map/key_side/pallas_call | solution.py:186
  157.3 0.8 fusion.26
  158.1 0.4 collective-permute-done.9
  158.5 1.3 fusion.5
  159.8 9.7 %collective-permute-done.24 = bf16[128,2048]{1,0:T(8,128)(2,1)S(1)} collective-permute-done((bf16[128,2048]{1,0:T(8,128)(2,1)S(1)}, bf16[128,2048]{1,0:T(8,128)(2,1)S(1)}, u32[]{:S(2)}, u32[]{:S(2)}) %collective-permute-start.24) | collective-permute-done | bytes 524320 | tf_op jit(solution)/shard_map/ppermute | solution.py:29
  169.6 1.0 fusion.19
  170.6 1.2 fusion.23
  (69 shorter events, 0.2 us)
Async XLA Ops:
  0.6 7.8 %copy-start = (bf16[2048,512]{1,0:T(8,128)(2,1)S(1)}, bf16[2048,512]{1,0:T(8,128)(2,1)}, u32[]{:S(2)}) copy-start(bf16[2048,512]{1,0:T(8,128)(2,1)} %param.11) | copy-start | bytes 6291460
  3.3 15.3 %copy-start.1 = (bf16[2048,512]{1,0:T(8,128)(2,1)S(1)}, bf16[2048,512]{1,0:T(8,128)(2,1)}, u32[]{:S(2)}) copy-start(bf16[2048,512]{1,0:T(8,128)(2,1)} %param.12) | copy-start | bytes 6291460
  3.3 15.3 %collective-permute-start = (bf16[128,2048]{1,0:T(8,128)(2,1)S(1)}, bf16[128,2048]{1,0:T(8,128)(2,1)S(1)}, u32[]{:S(2)}, u32[]{:S(2)}) collective-permute-start(bf16[128,2048]{1,0:T(8,128)(2,1)S(1)} %fusion.18), channel_id=1, source_target_pairs={{0,1},{1,0},{2,3},{3,2},{4,5},{5,4},{6,7},{7,6},{8,9},{9,8},{10,11... | collective-permute-start | bytes 1572872 | tf_op jit(solution)/shard_map/ppermute | solution.py:29
  8.5 11.0 %copy-start.17 = (bf16[1,128,512]{2,1,0:T(8,128)(2,1)}, bf16[1,128,512]{2,1,0:T(8,128)(2,1)S(1)}, u32[]{:S(2)}) copy-start(bf16[1,128,512]{2,1,0:T(8,128)(2,1)S(1)} %fusion.15) | copy-start | bytes 393220
  9.0 10.5 %copy-start.18 = (bf16[1,128,512]{2,1,0:T(8,128)(2,1)}, bf16[1,128,512]{2,1,0:T(8,128)(2,1)S(1)}, u32[]{:S(2)}) copy-start(bf16[1,128,512]{2,1,0:T(8,128)(2,1)S(1)} %fusion.14) | copy-start | bytes 393220
  19.0 5.3 %copy-start.9 = (bf16[128,2048]{1,0:T(8,128)(2,1)S(1)}, bf16[128,2048]{1,0:T(8,128)(2,1)}, u32[]{:S(2)}) copy-start(bf16[128,2048]{1,0:T(8,128)(2,1)} %param.14) | copy-start | bytes 1572868
  19.0 8.4 %copy-start.3 = (bf16[512,2048]{1,0:T(8,128)(2,1)S(1)}, bf16[512,2048]{1,0:T(8,128)(2,1)}, u32[]{:S(2)}) copy-start(bf16[512,2048]{1,0:T(8,128)(2,1)} %param.13) | copy-start | bytes 6291460
  19.5 8.8 %copy-start.5 = (bf16[2048,512]{1,0:T(8,128)(2,1)S(1)}, bf16[2048,512]{1,0:T(8,128)(2,1)}, u32[]{:S(2)}) copy-start(bf16[2048,512]{1,0:T(8,128)(2,1)} %param.10) | copy-start | bytes 6291460
  20.3 20.5 %collective-permute-start.2 = (bf16[2,256,512]{2,1,0:T(8,128)(2,1)}, bf16[2,256,512]{2,1,0:T(8,128)(2,1)S(1)}, u32[]{:S(2)}, u32[]{:S(2)}) collective-permute-start(bf16[2,256,512]{2,1,0:T(8,128)(2,1)} %maximum_maximum_fusion), channel_id=1, source_target_pairs={{0,4},{2,6},{4,8},{6,10},{8,12},{10,14},{12,16},{14,18},{16,20},{1... | collective-permute-start | bytes 1572872 | tf_op jit(solution)/shard_map/ppermute | solution.py:25
  24.3 36.6 %collective-permute-start.1 = (bf16[128,2048]{1,0:T(8,128)(2,1)S(1)}, bf16[128,2048]{1,0:T(8,128)(2,1)S(1)}, u32[]{:S(2)}, u32[]{:S(2)}) collective-permute-start(bf16[128,2048]{1,0:T(8,128)(2,1)S(1)} %copy-done.9), channel_id=1, source_target_pairs={{0,1},{1,0},{2,3},{3,2},{4,5},{5,4},{6,7},{7,6},{8,9},{9,8},{10,11... | collective-permute-start | bytes 1572872 | tf_op jit(solution)/shard_map/ppermute | solution.py:29
  28.3 33.4 %copy-start.13 = (bf16[1,128,512]{2,1,0:T(8,128)(2,1)}, bf16[1,128,512]{2,1,0:T(8,128)(2,1)S(1)}, u32[]{:S(2)}) copy-start(bf16[1,128,512]{2,1,0:T(8,128)(2,1)S(1)} %fusion.11) | copy-start | bytes 393220
  28.7 33.0 %copy-start.15 = (bf16[1,128,512]{2,1,0:T(8,128)(2,1)}, bf16[1,128,512]{2,1,0:T(8,128)(2,1)S(1)}, u32[]{:S(2)}) copy-start(bf16[1,128,512]{2,1,0:T(8,128)(2,1)S(1)} %fusion.10) | copy-start | bytes 393220
  28.8 42.5 %collective-permute-start.6 = (bf16[2,256,512]{2,1,0:T(8,128)(2,1)}, bf16[2,256,512]{2,1,0:T(8,128)(2,1)}, u32[]{:S(2)}, u32[]{:S(2)}) collective-permute-start(bf16[2,256,512]{2,1,0:T(8,128)(2,1)} %maximum_maximum_fusion), channel_id=1, source_target_pairs={{0,64},{2,66},{4,68},{6,70},{8,72},{10,74},{12,76},{14,78},{16,80}... | collective-permute-start | bytes 1572872 | tf_op jit(solution)/shard_map/ppermute | solution.py:25
  40.8 20.9 %copy-start.8 = (bf16[2,256,512]{2,1,0:T(8,128)(2,1)}, bf16[2,256,512]{2,1,0:T(8,128)(2,1)S(1)}, u32[]{:S(2)}) copy-start(bf16[2,256,512]{2,1,0:T(8,128)(2,1)S(1)} %collective-permute-done.2.refs_5_) | copy-start | bytes 1572868
  40.8 24.4 %collective-permute-start.3 = (bf16[2,256,512]{2,1,0:T(8,128)(2,1)S(1)}, bf16[2,256,512]{2,1,0:T(8,128)(2,1)}, u32[]{:S(2)}, u32[]{:S(2)}) collective-permute-start(bf16[2,256,512]{2,1,0:T(8,128)(2,1)S(1)} %collective-permute-done.2.refs_5_), channel_id=1, source_target_pairs={{0,4},{2,6},{4,8},{6,10},{8,12},{10,14},{12,16},{14,18},{16,20},{1... | collective-permute-start | bytes 1572872 | tf_op jit(solution)/shard_map/ppermute | solution.py:25
  43.2 26.6 %copy-start.23 = (s32[10]{0:T(128)S(1)}, s32[10]{0:T(128)}, u32[]{:S(2)}) copy-start(s32[10]{0:T(128)} %constant.89.clone) | copy-start | bytes 124
  61.7 0.7 copy-start.11
  63.3 13.9 %collective-permute-start.10 = (bf16[2,256,512]{2,1,0:T(8,128)(2,1)}, bf16[2,256,512]{2,1,0:T(8,128)(2,1)S(1)}, u32[]{:S(2)}, u32[]{:S(2)}) collective-permute-start(bf16[2,256,512]{2,1,0:T(8,128)(2,1)} %maximum_maximum_fusion.1), channel_id=1, source_target_pairs={{4,0},{6,2},{8,4},{10,6},{12,8},{14,10},{16,12},{18,14},{20,16},{2... | collective-permute-start | bytes 1572872 | tf_op jit(solution)/shard_map/ppermute | solution.py:25
  65.2 26.6 %collective-permute-start.4 = (bf16[2,256,512]{2,1,0:T(8,128)(2,1)}, bf16[2,256,512]{2,1,0:T(8,128)(2,1)}, u32[]{:S(2)}, u32[]{:S(2)}) collective-permute-start(bf16[2,256,512]{2,1,0:T(8,128)(2,1)} %collective-permute-done.3.refs_6_), channel_id=1, source_target_pairs={{0,8},{2,10},{4,12},{6,14},{8,16},{10,18},{12,20},{14,22},{16,24},... | collective-permute-start | bytes 1572872 | tf_op jit(solution)/shard_map/ppermute | solution.py:25
  67.1 26.1 %collective-permute-start.13 = (bf16[2,256,512]{2,1,0:T(8,128)(2,1)}, bf16[2,256,512]{2,1,0:T(8,128)(2,1)S(1)}, u32[]{:S(2)}, u32[]{:S(2)}) collective-permute-start(bf16[2,256,512]{2,1,0:T(8,128)(2,1)} %maximum_maximum_fusion.1), channel_id=1, source_target_pairs={{64,0},{66,2},{68,4},{70,6},{72,8},{74,10},{76,12},{78,14},{80,16}... | collective-permute-start | bytes 1572872 | tf_op jit(solution)/shard_map/ppermute | solution.py:25
  70.0 23.2 %copy-start.12 = (bf16[1,128,512]{2,1,0:T(8,128)(2,1)S(1)}, bf16[1,128,512]{2,1,0:T(8,128)(2,1)}, u32[]{:S(2)}) copy-start(bf16[1,128,512]{2,1,0:T(8,128)(2,1)} %copy-done.11) | copy-start | bytes 393220
  70.0 23.2 %copy-start.14 = (bf16[1,128,512]{2,1,0:T(8,128)(2,1)S(1)}, bf16[1,128,512]{2,1,0:T(8,128)(2,1)}, u32[]{:S(2)}) copy-start(bf16[1,128,512]{2,1,0:T(8,128)(2,1)} %copy-done.13) | copy-start | bytes 393220
  70.0 23.3 %copy-start.16 = (bf16[1,128,512]{2,1,0:T(8,128)(2,1)S(1)}, bf16[1,128,512]{2,1,0:T(8,128)(2,1)}, u32[]{:S(2)}) copy-start(bf16[1,128,512]{2,1,0:T(8,128)(2,1)} %copy-done.15) | copy-start | bytes 393220
  71.2 24.3 %collective-permute-start.8 = (bf16[2,256,512]{2,1,0:T(8,128)(2,1)}, bf16[2,256,512]{2,1,0:T(8,128)(2,1)S(1)}, u32[]{:S(2)}, u32[]{:S(2)}) collective-permute-start(bf16[2,256,512]{2,1,0:T(8,128)(2,1)} %collective-permute-done.6.refs_9_), channel_id=1, source_target_pairs={{0,64},{2,66},{4,68},{6,70},{8,72},{10,74},{12,76},{14,78},{16,80}... | collective-permute-start | bytes 1572872 | tf_op jit(solution)/shard_map/ppermute | solution.py:25
  77.2 18.6 %collective-permute-start.12 = (bf16[2,256,512]{2,1,0:T(8,128)(2,1)S(1)}, bf16[2,256,512]{2,1,0:T(8,128)(2,1)S(1)}, u32[]{:S(2)}, u32[]{:S(2)}) collective-permute-start(bf16[2,256,512]{2,1,0:T(8,128)(2,1)S(1)} %collective-permute-done.10.refs_5_), channel_id=1, source_target_pairs={{4,0},{6,2},{8,4},{10,6},{12,8},{14,10},{16,12},{18,14},{20,16},{2... | collective-permute-start | bytes 1572872 | tf_op jit(solution)/shard_map/ppermute | solution.py:25
  93.0 14.9 %collective-permute-start.7 = (bf16[2,256,512]{2,1,0:T(8,128)(2,1)S(1)}, bf16[2,256,512]{2,1,0:T(8,128)(2,1)S(1)}, u32[]{:S(2)}, u32[]{:S(2)}) collective-permute-start(bf16[2,256,512]{2,1,0:T(8,128)(2,1)S(1)} %get-tuple-element.28), channel_id=1, source_target_pairs={{0,32},{2,34},{4,36},{6,38},{8,40},{10,42},{12,44},{14,46},{16,48}... | collective-permute-start | bytes 1572872 | tf_op jit(solution)/shard_map/ppermute | solution.py:265
  93.1 16.8 %collective-permute-start.5 = (bf16[2,256,512]{2,1,0:T(8,128)(2,1)S(1)}, bf16[2,256,512]{2,1,0:T(8,128)(2,1)S(1)}, u32[]{:S(2)}, u32[]{:S(2)}) collective-permute-start(bf16[2,256,512]{2,1,0:T(8,128)(2,1)S(1)} %get-tuple-element.29), channel_id=1, source_target_pairs={{0,2},{2,0},{4,6},{6,4},{8,10},{10,8},{12,14},{14,12},{16,18},{18,... | collective-permute-start | bytes 1572872 | tf_op jit(solution)/shard_map/ppermute | solution.py:265
  93.5 23.1 %collective-permute-start.14 = (bf16[2,256,512]{2,1,0:T(8,128)(2,1)S(1)}, bf16[2,256,512]{2,1,0:T(8,128)(2,1)S(1)}, u32[]{:S(2)}, u32[]{:S(2)}) collective-permute-start(bf16[2,256,512]{2,1,0:T(8,128)(2,1)S(1)} %get-tuple-element.26), channel_id=1, source_target_pairs={{0,32},{2,34},{4,36},{6,38},{8,40},{10,42},{12,44},{14,46},{16,48}... | collective-permute-start | bytes 1572872 | tf_op jit(solution)/shard_map/ppermute | solution.py:265
  95.5 14.4 %copy-start.19 = (bf16[2,256,512]{2,1,0:T(8,128)(2,1)}, bf16[2,256,512]{2,1,0:T(8,128)(2,1)S(1)}, u32[]{:S(2)}) copy-start(bf16[2,256,512]{2,1,0:T(8,128)(2,1)S(1)} %collective-permute-done.8.refs_10_) | copy-start | bytes 1572868
  95.5 21.2 %collective-permute-start.11 = (bf16[2,256,512]{2,1,0:T(8,128)(2,1)S(1)}, bf16[2,256,512]{2,1,0:T(8,128)(2,1)S(1)}, u32[]{:S(2)}, u32[]{:S(2)}) collective-permute-start(bf16[2,256,512]{2,1,0:T(8,128)(2,1)S(1)} %get-tuple-element.27), channel_id=1, source_target_pairs={{0,2},{2,0},{4,6},{6,4},{8,10},{10,8},{12,14},{14,12},{16,18},{18,... | collective-permute-start | bytes 1572872 | tf_op jit(solution)/shard_map/ppermute | solution.py:265
  95.7 20.9 %collective-permute-start.15 = (bf16[2,256,512]{2,1,0:T(8,128)(2,1)S(1)}, bf16[2,256,512]{2,1,0:T(8,128)(2,1)S(1)}, u32[]{:S(2)}, u32[]{:S(2)}) collective-permute-start(bf16[2,256,512]{2,1,0:T(8,128)(2,1)S(1)} %collective-permute-done.13.refs_9_), channel_id=1, source_target_pairs={{64,0},{66,2},{68,4},{70,6},{72,8},{74,10},{76,12},{78,14},{80,16}... | collective-permute-start | bytes 1572872 | tf_op jit(solution)/shard_map/ppermute | solution.py:25
  108.0 2.0 %copy-start.20 = (bf16[2,256,512]{2,1,0:T(8,128)(2,1)}, bf16[2,256,512]{2,1,0:T(8,128)(2,1)S(1)}, u32[]{:S(2)}) copy-start(bf16[2,256,512]{2,1,0:T(8,128)(2,1)S(1)} %collective-permute-done.7.refs_8_) | copy-start | bytes 1572868
  108.0 32.8 %collective-permute-start.16 = (bf16[2,256,512]{2,1,0:T(8,128)(2,1)S(1)}, bf16[2,256,512]{2,1,0:T(8,128)(2,1)S(1)}, u32[]{:S(2)}, u32[]{:S(2)}) collective-permute-start(bf16[2,256,512]{2,1,0:T(8,128)(2,1)S(1)} %collective-permute-done.12.refs_6_), channel_id=1, source_target_pairs={{8,0},{10,2},{12,4},{14,6},{16,8},{18,10},{20,12},{22,14},{24,16},... | collective-permute-start | bytes 1572872 | tf_op jit(solution)/shard_map/ppermute | solution.py:25
  109.9 0.8 copy-start.21
  110.7 27.2 %copy-start.6 = (bf16[2048,512]{1,0:T(8,128)(2,1)S(1)}, bf16[2048,512]{1,0:T(8,128)(2,1)}, u32[]{:S(2)}) copy-start(bf16[2048,512]{1,0:T(8,128)(2,1)} %param.10) | copy-start | bytes 6291460
  116.7 24.7 %collective-permute-start.23 = (f32[4,2,256]{2,1,0:T(2,128)S(1)}, f32[4,2,256]{2,1,0:T(2,128)S(1)}, u32[]{:S(2)}, u32[]{:S(2)}) collective-permute-start(f32[4,2,256]{2,1,0:T(2,128)S(1)} %get-tuple-element.19.refs_3_), channel_id=1, source_target_pairs={{128,0},{130,2},{132,4},{134,6},{136,8},{138,10},{140,12},{142,14}... | collective-permute-start | bytes 24584 | tf_op jit(solution)/shard_map/ppermute | solution.py:25
  119.8 18.9 %collective-permute-start.21 = (f32[4,2,256]{2,1,0:T(2,128)S(1)}, f32[4,2,256]{2,1,0:T(2,128)S(1)}, u32[]{:S(2)}, u32[]{:S(2)}) collective-permute-start(f32[4,2,256]{2,1,0:T(2,128)S(1)} %get-tuple-element.19.refs_3_), channel_id=1, source_target_pairs={{64,0},{66,2},{68,4},{70,6},{72,8},{74,10},{76,12},{78,14},{80,16}... | collective-permute-start | bytes 24584 | tf_op jit(solution)/shard_map/ppermute | solution.py:25
  121.1 24.6 %collective-permute-start.20 = (f32[4,2,256]{2,1,0:T(2,128)S(1)}, f32[4,2,256]{2,1,0:T(2,128)S(1)}, u32[]{:S(2)}, u32[]{:S(2)}) collective-permute-start(f32[4,2,256]{2,1,0:T(2,128)S(1)} %get-tuple-element.19.refs_3_), channel_id=1, source_target_pairs={{16,0},{18,2},{20,4},{22,6},{24,8},{26,10},{28,12},{30,14},{32,16}... | collective-permute-start | bytes 24584 | tf_op jit(solution)/shard_map/ppermute | solution.py:25
  124.7 16.0 %collective-permute-start.17 = (f32[4,2,256]{2,1,0:T(2,128)S(1)}, f32[4,2,256]{2,1,0:T(2,128)S(1)}, u32[]{:S(2)}, u32[]{:S(2)}) collective-permute-start(f32[4,2,256]{2,1,0:T(2,128)S(1)} %get-tuple-element.19.refs_3_), channel_id=1, source_target_pairs={{4,0},{6,2},{8,4},{10,6},{12,8},{14,10},{16,12},{18,14},{20,16},{2... | collective-permute-start | bytes 24584 | tf_op jit(solution)/shard_map/ppermute | solution.py:25
  137.9 3.0 %copy-start.4 = (bf16[512,2048]{1,0:T(8,128)(2,1)S(1)}, bf16[512,2048]{1,0:T(8,128)(2,1)}, u32[]{:S(2)}) copy-start(bf16[512,2048]{1,0:T(8,128)(2,1)} %param.13) | copy-start | bytes 6291460
  138.7 7.0 %collective-permute-start.19 = (f32[4,2,256]{2,1,0:T(2,128)S(1)}, f32[4,2,256]{2,1,0:T(2,128)S(1)}, u32[]{:S(2)}, u32[]{:S(2)}) collective-permute-start(f32[4,2,256]{2,1,0:T(2,128)S(1)} %get-tuple-element.19.refs_3_), channel_id=1, source_target_pairs={{8,0},{10,2},{12,4},{14,6},{16,8},{18,10},{20,12},{22,14},{24,16},... | collective-permute-start | bytes 24584 | tf_op jit(solution)/shard_map/ppermute | solution.py:25
  140.7 5.1 %collective-permute-start.22 = (f32[4,2,256]{2,1,0:T(2,128)S(1)}, f32[4,2,256]{2,1,0:T(2,128)S(1)}, u32[]{:S(2)}, u32[]{:S(2)}) collective-permute-start(f32[4,2,256]{2,1,0:T(2,128)S(1)} %bitcast.64), channel_id=1, source_target_pairs={{0,32},{2,34},{4,36},{6,38},{8,40},{10,42},{12,44},{14,46},{16,48}... | collective-permute-start | bytes 24584 | tf_op jit(solution)/shard_map/ppermute | solution.py:265
  140.8 5.0 %collective-permute-start.18 = (f32[4,2,256]{2,1,0:T(2,128)S(1)}, f32[4,2,256]{2,1,0:T(2,128)S(1)}, u32[]{:S(2)}, u32[]{:S(2)}) collective-permute-start(f32[4,2,256]{2,1,0:T(2,128)S(1)} %bitcast.63), channel_id=1, source_target_pairs={{0,2},{2,0},{4,6},{6,4},{8,10},{10,8},{12,14},{14,12},{16,18},{18,... | collective-permute-start | bytes 24584 | tf_op jit(solution)/shard_map/ppermute | solution.py:265
  141.3 7.6 %copy-start.2 = (bf16[2048,512]{1,0:T(8,128)(2,1)S(1)}, bf16[2048,512]{1,0:T(8,128)(2,1)}, u32[]{:S(2)}) copy-start(bf16[2048,512]{1,0:T(8,128)(2,1)} %param.12) | copy-start | bytes 6291460
  141.4 17.1 %collective-permute-start.9 = (bf16[128,2048]{1,0:T(8,128)(2,1)S(1)}, bf16[128,2048]{1,0:T(8,128)(2,1)S(1)}, u32[]{:S(2)}, u32[]{:S(2)}) collective-permute-start(bf16[128,2048]{1,0:T(8,128)(2,1)S(1)} %convolution_convert_fusion), channel_id=1, source_target_pairs={{0,1},{1,0},{2,3},{3,2},{4,5},{5,4},{6,7},{7,6},{8,9},{9,8},{10,11... | collective-permute-start | bytes 1572872 | tf_op jit(solution)/shard_map/ppermute | solution.py:29
  150.6 19.0 %collective-permute-start.24 = (bf16[128,2048]{1,0:T(8,128)(2,1)S(1)}, bf16[128,2048]{1,0:T(8,128)(2,1)S(1)}, u32[]{:S(2)}, u32[]{:S(2)}) collective-permute-start(bf16[128,2048]{1,0:T(8,128)(2,1)S(1)} %fusion.6), channel_id=1, source_target_pairs={{0,1},{1,0},{2,3},{3,2},{4,5},{5,4},{6,7},{7,6},{8,9},{9,8},{10,11... | collective-permute-start | bytes 1572872 | tf_op jit(solution)/shard_map/ppermute | solution.py:29
  157.3 1.2 copy-start.7
  158.1 11.5 %copy-start.22 = (f32[2048]{0:T(1024)S(1)}, f32[2048]{0:T(1024)}, u32[]{:S(2)}) copy-start(f32[2048]{0:T(1024)} %param.9) | copy-start | bytes 24580
  159.8 10.8 %copy-start.10 = (bf16[128,2048]{1,0:T(8,128)(2,1)S(1)}, bf16[128,2048]{1,0:T(8,128)(2,1)}, u32[]{:S(2)}) copy-start(bf16[128,2048]{1,0:T(8,128)(2,1)} %param.14) | copy-start | bytes 1572868

commit v8 on v7

--- a/solution.py
+++ b/solution.py
@@ -191,9 +191,7 @@
         ),
         compiler_params=pltpu.CompilerParams(vmem_limit_bytes=10 * 2**20),
         cost_estimate=pl.CostEstimate(
-            flops=4 * 2 * rows * keys * HD * heads,
-            bytes_accessed=6 * 2**20,
-            transcendentals=rows * keys * heads,
+            flops=rows * keys, bytes_accessed=2**16, transcendentals=0
         ),
         name=name,
     )(where, *operands)
@@ -271,9 +269,7 @@
     four = shifted(two, sign * 2)
     eight = shifted(four, sign * 4)
     sixteen = swapped(rows, far, 16, sign)
-    two_last = two
-    if sign > 0:
-        two_last, eight = lax.optimization_barrier((two, eight))
+    two_last, eight = lax.optimization_barrier((two, eight))
     one = swapped(rows, two_last, 1, sign)
     return [one, two, four, eight, sixteen, far, shifted(far, sign * 32)]
 
@@ -303,8 +299,7 @@
     inv_rms = lax.rsqrt(jnp.mean(series_f * series_f, axis=-1, keepdims=True) + EPS)
     unit_rows = series_f * inv_rms
     normed = (unit_rows * norm_gain).astype(BF16)
-    normed_other = swap_tp(normed)
-    out_grad_other = swap_tp(out_grad)
+    normed_other, out_grad_other = swap_tp(jnp.stack([normed, out_grad]))
 
     def key_value(rows):
         return jnp.stack([matmul(rows, w_key).astype(BF16), matmul(rows, w_value).astype(BF16)])
@@ -316,14 +311,13 @@
 
     kv = (key_value(normed), key_value(normed_other))
     qg = (query_grad(normed, out_grad), query_grad(normed_other, out_grad_other))
-    kv_all = jnp.concatenate(kv, axis=1)
-    qg_all = jnp.concatenate(qg, axis=1)
+    kv_all, qg_all = lax.optimization_barrier(
+        (jnp.concatenate(kv, axis=1), jnp.concatenate(qg, axis=1))
+    )
     fetched = exchange(kv_all, 1)
     later = exchange(qg_all, -1)
     mixed, grad_query, stat = query_side(where, bias, qg, kv, [(f,) for f in fetched], 0)
-    last = later.pop(3)
     stat, later = lax.optimization_barrier((stat, later))
-    later.insert(3, last)
     later = [(f,) for f in later]
     later_stats = exchange_stats(stat)
     attn_other = swap_tp(matmul(mixed[half:], w_out).astype(BF16))

time: 174 us -> 174 us (level)
  waiting for transfers between devices: 71.2 us -> 64.3 us
  other arithmetic: 8.29 us -> 13.9 us
  starting transfers between devices: 65 us -> 67.3 us
  Pallas kernels: 12.2 us -> 14.1 us
    ppermute x15, starting transfers between devices: 48.3 us -> 55.6 us  [shifted(): return lax.ppermute(value, 'seq', pairs)]
    ppermute x4 -> x3, starting transfers between devices: 14.1 us -> 7.35 us  [swap_tp(): return lax.ppermute(value, 'tp', [(0, 1), (1, 0)])]
    ppermute x4 -> x3, waiting for transfers between devices: 37.4 us -> 30.9 us  [swap_tp(): return lax.ppermute(value, 'tp', [(0, 1), (1, 0)])]
    ppermute x6, waiting for transfers between devices: 9.41 us -> 4.94 us  [swapped(): return lax.ppermute(sent, 'seq', [(i, i ^ bit) for i in range(size)])]
    ppermute x15, waiting for transfers between devices: 24.4 us -> 28.5 us  [shifted(): return lax.ppermute(value, 'seq', pairs)]
    another operation x1 -> x2, other arithmetic: 0.03 us -> 2.6 us  [per_device(): normed_other, out_grad_other = swap_tp(jnp.stack([normed, out_grad]))]
    select_n x2, other arithmetic: 0.24 us -> 2.1 us  [swapped(): jnp.where(high, own, passed)]
    pallas_call x3, Pallas kernels: 12.2 us -> 14.1 us  [call(): pl.pallas_call(kernel, out_shape=outs, grid_spec=pltpu.PrefetchScalarGrid...]
  transfers between devices with their start and end apart: 25 -> 24, of which waited for: 8 -> 11; matrix products, arithmetic and copies ran while one was open for 8% -> 9% of each run, Pallas kernels for 7% -> 8%
where the time goes in v8:
time: 174 us; the launch traced here: 173 us
  starting transfers between devices  67.3 us (39%)
  waiting for transfers between devices  64.3 us (37%)
  Pallas kernels  14.1 us (8%)
  other arithmetic  13.9 us (8%)
  matrix products  10.5 us (6%)
  local copies, waits for them, and re-layouts  1.97 us (1%)
    ppermute x15, starting transfers between devices, shifted(): return lax.ppermute(value, 'seq', pairs)  55.6 us
    ppermute x3, waiting for transfers between devices, swap_tp(): return lax.ppermute(value, 'tp', [(0, 1), (1, 0)])  30.9 us
    ppermute x15, waiting for transfers between devices, shifted(): return lax.ppermute(value, 'seq', pairs)  28.5 us
    pallas_call x3, Pallas kernels, call(): pl.pallas_call(kernel, out_shape=outs, grid_spec=pltpu.PrefetchScalarGrid...  14.1 us
    ppermute x3, starting transfers between devices, swap_tp(): return lax.ppermute(value, 'tp', [(0, 1), (1, 0)])  7.35 us
    dot_general x7, matrix products, matmul_t(): return lax.dot_general(a, b, NT, preferred_element_type=F32)  5.84 us
    ppermute x6, waiting for transfers between devices, swapped(): return lax.ppermute(sent, 'seq', [(i, i ^ bit) for i in range(size)])  4.94 us
    dot_general x8, matrix products, matmul(): return jnp.dot(a, b, preferred_element_type=F32)  4.66 us
  transfers between devices with their start and end apart: 24, of which 11 were waited for; matrix products, arithmetic and copies ran while one was open for 9% of the time, Pallas kernels for 8%

profile of v8, /device:TPU:24, one launch (start us, length us, event | category | flops | bytes accessed | tf_op | source)
XLA Modules:
  0.0 173.3 jit_solution(18287168118576575447)
XLA Ops:
  0.6 0.0 copy-start
  0.7 1.4 fusion.19
  2.1 1.3 fusion.35
  3.4 1.3 pad_maximum_fusion
  4.7 3.1 %collective-permute-start = (bf16[2,128,2048]{2,1,0:T(8,128)(2,1)S(1)}, bf16[2,128,2048]{2,1,0:T(8,128)(2,1)S(1)}, u32[]{:S(2)}, u32[]{:S(2)}) collective-permute-start(bf16[2,128,2048]{2,1,0:T(8,128)(2,1)S(1)} %pad_maximum_fusion), channel_id=1, source_target_pairs={{0,1},{1,0},{2,3},{3,2},{4,5},{5,4},{6,7},{7,6},{8,9},{9,8},{10,11... | collective-permute-start | bytes 3145736 | tf_op jit(solution)/shard_map/ppermute | solution.py:29
  7.8 0.9 fusion.6
  8.7 0.5 fusion.9
  9.3 0.5 fusion.10
  9.8 1.1 copy-done.7
  10.9 0.5 fusion.5
  11.4 19.7 %collective-permute-done = bf16[2,128,2048]{2,1,0:T(8,128)(2,1)S(1)} collective-permute-done((bf16[2,128,2048]{2,1,0:T(8,128)(2,1)S(1)}, bf16[2,128,2048]{2,1,0:T(8,128)(2,1)S(1)}, u32[]{:S(2)}, u32[]{:S(2)}) %collective-permute-start) | collective-permute-done | bytes 1048608 | tf_op jit(solution)/shard_map/ppermute | solution.py:29
  31.2 0.4 fusion.11
  31.6 0.5 fusion.12
  32.1 0.8 fusion.8
  33.0 0.4 fusion.7
  33.5 1.0 maximum_maximum_fusion
  34.5 3.8 %collective-permute-start.1 = (bf16[2,256,512]{2,1,0:T(8,128)(2,1)}, bf16[2,256,512]{2,1,0:T(8,128)(2,1)S(1)}, u32[]{:S(2)}, u32[]{:S(2)}) collective-permute-start(bf16[2,256,512]{2,1,0:T(8,128)(2,1)} %get-tuple-element.19), channel_id=1, source_target_pairs={{0,4},{2,6},{4,8},{6,10},{8,12},{10,14},{12,16},{14,18},{16,20},{1... | collective-permute-start | bytes 1572872 | tf_op jit(solution)/shard_map/ppermute | solution.py:25
  38.4 7.0 %collective-permute-start.9 = (bf16[2,256,512]{2,1,0:T(8,128)(2,1)}, bf16[2,256,512]{2,1,0:T(8,128)(2,1)S(1)}, u32[]{:S(2)}, u32[]{:S(2)}) collective-permute-start(bf16[2,256,512]{2,1,0:T(8,128)(2,1)} %get-tuple-element.25), channel_id=1, source_target_pairs={{4,0},{6,2},{8,4},{10,6},{12,8},{14,10},{16,12},{18,14},{20,16},{2... | collective-permute-start | bytes 1572872 | tf_op jit(solution)/shard_map/ppermute | solution.py:25
  45.3 9.3 %collective-permute-done.1.refs_5_ = bf16[2,256,512]{2,1,0:T(8,128)(2,1)S(1)} collective-permute-done((bf16[2,256,512]{2,1,0:T(8,128)(2,1)}, bf16[2,256,512]{2,1,0:T(8,128)(2,1)S(1)}, u32[]{:S(2)}, u32[]{:S(2)}) %collective-permute-start.1) | collective-permute-done | bytes 524320 | tf_op jit(solution)/shard_map/ppermute | solution.py:25
  54.6 1.9 %collective-permute-start.2 = (bf16[2,256,512]{2,1,0:T(8,128)(2,1)S(1)}, bf16[2,256,512]{2,1,0:T(8,128)(2,1)}, u32[]{:S(2)}, u32[]{:S(2)}) collective-permute-start(bf16[2,256,512]{2,1,0:T(8,128)(2,1)S(1)} %collective-permute-done.1.refs_5_), channel_id=1, source_target_pairs={{0,4},{2,6},{4,8},{6,10},{8,12},{10,14},{12,16},{14,18},{16,20},{1... | collective-permute-start | bytes 1572872 | tf_op jit(solution)/shard_map/ppermute | solution.py:25
  56.6 6.9 %collective-permute-start.10 = (bf16[2,256,512]{2,1,0:T(8,128)(2,1)S(1)}, bf16[2,256,512]{2,1,0:T(8,128)(2,1)}, u32[]{:S(2)}, u32[]{:S(2)}) collective-permute-start(bf16[2,256,512]{2,1,0:T(8,128)(2,1)S(1)} %collective-permute-done.9.refs_5_), channel_id=1, source_target_pairs={{4,0},{6,2},{8,4},{10,6},{12,8},{14,10},{16,12},{18,14},{20,16},{2... | collective-permute-start | bytes 1572872 | tf_op jit(solution)/shard_map/ppermute | solution.py:25
  63.5 1.3 collective-permute-start.5
  64.8 4.6 %collective-permute-start.13 = (bf16[2,256,512]{2,1,0:T(8,128)(2,1)}, bf16[2,256,512]{2,1,0:T(8,128)(2,1)S(1)}, u32[]{:S(2)}, u32[]{:S(2)}) collective-permute-start(bf16[2,256,512]{2,1,0:T(8,128)(2,1)} %get-tuple-element.25), channel_id=1, source_target_pairs={{64,0},{66,2},{68,4},{70,6},{72,8},{74,10},{76,12},{78,14},{80,16}... | collective-permute-start | bytes 1572872 | tf_op jit(solution)/shard_map/ppermute | solution.py:25
  69.4 2.5 %collective-permute-done.2.refs_6_ = bf16[2,256,512]{2,1,0:T(8,128)(2,1)} collective-permute-done((bf16[2,256,512]{2,1,0:T(8,128)(2,1)S(1)}, bf16[2,256,512]{2,1,0:T(8,128)(2,1)}, u32[]{:S(2)}, u32[]{:S(2)}) %collective-permute-start.2) | collective-permute-done | bytes 524320 | tf_op jit(solution)/shard_map/ppermute | solution.py:25
  71.9 1.9 %collective-permute-start.3 = (bf16[2,256,512]{2,1,0:T(8,128)(2,1)}, bf16[2,256,512]{2,1,0:T(8,128)(2,1)}, u32[]{:S(2)}, u32[]{:S(2)}) collective-permute-start(bf16[2,256,512]{2,1,0:T(8,128)(2,1)} %collective-permute-done.2.refs_6_), channel_id=1, source_target_pairs={{0,8},{2,10},{4,12},{6,14},{8,16},{10,18},{12,20},{14,22},{16,24},... | collective-permute-start | bytes 1572872 | tf_op jit(solution)/shard_map/ppermute | solution.py:25
  73.8 7.8 %collective-permute-start.11 = (bf16[2,256,512]{2,1,0:T(8,128)(2,1)}, bf16[2,256,512]{2,1,0:T(8,128)(2,1)}, u32[]{:S(2)}, u32[]{:S(2)}) collective-permute-start(bf16[2,256,512]{2,1,0:T(8,128)(2,1)} %collective-permute-done.10.refs_6_), channel_id=1, source_target_pairs={{8,0},{10,2},{12,4},{14,6},{16,8},{18,10},{20,12},{22,14},{24,16},... | collective-permute-start | bytes 1572872 | tf_op jit(solution)/shard_map/ppermute | solution.py:25
  81.7 4.2 %collective-permute-done.5.refs_9_ = bf16[2,256,512]{2,1,0:T(8,128)(2,1)} collective-permute-done((bf16[2,256,512]{2,1,0:T(8,128)(2,1)}, bf16[2,256,512]{2,1,0:T(8,128)(2,1)}, u32[]{:S(2)}, u32[]{:S(2)}) %collective-permute-start.5) | collective-permute-done | bytes 524320 | tf_op jit(solution)/shard_map/ppermute | solution.py:25
  85.9 1.3 collective-permute-start.7
  87.2 5.4 %collective-permute-start.15 = (bf16[2,256,512]{2,1,0:T(8,128)(2,1)S(1)}, bf16[2,256,512]{2,1,0:T(8,128)(2,1)}, u32[]{:S(2)}, u32[]{:S(2)}) collective-permute-start(bf16[2,256,512]{2,1,0:T(8,128)(2,1)S(1)} %collective-permute-done.13.refs_9_), channel_id=1, source_target_pairs={{64,0},{66,2},{68,4},{70,6},{72,8},{74,10},{76,12},{78,14},{80,16}... | collective-permute-start | bytes 1572872 | tf_op jit(solution)/shard_map/ppermute | solution.py:25
  92.5 5.2 %collective-permute-done.3.refs_7_ = bf16[2,256,512]{2,1,0:T(8,128)(2,1)} collective-permute-done((bf16[2,256,512]{2,1,0:T(8,128)(2,1)}, bf16[2,256,512]{2,1,0:T(8,128)(2,1)}, u32[]{:S(2)}, u32[]{:S(2)}) %collective-permute-start.3) | collective-permute-done | bytes 524320 | tf_op jit(solution)/shard_map/ppermute | solution.py:25
  97.8 2.1 %broadcast_select_fusion.1 = (bf16[2,256,512]{2,1,0:T(8,128)(2,1)}, bf16[2,256,512]{2,1,0:T(8,128)(2,1)}) fusion(bf16[2,256,512]{2,1,0:T(8,128)(2,1)} %collective-permute-done.5.refs_9_, bf16[2,256,512]{2,1,0:T(8,128)(2,1)} %get-tuple-element.19, pred[]{:T(512)S(6)} %eq.20, bf16[2,256,512]{2,1,0:T(8,128)(2,1)} %copy-done.11, pred[]{:T(512)S(6)} %eq.19), kind=kLoop, calls=%fused_computation.45 | loop fusion | flops 524288 | bytes 2621442 | tf_op jit(solution)/shard_map/jit(_where)/select_n | solution.py:262
  99.9 2.1 %broadcast_select_fusion = (bf16[2,256,512]{2,1,0:T(8,128)(2,1)}, bf16[2,256,512]{2,1,0:T(8,128)(2,1)}) fusion(bf16[2,256,512]{2,1,0:T(8,128)(2,1)} %get-tuple-element.25, bf16[2,256,512]{2,1,0:T(8,128)(2,1)S(1)} %collective-permute-done.13.refs_9_, pred[]{:T(512)S(6)} %eq.20, bf16[2,256,512]{2,1,0:T(8,128)(2,1)S(1)} %collective-permute-done.9.refs_5_, ...), kind=kLoop, calls=%fused_computation.44 | loop fusion | flops 524288 | bytes 2621442 | tf_op jit(solution)/shard_map/jit(_where)/select_n | solution.py:262
  102.0 2.0 %collective-permute-start.14 = (bf16[2,256,512]{2,1,0:T(8,128)(2,1)}, bf16[2,256,512]{2,1,0:T(8,128)(2,1)}, u32[]{:S(2)}, u32[]{:S(2)}) collective-permute-start(bf16[2,256,512]{2,1,0:T(8,128)(2,1)} %get-tuple-element.36), channel_id=1, source_target_pairs={{0,32},{2,34},{4,36},{6,38},{8,40},{10,42},{12,44},{14,46},{16,48}... | collective-permute-start | bytes 1572872 | tf_op jit(solution)/shard_map/ppermute | solution.py:263
  104.0 4.8 %collective-permute-done.7.refs_10_ = bf16[2,256,512]{2,1,0:T(8,128)(2,1)} collective-permute-done((bf16[2,256,512]{2,1,0:T(8,128)(2,1)}, bf16[2,256,512]{2,1,0:T(8,128)(2,1)}, u32[]{:S(2)}, u32[]{:S(2)}) %collective-permute-start.7) | collective-permute-done | bytes 524320 | tf_op jit(solution)/shard_map/ppermute | solution.py:25
  108.8 0.6 fusion.31
  109.4 0.1 broadcast_in_dim.21
  109.5 0.7 ge.23
  110.1 1.1 pad_maximum_fusion.1
  111.3 0.8 compare_select_fusion.bias_ref
  112.1 1.0 pad_maximum_fusion.2
  113.0 2.0 %collective-permute-done.6.refs_8_ = bf16[2,256,512]{2,1,0:T(8,128)(2,1)} collective-permute-done((bf16[2,256,512]{2,1,0:T(8,128)(2,1)}, bf16[2,256,512]{2,1,0:T(8,128)(2,1)}, u32[]{:S(2)}, u32[]{:S(2)}) %collective-permute-start.6) | collective-permute-done | bytes 524320 | tf_op jit(solution)/shard_map/ppermute | solution.py:263
  115.0 5.9 %query_side.1 = (bf16[256,512]{1,0:T(8,128)(2,1)S(1)}, bf16[256,512]{1,0:T(8,128)(2,1)S(1)}, f32[4,2,256]{2,1,0:T(2,128)S(1)}) custom-call(s32[1]{0:T(128)} %bitcast.where_ref, f32[4,1,640]{2,1,0:T(1,128)S(1)} %compare_select_fusion.bias_ref, bf16[2,128,512]{2,1,0:T(8,128)(2,1)S(1)} %get-tuple-element.46.refs_0_.refs_1_, ...), custom_call_target="tpu_custom_call" | custom-call | flops 163840 | bytes 65536 | tf_op jit(solution)/shard_map/query_side/pallas_call | solution.py:186
  121.0 2.9 %collective-permute-done.14.refs_8_ = bf16[2,256,512]{2,1,0:T(8,128)(2,1)} collective-permute-done((bf16[2,256,512]{2,1,0:T(8,128)(2,1)}, bf16[2,256,512]{2,1,0:T(8,128)(2,1)}, u32[]{:S(2)}, u32[]{:S(2)}) %collective-permute-start.14) | collective-permute-done | bytes 524320 | tf_op jit(solution)/shard_map/ppermute | solution.py:263
  123.9 2.8 %collective-permute-start.22 = (f32[4,2,256]{2,1,0:T(2,128)S(1)}, f32[4,2,256]{2,1,0:T(2,128)S(1)}, u32[]{:S(2)}, u32[]{:S(2)}) collective-permute-start(f32[4,2,256]{2,1,0:T(2,128)S(1)} %get-tuple-element.28.refs_3_), channel_id=1, source_target_pairs={{128,0},{130,2},{132,4},{134,6},{136,8},{138,10},{140,12},{142,14}... | collective-permute-start | bytes 24584 | tf_op jit(solution)/shard_map/ppermute | solution.py:25
  126.8 1.3 collective-permute-start.20
  128.1 4.1 %collective-permute-start.19 = (f32[4,2,256]{2,1,0:T(2,128)S(1)}, f32[4,2,256]{2,1,0:T(2,128)S(1)}, u32[]{:S(2)}, u32[]{:S(2)}) collective-permute-start(f32[4,2,256]{2,1,0:T(2,128)S(1)} %get-tuple-element.28.refs_3_), channel_id=1, source_target_pairs={{16,0},{18,2},{20,4},{22,6},{24,8},{26,10},{28,12},{30,14},{32,16}... | collective-permute-start | bytes 24584 | tf_op jit(solution)/shard_map/ppermute | solution.py:25
  132.1 3.3 %collective-permute-start.18 = (f32[4,2,256]{2,1,0:T(2,128)S(1)}, f32[4,2,256]{2,1,0:T(2,128)S(1)}, u32[]{:S(2)}, u32[]{:S(2)}) collective-permute-start(f32[4,2,256]{2,1,0:T(2,128)S(1)} %get-tuple-element.28.refs_3_), channel_id=1, source_target_pairs={{8,0},{10,2},{12,4},{14,6},{16,8},{18,10},{20,12},{22,14},{24,16},... | collective-permute-start | bytes 24584 | tf_op jit(solution)/shard_map/ppermute | solution.py:25
  135.4 2.2 %collective-permute-start.16 = (f32[4,2,256]{2,1,0:T(2,128)S(1)}, f32[4,2,256]{2,1,0:T(2,128)S(1)}, u32[]{:S(2)}, u32[]{:S(2)}) collective-permute-start(f32[4,2,256]{2,1,0:T(2,128)S(1)} %get-tuple-element.28.refs_3_), channel_id=1, source_target_pairs={{4,0},{6,2},{8,4},{10,6},{12,8},{14,10},{16,12},{18,14},{20,16},{2... | collective-permute-start | bytes 24584 | tf_op jit(solution)/shard_map/ppermute | solution.py:25
  137.7 0.8 fusion.37
  138.4 2.5 %collective-permute-done.16.refs_12_ = f32[4,2,256]{2,1,0:T(2,128)S(1)} collective-permute-done((f32[4,2,256]{2,1,0:T(2,128)S(1)}, f32[4,2,256]{2,1,0:T(2,128)S(1)}, u32[]{:S(2)}, u32[]{:S(2)}) %collective-permute-start.16) | collective-permute-done | bytes 8224 | tf_op jit(solution)/shard_map/ppermute | solution.py:25
  141.0 2.3 %collective-permute-start.21 = (f32[4,2,256]{2,1,0:T(2,128)S(1)}, f32[4,2,256]{2,1,0:T(2,128)S(1)}, u32[]{:S(2)}, u32[]{:S(2)}) collective-permute-start(f32[4,2,256]{2,1,0:T(2,128)S(1)} %bitcast.73), channel_id=1, source_target_pairs={{0,32},{2,34},{4,36},{6,38},{8,40},{10,42},{12,44},{14,46},{16,48}... | collective-permute-start | bytes 24584 | tf_op jit(solution)/shard_map/ppermute | solution.py:263
  143.3 0.4 convolution_convert_fusion
  143.8 3.3 %collective-permute-start.8 = (bf16[128,2048]{1,0:T(8,128)(2,1)S(1)}, bf16[128,2048]{1,0:T(8,128)(2,1)S(1)}, u32[]{:S(2)}, u32[]{:S(2)}) collective-permute-start(bf16[128,2048]{1,0:T(8,128)(2,1)S(1)} %convolution_convert_fusion), channel_id=1, source_target_pairs={{0,1},{1,0},{2,3},{3,2},{4,5},{5,4},{6,7},{7,6},{8,9},{9,8},{10,11... | collective-permute-start | bytes 1572872 | tf_op jit(solution)/shard_map/ppermute | solution.py:29
  147.1 4.1 %key_side.3 = bf16[2,128,512]{2,1,0:T(8,128)(2,1)S(1)} custom-call(s32[1]{0:T(128)} %bitcast.where_ref, bf16[2,128,512]{2,1,0:T(8,128)(2,1)S(1)} %get-tuple-element.49.refs_3_.refs_0_, bf16[2,128,512]{2,1,0:T(8,128)(2,1)S(1)} %get-tuple-element.46.refs_0_.refs_1_, bf16[2,128,512]{2,1,0:T(8,128)(2,1)S(1)} %get-tuple-element.48.refs_1_.refs_2_, ...), custom_call_target="tpu_custom_call" | custom-call | flops 81920 | bytes 65536 | tf_op jit(solution)/shard_map/key_side/pallas_call | solution.py:186
  151.2 0.8 fusion.26
  152.0 0.8 fusion.21
  152.9 0.9 collective-permute-start.23
  153.8 4.1 %key_side.2 = bf16[2,128,512]{2,1,0:T(8,128)(2,1)S(1)} custom-call(s32[1]{0:T(128)} %bitcast.where_ref, bf16[2,128,512]{2,1,0:T(8,128)(2,1)S(1)} %get-tuple-element.47.refs_2_.refs_0_, bf16[2,128,512]{2,1,0:T(8,128)(2,1)S(1)} %get-tuple-element.46.refs_0_.refs_1_, bf16[2,128,512]{2,1,0:T(8,128)(2,1)S(1)} %get-tuple-element.48.refs_1_.refs_2_, ...), custom_call_target="tpu_custom_call" | custom-call | flops 81920 | bytes 65536 | tf_op jit(solution)/shard_map/key_side/pallas_call | solution.py:186
  157.9 0.8 fusion.28
  158.7 1.6 collective-permute-done.8
  160.3 1.3 fusion.1
  161.6 9.5 %collective-permute-done.23 = bf16[128,2048]{1,0:T(8,128)(2,1)S(1)} collective-permute-done((bf16[128,2048]{1,0:T(8,128)(2,1)S(1)}, bf16[128,2048]{1,0:T(8,128)(2,1)S(1)}, u32[]{:S(2)}, u32[]{:S(2)}) %collective-permute-start.23) | collective-permute-done | bytes 524320 | tf_op jit(solution)/shard_map/ppermute | solution.py:29
  171.1 1.0 fusion.14
  172.1 1.2 fusion.18
  (60 shorter events, 0.2 us)
Async XLA Ops:
  0.6 8.6 %copy-start = (bf16[2048,512]{1,0:T(8,128)(2,1)S(1)}, bf16[2048,512]{1,0:T(8,128)(2,1)}, u32[]{:S(2)}) copy-start(bf16[2048,512]{1,0:T(8,128)(2,1)} %param.12) | copy-start | bytes 6291460
  0.6 7.2 %copy-start.9 = (bf16[128,2048]{1,0:T(8,128)(2,1)S(1)}, bf16[128,2048]{1,0:T(8,128)(2,1)}, u32[]{:S(2)}) copy-start(bf16[128,2048]{1,0:T(8,128)(2,1)} %param.14) | copy-start | bytes 1572868
  0.7 7.2 %copy-start.1 = (bf16[512,2048]{1,0:T(8,128)(2,1)S(1)}, bf16[512,2048]{1,0:T(8,128)(2,1)}, u32[]{:S(2)}) copy-start(bf16[512,2048]{1,0:T(8,128)(2,1)} %param.13) | copy-start | bytes 6291460
  2.1 7.7 %copy-start.18 = (f32[128]{0:T(128)}, f32[128]{0:T(128)S(1)}, u32[]{:S(2)}) copy-start(f32[128]{0:T(128)S(1)} %add_rsqrt_fusion) | copy-start | bytes 1540
  3.4 5.3 %copy-start.3 = (bf16[2048,512]{1,0:T(8,128)(2,1)S(1)}, bf16[2048,512]{1,0:T(8,128)(2,1)}, u32[]{:S(2)}) copy-start(bf16[2048,512]{1,0:T(8,128)(2,1)} %param.11) | copy-start | bytes 6291460
  3.4 5.3 %copy-start.5 = (bf16[128,2048]{1,0:T(8,128)(2,1)S(1)}, bf16[128,2048]{1,0:T(8,128)(2,1)}, u32[]{:S(2)}) copy-start(bf16[128,2048]{1,0:T(8,128)(2,1)} %param.8) | copy-start | bytes 1572868
  3.4 5.3 %copy-start.17 = (f32[2048]{0:T(1024)S(1)}, f32[2048]{0:T(1024)}, u32[]{:S(2)}) copy-start(f32[2048]{0:T(1024)} %param.9) | copy-start | bytes 24580
  4.7 26.5 %collective-permute-start = (bf16[2,128,2048]{2,1,0:T(8,128)(2,1)S(1)}, bf16[2,128,2048]{2,1,0:T(8,128)(2,1)S(1)}, u32[]{:S(2)}, u32[]{:S(2)}) collective-permute-start(bf16[2,128,2048]{2,1,0:T(8,128)(2,1)S(1)} %pad_maximum_fusion), channel_id=1, source_target_pairs={{0,1},{1,0},{2,3},{3,2},{4,5},{5,4},{6,7},{7,6},{8,9},{9,8},{10,11... | collective-permute-start | bytes 3145736 | tf_op jit(solution)/shard_map/ppermute | solution.py:29
  8.7 24.7 %copy-start.13 = (bf16[1,128,512]{2,1,0:T(8,128)(2,1)}, bf16[1,128,512]{2,1,0:T(8,128)(2,1)S(1)}, u32[]{:S(2)}) copy-start(bf16[1,128,512]{2,1,0:T(8,128)(2,1)S(1)} %fusion.6) | copy-start | bytes 393220
  9.3 24.2 %copy-start.14 = (bf16[1,128,512]{2,1,0:T(8,128)(2,1)}, bf16[1,128,512]{2,1,0:T(8,128)(2,1)S(1)}, u32[]{:S(2)}) copy-start(bf16[1,128,512]{2,1,0:T(8,128)(2,1)S(1)} %fusion.9) | copy-start | bytes 393220
  9.3 1.6 copy-start.7
  10.9 22.5 %copy-start.15 = (bf16[1,128,512]{2,1,0:T(8,128)(2,1)}, bf16[1,128,512]{2,1,0:T(8,128)(2,1)S(1)}, u32[]{:S(2)}) copy-start(bf16[1,128,512]{2,1,0:T(8,128)(2,1)S(1)} %fusion.10) | copy-start | bytes 393220
  11.4 22.0 %copy-start.16 = (bf16[1,128,512]{2,1,0:T(8,128)(2,1)}, bf16[1,128,512]{2,1,0:T(8,128)(2,1)S(1)}, u32[]{:S(2)}) copy-start(bf16[1,128,512]{2,1,0:T(8,128)(2,1)S(1)} %fusion.5) | copy-start | bytes 393220
  33.5 4.9 %copy-start.12 = (bf16[1,128,512]{2,1,0:T(8,128)(2,1)}, bf16[1,128,512]{2,1,0:T(8,128)(2,1)S(1)}, u32[]{:S(2)}) copy-start(bf16[1,128,512]{2,1,0:T(8,128)(2,1)S(1)} %fusion.7) | copy-start | bytes 393220
  34.5 20.1 %collective-permute-start.1 = (bf16[2,256,512]{2,1,0:T(8,128)(2,1)}, bf16[2,256,512]{2,1,0:T(8,128)(2,1)S(1)}, u32[]{:S(2)}, u32[]{:S(2)}) collective-permute-start(bf16[2,256,512]{2,1,0:T(8,128)(2,1)} %get-tuple-element.19), channel_id=1, source_target_pairs={{0,4},{2,6},{4,8},{6,10},{8,12},{10,14},{12,16},{14,18},{16,20},{1... | collective-permute-start | bytes 1572872 | tf_op jit(solution)/shard_map/ppermute | solution.py:25
  38.4 18.2 %collective-permute-start.9 = (bf16[2,256,512]{2,1,0:T(8,128)(2,1)}, bf16[2,256,512]{2,1,0:T(8,128)(2,1)S(1)}, u32[]{:S(2)}, u32[]{:S(2)}) collective-permute-start(bf16[2,256,512]{2,1,0:T(8,128)(2,1)} %get-tuple-element.25), channel_id=1, source_target_pairs={{4,0},{6,2},{8,4},{10,6},{12,8},{14,10},{16,12},{18,14},{20,16},{2... | collective-permute-start | bytes 1572872 | tf_op jit(solution)/shard_map/ppermute | solution.py:25
  54.6 19.2 %copy-start.11 = (bf16[2,256,512]{2,1,0:T(8,128)(2,1)}, bf16[2,256,512]{2,1,0:T(8,128)(2,1)S(1)}, u32[]{:S(2)}) copy-start(bf16[2,256,512]{2,1,0:T(8,128)(2,1)S(1)} %collective-permute-done.1.refs_5_) | copy-start | bytes 1572868
  54.6 17.2 %collective-permute-start.2 = (bf16[2,256,512]{2,1,0:T(8,128)(2,1)S(1)}, bf16[2,256,512]{2,1,0:T(8,128)(2,1)}, u32[]{:S(2)}, u32[]{:S(2)}) collective-permute-start(bf16[2,256,512]{2,1,0:T(8,128)(2,1)S(1)} %collective-permute-done.1.refs_5_), channel_id=1, source_target_pairs={{0,4},{2,6},{4,8},{6,10},{8,12},{10,14},{12,16},{14,18},{16,20},{1... | collective-permute-start | bytes 1572872 | tf_op jit(solution)/shard_map/ppermute | solution.py:25
  56.6 17.2 %collective-permute-start.10 = (bf16[2,256,512]{2,1,0:T(8,128)(2,1)S(1)}, bf16[2,256,512]{2,1,0:T(8,128)(2,1)}, u32[]{:S(2)}, u32[]{:S(2)}) collective-permute-start(bf16[2,256,512]{2,1,0:T(8,128)(2,1)S(1)} %collective-permute-done.9.refs_5_), channel_id=1, source_target_pairs={{4,0},{6,2},{8,4},{10,6},{12,8},{14,10},{16,12},{18,14},{20,16},{2... | collective-permute-start | bytes 1572872 | tf_op jit(solution)/shard_map/ppermute | solution.py:25
  63.5 22.4 %collective-permute-start.5 = (bf16[2,256,512]{2,1,0:T(8,128)(2,1)}, bf16[2,256,512]{2,1,0:T(8,128)(2,1)}, u32[]{:S(2)}, u32[]{:S(2)}) collective-permute-start(bf16[2,256,512]{2,1,0:T(8,128)(2,1)} %get-tuple-element.19), channel_id=1, source_target_pairs={{0,64},{2,66},{4,68},{6,70},{8,72},{10,74},{12,76},{14,78},{16,80}... | collective-permute-start | bytes 1572872 | tf_op jit(solution)/shard_map/ppermute | solution.py:25
  64.8 22.4 %collective-permute-start.13 = (bf16[2,256,512]{2,1,0:T(8,128)(2,1)}, bf16[2,256,512]{2,1,0:T(8,128)(2,1)S(1)}, u32[]{:S(2)}, u32[]{:S(2)}) collective-permute-start(bf16[2,256,512]{2,1,0:T(8,128)(2,1)} %get-tuple-element.25), channel_id=1, source_target_pairs={{64,0},{66,2},{68,4},{70,6},{72,8},{74,10},{76,12},{78,14},{80,16}... | collective-permute-start | bytes 1572872 | tf_op jit(solution)/shard_map/ppermute | solution.py:25
  71.9 25.9 %collective-permute-start.3 = (bf16[2,256,512]{2,1,0:T(8,128)(2,1)}, bf16[2,256,512]{2,1,0:T(8,128)(2,1)}, u32[]{:S(2)}, u32[]{:S(2)}) collective-permute-start(bf16[2,256,512]{2,1,0:T(8,128)(2,1)} %collective-permute-done.2.refs_6_), channel_id=1, source_target_pairs={{0,8},{2,10},{4,12},{6,14},{8,16},{10,18},{12,20},{14,22},{16,24},... | collective-permute-start | bytes 1572872 | tf_op jit(solution)/shard_map/ppermute | solution.py:25
  73.8 26.1 %collective-permute-start.11 = (bf16[2,256,512]{2,1,0:T(8,128)(2,1)}, bf16[2,256,512]{2,1,0:T(8,128)(2,1)}, u32[]{:S(2)}, u32[]{:S(2)}) collective-permute-start(bf16[2,256,512]{2,1,0:T(8,128)(2,1)} %collective-permute-done.10.refs_6_), channel_id=1, source_target_pairs={{8,0},{10,2},{12,4},{14,6},{16,8},{18,10},{20,12},{22,14},{24,16},... | collective-permute-start | bytes 1572872 | tf_op jit(solution)/shard_map/ppermute | solution.py:25
  81.7 27.7 %copy-start.20 = (s32[10]{0:T(128)S(1)}, s32[10]{0:T(128)}, u32[]{:S(2)}) copy-start(s32[10]{0:T(128)} %constant.89.clone) | copy-start | bytes 124
  85.9 22.9 %collective-permute-start.7 = (bf16[2,256,512]{2,1,0:T(8,128)(2,1)}, bf16[2,256,512]{2,1,0:T(8,128)(2,1)}, u32[]{:S(2)}, u32[]{:S(2)}) collective-permute-start(bf16[2,256,512]{2,1,0:T(8,128)(2,1)} %collective-permute-done.5.refs_9_), channel_id=1, source_target_pairs={{0,64},{2,66},{4,68},{6,70},{8,72},{10,74},{12,76},{14,78},{16,80}... | collective-permute-start | bytes 1572872 | tf_op jit(solution)/shard_map/ppermute | solution.py:25
  87.2 33.8 %collective-permute-start.15 = (bf16[2,256,512]{2,1,0:T(8,128)(2,1)S(1)}, bf16[2,256,512]{2,1,0:T(8,128)(2,1)}, u32[]{:S(2)}, u32[]{:S(2)}) collective-permute-start(bf16[2,256,512]{2,1,0:T(8,128)(2,1)S(1)} %collective-permute-done.13.refs_9_), channel_id=1, source_target_pairs={{64,0},{66,2},{68,4},{70,6},{72,8},{74,10},{76,12},{78,14},{80,16}... | collective-permute-start | bytes 1572872 | tf_op jit(solution)/shard_map/ppermute | solution.py:25
  99.9 15.2 %collective-permute-start.6 = (bf16[2,256,512]{2,1,0:T(8,128)(2,1)}, bf16[2,256,512]{2,1,0:T(8,128)(2,1)}, u32[]{:S(2)}, u32[]{:S(2)}) collective-permute-start(bf16[2,256,512]{2,1,0:T(8,128)(2,1)} %get-tuple-element.38), channel_id=1, source_target_pairs={{0,32},{2,34},{4,36},{6,38},{8,40},{10,42},{12,44},{14,46},{16,48}... | collective-permute-start | bytes 1572872 | tf_op jit(solution)/shard_map/ppermute | solution.py:263
  99.9 15.2 %collective-permute-start.4 = (bf16[2,256,512]{2,1,0:T(8,128)(2,1)}, bf16[2,256,512]{2,1,0:T(8,128)(2,1)}, u32[]{:S(2)}, u32[]{:S(2)}) collective-permute-start(bf16[2,256,512]{2,1,0:T(8,128)(2,1)} %get-tuple-element.39), channel_id=1, source_target_pairs={{0,2},{2,0},{4,6},{6,4},{8,10},{10,8},{12,14},{14,12},{16,18},{18,... | collective-permute-start | bytes 1572872 | tf_op jit(solution)/shard_map/ppermute | solution.py:263
  102.0 21.9 %collective-permute-start.14 = (bf16[2,256,512]{2,1,0:T(8,128)(2,1)}, bf16[2,256,512]{2,1,0:T(8,128)(2,1)}, u32[]{:S(2)}, u32[]{:S(2)}) collective-permute-start(bf16[2,256,512]{2,1,0:T(8,128)(2,1)} %get-tuple-element.36), channel_id=1, source_target_pairs={{0,32},{2,34},{4,36},{6,38},{8,40},{10,42},{12,44},{14,46},{16,48}... | collective-permute-start | bytes 1572872 | tf_op jit(solution)/shard_map/ppermute | solution.py:263
  108.8 15.1 %collective-permute-start.12 = (bf16[2,256,512]{2,1,0:T(8,128)(2,1)}, bf16[2,256,512]{2,1,0:T(8,128)(2,1)}, u32[]{:S(2)}, u32[]{:S(2)}) collective-permute-start(bf16[2,256,512]{2,1,0:T(8,128)(2,1)} %get-tuple-element.37), channel_id=1, source_target_pairs={{0,2},{2,0},{4,6},{6,4},{8,10},{10,8},{12,14},{14,12},{16,18},{18,... | collective-permute-start | bytes 1572872 | tf_op jit(solution)/shard_map/ppermute | solution.py:263
  115.0 22.6 %copy-start.8 = (bf16[2048,512]{1,0:T(8,128)(2,1)S(1)}, bf16[2048,512]{1,0:T(8,128)(2,1)}, u32[]{:S(2)}) copy-start(bf16[2048,512]{1,0:T(8,128)(2,1)} %param.10) | copy-start | bytes 6291460
  123.9 19.9 %collective-permute-start.22 = (f32[4,2,256]{2,1,0:T(2,128)S(1)}, f32[4,2,256]{2,1,0:T(2,128)S(1)}, u32[]{:S(2)}, u32[]{:S(2)}) collective-permute-start(f32[4,2,256]{2,1,0:T(2,128)S(1)} %get-tuple-element.28.refs_3_), channel_id=1, source_target_pairs={{128,0},{130,2},{132,4},{134,6},{136,8},{138,10},{140,12},{142,14}... | collective-permute-start | bytes 24584 | tf_op jit(solution)/shard_map/ppermute | solution.py:25
  126.8 11.7 %collective-permute-start.20 = (f32[4,2,256]{2,1,0:T(2,128)S(1)}, f32[4,2,256]{2,1,0:T(2,128)S(1)}, u32[]{:S(2)}, u32[]{:S(2)}) collective-permute-start(f32[4,2,256]{2,1,0:T(2,128)S(1)} %get-tuple-element.28.refs_3_), channel_id=1, source_target_pairs={{64,0},{66,2},{68,4},{70,6},{72,8},{74,10},{76,12},{78,14},{80,16}... | collective-permute-start | bytes 24584 | tf_op jit(solution)/shard_map/ppermute | solution.py:25
  128.1 19.0 %collective-permute-start.19 = (f32[4,2,256]{2,1,0:T(2,128)S(1)}, f32[4,2,256]{2,1,0:T(2,128)S(1)}, u32[]{:S(2)}, u32[]{:S(2)}) collective-permute-start(f32[4,2,256]{2,1,0:T(2,128)S(1)} %get-tuple-element.28.refs_3_), channel_id=1, source_target_pairs={{16,0},{18,2},{20,4},{22,6},{24,8},{26,10},{28,12},{30,14},{32,16}... | collective-permute-start | bytes 24584 | tf_op jit(solution)/shard_map/ppermute | solution.py:25
  132.1 15.0 %collective-permute-start.18 = (f32[4,2,256]{2,1,0:T(2,128)S(1)}, f32[4,2,256]{2,1,0:T(2,128)S(1)}, u32[]{:S(2)}, u32[]{:S(2)}) collective-permute-start(f32[4,2,256]{2,1,0:T(2,128)S(1)} %get-tuple-element.28.refs_3_), channel_id=1, source_target_pairs={{8,0},{10,2},{12,4},{14,6},{16,8},{18,10},{20,12},{22,14},{24,16},... | collective-permute-start | bytes 24584 | tf_op jit(solution)/shard_map/ppermute | solution.py:25
  135.4 5.5 %collective-permute-start.16 = (f32[4,2,256]{2,1,0:T(2,128)S(1)}, f32[4,2,256]{2,1,0:T(2,128)S(1)}, u32[]{:S(2)}, u32[]{:S(2)}) collective-permute-start(f32[4,2,256]{2,1,0:T(2,128)S(1)} %get-tuple-element.28.refs_3_), channel_id=1, source_target_pairs={{4,0},{6,2},{8,4},{10,6},{12,8},{14,10},{16,12},{18,14},{20,16},{2... | collective-permute-start | bytes 24584 | tf_op jit(solution)/shard_map/ppermute | solution.py:25
  137.7 5.7 %copy-start.2 = (bf16[512,2048]{1,0:T(8,128)(2,1)S(1)}, bf16[512,2048]{1,0:T(8,128)(2,1)}, u32[]{:S(2)}) copy-start(bf16[512,2048]{1,0:T(8,128)(2,1)} %param.13) | copy-start | bytes 6291460
  141.0 6.2 %collective-permute-start.21 = (f32[4,2,256]{2,1,0:T(2,128)S(1)}, f32[4,2,256]{2,1,0:T(2,128)S(1)}, u32[]{:S(2)}, u32[]{:S(2)}) collective-permute-start(f32[4,2,256]{2,1,0:T(2,128)S(1)} %bitcast.73), channel_id=1, source_target_pairs={{0,32},{2,34},{4,36},{6,38},{8,40},{10,42},{12,44},{14,46},{16,48}... | collective-permute-start | bytes 24584 | tf_op jit(solution)/shard_map/ppermute | solution.py:263
  143.3 3.8 %collective-permute-start.17 = (f32[4,2,256]{2,1,0:T(2,128)S(1)}, f32[4,2,256]{2,1,0:T(2,128)S(1)}, u32[]{:S(2)}, u32[]{:S(2)}) collective-permute-start(f32[4,2,256]{2,1,0:T(2,128)S(1)} %bitcast.72), channel_id=1, source_target_pairs={{0,2},{2,0},{4,6},{6,4},{8,10},{10,8},{12,14},{14,12},{16,18},{18,... | collective-permute-start | bytes 24584 | tf_op jit(solution)/shard_map/ppermute | solution.py:263
  143.8 7.5 %copy-start.4 = (bf16[2048,512]{1,0:T(8,128)(2,1)S(1)}, bf16[2048,512]{1,0:T(8,128)(2,1)}, u32[]{:S(2)}) copy-start(bf16[2048,512]{1,0:T(8,128)(2,1)} %param.11) | copy-start | bytes 6291460
  143.8 16.5 %collective-permute-start.8 = (bf16[128,2048]{1,0:T(8,128)(2,1)S(1)}, bf16[128,2048]{1,0:T(8,128)(2,1)S(1)}, u32[]{:S(2)}, u32[]{:S(2)}) collective-permute-start(bf16[128,2048]{1,0:T(8,128)(2,1)S(1)} %convolution_convert_fusion), channel_id=1, source_target_pairs={{0,1},{1,0},{2,3},{3,2},{4,5},{5,4},{6,7},{7,6},{8,9},{9,8},{10,11... | collective-permute-start | bytes 1572872 | tf_op jit(solution)/shard_map/ppermute | solution.py:29
  152.9 18.3 %collective-permute-start.23 = (bf16[128,2048]{1,0:T(8,128)(2,1)S(1)}, bf16[128,2048]{1,0:T(8,128)(2,1)S(1)}, u32[]{:S(2)}, u32[]{:S(2)}) collective-permute-start(bf16[128,2048]{1,0:T(8,128)(2,1)S(1)} %fusion.21), channel_id=1, source_target_pairs={{0,1},{1,0},{2,3},{3,2},{4,5},{5,4},{6,7},{7,6},{8,9},{9,8},{10,11... | collective-permute-start | bytes 1572872 | tf_op jit(solution)/shard_map/ppermute | solution.py:29
  157.9 2.4 %copy-start.6 = (bf16[128,2048]{1,0:T(8,128)(2,1)S(1)}, bf16[128,2048]{1,0:T(8,128)(2,1)}, u32[]{:S(2)}) copy-start(bf16[128,2048]{1,0:T(8,128)(2,1)} %param.8) | copy-start | bytes 1572868
  158.7 12.4 %copy-start.19 = (f32[128]{0:T(128)S(1)}, f32[128]{0:T(128)}, u32[]{:S(2)}) copy-start(f32[128]{0:T(128)} %copy-done.18) | copy-start | bytes 1540
  161.6 10.5 %copy-start.10 = (bf16[128,2048]{1,0:T(8,128)(2,1)S(1)}, bf16[128,2048]{1,0:T(8,128)(2,1)}, u32[]{:S(2)}) copy-start(bf16[128,2048]{1,0:T(8,128)(2,1)} %param.14) | copy-start | bytes 1572868

commit v9 on v8

--- a/solution.py
+++ b/solution.py
@@ -60,10 +60,9 @@
     return jnp.where(rows >= keys, 0.0, NEG).astype(F32)
 
 
-def query_kernel(groups, n_back, where_ref, bias_ref, *refs):
+def query_kernel(groups, n_back, where_ref, *refs):
     refs = list(refs)
-    qg = [refs.pop(0) for _ in range(2)]
-    kv = [refs.pop(0) for _ in range(2)]
+    qg, kv = [refs.pop(0)], [refs.pop(0)]
     fetched = [[refs.pop(0) for _ in range(n)] for n in groups]
     mixed_ref, dq_ref, stat_ref, *back_refs = refs
     is_second = where_ref[0] == 1
@@ -83,13 +82,16 @@
     def rows(slot):
         return slice(slot * BLOCK, (slot + 1) * BLOCK)
 
+    part = lax.broadcasted_iota(jnp.int32, (1, (4 + len(groups) - 1) * BLOCK), 1) // BLOCK
+    reach = jnp.where(part == 0, 0, jnp.left_shift(1, jnp.maximum(part - 1, 0)))
     query = [piece(qg, 0, slot) for slot in slots]
     grad = [piece(qg, 1, slot) for slot in slots]
     keys = [gather(0, slot) for slot in slots]
     values = [gather(1, slot) for slot in slots]
     score = []
     for slot in slots:
-        s = dot(query[slot], keys[slot], NT) * factor + bias_ref[slot]
+        block = where_ref[1] + (slot + 2 * where_ref[0]) % 4
+        s = dot(query[slot], keys[slot], NT) * factor + jnp.where(reach <= block, 0.0, NEG)
         score.append(jnp.concatenate([s[:, :BLOCK] + causal, s[:, BLOCK:]], axis=1))
     grad_prob = [dot(grad[slot], values[slot], NT) for slot in slots]
     peak = [jnp.max(s, axis=-1, keepdims=True) for s in score]
@@ -123,7 +125,7 @@
 def key_kernel(half, groups, where_ref, *refs):
     refs = list(refs)
     kv = refs.pop(0)
-    qg = [refs.pop(0) for _ in range(2)]
+    qg = [refs.pop(0)]
     stat = refs.pop(0)
     later = [[refs.pop(0) for _ in range(n)] for n in groups]
     later_stats = [refs.pop(0) for _ in groups]
@@ -189,7 +191,7 @@
         grid_spec=pltpu.PrefetchScalarGridSpec(
             num_scalar_prefetch=1, grid=(heads,), in_specs=in_specs, out_specs=out_specs
         ),
-        compiler_params=pltpu.CompilerParams(vmem_limit_bytes=10 * 2**20),
+        compiler_params=pltpu.CompilerParams(vmem_limit_bytes=6 * 2**20),
         cost_estimate=pl.CostEstimate(
             flops=rows * keys, bytes_accessed=2**16, transcendentals=0
         ),
@@ -197,11 +199,11 @@
     )(where, *operands)
 
 
-def query_side(where, bias, qg, kv, fetched, n_back):
-    rows, width = 2 * qg[0].shape[1], qg[0].shape[2]
+def query_side(where, qg, kv, fetched, n_back):
+    rows, width = qg.shape[1], qg.shape[2]
     heads = width // HD
-    far = [pltpu.with_memory_space_constraint(a, pltpu.HBM) for f in fetched for a in f]
-    operands = [*qg, *kv, *far]
+    far = [a for f in fetched for a in f]
+    operands = [qg, kv, *far]
     row_out = jax.ShapeDtypeStruct((rows, width), BF16)
     stat_out = jax.ShapeDtypeStruct((heads, 2, rows), F32)
     back_out = jax.ShapeDtypeStruct((2, rows, width), BF16)
@@ -209,24 +211,25 @@
     return call(
         functools.partial(query_kernel, tuple(len(f) for f in fetched), n_back),
         where,
-        [bias, *operands],
-        [pl.BlockSpec(bias.shape, lambda h, w: (0, 0, 0))] + [head_spec(a) for a in operands],
+        operands,
+        [head_spec(a) for a in operands],
         outs,
         [head_spec(row_out), head_spec(row_out), stat_spec(stat_out)] + [head_spec(back_out)] * n_back,
         heads,
-        bias.shape[2],
+        (3 + len(fetched)) * BLOCK,
         "query_side",
     )
 
 
 def key_side(half, where, kv, qg, stat, later, later_stats):
-    rows, width = kv[0].shape[1], kv[0].shape[2]
+    rows, width = kv.shape[1] // 2, kv.shape[2]
     heads = width // HD
     half_of_whole = pl.BlockSpec((2, rows, HD), lambda h, w: (0, half, h))
     far = [f[-1] if len(f) == 1 else f[half] for f in later[1:]]
-    operands = [kv[half], *qg, stat, *later[0], *far, *later_stats]
+    first, *far = [pltpu.with_memory_space_constraint(a, pltpu.HBM) for a in (*later[0], *far)]
+    operands = [kv, qg, stat, first, *far, *later_stats]
     in_specs = (
-        [head_spec(a) for a in (kv[half], *qg)]
+        [half_of_whole, head_spec(qg)]
         + [stat_spec(stat)]
         + [head_spec(a) for a in later[0]]
         + [half_of_whole if len(f) == 1 else head_spec(f[half]) for f in later[1:]]
@@ -248,6 +251,35 @@
     return result
 
 
+def norm_kernel(series_ref, gain_ref, grad_ref, sent_ref, inv_ref):
+    rows = series_ref[...].astype(F32)
+    inv_rms = lax.rsqrt(jnp.mean(rows * rows, axis=-1, keepdims=True) + EPS)
+    inv_ref[...] = inv_rms
+    sent_ref[0] = (rows * inv_rms * gain_ref[...]).astype(BF16)
+    sent_ref[1] = grad_ref[...]
+
+
+def normalize(series, gain, out_grad):
+    rows, width = series.shape
+    step = rows // 4
+    row_spec = pl.BlockSpec((step, width), lambda i: (i, 0))
+    return pl.pallas_call(
+        norm_kernel,
+        out_shape=[
+            jax.ShapeDtypeStruct((2, rows, width), BF16),
+            jax.ShapeDtypeStruct((rows, 1), F32),
+        ],
+        grid=(4,),
+        in_specs=[row_spec, pl.BlockSpec((1, width), lambda i: (0, 0)), row_spec],
+        out_specs=[
+            pl.BlockSpec((2, step, width), lambda i: (0, i, 0)),
+            pl.BlockSpec((step, 1), lambda i: (i, 0)),
+        ],
+        compiler_params=pltpu.CompilerParams(vmem_limit_bytes=6 * 2**20),
+        name="normalize",
+    )(series, gain[None], out_grad)
+
+
 def matmul(a, b):
     return jnp.dot(a, b, preferred_element_type=F32)
 
@@ -269,17 +301,18 @@
     four = shifted(two, sign * 2)
     eight = shifted(four, sign * 4)
     sixteen = swapped(rows, far, 16, sign)
-    two_last, eight = lax.optimization_barrier((two, eight))
-    one = swapped(rows, two_last, 1, sign)
+    rows_last, two_last, eight = lax.optimization_barrier((rows, two, eight))
+    one = swapped(rows_last, two_last, 1, sign)
     return [one, two, four, eight, sixteen, far, shifted(far, sign * 32)]
 
 
-def exchange_stats(stat):
+def exchange_stats(stat, attn_other):
     two, far = shifted(stat, -2), shifted(stat, -32)
     direct = [shifted(stat, -by) for by in (64, 8, 4)]
-    one = swapped(stat, two, 1, -1)
     sixteen = swapped(stat, far, 16, -1)
-    return [one, two, direct[2], direct[1], sixteen, far, direct[0]]
+    two_last, attn_other = lax.optimization_barrier((two, attn_other))
+    one = swapped(stat, two_last, 1, -1)
+    return attn_other, [one, two, direct[2], direct[1], sixteen, far, direct[0]]
 
 
 def per_device(series, norm_gain, w_query, w_key, w_value, w_out, out_grad):
@@ -288,18 +321,12 @@
     blocks = 2 * half // BLOCK
     tp_index = lax.axis_index("tp").astype(jnp.int32)
     seq_index = lax.axis_index("seq").astype(jnp.int32)
-    where = tp_index[None]
-    slots = jnp.arange(blocks, dtype=jnp.int32)
-    global_block = seq_index * blocks + (slots + 2 * tp_index) % blocks
-    distances = [1, 2, 4] + [blocks * 2**s for s in range(1, levels)]
-    reach = jnp.repeat(jnp.array([0] + distances, jnp.int32), BLOCK)
-    bias = jnp.where(global_block[:, None] >= reach[None], 0.0, NEG).astype(F32)[:, None, :]
-
+    where = jnp.stack([tp_index, seq_index * blocks])
     series_f = series.astype(F32)
-    inv_rms = lax.rsqrt(jnp.mean(series_f * series_f, axis=-1, keepdims=True) + EPS)
+    sent, inv_rms = normalize(series, norm_gain, out_grad)
+    normed = sent[0]
     unit_rows = series_f * inv_rms
-    normed = (unit_rows * norm_gain).astype(BF16)
-    normed_other, out_grad_other = swap_tp(jnp.stack([normed, out_grad]))
+    normed_other, out_grad_other = swap_tp(sent)
 
     def key_value(rows):
         return jnp.stack([matmul(rows, w_key).astype(BF16), matmul(rows, w_value).astype(BF16)])
@@ -316,18 +343,18 @@
     )
     fetched = exchange(kv_all, 1)
     later = exchange(qg_all, -1)
-    mixed, grad_query, stat = query_side(where, bias, qg, kv, [(f,) for f in fetched], 0)
+    mixed, grad_query, stat = query_side(where, qg_all, kv_all, [(f,) for f in fetched], 0)
     stat, later = lax.optimization_barrier((stat, later))
     later = [(f,) for f in later]
-    later_stats = exchange_stats(stat)
     attn_other = swap_tp(matmul(mixed[half:], w_out).astype(BF16))
+    attn_other, later_stats = exchange_stats(stat, attn_other)
     attn_rows = matmul(mixed[:half], w_out) + attn_other.astype(F32)
     layer_out = (series_f + attn_rows).astype(BF16)
 
     grad_queries = lax.optimization_barrier(matmul_t(grad_query, w_query))
 
     def back(at):
-        grad_kv = key_side(at, where, kv, qg, stat, later, later_stats)
+        grad_kv = key_side(at, where, kv_all, qg_all, stat, later, later_stats)
         rows = slice(at * half, (at + 1) * half)
         return (
             grad_queries[rows]

time: 174 us -> 166 us (0.954)
  other arithmetic: 13.9 us -> 2.74 us
  matrix products: 10.5 us -> 15.5 us
  waiting for transfers between devices: 64.3 us -> 59.5 us
  local copies, waits for them, and re-layouts: 1.97 us -> 5.12 us
  starting transfers between devices: 67.3 us -> 65 us
  Pallas kernels: 14.1 us -> 16.2 us
    ppermute x15, waiting for transfers between devices: 28.5 us -> 36.1 us  [shifted(): return lax.ppermute(value, 'seq', pairs)]
    ppermute x3, waiting for transfers between devices: 30.9 us -> 23.4 us  [swap_tp(): return lax.ppermute(value, 'tp', [(0, 1), (1, 0)])]
    ppermute x6, waiting for transfers between devices: 4.94 us -> 0.02 us  [swapped(): return lax.ppermute(sent, 'seq', [(i, i ^ bit) for i in range(size)])]
    another operation x4 -> x1, other arithmetic: 4.69 us -> 0.08 us  [per_device(): where = jnp.stack([tp_index, seq_index * blocks])]
    unnamed x42 -> x44, local copies, waits for them, and re-layouts: 1.24 us -> 5.12 us
    dot_general x7, matrix products: 5.84 us -> 9.16 us  [matmul_t(): return lax.dot_general(a, b, NT, preferred_element_type=F32)]
    ppermute x15, starting transfers between devices: 55.6 us -> 52.7 us  [shifted(): return lax.ppermute(value, 'seq', pairs)]
    select_n x1 -> x2, other arithmetic: 2.1 us -> 0.12 us  [swapped(): jnp.where(high, passed, own)]
  transfers between devices with their start and end apart: 24 -> 24, of which waited for: 11 -> 7; matrix products, arithmetic and copies ran while one was open for 9% -> 7% of each run, Pallas kernels for 8% -> 7%
where the time goes in v9:
time: 166 us; the launch traced here: 165 us
  starting transfers between devices  65 us (39%)
  waiting for transfers between devices  59.5 us (36%)
  Pallas kernels  16.2 us (10%)
  matrix products  15.5 us (9%)
  local copies, waits for them, and re-layouts  5.12 us (3%)
  other arithmetic  2.74 us (2%)
    ppermute x15, starting transfers between devices, shifted(): return lax.ppermute(value, 'seq', pairs)  52.7 us
    ppermute x15, waiting for transfers between devices, shifted(): return lax.ppermute(value, 'seq', pairs)  36.1 us
    ppermute x3, waiting for transfers between devices, swap_tp(): return lax.ppermute(value, 'tp', [(0, 1), (1, 0)])  23.4 us
    pallas_call x3, Pallas kernels, call(): pl.pallas_call(kernel, out_shape=outs, grid_spec=pltpu.PrefetchScalarGrid...  15.6 us
    dot_general x7, matrix products, matmul_t(): return lax.dot_general(a, b, NT, preferred_element_type=F32)  9.16 us
    ppermute x3, starting transfers between devices, swap_tp(): return lax.ppermute(value, 'tp', [(0, 1), (1, 0)])  8.69 us
    dot_general x8, matrix products, matmul(): return jnp.dot(a, b, preferred_element_type=F32)  6.37 us
    unnamed x44, local copies, waits for them, and re-layouts  5.12 us
  transfers between devices with their start and end apart: 24, of which 7 were waited for; matrix products, arithmetic and copies ran while one was open for 7% of the time, Pallas kernels for 7%

profile of v9, /device:TPU:24, one launch (start us, length us, event | category | flops | bytes accessed | tf_op | source)
XLA Modules:
  0.0 165.4 jit_solution(4914396124737194947)
XLA Ops:
  0.7 1.2 copy-done.1
  1.8 1.0 copy-done.3
  2.9 0.7 copy-done.9
  3.6 0.6 normalize.1
  4.2 3.1 %collective-permute-start = (bf16[2,128,2048]{2,1,0:T(8,128)(2,1)S(1)}, bf16[2,128,2048]{2,1,0:T(8,128)(2,1)S(1)}, u32[]{:S(2)}, u32[]{:S(2)}) collective-permute-start(bf16[2,128,2048]{2,1,0:T(8,128)(2,1)S(1)} %get-tuple-element.25), channel_id=1, source_target_pairs={{0,1},{1,0},{2,3},{3,2},{4,5},{5,4},{6,7},{7,6},{8,9},{9,8},{10,11... | collective-permute-start | bytes 3145736 | tf_op jit(solution)/shard_map/ppermute | solution.py:29
  7.3 2.6 %fusion.9 = bf16[1,128,512]{2,1,0:T(8,128)(2,1)S(1)} fusion(bf16[128,2048]{1,0:T(8,128)(2,1)} %grad_ref.1, bf16[512,2048]{1,0:T(8,128)(2,1)} %param.12), kind=kOutput, calls=%fused_computation.20 | convolution fusion | flops 268500992 | bytes 2752512 | tf_op jit(solution)/shard_map/dot_general | solution.py:288
  9.9 0.5 fusion.4
  10.4 0.5 fusion.5
  10.9 0.6 copy-done.16
  11.5 0.4 fusion.8
  12.0 18.7 %collective-permute-done = bf16[2,128,2048]{2,1,0:T(8,128)(2,1)S(1)} collective-permute-done((bf16[2,128,2048]{2,1,0:T(8,128)(2,1)S(1)}, bf16[2,128,2048]{2,1,0:T(8,128)(2,1)S(1)}, u32[]{:S(2)}, u32[]{:S(2)}) %collective-permute-start) | collective-permute-done | bytes 1048608 | tf_op jit(solution)/shard_map/ppermute | solution.py:29
  30.7 0.5 fusion.10
  31.2 0.8 fusion.11
  32.0 0.5 fusion.6
  32.5 0.5 fusion.7
  33.0 0.1 maximum_maximum_fusion
  33.0 3.8 %collective-permute-start.1 = (bf16[2,256,512]{2,1,0:T(8,128)(2,1)S(1)}, bf16[2,256,512]{2,1,0:T(8,128)(2,1)S(1)}, u32[]{:S(2)}, u32[]{:S(2)}) collective-permute-start(bf16[2,256,512]{2,1,0:T(8,128)(2,1)S(1)} %get-tuple-element.29.refs_1_.refs_0_), channel_id=1, source_target_pairs={{0,4},{2,6},{4,8},{6,10},{8,12},{10,14},{12,16},{14,18},{16,20},{1... | collective-permute-start | bytes 1572872 | tf_op jit(solution)/shard_map/ppermute | solution.py:25
  36.9 7.0 %collective-permute-start.8 = (bf16[2,256,512]{2,1,0:T(8,128)(2,1)S(1)}, bf16[2,256,512]{2,1,0:T(8,128)(2,1)}, u32[]{:S(2)}, u32[]{:S(2)}) collective-permute-start(bf16[2,256,512]{2,1,0:T(8,128)(2,1)S(1)} %get-tuple-element.33.refs_0_.refs_1_), channel_id=1, source_target_pairs={{4,0},{6,2},{8,4},{10,6},{12,8},{14,10},{16,12},{18,14},{20,16},{2... | collective-permute-start | bytes 1572872 | tf_op jit(solution)/shard_map/ppermute | solution.py:25
  43.9 9.1 %collective-permute-done.1.refs_3_ = bf16[2,256,512]{2,1,0:T(8,128)(2,1)S(1)} collective-permute-done((bf16[2,256,512]{2,1,0:T(8,128)(2,1)S(1)}, bf16[2,256,512]{2,1,0:T(8,128)(2,1)S(1)}, u32[]{:S(2)}, u32[]{:S(2)}) %collective-permute-start.1) | collective-permute-done | bytes 524320 | tf_op jit(solution)/shard_map/ppermute | solution.py:25
  53.0 1.9 %collective-permute-start.2 = (bf16[2,256,512]{2,1,0:T(8,128)(2,1)S(1)}, bf16[2,256,512]{2,1,0:T(8,128)(2,1)}, u32[]{:S(2)}, u32[]{:S(2)}) collective-permute-start(bf16[2,256,512]{2,1,0:T(8,128)(2,1)S(1)} %collective-permute-done.1.refs_3_), channel_id=1, source_target_pairs={{0,4},{2,6},{4,8},{6,10},{8,12},{10,14},{12,16},{14,18},{16,20},{1... | collective-permute-start | bytes 1572872 | tf_op jit(solution)/shard_map/ppermute | solution.py:25
  54.9 1.3 collective-permute-start.5
  56.2 7.6 %collective-permute-start.9 = (bf16[2,256,512]{2,1,0:T(8,128)(2,1)}, bf16[2,256,512]{2,1,0:T(8,128)(2,1)}, u32[]{:S(2)}, u32[]{:S(2)}) collective-permute-start(bf16[2,256,512]{2,1,0:T(8,128)(2,1)} %collective-permute-done.8.refs_4_), channel_id=1, source_target_pairs={{4,0},{6,2},{8,4},{10,6},{12,8},{14,10},{16,12},{18,14},{20,16},{2... | collective-permute-start | bytes 1572872 | tf_op jit(solution)/shard_map/ppermute | solution.py:25
  63.8 6.4 %collective-permute-done.2.refs_4_ = bf16[2,256,512]{2,1,0:T(8,128)(2,1)} collective-permute-done((bf16[2,256,512]{2,1,0:T(8,128)(2,1)S(1)}, bf16[2,256,512]{2,1,0:T(8,128)(2,1)}, u32[]{:S(2)}, u32[]{:S(2)}) %collective-permute-start.2) | collective-permute-done | bytes 524320 | tf_op jit(solution)/shard_map/ppermute | solution.py:25
  70.2 1.9 %collective-permute-start.3 = (bf16[2,256,512]{2,1,0:T(8,128)(2,1)}, bf16[2,256,512]{2,1,0:T(8,128)(2,1)}, u32[]{:S(2)}, u32[]{:S(2)}) collective-permute-start(bf16[2,256,512]{2,1,0:T(8,128)(2,1)} %collective-permute-done.2.refs_4_), channel_id=1, source_target_pairs={{0,8},{2,10},{4,12},{6,14},{8,16},{10,18},{12,20},{14,22},{16,24},... | collective-permute-start | bytes 1572872 | tf_op jit(solution)/shard_map/ppermute | solution.py:25
  72.2 0.1 pad_add_fusion.where_ref
  72.2 2.4 %collective-permute-start.12 = (bf16[2,256,512]{2,1,0:T(8,128)(2,1)S(1)}, bf16[2,256,512]{2,1,0:T(8,128)(2,1)S(1)}, u32[]{:S(2)}, u32[]{:S(2)}) collective-permute-start(bf16[2,256,512]{2,1,0:T(8,128)(2,1)S(1)} %get-tuple-element.33.refs_0_.refs_1_), channel_id=1, source_target_pairs={{64,0},{66,2},{68,4},{70,6},{72,8},{74,10},{76,12},{78,14},{80,16}... | collective-permute-start | bytes 1572872 | tf_op jit(solution)/shard_map/ppermute | solution.py:25
  74.7 7.1 %collective-permute-done.5.refs_7_ = bf16[2,256,512]{2,1,0:T(8,128)(2,1)} collective-permute-done((bf16[2,256,512]{2,1,0:T(8,128)(2,1)S(1)}, bf16[2,256,512]{2,1,0:T(8,128)(2,1)}, u32[]{:S(2)}, u32[]{:S(2)}) %collective-permute-start.5) | collective-permute-done | bytes 524320 | tf_op jit(solution)/shard_map/ppermute | solution.py:25
  81.7 0.1 broadcast_select_fusion.1
  81.8 0.1 collective-permute-start.6
  81.9 1.4 collective-permute-start.7
  83.3 4.0 %collective-permute-start.10 = (bf16[2,256,512]{2,1,0:T(8,128)(2,1)}, bf16[2,256,512]{2,1,0:T(8,128)(2,1)S(1)}, u32[]{:S(2)}, u32[]{:S(2)}) collective-permute-start(bf16[2,256,512]{2,1,0:T(8,128)(2,1)} %collective-permute-done.9.refs_5_), channel_id=1, source_target_pairs={{8,0},{10,2},{12,4},{14,6},{16,8},{18,10},{20,12},{22,14},{24,16},... | collective-permute-start | bytes 1572872 | tf_op jit(solution)/shard_map/ppermute | solution.py:25
  87.3 8.8 %collective-permute-done.3.refs_5_ = bf16[2,256,512]{2,1,0:T(8,128)(2,1)} collective-permute-done((bf16[2,256,512]{2,1,0:T(8,128)(2,1)}, bf16[2,256,512]{2,1,0:T(8,128)(2,1)}, u32[]{:S(2)}, u32[]{:S(2)}) %collective-permute-start.3) | collective-permute-done | bytes 524320 | tf_op jit(solution)/shard_map/ppermute | solution.py:25
  96.1 0.1 broadcast_select_fusion.3
  96.1 0.1 collective-permute-start.4
  96.3 0.1 broadcast_select_fusion
  96.3 0.3 collective-permute-start.13
  96.6 4.7 %collective-permute-done.10.refs_6_ = bf16[2,256,512]{2,1,0:T(8,128)(2,1)S(1)} collective-permute-done((bf16[2,256,512]{2,1,0:T(8,128)(2,1)}, bf16[2,256,512]{2,1,0:T(8,128)(2,1)S(1)}, u32[]{:S(2)}, u32[]{:S(2)}) %collective-permute-start.10) | collective-permute-done | bytes 524320 | tf_op jit(solution)/shard_map/ppermute | solution.py:25
  101.3 4.3 %collective-permute-start.14 = (bf16[2,256,512]{2,1,0:T(8,128)(2,1)S(1)}, bf16[2,256,512]{2,1,0:T(8,128)(2,1)S(1)}, u32[]{:S(2)}, u32[]{:S(2)}) collective-permute-start(bf16[2,256,512]{2,1,0:T(8,128)(2,1)S(1)} %collective-permute-done.12.refs_8_), channel_id=1, source_target_pairs={{64,0},{66,2},{68,4},{70,6},{72,8},{74,10},{76,12},{78,14},{80,16}... | collective-permute-start | bytes 1572872 | tf_op jit(solution)/shard_map/ppermute | solution.py:25
  105.6 1.1 broadcast_select_fusion.2
  106.7 0.1 collective-permute-start.11
  106.9 6.2 %query_side.1 = (bf16[256,512]{1,0:T(8,128)(2,1)S(1)}, bf16[256,512]{1,0:T(8,128)(2,1)S(1)}, f32[4,2,256]{2,1,0:T(2,128)S(1)}) custom-call(s32[2]{0:T(128)S(1)} %pad_add_fusion.where_ref, bf16[2,256,512]{2,1,0:T(8,128)(2,1)S(1)} %get-tuple-element.33.refs_0_.refs_1_, bf16[2,256,512]{2,1,0:T(8,128)(2,1)S(1)} %get-tuple-element.29.refs_1_.refs_0_, ...), custom_call_target="tpu_custom_call" | custom-call | flops 163840 | bytes 65536 | tf_op jit(solution)/shard_map/query_side/pallas_call | solution.py:188
  113.1 0.7 copy-done.7
  113.7 1.2 convolution_convert_fusion
  115.0 2.8 %collective-permute-start.16 = (bf16[128,2048]{1,0:T(8,128)(2,1)}, bf16[128,2048]{1,0:T(8,128)(2,1)}, u32[]{:S(2)}, u32[]{:S(2)}) collective-permute-start(bf16[128,2048]{1,0:T(8,128)(2,1)} %convolution_convert_fusion), channel_id=1, source_target_pairs={{0,1},{1,0},{2,3},{3,2},{4,5},{5,4},{6,7},{7,6},{8,9},{9,8},{10,11... | collective-permute-start | bytes 1572872 | tf_op jit(solution)/shard_map/ppermute | solution.py:29
  117.8 0.8 copy-done.19
  118.6 7.3 %collective-permute-start.15 = (f32[4,2,256]{2,1,0:T(2,128)S(1)}, f32[4,2,256]{2,1,0:T(2,128)S(1)}, u32[]{:S(2)}, u32[]{:S(2)}) collective-permute-start(f32[4,2,256]{2,1,0:T(2,128)S(1)} %get-tuple-element.36.refs_2_), channel_id=1, source_target_pairs={{4,0},{6,2},{8,4},{10,6},{12,8},{14,10},{16,12},{18,14},{20,16},{2... | collective-permute-start | bytes 24584 | tf_op jit(solution)/shard_map/ppermute | solution.py:25
  125.9 2.4 %collective-permute-start.20 = (f32[4,2,256]{2,1,0:T(2,128)S(1)}, f32[4,2,256]{2,1,0:T(2,128)S(1)}, u32[]{:S(2)}, u32[]{:S(2)}) collective-permute-start(f32[4,2,256]{2,1,0:T(2,128)S(1)} %get-tuple-element.36.refs_2_), channel_id=1, source_target_pairs={{64,0},{66,2},{68,4},{70,6},{72,8},{74,10},{76,12},{78,14},{80,16}... | collective-permute-start | bytes 24584 | tf_op jit(solution)/shard_map/ppermute | solution.py:25
  128.3 0.1 reduce
  128.4 2.1 %collective-permute-start.18 = (f32[4,2,256]{2,1,0:T(2,128)S(1)}, f32[4,2,256]{2,1,0:T(2,128)S(1)}, u32[]{:S(2)}, u32[]{:S(2)}) collective-permute-start(f32[4,2,256]{2,1,0:T(2,128)S(1)} %get-tuple-element.36.refs_2_), channel_id=1, source_target_pairs={{8,0},{10,2},{12,4},{14,6},{16,8},{18,10},{20,12},{22,14},{24,16},... | collective-permute-start | bytes 24584 | tf_op jit(solution)/shard_map/ppermute | solution.py:25
  130.6 3.4 %collective-permute-start.19 = (f32[4,2,256]{2,1,0:T(2,128)S(1)}, f32[4,2,256]{2,1,0:T(2,128)S(1)}, u32[]{:S(2)}, u32[]{:S(2)}) collective-permute-start(f32[4,2,256]{2,1,0:T(2,128)S(1)} %get-tuple-element.36.refs_2_), channel_id=1, source_target_pairs={{16,0},{18,2},{20,4},{22,6},{24,8},{26,10},{28,12},{30,14},{32,16}... | collective-permute-start | bytes 24584 | tf_op jit(solution)/shard_map/ppermute | solution.py:25
  134.0 1.8 %collective-permute-start.22 = (f32[4,2,256]{2,1,0:T(2,128)S(1)}, f32[4,2,256]{2,1,0:T(2,128)S(1)}, u32[]{:S(2)}, u32[]{:S(2)}) collective-permute-start(f32[4,2,256]{2,1,0:T(2,128)S(1)} %get-tuple-element.36.refs_2_), channel_id=1, source_target_pairs={{128,0},{130,2},{132,4},{134,6},{136,8},{138,10},{140,12},{142,14}... | collective-permute-start | bytes 24584 | tf_op jit(solution)/shard_map/ppermute | solution.py:25
  135.9 0.1 collective-permute-start.17
  136.0 3.0 %collective-permute-start.21 = (f32[4,2,256]{2,1,0:T(2,128)S(1)}, f32[4,2,256]{2,1,0:T(2,128)S(1)}, u32[]{:S(2)}, u32[]{:S(2)}) collective-permute-start(f32[4,2,256]{2,1,0:T(2,128)S(1)} %bitcast.78), channel_id=1, source_target_pairs={{0,32},{2,34},{4,36},{6,38},{8,40},{10,42},{12,44},{14,46},{16,48}... | collective-permute-start | bytes 24584 | tf_op jit(solution)/shard_map/ppermute | solution.py:295
  139.0 2.3 %fusion.34 = f32[256,2048]{1,0:T(8,128)S(1)} fusion(bf16[256,512]{1,0:T(8,128)(2,1)S(1)} %get-tuple-element.39, bf16[2048,512]{1,0:T(8,128)(2,1)} %param.9), kind=kOutput, calls=%fused_computation.63 | convolution fusion | flops 536870912 | bytes 4456448 | tf_op jit(solution)/shard_map/dot_general | solution.py:288
  141.4 4.7 %key_side.3 = bf16[2,128,512]{2,1,0:T(8,128)(2,1)S(1)} custom-call(s32[2]{0:T(128)S(1)} %pad_add_fusion.where_ref, bf16[2,256,512]{2,1,0:T(8,128)(2,1)S(1)} %get-tuple-element.29.refs_1_.refs_0_, bf16[2,256,512]{2,1,0:T(8,128)(2,1)S(1)} %get-tuple-element.33.refs_0_.refs_1_, f32[4,2,256]{2,1,0:T(2,128)S(1)} %get-tuple-element.36.refs_2_, ...), custom_call_target="tpu_custom_call" | custom-call | flops 81920 | bytes 65536 | tf_op jit(solution)/shard_map/key_side/pallas_call | solution.py:188
  146.2 0.8 fusion.29
  147.0 0.8 fusion.18
  147.8 2.8 %collective-permute-start.23 = (bf16[128,2048]{1,0:T(8,128)(2,1)S(1)}, bf16[128,2048]{1,0:T(8,128)(2,1)S(1)}, u32[]{:S(2)}, u32[]{:S(2)}) collective-permute-start(bf16[128,2048]{1,0:T(8,128)(2,1)S(1)} %fusion.18), channel_id=1, source_target_pairs={{0,1},{1,0},{2,3},{3,2},{4,5},{5,4},{6,7},{7,6},{8,9},{9,8},{10,11... | collective-permute-start | bytes 1572872 | tf_op jit(solution)/shard_map/ppermute | solution.py:29
  150.6 2.4 %fusion.1 = bf16[128,2048]{1,0:T(8,128)(2,1)} fusion(bf16[512,2048]{1,0:T(8,128)(2,1)S(1)} %copy-done.13, bf16[128,2048]{1,0:T(8,128)(2,1)S(1)} %copy-done.2, bf16[128,2048]{1,0:T(8,128)(2,1)} %collective-permute-done.16, bf16[256,512]{1,0:T(8,128)(2,1)S(1)} %copy-done.8), kind=kOutput, calls=%fused_computation.2 | convolution fusion | flops 269746176 | bytes 3801088 | tf_op jit(solution)/shard_map/dot_general | solution.py:284
  153.0 4.7 %key_side.2 = bf16[2,128,512]{2,1,0:T(8,128)(2,1)S(1)} custom-call(s32[2]{0:T(128)S(1)} %pad_add_fusion.where_ref, bf16[2,256,512]{2,1,0:T(8,128)(2,1)S(1)} %get-tuple-element.29.refs_1_.refs_0_, bf16[2,256,512]{2,1,0:T(8,128)(2,1)S(1)} %get-tuple-element.33.refs_0_.refs_1_, f32[4,2,256]{2,1,0:T(2,128)S(1)} %get-tuple-element.36.refs_2_, ...), custom_call_target="tpu_custom_call" | custom-call | flops 81920 | bytes 65536 | tf_op jit(solution)/shard_map/key_side/pallas_call | solution.py:188
  157.7 0.8 fusion.31
  158.5 4.7 %collective-permute-done.23 = bf16[128,2048]{1,0:T(8,128)(2,1)S(1)} collective-permute-done((bf16[128,2048]{1,0:T(8,128)(2,1)S(1)}, bf16[128,2048]{1,0:T(8,128)(2,1)S(1)}, u32[]{:S(2)}, u32[]{:S(2)}) %collective-permute-start.23) | collective-permute-done | bytes 524320 | tf_op jit(solution)/shard_map/ppermute | solution.py:29
  163.2 1.0 fusion.12
  164.2 1.2 fusion.16
  (57 shorter events, 0.2 us)
Async XLA Ops:
  0.6 9.8 %copy-start = (bf16[2048,512]{1,0:T(8,128)(2,1)S(1)}, bf16[2048,512]{1,0:T(8,128)(2,1)}, u32[]{:S(2)}) copy-start(bf16[2048,512]{1,0:T(8,128)(2,1)} %param.11) | copy-start | bytes 6291460
  0.6 1.2 copy-start.1
  1.8 1.0 copy-start.3
  2.9 0.7 copy-start.9
  3.6 6.4 %copy-start.14 = (bf16[2048,512]{1,0:T(8,128)(2,1)S(1)}, bf16[2048,512]{1,0:T(8,128)(2,1)}, u32[]{:S(2)}) copy-start(bf16[2048,512]{1,0:T(8,128)(2,1)} %param.10) | copy-start | bytes 6291460
  4.2 26.5 %collective-permute-start = (bf16[2,128,2048]{2,1,0:T(8,128)(2,1)S(1)}, bf16[2,128,2048]{2,1,0:T(8,128)(2,1)S(1)}, u32[]{:S(2)}, u32[]{:S(2)}) collective-permute-start(bf16[2,128,2048]{2,1,0:T(8,128)(2,1)S(1)} %get-tuple-element.25), channel_id=1, source_target_pairs={{0,1},{1,0},{2,3},{3,2},{4,5},{5,4},{6,7},{7,6},{8,9},{9,8},{10,11... | collective-permute-start | bytes 3145736 | tf_op jit(solution)/shard_map/ppermute | solution.py:29
  9.9 1.6 copy-start.16
  11.5 19.6 %copy-start.11 = (bf16[512,2048]{1,0:T(8,128)(2,1)S(1)}, bf16[512,2048]{1,0:T(8,128)(2,1)}, u32[]{:S(2)}) copy-start(bf16[512,2048]{1,0:T(8,128)(2,1)} %param.12) | copy-start | bytes 6291460
  33.0 19.9 %collective-permute-start.1 = (bf16[2,256,512]{2,1,0:T(8,128)(2,1)S(1)}, bf16[2,256,512]{2,1,0:T(8,128)(2,1)S(1)}, u32[]{:S(2)}, u32[]{:S(2)}) collective-permute-start(bf16[2,256,512]{2,1,0:T(8,128)(2,1)S(1)} %get-tuple-element.29.refs_1_.refs_0_), channel_id=1, source_target_pairs={{0,4},{2,6},{4,8},{6,10},{8,12},{10,14},{12,16},{14,18},{16,20},{1... | collective-permute-start | bytes 1572872 | tf_op jit(solution)/shard_map/ppermute | solution.py:25
  36.9 19.3 %collective-permute-start.8 = (bf16[2,256,512]{2,1,0:T(8,128)(2,1)S(1)}, bf16[2,256,512]{2,1,0:T(8,128)(2,1)}, u32[]{:S(2)}, u32[]{:S(2)}) collective-permute-start(bf16[2,256,512]{2,1,0:T(8,128)(2,1)S(1)} %get-tuple-element.33.refs_0_.refs_1_), channel_id=1, source_target_pairs={{4,0},{6,2},{8,4},{10,6},{12,8},{14,10},{16,12},{18,14},{20,16},{2... | collective-permute-start | bytes 1572872 | tf_op jit(solution)/shard_map/ppermute | solution.py:25
  53.0 3.2 %copy-start.5 = (bf16[2,256,512]{2,1,0:T(8,128)(2,1)}, bf16[2,256,512]{2,1,0:T(8,128)(2,1)S(1)}, u32[]{:S(2)}) copy-start(bf16[2,256,512]{2,1,0:T(8,128)(2,1)S(1)} %collective-permute-done.1.refs_3_) | copy-start | bytes 1572868
  53.0 17.2 %collective-permute-start.2 = (bf16[2,256,512]{2,1,0:T(8,128)(2,1)S(1)}, bf16[2,256,512]{2,1,0:T(8,128)(2,1)}, u32[]{:S(2)}, u32[]{:S(2)}) collective-permute-start(bf16[2,256,512]{2,1,0:T(8,128)(2,1)S(1)} %collective-permute-done.1.refs_3_), channel_id=1, source_target_pairs={{0,4},{2,6},{4,8},{6,10},{8,12},{10,14},{12,16},{14,18},{16,20},{1... | collective-permute-start | bytes 1572872 | tf_op jit(solution)/shard_map/ppermute | solution.py:25
  54.9 26.8 %collective-permute-start.5 = (bf16[2,256,512]{2,1,0:T(8,128)(2,1)S(1)}, bf16[2,256,512]{2,1,0:T(8,128)(2,1)}, u32[]{:S(2)}, u32[]{:S(2)}) collective-permute-start(bf16[2,256,512]{2,1,0:T(8,128)(2,1)S(1)} %get-tuple-element.29.refs_1_.refs_0_), channel_id=1, source_target_pairs={{0,64},{2,66},{4,68},{6,70},{8,72},{10,74},{12,76},{14,78},{16,80}... | collective-permute-start | bytes 1572872 | tf_op jit(solution)/shard_map/ppermute | solution.py:25
  56.2 27.1 %collective-permute-start.9 = (bf16[2,256,512]{2,1,0:T(8,128)(2,1)}, bf16[2,256,512]{2,1,0:T(8,128)(2,1)}, u32[]{:S(2)}, u32[]{:S(2)}) collective-permute-start(bf16[2,256,512]{2,1,0:T(8,128)(2,1)} %collective-permute-done.8.refs_4_), channel_id=1, source_target_pairs={{4,0},{6,2},{8,4},{10,6},{12,8},{14,10},{16,12},{18,14},{20,16},{2... | collective-permute-start | bytes 1572872 | tf_op jit(solution)/shard_map/ppermute | solution.py:25
  70.2 25.9 %collective-permute-start.3 = (bf16[2,256,512]{2,1,0:T(8,128)(2,1)}, bf16[2,256,512]{2,1,0:T(8,128)(2,1)}, u32[]{:S(2)}, u32[]{:S(2)}) collective-permute-start(bf16[2,256,512]{2,1,0:T(8,128)(2,1)} %collective-permute-done.2.refs_4_), channel_id=1, source_target_pairs={{0,8},{2,10},{4,12},{6,14},{8,16},{10,18},{12,20},{14,22},{16,24},... | collective-permute-start | bytes 1572872 | tf_op jit(solution)/shard_map/ppermute | solution.py:25
  72.2 24.0 %collective-permute-start.12 = (bf16[2,256,512]{2,1,0:T(8,128)(2,1)S(1)}, bf16[2,256,512]{2,1,0:T(8,128)(2,1)S(1)}, u32[]{:S(2)}, u32[]{:S(2)}) collective-permute-start(bf16[2,256,512]{2,1,0:T(8,128)(2,1)S(1)} %get-tuple-element.33.refs_0_.refs_1_), channel_id=1, source_target_pairs={{64,0},{66,2},{68,4},{70,6},{72,8},{74,10},{76,12},{78,14},{80,16}... | collective-permute-start | bytes 1572872 | tf_op jit(solution)/shard_map/ppermute | solution.py:25
  81.8 25.1 %copy-start.6 = (bf16[2,256,512]{2,1,0:T(8,128)(2,1)S(1)}, bf16[2,256,512]{2,1,0:T(8,128)(2,1)}, u32[]{:S(2)}) copy-start(bf16[2,256,512]{2,1,0:T(8,128)(2,1)} %copy-done.5) | copy-start | bytes 1572868
  81.8 24.9 %collective-permute-start.6 = (bf16[2,256,512]{2,1,0:T(8,128)(2,1)S(1)}, bf16[2,256,512]{2,1,0:T(8,128)(2,1)S(1)}, u32[]{:S(2)}, u32[]{:S(2)}) collective-permute-start(bf16[2,256,512]{2,1,0:T(8,128)(2,1)S(1)} %broadcast_select_fusion.1), channel_id=1, source_target_pairs={{0,32},{2,34},{4,36},{6,38},{8,40},{10,42},{12,44},{14,46},{16,48}... | collective-permute-start | bytes 1572872 | tf_op jit(solution)/shard_map/ppermute | solution.py:295
  81.9 24.9 %collective-permute-start.7 = (bf16[2,256,512]{2,1,0:T(8,128)(2,1)}, bf16[2,256,512]{2,1,0:T(8,128)(2,1)S(1)}, u32[]{:S(2)}, u32[]{:S(2)}) collective-permute-start(bf16[2,256,512]{2,1,0:T(8,128)(2,1)} %collective-permute-done.5.refs_7_), channel_id=1, source_target_pairs={{0,64},{2,66},{4,68},{6,70},{8,72},{10,74},{12,76},{14,78},{16,80}... | collective-permute-start | bytes 1572872 | tf_op jit(solution)/shard_map/ppermute | solution.py:25
  83.3 18.0 %collective-permute-start.10 = (bf16[2,256,512]{2,1,0:T(8,128)(2,1)}, bf16[2,256,512]{2,1,0:T(8,128)(2,1)S(1)}, u32[]{:S(2)}, u32[]{:S(2)}) collective-permute-start(bf16[2,256,512]{2,1,0:T(8,128)(2,1)} %collective-permute-done.9.refs_5_), channel_id=1, source_target_pairs={{8,0},{10,2},{12,4},{14,6},{16,8},{18,10},{20,12},{22,14},{24,16},... | collective-permute-start | bytes 1572872 | tf_op jit(solution)/shard_map/ppermute | solution.py:25
  96.1 10.7 %collective-permute-start.4 = (bf16[2,256,512]{2,1,0:T(8,128)(2,1)S(1)}, bf16[2,256,512]{2,1,0:T(8,128)(2,1)S(1)}, u32[]{:S(2)}, u32[]{:S(2)}) collective-permute-start(bf16[2,256,512]{2,1,0:T(8,128)(2,1)S(1)} %broadcast_select_fusion.3), channel_id=1, source_target_pairs={{0,2},{2,0},{4,6},{6,4},{8,10},{10,8},{12,14},{14,12},{16,18},{18,... | collective-permute-start | bytes 1572872 | tf_op jit(solution)/shard_map/ppermute | solution.py:295
  96.3 16.8 %copy-start.17 = (bf16[2,256,512]{2,1,0:T(8,128)(2,1)}, bf16[2,256,512]{2,1,0:T(8,128)(2,1)S(1)}, u32[]{:S(2)}) copy-start(bf16[2,256,512]{2,1,0:T(8,128)(2,1)S(1)} %collective-permute-done.12.refs_8_) | copy-start | bytes 1572868
  96.3 21.4 %collective-permute-start.13 = (bf16[2,256,512]{2,1,0:T(8,128)(2,1)S(1)}, bf16[2,256,512]{2,1,0:T(8,128)(2,1)S(1)}, u32[]{:S(2)}, u32[]{:S(2)}) collective-permute-start(bf16[2,256,512]{2,1,0:T(8,128)(2,1)S(1)} %broadcast_select_fusion), channel_id=1, source_target_pairs={{0,32},{2,34},{4,36},{6,38},{8,40},{10,42},{12,44},{14,46},{16,48}... | collective-permute-start | bytes 1572872 | tf_op jit(solution)/shard_map/ppermute | solution.py:295
  101.3 4.3 %copy-start.18 = (bf16[2,256,512]{2,1,0:T(8,128)(2,1)}, bf16[2,256,512]{2,1,0:T(8,128)(2,1)S(1)}, u32[]{:S(2)}) copy-start(bf16[2,256,512]{2,1,0:T(8,128)(2,1)S(1)} %collective-permute-done.10.refs_6_) | copy-start | bytes 1572868
  101.3 16.5 %collective-permute-start.14 = (bf16[2,256,512]{2,1,0:T(8,128)(2,1)S(1)}, bf16[2,256,512]{2,1,0:T(8,128)(2,1)S(1)}, u32[]{:S(2)}, u32[]{:S(2)}) collective-permute-start(bf16[2,256,512]{2,1,0:T(8,128)(2,1)S(1)} %collective-permute-done.12.refs_8_), channel_id=1, source_target_pairs={{64,0},{66,2},{68,4},{70,6},{72,8},{74,10},{76,12},{78,14},{80,16}... | collective-permute-start | bytes 1572872 | tf_op jit(solution)/shard_map/ppermute | solution.py:25
  106.7 7.1 %copy-start.12 = (bf16[512,2048]{1,0:T(8,128)(2,1)S(1)}, bf16[512,2048]{1,0:T(8,128)(2,1)}, u32[]{:S(2)}) copy-start(bf16[512,2048]{1,0:T(8,128)(2,1)} %param.12) | copy-start | bytes 6291460
  106.7 11.1 %collective-permute-start.11 = (bf16[2,256,512]{2,1,0:T(8,128)(2,1)S(1)}, bf16[2,256,512]{2,1,0:T(8,128)(2,1)S(1)}, u32[]{:S(2)}, u32[]{:S(2)}) collective-permute-start(bf16[2,256,512]{2,1,0:T(8,128)(2,1)S(1)} %broadcast_select_fusion.2), channel_id=1, source_target_pairs={{0,2},{2,0},{4,6},{6,4},{8,10},{10,8},{12,14},{14,12},{16,18},{18,... | collective-permute-start | bytes 1572872 | tf_op jit(solution)/shard_map/ppermute | solution.py:295
  113.0 0.7 copy-start.7
  115.0 20.9 %collective-permute-start.16 = (bf16[128,2048]{1,0:T(8,128)(2,1)}, bf16[128,2048]{1,0:T(8,128)(2,1)}, u32[]{:S(2)}, u32[]{:S(2)}) collective-permute-start(bf16[128,2048]{1,0:T(8,128)(2,1)} %convolution_convert_fusion), channel_id=1, source_target_pairs={{0,1},{1,0},{2,3},{3,2},{4,5},{5,4},{6,7},{7,6},{8,9},{9,8},{10,11... | collective-permute-start | bytes 1572872 | tf_op jit(solution)/shard_map/ppermute | solution.py:29
  117.8 0.8 copy-start.19
  117.8 8.1 %copy-start.20 = (bf16[2,256,512]{2,1,0:T(8,128)(2,1)}, bf16[2,256,512]{2,1,0:T(8,128)(2,1)S(1)}, u32[]{:S(2)}) copy-start(bf16[2,256,512]{2,1,0:T(8,128)(2,1)S(1)} %collective-permute-done.14.refs_9_) | copy-start | bytes 1572868
  117.8 10.6 %copy-start.21 = (bf16[2,256,512]{2,1,0:T(8,128)(2,1)}, bf16[2,256,512]{2,1,0:T(8,128)(2,1)S(1)}, u32[]{:S(2)}) copy-start(bf16[2,256,512]{2,1,0:T(8,128)(2,1)S(1)} %collective-permute-done.11.refs_3_) | copy-start | bytes 1572868
  118.6 15.4 %collective-permute-start.15 = (f32[4,2,256]{2,1,0:T(2,128)S(1)}, f32[4,2,256]{2,1,0:T(2,128)S(1)}, u32[]{:S(2)}, u32[]{:S(2)}) collective-permute-start(f32[4,2,256]{2,1,0:T(2,128)S(1)} %get-tuple-element.36.refs_2_), channel_id=1, source_target_pairs={{4,0},{6,2},{8,4},{10,6},{12,8},{14,10},{16,12},{18,14},{20,16},{2... | collective-permute-start | bytes 24584 | tf_op jit(solution)/shard_map/ppermute | solution.py:25
  125.9 10.0 %collective-permute-start.20 = (f32[4,2,256]{2,1,0:T(2,128)S(1)}, f32[4,2,256]{2,1,0:T(2,128)S(1)}, u32[]{:S(2)}, u32[]{:S(2)}) collective-permute-start(f32[4,2,256]{2,1,0:T(2,128)S(1)} %get-tuple-element.36.refs_2_), channel_id=1, source_target_pairs={{64,0},{66,2},{68,4},{70,6},{72,8},{74,10},{76,12},{78,14},{80,16}... | collective-permute-start | bytes 24584 | tf_op jit(solution)/shard_map/ppermute | solution.py:25
  128.4 12.9 %collective-permute-start.18 = (f32[4,2,256]{2,1,0:T(2,128)S(1)}, f32[4,2,256]{2,1,0:T(2,128)S(1)}, u32[]{:S(2)}, u32[]{:S(2)}) collective-permute-start(f32[4,2,256]{2,1,0:T(2,128)S(1)} %get-tuple-element.36.refs_2_), channel_id=1, source_target_pairs={{8,0},{10,2},{12,4},{14,6},{16,8},{18,10},{20,12},{22,14},{24,16},... | collective-permute-start | bytes 24584 | tf_op jit(solution)/shard_map/ppermute | solution.py:25
  130.6 10.8 %collective-permute-start.19 = (f32[4,2,256]{2,1,0:T(2,128)S(1)}, f32[4,2,256]{2,1,0:T(2,128)S(1)}, u32[]{:S(2)}, u32[]{:S(2)}) collective-permute-start(f32[4,2,256]{2,1,0:T(2,128)S(1)} %get-tuple-element.36.refs_2_), channel_id=1, source_target_pairs={{16,0},{18,2},{20,4},{22,6},{24,8},{26,10},{28,12},{30,14},{32,16}... | collective-permute-start | bytes 24584 | tf_op jit(solution)/shard_map/ppermute | solution.py:25
  134.0 7.4 %collective-permute-start.22 = (f32[4,2,256]{2,1,0:T(2,128)S(1)}, f32[4,2,256]{2,1,0:T(2,128)S(1)}, u32[]{:S(2)}, u32[]{:S(2)}) collective-permute-start(f32[4,2,256]{2,1,0:T(2,128)S(1)} %get-tuple-element.36.refs_2_), channel_id=1, source_target_pairs={{128,0},{130,2},{132,4},{134,6},{136,8},{138,10},{140,12},{142,14}... | collective-permute-start | bytes 24584 | tf_op jit(solution)/shard_map/ppermute | solution.py:25
  135.9 5.5 %collective-permute-start.17 = (f32[4,2,256]{2,1,0:T(2,128)S(1)}, f32[4,2,256]{2,1,0:T(2,128)S(1)}, u32[]{:S(2)}, u32[]{:S(2)}) collective-permute-start(f32[4,2,256]{2,1,0:T(2,128)S(1)} %bitcast.79), channel_id=1, source_target_pairs={{0,2},{2,0},{4,6},{6,4},{8,10},{10,8},{12,14},{14,12},{16,18},{18,... | collective-permute-start | bytes 24584 | tf_op jit(solution)/shard_map/ppermute | solution.py:295
  136.0 5.4 %collective-permute-start.21 = (f32[4,2,256]{2,1,0:T(2,128)S(1)}, f32[4,2,256]{2,1,0:T(2,128)S(1)}, u32[]{:S(2)}, u32[]{:S(2)}) collective-permute-start(f32[4,2,256]{2,1,0:T(2,128)S(1)} %bitcast.78), channel_id=1, source_target_pairs={{0,32},{2,34},{4,36},{6,38},{8,40},{10,42},{12,44},{14,46},{16,48}... | collective-permute-start | bytes 24584 | tf_op jit(solution)/shard_map/ppermute | solution.py:295
  141.4 4.8 %copy-start.15 = (bf16[2048,512]{1,0:T(8,128)(2,1)S(1)}, bf16[2048,512]{1,0:T(8,128)(2,1)}, u32[]{:S(2)}) copy-start(bf16[2048,512]{1,0:T(8,128)(2,1)} %param.10) | copy-start | bytes 6291460
  147.0 3.7 %copy-start.2 = (bf16[128,2048]{1,0:T(8,128)(2,1)S(1)}, bf16[128,2048]{1,0:T(8,128)(2,1)}, u32[]{:S(2)}) copy-start(bf16[128,2048]{1,0:T(8,128)(2,1)} %series_ref.1) | copy-start | bytes 1572868
  147.0 3.7 %copy-start.8 = (bf16[256,512]{1,0:T(8,128)(2,1)S(1)}, bf16[256,512]{1,0:T(8,128)(2,1)}, u32[]{:S(2)}) copy-start(bf16[256,512]{1,0:T(8,128)(2,1)} %copy-done.7) | copy-start | bytes 786436
  147.0 3.7 %copy-start.13 = (bf16[512,2048]{1,0:T(8,128)(2,1)S(1)}, bf16[512,2048]{1,0:T(8,128)(2,1)}, u32[]{:S(2)}) copy-start(bf16[512,2048]{1,0:T(8,128)(2,1)} %param.12) | copy-start | bytes 6291460
  147.8 15.4 %collective-permute-start.23 = (bf16[128,2048]{1,0:T(8,128)(2,1)S(1)}, bf16[128,2048]{1,0:T(8,128)(2,1)S(1)}, u32[]{:S(2)}, u32[]{:S(2)}) collective-permute-start(bf16[128,2048]{1,0:T(8,128)(2,1)S(1)} %fusion.18), channel_id=1, source_target_pairs={{0,1},{1,0},{2,3},{3,2},{4,5},{5,4},{6,7},{7,6},{8,9},{9,8},{10,11... | collective-permute-start | bytes 1572872 | tf_op jit(solution)/shard_map/ppermute | solution.py:29
  157.7 5.5 %copy-start.10 = (f32[2048]{0:T(1024)S(1)}, f32[2048]{0:T(1024)}, u32[]{:S(2)}) copy-start(f32[2048]{0:T(1024)} %param.8) | copy-start | bytes 24580
  158.5 5.7 %copy-start.4 = (bf16[128,2048]{1,0:T(8,128)(2,1)S(1)}, bf16[128,2048]{1,0:T(8,128)(2,1)}, u32[]{:S(2)}) copy-start(bf16[128,2048]{1,0:T(8,128)(2,1)} %grad_ref.1) | copy-start | bytes 1572868

commit v10 on v9

--- a/solution.py
+++ b/solution.py
@@ -262,6 +262,9 @@
 def normalize(series, gain, out_grad):
     rows, width = series.shape
     step = rows // 4
+    series, out_grad = [
+        pltpu.with_memory_space_constraint(a, pltpu.HBM) for a in (series, out_grad)
+    ]
     row_spec = pl.BlockSpec((step, width), lambda i: (i, 0))
     return pl.pallas_call(
         norm_kernel,
@@ -295,15 +298,26 @@
     return lax.ppermute(sent, "seq", [(i, i ^ bit) for i in range(size)])
 
 
-def exchange(rows, sign):
-    two = shifted(rows, sign * 2)
-    far = shifted(rows, sign * 32)
-    four = shifted(two, sign * 2)
-    eight = shifted(four, sign * 4)
-    sixteen = swapped(rows, far, 16, sign)
-    rows_last, two_last, eight = lax.optimization_barrier((rows, two, eight))
-    one = swapped(rows_last, two_last, 1, sign)
-    return [one, two, four, eight, sixteen, far, shifted(far, sign * 32)]
+def exchange(keys, queries):
+    two, two_q = shifted(keys, 2), shifted(queries, -2)
+    far, far_q = shifted(keys, 32), shifted(queries, -32)
+    two, far = lax.optimization_barrier((two, far))
+    two_q, far_q = lax.optimization_barrier((two_q, far_q))
+    four, four_q = shifted(two, 2), shifted(two_q, -2)
+    eight, eight_q = shifted(four, 4), shifted(four_q, -4)
+    last, last_q = shifted(far, 32), shifted(far_q, -32)
+    sixteen = swapped(keys, far, 16, 1)
+    sixteen_q = swapped(queries, far_q, 16, -1)
+    keys_late, two_late, eight, last_q, sixteen_q = lax.optimization_barrier(
+        (keys, two, eight, last_q, sixteen_q)
+    )
+    one = swapped(keys_late, two_late, 1, 1)
+    queries_late, two_q_late, eight_q = lax.optimization_barrier((queries, two_q, eight_q))
+    one_q = swapped(queries_late, two_q_late, 1, -1)
+    return (
+        [one, two, four, eight, sixteen, far, last],
+        [one_q, two_q, four_q, eight_q, sixteen_q, far_q, last_q],
+    )
 
 
 def exchange_stats(stat, attn_other):
@@ -341,8 +355,7 @@
     kv_all, qg_all = lax.optimization_barrier(
         (jnp.concatenate(kv, axis=1), jnp.concatenate(qg, axis=1))
     )
-    fetched = exchange(kv_all, 1)
-    later = exchange(qg_all, -1)
+    fetched, later = exchange(kv_all, qg_all)
     mixed, grad_query, stat = query_side(where, qg_all, kv_all, [(f,) for f in fetched], 0)
     stat, later = lax.optimization_barrier((stat, later))
     later = [(f,) for f in later]

time: 166 us -> 173 us (1.042)
  starting transfers between devices: 65 us -> 77 us
  waiting for transfers between devices: 59.5 us -> 48.3 us
  other arithmetic: 2.74 us -> 6.17 us
  Pallas kernels: 16.2 us -> 18.3 us
    ppermute x15, starting transfers between devices: 52.7 us -> 66.2 us  [shifted(): return lax.ppermute(value, 'seq', pairs)]
    ppermute x15, waiting for transfers between devices: 36.1 us -> 24.7 us  [shifted(): return lax.ppermute(value, 'seq', pairs)]
    pallas_call x1, Pallas kernels: 0.62 us -> 2.63 us  [normalize(): pl.pallas_call(norm_kernel, out_shape=[jax.ShapeDtypeStruct((2, rows, wid...]
    select_n x3, other arithmetic: 1.17 us -> 3 us  [swapped(): jnp.where(high, own, passed)]
    unnamed x44 -> x32, local copies, waits for them, and re-layouts: 5.12 us -> 4.85 us
  transfers between devices with their start and end apart: 24 -> 24, of which waited for: 7 -> 7; matrix products, arithmetic and copies ran while one was open for 7% -> 9% of each run, Pallas kernels for 7% -> 6%
where the time goes in v10:
time: 173 us; the launch traced here: 171 us
  starting transfers between devices  77 us (45%)
  waiting for transfers between devices  48.3 us (28%)
  Pallas kernels  18.3 us (11%)
  matrix products  15.5 us (9%)
  other arithmetic  6.17 us (4%)
  local copies, waits for them, and re-layouts  4.85 us (3%)
    ppermute x15, starting transfers between devices, shifted(): return lax.ppermute(value, 'seq', pairs)  66.2 us
    ppermute x15, waiting for transfers between devices, shifted(): return lax.ppermute(value, 'seq', pairs)  24.7 us
    ppermute x3, waiting for transfers between devices, swap_tp(): return lax.ppermute(value, 'tp', [(0, 1), (1, 0)])  22.9 us
    pallas_call x3, Pallas kernels, call(): pl.pallas_call(kernel, out_shape=outs, grid_spec=pltpu.PrefetchScalarGrid...  15.7 us
    dot_general x7, matrix products, matmul_t(): return lax.dot_general(a, b, NT, preferred_element_type=F32)  9.16 us
    ppermute x3, starting transfers between devices, swap_tp(): return lax.ppermute(value, 'tp', [(0, 1), (1, 0)])  8.39 us
    dot_general x8, matrix products, matmul(): return jnp.dot(a, b, preferred_element_type=F32)  6.36 us
    unnamed x32, local copies, waits for them, and re-layouts  4.85 us
  transfers between devices with their start and end apart: 24, of which 7 were waited for; matrix products, arithmetic and copies ran while one was open for 9% of the time, Pallas kernels for 6%

profile of v10, /device:TPU:24, one launch (start us, length us, event | category | flops | bytes accessed | tf_op | source)
XLA Modules:
  0.0 171.4 jit_solution(13091028255377494188)
XLA Ops:
  0.6 0.0 copy-start
  0.7 0.8 copy-done.5
  1.5 2.6 %normalize.1 = (bf16[2,128,2048]{2,1,0:T(8,128)(2,1)S(1)}, f32[128,1]{1,0:T(8,128)S(1)}) custom-call(bf16[128,2048]{1,0:T(8,128)(2,1)} %series_ref.1, f32[1,2048]{1,0:T(1,128)S(1)} %bitcast.77, bf16[128,2048]{1,0:T(8,128)(2,1)} %grad_ref.1), custom_call_target="tpu_custom_call" | custom-call | tf_op jit(solution)/shard_map/normalize/pallas_call | solution.py:269
  4.1 3.1 %collective-permute-start = (bf16[2,128,2048]{2,1,0:T(8,128)(2,1)S(1)}, bf16[2,128,2048]{2,1,0:T(8,128)(2,1)S(1)}, u32[]{:S(2)}, u32[]{:S(2)}) collective-permute-start(bf16[2,128,2048]{2,1,0:T(8,128)(2,1)S(1)} %get-tuple-element.31), channel_id=1, source_target_pairs={{0,1},{1,0},{2,3},{3,2},{4,5},{5,4},{6,7},{7,6},{8,9},{9,8},{10,11... | collective-permute-start | bytes 3145736 | tf_op jit(solution)/shard_map/ppermute | solution.py:29
  7.2 2.6 %fusion.9 = bf16[1,128,512]{2,1,0:T(8,128)(2,1)S(1)} fusion(bf16[128,2048]{1,0:T(8,128)(2,1)} %grad_ref.1, bf16[512,2048]{1,0:T(8,128)(2,1)} %param.12), kind=kOutput, calls=%fused_computation.20 | convolution fusion | flops 268500992 | bytes 2752512 | tf_op jit(solution)/shard_map/dot_general | solution.py:291
  9.9 0.0 copy-start.10
  9.9 0.5 fusion.8
  10.4 0.4 fusion.5
  10.8 0.6 copy-done.10
  11.5 0.5 fusion.4
  11.9 18.7 %collective-permute-done = bf16[2,128,2048]{2,1,0:T(8,128)(2,1)S(1)} collective-permute-done((bf16[2,128,2048]{2,1,0:T(8,128)(2,1)S(1)}, bf16[2,128,2048]{2,1,0:T(8,128)(2,1)S(1)}, u32[]{:S(2)}, u32[]{:S(2)}) %collective-permute-start) | collective-permute-done | bytes 1048608 | tf_op jit(solution)/shard_map/ppermute | solution.py:29
  30.6 0.5 fusion.7
  31.1 0.5 fusion.10
  31.6 0.8 fusion.11
  32.4 0.4 fusion.6
  32.9 0.1 maximum_maximum_fusion
  33.0 1.3 collective-permute-start.2
  34.3 3.8 %collective-permute-start.1 = (bf16[2,256,512]{2,1,0:T(8,128)(2,1)S(1)}, bf16[2,256,512]{2,1,0:T(8,128)(2,1)}, u32[]{:S(2)}, u32[]{:S(2)}) collective-permute-start(bf16[2,256,512]{2,1,0:T(8,128)(2,1)S(1)} %get-tuple-element.37.refs_1_.refs_0_), channel_id=1, source_target_pairs={{0,4},{2,6},{4,8},{6,10},{8,12},{10,14},{12,16},{14,18},{16,20},{1... | collective-permute-start | bytes 1572872 | tf_op jit(solution)/shard_map/ppermute | solution.py:25
  38.1 5.4 %collective-permute-start.6 = (bf16[2,256,512]{2,1,0:T(8,128)(2,1)S(1)}, bf16[2,256,512]{2,1,0:T(8,128)(2,1)}, u32[]{:S(2)}, u32[]{:S(2)}) collective-permute-start(bf16[2,256,512]{2,1,0:T(8,128)(2,1)S(1)} %get-tuple-element.43.refs_0_.refs_1_), channel_id=1, source_target_pairs={{64,0},{66,2},{68,4},{70,6},{72,8},{74,10},{76,12},{78,14},{80,16}... | collective-permute-start | bytes 1572872 | tf_op jit(solution)/shard_map/ppermute | solution.py:25
  43.4 6.2 %collective-permute-start.5 = (bf16[2,256,512]{2,1,0:T(8,128)(2,1)S(1)}, bf16[2,256,512]{2,1,0:T(8,128)(2,1)}, u32[]{:S(2)}, u32[]{:S(2)}) collective-permute-start(bf16[2,256,512]{2,1,0:T(8,128)(2,1)S(1)} %get-tuple-element.43.refs_0_.refs_1_), channel_id=1, source_target_pairs={{4,0},{6,2},{8,4},{10,6},{12,8},{14,10},{16,12},{18,14},{20,16},{2... | collective-permute-start | bytes 1572872 | tf_op jit(solution)/shard_map/ppermute | solution.py:25
  49.6 9.3 %collective-permute-done.2.refs_7_ = bf16[2,256,512]{2,1,0:T(8,128)(2,1)S(1)} collective-permute-done((bf16[2,256,512]{2,1,0:T(8,128)(2,1)S(1)}, bf16[2,256,512]{2,1,0:T(8,128)(2,1)S(1)}, u32[]{:S(2)}, u32[]{:S(2)}) %collective-permute-start.2) | collective-permute-done | bytes 524320 | tf_op jit(solution)/shard_map/ppermute | solution.py:25
  58.9 0.8 copy-done.1
  59.7 1.9 %collective-permute-start.3 = (bf16[2,256,512]{2,1,0:T(8,128)(2,1)}, bf16[2,256,512]{2,1,0:T(8,128)(2,1)}, u32[]{:S(2)}, u32[]{:S(2)}) collective-permute-start(bf16[2,256,512]{2,1,0:T(8,128)(2,1)} %collective-permute-done.1.refs_3_), channel_id=1, source_target_pairs={{0,4},{2,6},{4,8},{6,10},{8,12},{10,14},{12,16},{14,18},{16,20},{1... | collective-permute-start | bytes 1572872 | tf_op jit(solution)/shard_map/ppermute | solution.py:25
  61.7 11.0 %collective-permute-start.12 = (bf16[2,256,512]{2,1,0:T(8,128)(2,1)}, bf16[2,256,512]{2,1,0:T(8,128)(2,1)}, u32[]{:S(2)}, u32[]{:S(2)}) collective-permute-start(bf16[2,256,512]{2,1,0:T(8,128)(2,1)} %collective-permute-done.5.refs_4_), channel_id=1, source_target_pairs={{4,0},{6,2},{8,4},{10,6},{12,8},{14,10},{16,12},{18,14},{20,16},{2... | collective-permute-start | bytes 1572872 | tf_op jit(solution)/shard_map/ppermute | solution.py:25
  72.7 1.9 %broadcast_select_fusion.1 = bf16[2,256,512]{2,1,0:T(8,128)(2,1)} fusion(bf16[2,256,512]{2,1,0:T(8,128)(2,1)S(1)} %get-tuple-element.43.refs_0_.refs_1_, bf16[2,256,512]{2,1,0:T(8,128)(2,1)} %collective-permute-done.6.refs_8_, pred[]{:T(512)S(6)} %eq.18), kind=kLoop, calls=%fused_computation.43 | loop fusion | flops 262144 | bytes 1572865 | tf_op jit(solution)/shard_map/jit(_where)/select_n | solution.py:297
  74.6 3.5 %collective-permute-start.7 = (bf16[2,256,512]{2,1,0:T(8,128)(2,1)}, bf16[2,256,512]{2,1,0:T(8,128)(2,1)}, u32[]{:S(2)}, u32[]{:S(2)}) collective-permute-start(bf16[2,256,512]{2,1,0:T(8,128)(2,1)} %collective-permute-done.6.refs_8_), channel_id=1, source_target_pairs={{64,0},{66,2},{68,4},{70,6},{72,8},{74,10},{76,12},{78,14},{80,16}... | collective-permute-start | bytes 1572872 | tf_op jit(solution)/shard_map/ppermute | solution.py:25
  78.0 1.9 %collective-permute-start.4 = (bf16[2,256,512]{2,1,0:T(8,128)(2,1)}, bf16[2,256,512]{2,1,0:T(8,128)(2,1)}, u32[]{:S(2)}, u32[]{:S(2)}) collective-permute-start(bf16[2,256,512]{2,1,0:T(8,128)(2,1)} %collective-permute-done.3.refs_4_), channel_id=1, source_target_pairs={{0,8},{2,10},{4,12},{6,14},{8,16},{10,18},{12,20},{14,22},{16,24},... | collective-permute-start | bytes 1572872 | tf_op jit(solution)/shard_map/ppermute | solution.py:25
  80.0 1.3 collective-permute-start.11
  81.3 0.9 broadcast_select_fusion
  82.1 9.5 %collective-permute-start.13 = (bf16[2,256,512]{2,1,0:T(8,128)(2,1)}, bf16[2,256,512]{2,1,0:T(8,128)(2,1)}, u32[]{:S(2)}, u32[]{:S(2)}) collective-permute-start(bf16[2,256,512]{2,1,0:T(8,128)(2,1)} %collective-permute-done.12.refs_5_), channel_id=1, source_target_pairs={{8,0},{10,2},{12,4},{14,6},{16,8},{18,10},{20,12},{22,14},{24,16},... | collective-permute-start | bytes 1572872 | tf_op jit(solution)/shard_map/ppermute | solution.py:25
  91.7 0.1 collective-permute-start.10
  91.8 9.8 %collective-permute-done.4.refs_5_ = bf16[2,256,512]{2,1,0:T(8,128)(2,1)} collective-permute-done((bf16[2,256,512]{2,1,0:T(8,128)(2,1)}, bf16[2,256,512]{2,1,0:T(8,128)(2,1)}, u32[]{:S(2)}, u32[]{:S(2)}) %collective-permute-start.4) | collective-permute-done | bytes 524320 | tf_op jit(solution)/shard_map/ppermute | solution.py:25
  101.6 0.9 broadcast_select_fusion.3
  102.4 0.8 collective-permute-start.9
  103.2 0.1 pad_add_fusion.where_ref
  103.3 3.9 %collective-permute-done.13.refs_6_ = bf16[2,256,512]{2,1,0:T(8,128)(2,1)} collective-permute-done((bf16[2,256,512]{2,1,0:T(8,128)(2,1)}, bf16[2,256,512]{2,1,0:T(8,128)(2,1)}, u32[]{:S(2)}, u32[]{:S(2)}) %collective-permute-start.13) | collective-permute-done | bytes 524320 | tf_op jit(solution)/shard_map/ppermute | solution.py:25
  107.2 1.1 broadcast_select_fusion.2
  108.3 0.1 collective-permute-start.14
  108.4 0.7 collective-permute-done.10.refs_6_
  109.0 1.0 copy-done.2
  110.1 6.3 %query_side.1 = (bf16[256,512]{1,0:T(8,128)(2,1)S(1)}, bf16[256,512]{1,0:T(8,128)(2,1)S(1)}, f32[4,2,256]{2,1,0:T(2,128)S(1)}) custom-call(s32[2]{0:T(128)S(1)} %pad_add_fusion.where_ref, bf16[2,256,512]{2,1,0:T(8,128)(2,1)S(1)} %get-tuple-element.43.refs_0_.refs_1_, bf16[2,256,512]{2,1,0:T(8,128)(2,1)S(1)} %get-tuple-element.37.refs_1_.refs_0_, ...), custom_call_target="tpu_custom_call" | custom-call | flops 163840 | bytes 65536 | tf_op jit(solution)/shard_map/query_side/pallas_call | solution.py:188
  116.4 0.7 copy-done.3
  117.1 1.2 convolution_convert_fusion
  118.4 3.2 %collective-permute-start.16 = (bf16[128,2048]{1,0:T(8,128)(2,1)}, bf16[128,2048]{1,0:T(8,128)(2,1)}, u32[]{:S(2)}, u32[]{:S(2)}) collective-permute-start(bf16[128,2048]{1,0:T(8,128)(2,1)} %convolution_convert_fusion), channel_id=1, source_target_pairs={{0,1},{1,0},{2,3},{3,2},{4,5},{5,4},{6,7},{7,6},{8,9},{9,8},{10,11... | collective-permute-start | bytes 1572872 | tf_op jit(solution)/shard_map/ppermute | solution.py:29
  121.5 0.8 copy-done.15
  122.3 12.4 %collective-permute-start.15 = (f32[4,2,256]{2,1,0:T(2,128)S(1)}, f32[4,2,256]{2,1,0:T(2,128)S(1)}, u32[]{:S(2)}, u32[]{:S(2)}) collective-permute-start(f32[4,2,256]{2,1,0:T(2,128)S(1)} %get-tuple-element.48.refs_2_), channel_id=1, source_target_pairs={{4,0},{6,2},{8,4},{10,6},{12,8},{14,10},{16,12},{18,14},{20,16},{2... | collective-permute-start | bytes 24584 | tf_op jit(solution)/shard_map/ppermute | solution.py:25
  134.8 2.9 %collective-permute-start.20 = (f32[4,2,256]{2,1,0:T(2,128)S(1)}, f32[4,2,256]{2,1,0:T(2,128)S(1)}, u32[]{:S(2)}, u32[]{:S(2)}) collective-permute-start(f32[4,2,256]{2,1,0:T(2,128)S(1)} %get-tuple-element.48.refs_2_), channel_id=1, source_target_pairs={{64,0},{66,2},{68,4},{70,6},{72,8},{74,10},{76,12},{78,14},{80,16}... | collective-permute-start | bytes 24584 | tf_op jit(solution)/shard_map/ppermute | solution.py:25
  137.7 0.1 reduce
  137.8 1.3 collective-permute-start.22
  139.1 1.9 %collective-permute-start.19 = (f32[4,2,256]{2,1,0:T(2,128)S(1)}, f32[4,2,256]{2,1,0:T(2,128)S(1)}, u32[]{:S(2)}, u32[]{:S(2)}) collective-permute-start(f32[4,2,256]{2,1,0:T(2,128)S(1)} %get-tuple-element.48.refs_2_), channel_id=1, source_target_pairs={{16,0},{18,2},{20,4},{22,6},{24,8},{26,10},{28,12},{30,14},{32,16}... | collective-permute-start | bytes 24584 | tf_op jit(solution)/shard_map/ppermute | solution.py:25
  141.0 1.9 %collective-permute-start.18 = (f32[4,2,256]{2,1,0:T(2,128)S(1)}, f32[4,2,256]{2,1,0:T(2,128)S(1)}, u32[]{:S(2)}, u32[]{:S(2)}) collective-permute-start(f32[4,2,256]{2,1,0:T(2,128)S(1)} %get-tuple-element.48.refs_2_), channel_id=1, source_target_pairs={{8,0},{10,2},{12,4},{14,6},{16,8},{18,10},{20,12},{22,14},{24,16},... | collective-permute-start | bytes 24584 | tf_op jit(solution)/shard_map/ppermute | solution.py:25
  143.0 1.5 collective-permute-start.21
  144.5 2.3 %fusion.34 = f32[256,2048]{1,0:T(8,128)S(1)} fusion(bf16[256,512]{1,0:T(8,128)(2,1)S(1)} %get-tuple-element.51, bf16[2048,512]{1,0:T(8,128)(2,1)} %param.9), kind=kOutput, calls=%fused_computation.63 | convolution fusion | flops 536870912 | bytes 4456448 | tf_op jit(solution)/shard_map/dot_general | solution.py:291
  146.8 1.7 collective-permute-done.19.refs_13_
  148.5 4.7 %key_side.3 = bf16[2,128,512]{2,1,0:T(8,128)(2,1)S(1)} custom-call(s32[2]{0:T(128)S(1)} %pad_add_fusion.where_ref, bf16[2,256,512]{2,1,0:T(8,128)(2,1)S(1)} %get-tuple-element.37.refs_1_.refs_0_, bf16[2,256,512]{2,1,0:T(8,128)(2,1)S(1)} %get-tuple-element.43.refs_0_.refs_1_, f32[4,2,256]{2,1,0:T(2,128)S(1)} %get-tuple-element.48.refs_2_, ...), custom_call_target="tpu_custom_call" | custom-call | flops 81920 | bytes 65536 | tf_op jit(solution)/shard_map/key_side/pallas_call | solution.py:188
  153.3 0.8 fusion.29
  154.1 0.8 fusion.18
  154.9 2.1 %collective-permute-start.23 = (bf16[128,2048]{1,0:T(8,128)(2,1)S(1)}, bf16[128,2048]{1,0:T(8,128)(2,1)S(1)}, u32[]{:S(2)}, u32[]{:S(2)}) collective-permute-start(bf16[128,2048]{1,0:T(8,128)(2,1)S(1)} %fusion.18), channel_id=1, source_target_pairs={{0,1},{1,0},{2,3},{3,2},{4,5},{5,4},{6,7},{7,6},{8,9},{9,8},{10,11... | collective-permute-start | bytes 1572872 | tf_op jit(solution)/shard_map/ppermute | solution.py:29
  157.0 2.4 %fusion.1 = bf16[128,2048]{1,0:T(8,128)(2,1)} fusion(bf16[512,2048]{1,0:T(8,128)(2,1)S(1)} %copy-done.9, bf16[128,2048]{1,0:T(8,128)(2,1)S(1)} %copy-done.13, bf16[128,2048]{1,0:T(8,128)(2,1)} %collective-permute-done.16, bf16[256,512]{1,0:T(8,128)(2,1)S(1)} %copy-done.4), kind=kOutput, calls=%fused_computation.2 | convolution fusion | flops 269746176 | bytes 3801088 | tf_op jit(solution)/shard_map/dot_general | solution.py:287
  159.4 4.7 %key_side.2 = bf16[2,128,512]{2,1,0:T(8,128)(2,1)S(1)} custom-call(s32[2]{0:T(128)S(1)} %pad_add_fusion.where_ref, bf16[2,256,512]{2,1,0:T(8,128)(2,1)S(1)} %get-tuple-element.37.refs_1_.refs_0_, bf16[2,256,512]{2,1,0:T(8,128)(2,1)S(1)} %get-tuple-element.43.refs_0_.refs_1_, f32[4,2,256]{2,1,0:T(2,128)S(1)} %get-tuple-element.48.refs_2_, ...), custom_call_target="tpu_custom_call" | custom-call | flops 81920 | bytes 65536 | tf_op jit(solution)/shard_map/key_side/pallas_call | solution.py:188
  164.1 0.8 fusion.31
  164.9 4.3 %collective-permute-done.23 = bf16[128,2048]{1,0:T(8,128)(2,1)S(1)} collective-permute-done((bf16[128,2048]{1,0:T(8,128)(2,1)S(1)}, bf16[128,2048]{1,0:T(8,128)(2,1)S(1)}, u32[]{:S(2)}, u32[]{:S(2)}) %collective-permute-start.23) | collective-permute-done | bytes 524320 | tf_op jit(solution)/shard_map/ppermute | solution.py:29
  169.2 1.0 fusion.12
  170.2 1.2 fusion.16
  (45 shorter events, 0.1 us)
Async XLA Ops:
  0.6 9.7 %copy-start = (bf16[2048,512]{1,0:T(8,128)(2,1)S(1)}, bf16[2048,512]{1,0:T(8,128)(2,1)}, u32[]{:S(2)}) copy-start(bf16[2048,512]{1,0:T(8,128)(2,1)} %param.11) | copy-start | bytes 6291460
  0.6 0.8 copy-start.5
  1.5 8.4 %copy-start.12 = (bf16[2048,512]{1,0:T(8,128)(2,1)S(1)}, bf16[2048,512]{1,0:T(8,128)(2,1)}, u32[]{:S(2)}) copy-start(bf16[2048,512]{1,0:T(8,128)(2,1)} %param.9) | copy-start | bytes 6291460
  4.1 26.5 %collective-permute-start = (bf16[2,128,2048]{2,1,0:T(8,128)(2,1)S(1)}, bf16[2,128,2048]{2,1,0:T(8,128)(2,1)S(1)}, u32[]{:S(2)}, u32[]{:S(2)}) collective-permute-start(bf16[2,128,2048]{2,1,0:T(8,128)(2,1)S(1)} %get-tuple-element.31), channel_id=1, source_target_pairs={{0,1},{1,0},{2,3},{3,2},{4,5},{5,4},{6,7},{7,6},{8,9},{9,8},{10,11... | collective-permute-start | bytes 3145736 | tf_op jit(solution)/shard_map/ppermute | solution.py:29
  9.9 1.6 copy-start.10
  11.9 19.6 %copy-start.7 = (bf16[512,2048]{1,0:T(8,128)(2,1)S(1)}, bf16[512,2048]{1,0:T(8,128)(2,1)}, u32[]{:S(2)}) copy-start(bf16[512,2048]{1,0:T(8,128)(2,1)} %param.12) | copy-start | bytes 6291460
  33.0 25.9 %collective-permute-start.2 = (bf16[2,256,512]{2,1,0:T(8,128)(2,1)S(1)}, bf16[2,256,512]{2,1,0:T(8,128)(2,1)S(1)}, u32[]{:S(2)}, u32[]{:S(2)}) collective-permute-start(bf16[2,256,512]{2,1,0:T(8,128)(2,1)S(1)} %get-tuple-element.37.refs_1_.refs_0_), channel_id=1, source_target_pairs={{0,64},{2,66},{4,68},{6,70},{8,72},{10,74},{12,76},{14,78},{16,80}... | collective-permute-start | bytes 1572872 | tf_op jit(solution)/shard_map/ppermute | solution.py:25
  34.3 24.6 %collective-permute-start.1 = (bf16[2,256,512]{2,1,0:T(8,128)(2,1)S(1)}, bf16[2,256,512]{2,1,0:T(8,128)(2,1)}, u32[]{:S(2)}, u32[]{:S(2)}) collective-permute-start(bf16[2,256,512]{2,1,0:T(8,128)(2,1)S(1)} %get-tuple-element.37.refs_1_.refs_0_), channel_id=1, source_target_pairs={{0,4},{2,6},{4,8},{6,10},{8,12},{10,14},{12,16},{14,18},{16,20},{1... | collective-permute-start | bytes 1572872 | tf_op jit(solution)/shard_map/ppermute | solution.py:25
  38.1 23.6 %collective-permute-start.6 = (bf16[2,256,512]{2,1,0:T(8,128)(2,1)S(1)}, bf16[2,256,512]{2,1,0:T(8,128)(2,1)}, u32[]{:S(2)}, u32[]{:S(2)}) collective-permute-start(bf16[2,256,512]{2,1,0:T(8,128)(2,1)S(1)} %get-tuple-element.43.refs_0_.refs_1_), channel_id=1, source_target_pairs={{64,0},{66,2},{68,4},{70,6},{72,8},{74,10},{76,12},{78,14},{80,16}... | collective-permute-start | bytes 1572872 | tf_op jit(solution)/shard_map/ppermute | solution.py:25
  43.4 18.2 %collective-permute-start.5 = (bf16[2,256,512]{2,1,0:T(8,128)(2,1)S(1)}, bf16[2,256,512]{2,1,0:T(8,128)(2,1)}, u32[]{:S(2)}, u32[]{:S(2)}) collective-permute-start(bf16[2,256,512]{2,1,0:T(8,128)(2,1)S(1)} %get-tuple-element.43.refs_0_.refs_1_), channel_id=1, source_target_pairs={{4,0},{6,2},{8,4},{10,6},{12,8},{14,10},{16,12},{18,14},{20,16},{2... | collective-permute-start | bytes 1572872 | tf_op jit(solution)/shard_map/ppermute | solution.py:25
  58.9 0.8 copy-start.1
  59.7 18.4 %collective-permute-start.3 = (bf16[2,256,512]{2,1,0:T(8,128)(2,1)}, bf16[2,256,512]{2,1,0:T(8,128)(2,1)}, u32[]{:S(2)}, u32[]{:S(2)}) collective-permute-start(bf16[2,256,512]{2,1,0:T(8,128)(2,1)} %collective-permute-done.1.refs_3_), channel_id=1, source_target_pairs={{0,4},{2,6},{4,8},{6,10},{8,12},{10,14},{12,16},{14,18},{16,20},{1... | collective-permute-start | bytes 1572872 | tf_op jit(solution)/shard_map/ppermute | solution.py:25
  61.7 20.5 %collective-permute-start.12 = (bf16[2,256,512]{2,1,0:T(8,128)(2,1)}, bf16[2,256,512]{2,1,0:T(8,128)(2,1)}, u32[]{:S(2)}, u32[]{:S(2)}) collective-permute-start(bf16[2,256,512]{2,1,0:T(8,128)(2,1)} %collective-permute-done.5.refs_4_), channel_id=1, source_target_pairs={{4,0},{6,2},{8,4},{10,6},{12,8},{14,10},{16,12},{18,14},{20,16},{2... | collective-permute-start | bytes 1572872 | tf_op jit(solution)/shard_map/ppermute | solution.py:25
  74.6 17.1 %collective-permute-start.8 = (bf16[2,256,512]{2,1,0:T(8,128)(2,1)}, bf16[2,256,512]{2,1,0:T(8,128)(2,1)}, u32[]{:S(2)}, u32[]{:S(2)}) collective-permute-start(bf16[2,256,512]{2,1,0:T(8,128)(2,1)} %broadcast_select_fusion.1), channel_id=1, source_target_pairs={{0,32},{2,34},{4,36},{6,38},{8,40},{10,42},{12,44},{14,46},{16,48}... | collective-permute-start | bytes 1572872 | tf_op jit(solution)/shard_map/ppermute | solution.py:298
  74.6 17.2 %collective-permute-start.7 = (bf16[2,256,512]{2,1,0:T(8,128)(2,1)}, bf16[2,256,512]{2,1,0:T(8,128)(2,1)}, u32[]{:S(2)}, u32[]{:S(2)}) collective-permute-start(bf16[2,256,512]{2,1,0:T(8,128)(2,1)} %collective-permute-done.6.refs_8_), channel_id=1, source_target_pairs={{64,0},{66,2},{68,4},{70,6},{72,8},{74,10},{76,12},{78,14},{80,16}... | collective-permute-start | bytes 1572872 | tf_op jit(solution)/shard_map/ppermute | solution.py:25
  78.0 23.5 %collective-permute-start.4 = (bf16[2,256,512]{2,1,0:T(8,128)(2,1)}, bf16[2,256,512]{2,1,0:T(8,128)(2,1)}, u32[]{:S(2)}, u32[]{:S(2)}) collective-permute-start(bf16[2,256,512]{2,1,0:T(8,128)(2,1)} %collective-permute-done.3.refs_4_), channel_id=1, source_target_pairs={{0,8},{2,10},{4,12},{6,14},{8,16},{10,18},{12,20},{14,22},{16,24},... | collective-permute-start | bytes 1572872 | tf_op jit(solution)/shard_map/ppermute | solution.py:25
  80.0 29.1 %collective-permute-start.11 = (bf16[2,256,512]{2,1,0:T(8,128)(2,1)}, bf16[2,256,512]{2,1,0:T(8,128)(2,1)}, u32[]{:S(2)}, u32[]{:S(2)}) collective-permute-start(bf16[2,256,512]{2,1,0:T(8,128)(2,1)} %copy-done.1), channel_id=1, source_target_pairs={{0,64},{2,66},{4,68},{6,70},{8,72},{10,74},{12,76},{14,78},{16,80}... | collective-permute-start | bytes 1572872 | tf_op jit(solution)/shard_map/ppermute | solution.py:25
  82.1 25.0 %collective-permute-start.13 = (bf16[2,256,512]{2,1,0:T(8,128)(2,1)}, bf16[2,256,512]{2,1,0:T(8,128)(2,1)}, u32[]{:S(2)}, u32[]{:S(2)}) collective-permute-start(bf16[2,256,512]{2,1,0:T(8,128)(2,1)} %collective-permute-done.12.refs_5_), channel_id=1, source_target_pairs={{8,0},{10,2},{12,4},{14,6},{16,8},{18,10},{20,12},{22,14},{24,16},... | collective-permute-start | bytes 1572872 | tf_op jit(solution)/shard_map/ppermute | solution.py:25
  91.7 17.4 %collective-permute-start.10 = (bf16[2,256,512]{2,1,0:T(8,128)(2,1)}, bf16[2,256,512]{2,1,0:T(8,128)(2,1)}, u32[]{:S(2)}, u32[]{:S(2)}) collective-permute-start(bf16[2,256,512]{2,1,0:T(8,128)(2,1)} %broadcast_select_fusion), channel_id=1, source_target_pairs={{0,32},{2,34},{4,36},{6,38},{8,40},{10,42},{12,44},{14,46},{16,48}... | collective-permute-start | bytes 1572872 | tf_op jit(solution)/shard_map/ppermute | solution.py:298
  102.4 6.6 %collective-permute-start.9 = (bf16[2,256,512]{2,1,0:T(8,128)(2,1)}, bf16[2,256,512]{2,1,0:T(8,128)(2,1)}, u32[]{:S(2)}, u32[]{:S(2)}) collective-permute-start(bf16[2,256,512]{2,1,0:T(8,128)(2,1)} %broadcast_select_fusion.3), channel_id=1, source_target_pairs={{0,2},{2,0},{4,6},{6,4},{8,10},{10,8},{12,14},{14,12},{16,18},{18,... | collective-permute-start | bytes 1572872 | tf_op jit(solution)/shard_map/ppermute | solution.py:298
  108.3 13.3 %collective-permute-start.14 = (bf16[2,256,512]{2,1,0:T(8,128)(2,1)S(1)}, bf16[2,256,512]{2,1,0:T(8,128)(2,1)S(1)}, u32[]{:S(2)}, u32[]{:S(2)}) collective-permute-start(bf16[2,256,512]{2,1,0:T(8,128)(2,1)S(1)} %broadcast_select_fusion.2), channel_id=1, source_target_pairs={{0,2},{2,0},{4,6},{6,4},{8,10},{10,8},{12,14},{14,12},{16,18},{18,... | collective-permute-start | bytes 1572872 | tf_op jit(solution)/shard_map/ppermute | solution.py:298
  109.0 1.0 copy-start.2
  110.1 7.0 %copy-start.8 = (bf16[512,2048]{1,0:T(8,128)(2,1)S(1)}, bf16[512,2048]{1,0:T(8,128)(2,1)}, u32[]{:S(2)}) copy-start(bf16[512,2048]{1,0:T(8,128)(2,1)} %param.12) | copy-start | bytes 6291460
  116.4 0.7 copy-start.3
  118.4 24.6 %collective-permute-start.16 = (bf16[128,2048]{1,0:T(8,128)(2,1)}, bf16[128,2048]{1,0:T(8,128)(2,1)}, u32[]{:S(2)}, u32[]{:S(2)}) collective-permute-start(bf16[128,2048]{1,0:T(8,128)(2,1)} %convolution_convert_fusion), channel_id=1, source_target_pairs={{0,1},{1,0},{2,3},{3,2},{4,5},{5,4},{6,7},{7,6},{8,9},{9,8},{10,11... | collective-permute-start | bytes 1572872 | tf_op jit(solution)/shard_map/ppermute | solution.py:29
  121.5 0.8 copy-start.15
  122.3 18.7 %collective-permute-start.15 = (f32[4,2,256]{2,1,0:T(2,128)S(1)}, f32[4,2,256]{2,1,0:T(2,128)S(1)}, u32[]{:S(2)}, u32[]{:S(2)}) collective-permute-start(f32[4,2,256]{2,1,0:T(2,128)S(1)} %get-tuple-element.48.refs_2_), channel_id=1, source_target_pairs={{4,0},{6,2},{8,4},{10,6},{12,8},{14,10},{16,12},{18,14},{20,16},{2... | collective-permute-start | bytes 24584 | tf_op jit(solution)/shard_map/ppermute | solution.py:25
  134.8 8.2 %collective-permute-start.20 = (f32[4,2,256]{2,1,0:T(2,128)S(1)}, f32[4,2,256]{2,1,0:T(2,128)S(1)}, u32[]{:S(2)}, u32[]{:S(2)}) collective-permute-start(f32[4,2,256]{2,1,0:T(2,128)S(1)} %get-tuple-element.48.refs_2_), channel_id=1, source_target_pairs={{64,0},{66,2},{68,4},{70,6},{72,8},{74,10},{76,12},{78,14},{80,16}... | collective-permute-start | bytes 24584 | tf_op jit(solution)/shard_map/ppermute | solution.py:25
  137.8 9.0 %collective-permute-start.22 = (f32[4,2,256]{2,1,0:T(2,128)S(1)}, f32[4,2,256]{2,1,0:T(2,128)S(1)}, u32[]{:S(2)}, u32[]{:S(2)}) collective-permute-start(f32[4,2,256]{2,1,0:T(2,128)S(1)} %get-tuple-element.48.refs_2_), channel_id=1, source_target_pairs={{128,0},{130,2},{132,4},{134,6},{136,8},{138,10},{140,12},{142,14}... | collective-permute-start | bytes 24584 | tf_op jit(solution)/shard_map/ppermute | solution.py:25
  139.1 9.5 %collective-permute-start.19 = (f32[4,2,256]{2,1,0:T(2,128)S(1)}, f32[4,2,256]{2,1,0:T(2,128)S(1)}, u32[]{:S(2)}, u32[]{:S(2)}) collective-permute-start(f32[4,2,256]{2,1,0:T(2,128)S(1)} %get-tuple-element.48.refs_2_), channel_id=1, source_target_pairs={{16,0},{18,2},{20,4},{22,6},{24,8},{26,10},{28,12},{30,14},{32,16}... | collective-permute-start | bytes 24584 | tf_op jit(solution)/shard_map/ppermute | solution.py:25
  141.0 7.5 %collective-permute-start.18 = (f32[4,2,256]{2,1,0:T(2,128)S(1)}, f32[4,2,256]{2,1,0:T(2,128)S(1)}, u32[]{:S(2)}, u32[]{:S(2)}) collective-permute-start(f32[4,2,256]{2,1,0:T(2,128)S(1)} %get-tuple-element.48.refs_2_), channel_id=1, source_target_pairs={{8,0},{10,2},{12,4},{14,6},{16,8},{18,10},{20,12},{22,14},{24,16},... | collective-permute-start | bytes 24584 | tf_op jit(solution)/shard_map/ppermute | solution.py:25
  143.0 5.6 %collective-permute-start.21 = (f32[4,2,256]{2,1,0:T(2,128)S(1)}, f32[4,2,256]{2,1,0:T(2,128)S(1)}, u32[]{:S(2)}, u32[]{:S(2)}) collective-permute-start(f32[4,2,256]{2,1,0:T(2,128)S(1)} %bitcast.79), channel_id=1, source_target_pairs={{0,32},{2,34},{4,36},{6,38},{8,40},{10,42},{12,44},{14,46},{16,48}... | collective-permute-start | bytes 24584 | tf_op jit(solution)/shard_map/ppermute | solution.py:298
  144.5 4.1 %collective-permute-start.17 = (f32[4,2,256]{2,1,0:T(2,128)S(1)}, f32[4,2,256]{2,1,0:T(2,128)S(1)}, u32[]{:S(2)}, u32[]{:S(2)}) collective-permute-start(f32[4,2,256]{2,1,0:T(2,128)S(1)} %bitcast.78), channel_id=1, source_target_pairs={{0,2},{2,0},{4,6},{6,4},{8,10},{10,8},{12,14},{14,12},{16,18},{18,... | collective-permute-start | bytes 24584 | tf_op jit(solution)/shard_map/ppermute | solution.py:298
  146.8 6.4 %copy-start.11 = (bf16[2048,512]{1,0:T(8,128)(2,1)S(1)}, bf16[2048,512]{1,0:T(8,128)(2,1)}, u32[]{:S(2)}) copy-start(bf16[2048,512]{1,0:T(8,128)(2,1)} %param.10) | copy-start | bytes 6291460
  154.1 3.0 %copy-start.4 = (bf16[256,512]{1,0:T(8,128)(2,1)S(1)}, bf16[256,512]{1,0:T(8,128)(2,1)}, u32[]{:S(2)}) copy-start(bf16[256,512]{1,0:T(8,128)(2,1)} %copy-done.3) | copy-start | bytes 786436
  154.1 2.9 %copy-start.9 = (bf16[512,2048]{1,0:T(8,128)(2,1)S(1)}, bf16[512,2048]{1,0:T(8,128)(2,1)}, u32[]{:S(2)}) copy-start(bf16[512,2048]{1,0:T(8,128)(2,1)} %param.12) | copy-start | bytes 6291460
  154.1 2.9 %copy-start.13 = (bf16[128,2048]{1,0:T(8,128)(2,1)S(1)}, bf16[128,2048]{1,0:T(8,128)(2,1)}, u32[]{:S(2)}) copy-start(bf16[128,2048]{1,0:T(8,128)(2,1)} %series_ref.1) | copy-start | bytes 1572868
  154.9 14.2 %collective-permute-start.23 = (bf16[128,2048]{1,0:T(8,128)(2,1)S(1)}, bf16[128,2048]{1,0:T(8,128)(2,1)S(1)}, u32[]{:S(2)}, u32[]{:S(2)}) collective-permute-start(bf16[128,2048]{1,0:T(8,128)(2,1)S(1)} %fusion.18), channel_id=1, source_target_pairs={{0,1},{1,0},{2,3},{3,2},{4,5},{5,4},{6,7},{7,6},{8,9},{9,8},{10,11... | collective-permute-start | bytes 1572872 | tf_op jit(solution)/shard_map/ppermute | solution.py:29
  164.1 5.1 %copy-start.6 = (f32[2048]{0:T(1024)S(1)}, f32[2048]{0:T(1024)}, u32[]{:S(2)}) copy-start(f32[2048]{0:T(1024)} %param.8) | copy-start | bytes 24580
  164.9 5.2 %copy-start.14 = (bf16[128,2048]{1,0:T(8,128)(2,1)S(1)}, bf16[128,2048]{1,0:T(8,128)(2,1)}, u32[]{:S(2)}) copy-start(bf16[128,2048]{1,0:T(8,128)(2,1)} %grad_ref.1) | copy-start | bytes 1572868

commit v11 on v10

--- a/solution.py
+++ b/solution.py
@@ -60,7 +60,7 @@
     return jnp.where(rows >= keys, 0.0, NEG).astype(F32)
 
 
-def query_kernel(groups, n_back, where_ref, *refs):
+def query_kernel(groups, backs, where_ref, *refs):
     refs = list(refs)
     qg, kv = [refs.pop(0)], [refs.pop(0)]
     fetched = [[refs.pop(0) for _ in range(n)] for n in groups]
@@ -107,28 +107,26 @@
     grad_score = [
         (prob[slot] * (grad_prob[slot] - inner[slot])).astype(BF16) for slot in slots
     ]
-    first = keys[0].shape[0] - n_back * BLOCK
     for slot in slots:
         out = rows(slot)
         mixed_ref[out, :] = mixed[slot]
         dq_ref[out, :] = (dot(grad_score[slot], keys[slot], NN) * factor).astype(BF16)
         stat = jnp.where(lane == 0, peak[slot] + jnp.log(total[slot]), inner[slot])
         stat_ref[0, :, out] = jnp.transpose(stat)[:2]
-        if n_back:
-            grad_keys = (dot(grad_score[slot][:, first:], query[slot], TN) * factor).astype(BF16)
-            grad_values = dot(prob_b[slot][:, first:], grad[slot], TN).astype(BF16)
-            for at, ref in enumerate(back_refs):
-                ref[0, out, :] = grad_keys[at * BLOCK : (at + 1) * BLOCK]
-                ref[1, out, :] = grad_values[at * BLOCK : (at + 1) * BLOCK]
-
-
-def key_kernel(half, groups, where_ref, *refs):
+        for at, ref in zip(backs, back_refs):
+            part = slice((3 + at) * BLOCK, (4 + at) * BLOCK)
+            ref[0, out, :] = (dot(grad_score[slot][:, part], query[slot], TN) * factor).astype(BF16)
+            ref[1, out, :] = dot(prob_b[slot][:, part], grad[slot], TN).astype(BF16)
+
+
+def key_kernel(half, groups, n_back, where_ref, *refs):
     refs = list(refs)
     kv = refs.pop(0)
     qg = [refs.pop(0)]
     stat = refs.pop(0)
     later = [[refs.pop(0) for _ in range(n)] for n in groups]
     later_stats = [refs.pop(0) for _ in groups]
+    back = [refs.pop(0) for _ in range(n_back)]
     (out_ref,) = refs
     is_second = where_ref[0] == 1
     factor = HD ** (-0.5)
@@ -168,9 +166,12 @@
     prob_b = [p.astype(BF16) for p in prob]
     grad_keys = [dot(grad_score[at], queries[at], NN) * factor for at in both]
     grad_values = [dot(prob_b[at], grads[at], NN) for at in both]
-    for at in both:
-        out_ref[0, rows[at], :] = grad_keys[at].astype(BF16)
-        out_ref[1, rows[at], :] = grad_values[at].astype(BF16)
+    for which, totals in enumerate((grad_keys, grad_values)):
+        for at in both:
+            total = totals[at]
+            for ref in back:
+                total += ref[which, rows[at], :].astype(F32)
+            out_ref[which, rows[at], :] = total.astype(BF16)
 
 
 def head_spec(a):
@@ -199,7 +200,7 @@
     )(where, *operands)
 
 
-def query_side(where, qg, kv, fetched, n_back):
+def query_side(where, qg, kv, fetched, backs):
     rows, width = qg.shape[1], qg.shape[2]
     heads = width // HD
     far = [a for f in fetched for a in f]
@@ -207,38 +208,39 @@
     row_out = jax.ShapeDtypeStruct((rows, width), BF16)
     stat_out = jax.ShapeDtypeStruct((heads, 2, rows), F32)
     back_out = jax.ShapeDtypeStruct((2, rows, width), BF16)
-    outs = [row_out, row_out, stat_out] + [back_out] * n_back
+    outs = [row_out, pltpu.HBM(row_out.shape, BF16), stat_out] + [pltpu.HBM(back_out.shape, BF16)] * len(backs)
     return call(
-        functools.partial(query_kernel, tuple(len(f) for f in fetched), n_back),
+        functools.partial(query_kernel, tuple(len(f) for f in fetched), backs),
         where,
         operands,
         [head_spec(a) for a in operands],
         outs,
-        [head_spec(row_out), head_spec(row_out), stat_spec(stat_out)] + [head_spec(back_out)] * n_back,
+        [head_spec(row_out), head_spec(row_out), stat_spec(stat_out)] + [head_spec(back_out)] * len(backs),
         heads,
         (3 + len(fetched)) * BLOCK,
         "query_side",
     )
 
 
-def key_side(half, where, kv, qg, stat, later, later_stats):
+def key_side(half, where, kv, qg, stat, later, later_stats, returned):
     rows, width = kv.shape[1] // 2, kv.shape[2]
     heads = width // HD
     half_of_whole = pl.BlockSpec((2, rows, HD), lambda h, w: (0, half, h))
     far = [f[-1] if len(f) == 1 else f[half] for f in later[1:]]
     first, *far = [pltpu.with_memory_space_constraint(a, pltpu.HBM) for a in (*later[0], *far)]
-    operands = [kv, qg, stat, first, *far, *later_stats]
+    operands = [kv, qg, stat, first, *far, *later_stats, *returned]
     in_specs = (
         [half_of_whole, head_spec(qg)]
         + [stat_spec(stat)]
         + [head_spec(a) for a in later[0]]
         + [half_of_whole if len(f) == 1 else head_spec(f[half]) for f in later[1:]]
         + [stat_spec(a) for a in later_stats]
+        + [half_of_whole] * len(returned)
     )
     out = jax.ShapeDtypeStruct((2, rows, width), BF16)
     groups = (len(later[0]),) + (1,) * len(far)
     (result,) = call(
-        functools.partial(key_kernel, half, groups),
+        functools.partial(key_kernel, half, groups, len(returned)),
         where,
         operands,
         in_specs,
@@ -300,33 +302,27 @@
 
 def exchange(keys, queries):
     two, two_q = shifted(keys, 2), shifted(queries, -2)
-    far, far_q = shifted(keys, 32), shifted(queries, -32)
-    two, far = lax.optimization_barrier((two, far))
-    two_q, far_q = lax.optimization_barrier((two_q, far_q))
+    far = shifted(keys, 32)
+    two, far, two_q = lax.optimization_barrier((two, far, two_q))
     four, four_q = shifted(two, 2), shifted(two_q, -2)
-    eight, eight_q = shifted(four, 4), shifted(four_q, -4)
-    last, last_q = shifted(far, 32), shifted(far_q, -32)
-    sixteen = swapped(keys, far, 16, 1)
-    sixteen_q = swapped(queries, far_q, 16, -1)
-    keys_late, two_late, eight, last_q, sixteen_q = lax.optimization_barrier(
-        (keys, two, eight, last_q, sixteen_q)
-    )
-    one = swapped(keys_late, two_late, 1, 1)
-    queries_late, two_q_late, eight_q = lax.optimization_barrier((queries, two_q, eight_q))
-    one_q = swapped(queries_late, two_q_late, 1, -1)
+    eight = shifted(four, 4)
+    far_q = shifted(queries, -32)
+    sixteen, sixteen_q = swapped(keys, far, 16, 1), swapped(queries, far_q, 16, -1)
+    keys_late, two_late, eight, four_q = lax.optimization_barrier((keys, two, eight, four_q))
+    one, one_q = swapped(keys_late, two_late, 1, 1), swapped(queries, two_q, 1, -1)
     return (
-        [one, two, four, eight, sixteen, far, last],
-        [one_q, two_q, four_q, eight_q, sixteen_q, far_q, last_q],
+        [one, two, four, eight, sixteen, far, shifted(far, 32)],
+        [one_q, two_q, four_q, sixteen_q, far_q],
     )
 
 
 def exchange_stats(stat, attn_other):
     two, far = shifted(stat, -2), shifted(stat, -32)
-    direct = [shifted(stat, -by) for by in (64, 8, 4)]
+    stat_late, far = lax.optimization_barrier((stat, far))
+    four = shifted(stat_late, -4)
     sixteen = swapped(stat, far, 16, -1)
     two_last, attn_other = lax.optimization_barrier((two, attn_other))
-    one = swapped(stat, two_last, 1, -1)
-    return attn_other, [one, two, direct[2], direct[1], sixteen, far, direct[0]]
+    return attn_other, [swapped(stat, two_last, 1, -1), two, four, sixteen, far]
 
 
 def per_device(series, norm_gain, w_query, w_key, w_value, w_out, out_grad):
@@ -356,8 +352,11 @@
         (jnp.concatenate(kv, axis=1), jnp.concatenate(qg, axis=1))
     )
     fetched, later = exchange(kv_all, qg_all)
-    mixed, grad_query, stat = query_side(where, qg_all, kv_all, [(f,) for f in fetched], 0)
-    stat, later = lax.optimization_barrier((stat, later))
+    mixed, grad_query, stat, *backs = query_side(
+        where, qg_all, kv_all, [(f,) for f in fetched], (3, 6)
+    )
+    stat, backs, later = lax.optimization_barrier((stat, backs, later))
+    returned = [shifted(b, -by) for b, by in zip(backs, (8, 64))]
     later = [(f,) for f in later]
     attn_other = swap_tp(matmul(mixed[half:], w_out).astype(BF16))
     attn_other, later_stats = exchange_stats(stat, attn_other)
@@ -367,7 +366,7 @@
     grad_queries = lax.optimization_barrier(matmul_t(grad_query, w_query))
 
     def back(at):
-        grad_kv = key_side(at, where, kv_all, qg_all, stat, later, later_stats)
+        grad_kv = key_side(at, where, kv_all, qg_all, stat, later, later_stats, returned)
         rows = slice(at * half, (at + 1) * half)
         return (
             grad_queries[rows]

time: 173 us -> 188 us (1.087)
  waiting for transfers between devices: 48.3 us -> 88.8 us
  starting transfers between devices: 77 us -> 51.9 us
    ppermute x15 -> x13, waiting for transfers between devices: 24.7 us -> 64.6 us  [shifted(): return lax.ppermute(value, 'seq', pairs)]
    ppermute x15 -> x13, starting transfers between devices: 66.2 us -> 39.1 us  [shifted(): return lax.ppermute(value, 'seq', pairs)]
    ppermute x6, starting transfers between devices: 2.47 us -> 4.94 us  [swapped(): return lax.ppermute(sent, 'seq', [(i, i ^ bit) for i in range(size)])]
    unnamed x32 -> x34, local copies, waits for them, and re-layouts: 4.85 us -> 3.14 us
  transfers between devices with their start and end apart: 24 -> 22, of which waited for: 7 -> 10; matrix products, arithmetic and copies ran while one was open for 9% -> 8% of each run, Pallas kernels for 6% -> 7%
where the time goes in v11:
time: 188 us; the launch traced here: 185 us
  waiting for transfers between devices  88.8 us (47%)
  starting transfers between devices  51.9 us (28%)
  Pallas kernels  19.6 us (10%)
  matrix products  15.7 us (8%)
  other arithmetic  4.55 us (2%)
  local copies, waits for them, and re-layouts  3.14 us (2%)
    ppermute x13, waiting for transfers between devices, shifted(): return lax.ppermute(value, 'seq', pairs)  64.6 us
    ppermute x13, starting transfers between devices, shifted(): return lax.ppermute(value, 'seq', pairs)  39.1 us
    ppermute x3, waiting for transfers between devices, swap_tp(): return lax.ppermute(value, 'tp', [(0, 1), (1, 0)])  22.8 us
    pallas_call x3, Pallas kernels, call(): pl.pallas_call(kernel, out_shape=outs, grid_spec=pltpu.PrefetchScalarGrid...  16.9 us
    dot_general x7, matrix products, matmul_t(): return lax.dot_general(a, b, NT, preferred_element_type=F32)  9.31 us
    ppermute x3, starting transfers between devices, swap_tp(): return lax.ppermute(value, 'tp', [(0, 1), (1, 0)])  7.86 us
    dot_general x8, matrix products, matmul(): return jnp.dot(a, b, preferred_element_type=F32)  6.39 us
    ppermute x6, starting transfers between devices, swapped(): return lax.ppermute(sent, 'seq', [(i, i ^ bit) for i in range(size)])  4.94 us
  transfers between devices with their start and end apart: 22, of which 10 were waited for; matrix products, arithmetic and copies ran while one was open for 8% of the time, Pallas kernels for 7%

profile of v11, /device:TPU:24, one launch (start us, length us, event | category | flops | bytes accessed | tf_op | source)
XLA Modules:
  0.0 184.8 jit_solution(10350150257764346676)
XLA Ops:
  0.6 0.0 copy-start
  0.6 0.0 copy-start.5
  0.7 0.8 copy-done.5
  1.5 2.6 %normalize.1 = (bf16[2,128,2048]{2,1,0:T(8,128)(2,1)S(1)}, f32[128,1]{1,0:T(8,128)S(1)}) custom-call(bf16[128,2048]{1,0:T(8,128)(2,1)} %series_ref.1, f32[1,2048]{1,0:T(1,128)S(1)} %bitcast.77, bf16[128,2048]{1,0:T(8,128)(2,1)} %grad_ref.1), custom_call_target="tpu_custom_call" | custom-call | tf_op jit(solution)/shard_map/normalize/pallas_call | solution.py:271
  4.1 3.1 %collective-permute-start = (bf16[2,128,2048]{2,1,0:T(8,128)(2,1)S(1)}, bf16[2,128,2048]{2,1,0:T(8,128)(2,1)S(1)}, u32[]{:S(2)}, u32[]{:S(2)}) collective-permute-start(bf16[2,128,2048]{2,1,0:T(8,128)(2,1)S(1)} %get-tuple-element.30), channel_id=1, source_target_pairs={{0,1},{1,0},{2,3},{3,2},{4,5},{5,4},{6,7},{7,6},{8,9},{9,8},{10,11... | collective-permute-start | bytes 3145736 | tf_op jit(solution)/shard_map/ppermute | solution.py:29
  7.2 2.6 %fusion.9 = bf16[1,128,512]{2,1,0:T(8,128)(2,1)S(1)} fusion(bf16[128,2048]{1,0:T(8,128)(2,1)} %grad_ref.1, bf16[512,2048]{1,0:T(8,128)(2,1)} %param.12), kind=kOutput, calls=%fused_computation.20 | convolution fusion | flops 268500992 | bytes 2752512 | tf_op jit(solution)/shard_map/dot_general | solution.py:293
  9.9 0.0 copy-start.10
  9.9 0.4 fusion.8
  10.3 0.5 fusion.5
  10.8 0.6 copy-done.10
  11.5 0.4 fusion.4
  11.9 0.0 copy-start.7
  11.9 18.7 %collective-permute-done = bf16[2,128,2048]{2,1,0:T(8,128)(2,1)S(1)} collective-permute-done((bf16[2,128,2048]{2,1,0:T(8,128)(2,1)S(1)}, bf16[2,128,2048]{2,1,0:T(8,128)(2,1)S(1)}, u32[]{:S(2)}, u32[]{:S(2)}) %collective-permute-start) | collective-permute-done | bytes 1048608 | tf_op jit(solution)/shard_map/ppermute | solution.py:29
  30.6 0.4 fusion.7
  31.1 0.5 fusion.10
  31.6 0.9 fusion.11
  32.4 0.5 fusion.6
  32.9 0.1 maximum_maximum_fusion
  33.0 8.9 %collective-permute-start.3 = (bf16[2,256,512]{2,1,0:T(8,128)(2,1)S(1)}, bf16[2,256,512]{2,1,0:T(8,128)(2,1)}, u32[]{:S(2)}, u32[]{:S(2)}) collective-permute-start(bf16[2,256,512]{2,1,0:T(8,128)(2,1)S(1)} %get-tuple-element.31.refs_0_.refs_1_), channel_id=1, source_target_pairs={{4,0},{6,2},{8,4},{10,6},{12,8},{14,10},{16,12},{18,14},{20,16},{2... | collective-permute-start | bytes 1572872 | tf_op jit(solution)/shard_map/ppermute | solution.py:25
  41.9 1.3 collective-permute-start.2
  43.2 1.9 %collective-permute-start.1 = (bf16[2,256,512]{2,1,0:T(8,128)(2,1)S(1)}, bf16[2,256,512]{2,1,0:T(8,128)(2,1)S(1)}, u32[]{:S(2)}, u32[]{:S(2)}) collective-permute-start(bf16[2,256,512]{2,1,0:T(8,128)(2,1)S(1)} %get-tuple-element.36.refs_1_.refs_0_), channel_id=1, source_target_pairs={{0,4},{2,6},{4,8},{6,10},{8,12},{10,14},{12,16},{14,18},{16,20},{1... | collective-permute-start | bytes 1572872 | tf_op jit(solution)/shard_map/ppermute | solution.py:25
  45.1 7.1 %collective-permute-done.3.refs_4_ = bf16[2,256,512]{2,1,0:T(8,128)(2,1)} collective-permute-done((bf16[2,256,512]{2,1,0:T(8,128)(2,1)S(1)}, bf16[2,256,512]{2,1,0:T(8,128)(2,1)}, u32[]{:S(2)}, u32[]{:S(2)}) %collective-permute-start.3) | collective-permute-done | bytes 524320 | tf_op jit(solution)/shard_map/ppermute | solution.py:25
  52.2 15.4 %collective-permute-done.2.refs_7_ = bf16[2,256,512]{2,1,0:T(8,128)(2,1)S(1)} collective-permute-done((bf16[2,256,512]{2,1,0:T(8,128)(2,1)S(1)}, bf16[2,256,512]{2,1,0:T(8,128)(2,1)S(1)}, u32[]{:S(2)}, u32[]{:S(2)}) %collective-permute-start.2) | collective-permute-done | bytes 524320 | tf_op jit(solution)/shard_map/ppermute | solution.py:25
  67.5 0.8 copy-done.1
  68.3 1.9 %collective-permute-start.4 = (bf16[2,256,512]{2,1,0:T(8,128)(2,1)S(1)}, bf16[2,256,512]{2,1,0:T(8,128)(2,1)}, u32[]{:S(2)}, u32[]{:S(2)}) collective-permute-start(bf16[2,256,512]{2,1,0:T(8,128)(2,1)S(1)} %collective-permute-done.1.refs_3_), channel_id=1, source_target_pairs={{0,4},{2,6},{4,8},{6,10},{8,12},{10,14},{12,16},{14,18},{16,20},{1... | collective-permute-start | bytes 1572872 | tf_op jit(solution)/shard_map/ppermute | solution.py:25
  70.2 6.9 %collective-permute-start.6 = (bf16[2,256,512]{2,1,0:T(8,128)(2,1)}, bf16[2,256,512]{2,1,0:T(8,128)(2,1)}, u32[]{:S(2)}, u32[]{:S(2)}) collective-permute-start(bf16[2,256,512]{2,1,0:T(8,128)(2,1)} %collective-permute-done.3.refs_4_), channel_id=1, source_target_pairs={{4,0},{6,2},{8,4},{10,6},{12,8},{14,10},{16,12},{18,14},{20,16},{2... | collective-permute-start | bytes 1572872 | tf_op jit(solution)/shard_map/ppermute | solution.py:25
  77.2 7.7 %collective-permute-done.4.refs_4_ = bf16[2,256,512]{2,1,0:T(8,128)(2,1)} collective-permute-done((bf16[2,256,512]{2,1,0:T(8,128)(2,1)S(1)}, bf16[2,256,512]{2,1,0:T(8,128)(2,1)}, u32[]{:S(2)}, u32[]{:S(2)}) %collective-permute-start.4) | collective-permute-done | bytes 524320 | tf_op jit(solution)/shard_map/ppermute | solution.py:25
  84.9 1.9 %collective-permute-start.5 = (bf16[2,256,512]{2,1,0:T(8,128)(2,1)}, bf16[2,256,512]{2,1,0:T(8,128)(2,1)}, u32[]{:S(2)}, u32[]{:S(2)}) collective-permute-start(bf16[2,256,512]{2,1,0:T(8,128)(2,1)} %collective-permute-done.4.refs_4_), channel_id=1, source_target_pairs={{0,8},{2,10},{4,12},{6,14},{8,16},{10,18},{12,20},{14,22},{16,24},... | collective-permute-start | bytes 1572872 | tf_op jit(solution)/shard_map/ppermute | solution.py:25
  86.9 3.2 %collective-permute-start.11 = (bf16[2,256,512]{2,1,0:T(8,128)(2,1)S(1)}, bf16[2,256,512]{2,1,0:T(8,128)(2,1)}, u32[]{:S(2)}, u32[]{:S(2)}) collective-permute-start(bf16[2,256,512]{2,1,0:T(8,128)(2,1)S(1)} %get-tuple-element.31.refs_0_.refs_1_), channel_id=1, source_target_pairs={{64,0},{66,2},{68,4},{70,6},{72,8},{74,10},{76,12},{78,14},{80,16}... | collective-permute-start | bytes 1572872 | tf_op jit(solution)/shard_map/ppermute | solution.py:25
  90.1 1.3 collective-permute-start.9
  91.3 0.9 broadcast_select_fusion.1
  92.2 20.8 %collective-permute-done.5.refs_5_ = bf16[2,256,512]{2,1,0:T(8,128)(2,1)} collective-permute-done((bf16[2,256,512]{2,1,0:T(8,128)(2,1)}, bf16[2,256,512]{2,1,0:T(8,128)(2,1)}, u32[]{:S(2)}, u32[]{:S(2)}) %collective-permute-start.5) | collective-permute-done | bytes 524320 | tf_op jit(solution)/shard_map/ppermute | solution.py:25
  113.0 0.9 broadcast_select_fusion.3
  113.9 0.1 pad_add_fusion.where_ref
  114.0 1.4 broadcast_select_fusion
  115.3 0.1 collective-permute-start.12
  115.4 0.0 copy-start.8
  115.4 0.4 collective-permute-start.10
  115.9 0.2 collective-permute-done.7.refs_2_
  116.1 8.3 %query_side.1 = (bf16[256,512]{1,0:T(8,128)(2,1)S(1)}, bf16[256,512]{1,0:T(8,128)(2,1)}, f32[4,2,256]{2,1,0:T(2,128)S(1)}, bf16[2,256,512]{2,1,0:T(8,128)(2,1)}, bf16[2,256,512]{2,1,0:T(8,128)(2,1)}) custom-call(s32[2]{0:T(128)S(1)} %pad_add_fusion.where_ref, bf16[2,256,512]{2,1,0:T(8,128)(2,1)S(1)} %get-tuple-element.31.refs_0_.refs_1_, ...), custom_call_target="tpu_custom_call" | custom-call | flops 163840 | bytes 65536 | tf_op jit(solution)/shard_map/query_side/pallas_call | solution.py:189
  124.5 1.3 convolution_convert_fusion
  125.7 2.7 %collective-permute-start.14 = (bf16[128,2048]{1,0:T(8,128)(2,1)}, bf16[128,2048]{1,0:T(8,128)(2,1)}, u32[]{:S(2)}, u32[]{:S(2)}) collective-permute-start(bf16[128,2048]{1,0:T(8,128)(2,1)} %convolution_convert_fusion), channel_id=1, source_target_pairs={{0,1},{1,0},{2,3},{3,2},{4,5},{5,4},{6,7},{7,6},{8,9},{9,8},{10,11... | collective-permute-start | bytes 1572872 | tf_op jit(solution)/shard_map/ppermute | solution.py:29
  128.5 1.1 collective-permute-done.12.refs_6_
  129.6 0.8 copy-done.15
  130.4 2.4 %collective-permute-start.16 = (f32[4,2,256]{2,1,0:T(2,128)S(1)}, f32[4,2,256]{2,1,0:T(2,128)S(1)}, u32[]{:S(2)}, u32[]{:S(2)}) collective-permute-start(f32[4,2,256]{2,1,0:T(2,128)S(1)} %get-tuple-element.54.refs_2_), channel_id=1, source_target_pairs={{64,0},{66,2},{68,4},{70,6},{72,8},{74,10},{76,12},{78,14},{80,16}... | collective-permute-start | bytes 24584 | tf_op jit(solution)/shard_map/ppermute | solution.py:25
  132.8 1.9 %collective-permute-start.13 = (f32[4,2,256]{2,1,0:T(2,128)S(1)}, f32[4,2,256]{2,1,0:T(2,128)S(1)}, u32[]{:S(2)}, u32[]{:S(2)}) collective-permute-start(f32[4,2,256]{2,1,0:T(2,128)S(1)} %get-tuple-element.54.refs_2_), channel_id=1, source_target_pairs={{4,0},{6,2},{8,4},{10,6},{12,8},{14,10},{16,12},{18,14},{20,16},{2... | collective-permute-start | bytes 24584 | tf_op jit(solution)/shard_map/ppermute | solution.py:25
  134.7 0.1 reduce
  134.8 1.9 %collective-permute-start.19 = (bf16[2,256,512]{2,1,0:T(8,128)(2,1)}, bf16[2,256,512]{2,1,0:T(8,128)(2,1)S(1)}, u32[]{:S(2)}, u32[]{:S(2)}) collective-permute-start(bf16[2,256,512]{2,1,0:T(8,128)(2,1)} %get-tuple-element.56), channel_id=1, source_target_pairs={{16,0},{18,2},{20,4},{22,6},{24,8},{26,10},{28,12},{30,14},{32,16}... | collective-permute-start | bytes 1572872 | tf_op jit(solution)/shard_map/ppermute | solution.py:25
  136.7 2.4 %collective-permute-start.20 = (bf16[2,256,512]{2,1,0:T(8,128)(2,1)}, bf16[2,256,512]{2,1,0:T(8,128)(2,1)S(1)}, u32[]{:S(2)}, u32[]{:S(2)}) collective-permute-start(bf16[2,256,512]{2,1,0:T(8,128)(2,1)} %get-tuple-element.57), channel_id=1, source_target_pairs={{128,0},{130,2},{132,4},{134,6},{136,8},{138,10},{140,12},{142,14}... | collective-permute-start | bytes 1572872 | tf_op jit(solution)/shard_map/ppermute | solution.py:25
  139.1 3.3 %collective-permute-start.17 = (f32[4,2,256]{2,1,0:T(2,128)S(1)}, f32[4,2,256]{2,1,0:T(2,128)S(1)}, u32[]{:S(2)}, u32[]{:S(2)}) collective-permute-start(f32[4,2,256]{2,1,0:T(2,128)S(1)} %get-tuple-element.54.refs_2_), channel_id=1, source_target_pairs={{8,0},{10,2},{12,4},{14,6},{16,8},{18,10},{20,12},{22,14},{24,16},... | collective-permute-start | bytes 24584 | tf_op jit(solution)/shard_map/ppermute | solution.py:25
  142.4 4.4 %collective-permute-start.18 = (f32[4,2,256]{2,1,0:T(2,128)S(1)}, f32[4,2,256]{2,1,0:T(2,128)S(1)}, u32[]{:S(2)}, u32[]{:S(2)}) collective-permute-start(f32[4,2,256]{2,1,0:T(2,128)S(1)} %bitcast.79), channel_id=1, source_target_pairs={{0,32},{2,34},{4,36},{6,38},{8,40},{10,42},{12,44},{14,46},{16,48}... | collective-permute-start | bytes 24584 | tf_op jit(solution)/shard_map/ppermute | solution.py:300
  146.8 2.4 %fusion.34 = f32[256,2048]{1,0:T(8,128)S(1)} fusion(bf16[256,512]{1,0:T(8,128)(2,1)} %get-tuple-element.47, bf16[2048,512]{1,0:T(8,128)(2,1)} %param.9), kind=kOutput, calls=%fused_computation.63 | convolution fusion | flops 536870912 | bytes 4456448 | tf_op jit(solution)/shard_map/dot_general | solution.py:293
  149.3 0.7 collective-permute-done.17.refs_10_
  150.0 12.9 %collective-permute-done.19.refs_13_ = bf16[2,256,512]{2,1,0:T(8,128)(2,1)S(1)} collective-permute-done((bf16[2,256,512]{2,1,0:T(8,128)(2,1)}, bf16[2,256,512]{2,1,0:T(8,128)(2,1)S(1)}, u32[]{:S(2)}, u32[]{:S(2)}) %collective-permute-start.19) | collective-permute-done | bytes 524320 | tf_op jit(solution)/shard_map/ppermute | solution.py:25
  162.9 4.3 %key_side.3 = bf16[2,128,512]{2,1,0:T(8,128)(2,1)S(1)} custom-call(s32[2]{0:T(128)S(1)} %pad_add_fusion.where_ref, bf16[2,256,512]{2,1,0:T(8,128)(2,1)S(1)} %get-tuple-element.36.refs_1_.refs_0_, bf16[2,256,512]{2,1,0:T(8,128)(2,1)S(1)} %get-tuple-element.31.refs_0_.refs_1_, f32[4,2,256]{2,1,0:T(2,128)S(1)} %get-tuple-element.54.refs_2_, ...), custom_call_target="tpu_custom_call" | custom-call | flops 65536 | bytes 65536 | tf_op jit(solution)/shard_map/key_side/pallas_call | solution.py:189
  167.3 0.8 fusion.29
  168.1 0.8 fusion.18
  168.9 2.0 %collective-permute-start.21 = (bf16[128,2048]{1,0:T(8,128)(2,1)S(1)}, bf16[128,2048]{1,0:T(8,128)(2,1)S(1)}, u32[]{:S(2)}, u32[]{:S(2)}) collective-permute-start(bf16[128,2048]{1,0:T(8,128)(2,1)S(1)} %fusion.18), channel_id=1, source_target_pairs={{0,1},{1,0},{2,3},{3,2},{4,5},{5,4},{6,7},{7,6},{8,9},{9,8},{10,11... | collective-permute-start | bytes 1572872 | tf_op jit(solution)/shard_map/ppermute | solution.py:29
  170.9 2.4 %fusion.1 = bf16[128,2048]{1,0:T(8,128)(2,1)} fusion(bf16[512,2048]{1,0:T(8,128)(2,1)S(1)} %copy-done.9, bf16[128,2048]{1,0:T(8,128)(2,1)S(1)} %copy-done.13, bf16[128,2048]{1,0:T(8,128)(2,1)} %collective-permute-done.14, bf16[256,512]{1,0:T(8,128)(2,1)S(1)} %get-tuple-element.39), kind=kOutput, calls=%fused_computation.2 | convolution fusion | flops 269746176 | bytes 3801088 | tf_op jit(solution)/shard_map/dot_general | solution.py:289
  173.3 4.3 %key_side.2 = bf16[2,128,512]{2,1,0:T(8,128)(2,1)S(1)} custom-call(s32[2]{0:T(128)S(1)} %pad_add_fusion.where_ref, bf16[2,256,512]{2,1,0:T(8,128)(2,1)S(1)} %get-tuple-element.36.refs_1_.refs_0_, bf16[2,256,512]{2,1,0:T(8,128)(2,1)S(1)} %get-tuple-element.31.refs_0_.refs_1_, f32[4,2,256]{2,1,0:T(2,128)S(1)} %get-tuple-element.54.refs_2_, ...), custom_call_target="tpu_custom_call" | custom-call | flops 65536 | bytes 65536 | tf_op jit(solution)/shard_map/key_side/pallas_call | solution.py:189
  177.6 0.8 fusion.31
  178.5 4.1 %collective-permute-done.21 = bf16[128,2048]{1,0:T(8,128)(2,1)S(1)} collective-permute-done((bf16[128,2048]{1,0:T(8,128)(2,1)S(1)}, bf16[128,2048]{1,0:T(8,128)(2,1)S(1)}, u32[]{:S(2)}, u32[]{:S(2)}) %collective-permute-start.21) | collective-permute-done | bytes 524320 | tf_op jit(solution)/shard_map/ppermute | solution.py:29
  182.5 1.0 fusion.12
  183.6 1.2 fusion.16
  (42 shorter events, 0.1 us)
Async XLA Ops:
  0.6 9.7 %copy-start = (bf16[2048,512]{1,0:T(8,128)(2,1)S(1)}, bf16[2048,512]{1,0:T(8,128)(2,1)}, u32[]{:S(2)}) copy-start(bf16[2048,512]{1,0:T(8,128)(2,1)} %param.11) | copy-start | bytes 6291460
  0.6 0.8 copy-start.5
  1.5 8.4 %copy-start.12 = (bf16[2048,512]{1,0:T(8,128)(2,1)S(1)}, bf16[2048,512]{1,0:T(8,128)(2,1)}, u32[]{:S(2)}) copy-start(bf16[2048,512]{1,0:T(8,128)(2,1)} %param.9) | copy-start | bytes 6291460
  4.1 26.5 %collective-permute-start = (bf16[2,128,2048]{2,1,0:T(8,128)(2,1)S(1)}, bf16[2,128,2048]{2,1,0:T(8,128)(2,1)S(1)}, u32[]{:S(2)}, u32[]{:S(2)}) collective-permute-start(bf16[2,128,2048]{2,1,0:T(8,128)(2,1)S(1)} %get-tuple-element.30), channel_id=1, source_target_pairs={{0,1},{1,0},{2,3},{3,2},{4,5},{5,4},{6,7},{7,6},{8,9},{9,8},{10,11... | collective-permute-start | bytes 3145736 | tf_op jit(solution)/shard_map/ppermute | solution.py:29
  9.9 1.6 copy-start.10
  11.9 19.6 %copy-start.7 = (bf16[512,2048]{1,0:T(8,128)(2,1)S(1)}, bf16[512,2048]{1,0:T(8,128)(2,1)}, u32[]{:S(2)}) copy-start(bf16[512,2048]{1,0:T(8,128)(2,1)} %param.12) | copy-start | bytes 6291460
  33.0 19.2 %collective-permute-start.3 = (bf16[2,256,512]{2,1,0:T(8,128)(2,1)S(1)}, bf16[2,256,512]{2,1,0:T(8,128)(2,1)}, u32[]{:S(2)}, u32[]{:S(2)}) collective-permute-start(bf16[2,256,512]{2,1,0:T(8,128)(2,1)S(1)} %get-tuple-element.31.refs_0_.refs_1_), channel_id=1, source_target_pairs={{4,0},{6,2},{8,4},{10,6},{12,8},{14,10},{16,12},{18,14},{20,16},{2... | collective-permute-start | bytes 1572872 | tf_op jit(solution)/shard_map/ppermute | solution.py:25
  41.9 25.6 %collective-permute-start.2 = (bf16[2,256,512]{2,1,0:T(8,128)(2,1)S(1)}, bf16[2,256,512]{2,1,0:T(8,128)(2,1)S(1)}, u32[]{:S(2)}, u32[]{:S(2)}) collective-permute-start(bf16[2,256,512]{2,1,0:T(8,128)(2,1)S(1)} %get-tuple-element.36.refs_1_.refs_0_), channel_id=1, source_target_pairs={{0,64},{2,66},{4,68},{6,70},{8,72},{10,74},{12,76},{14,78},{16,80}... | collective-permute-start | bytes 1572872 | tf_op jit(solution)/shard_map/ppermute | solution.py:25
  43.2 24.3 %collective-permute-start.1 = (bf16[2,256,512]{2,1,0:T(8,128)(2,1)S(1)}, bf16[2,256,512]{2,1,0:T(8,128)(2,1)S(1)}, u32[]{:S(2)}, u32[]{:S(2)}) collective-permute-start(bf16[2,256,512]{2,1,0:T(8,128)(2,1)S(1)} %get-tuple-element.36.refs_1_.refs_0_), channel_id=1, source_target_pairs={{0,4},{2,6},{4,8},{6,10},{8,12},{10,14},{12,16},{14,18},{16,20},{1... | collective-permute-start | bytes 1572872 | tf_op jit(solution)/shard_map/ppermute | solution.py:25
  67.5 0.8 copy-start.1
  68.3 1.9 %copy-start.3 = (bf16[2,256,512]{2,1,0:T(8,128)(2,1)}, bf16[2,256,512]{2,1,0:T(8,128)(2,1)S(1)}, u32[]{:S(2)}) copy-start(bf16[2,256,512]{2,1,0:T(8,128)(2,1)S(1)} %collective-permute-done.1.refs_3_) | copy-start | bytes 1572868
  68.3 16.6 %collective-permute-start.4 = (bf16[2,256,512]{2,1,0:T(8,128)(2,1)S(1)}, bf16[2,256,512]{2,1,0:T(8,128)(2,1)}, u32[]{:S(2)}, u32[]{:S(2)}) collective-permute-start(bf16[2,256,512]{2,1,0:T(8,128)(2,1)S(1)} %collective-permute-done.1.refs_3_), channel_id=1, source_target_pairs={{0,4},{2,6},{4,8},{6,10},{8,12},{10,14},{12,16},{14,18},{16,20},{1... | collective-permute-start | bytes 1572872 | tf_op jit(solution)/shard_map/ppermute | solution.py:25
  70.2 22.0 %collective-permute-start.6 = (bf16[2,256,512]{2,1,0:T(8,128)(2,1)}, bf16[2,256,512]{2,1,0:T(8,128)(2,1)}, u32[]{:S(2)}, u32[]{:S(2)}) collective-permute-start(bf16[2,256,512]{2,1,0:T(8,128)(2,1)} %collective-permute-done.3.refs_4_), channel_id=1, source_target_pairs={{4,0},{6,2},{8,4},{10,6},{12,8},{14,10},{16,12},{18,14},{20,16},{2... | collective-permute-start | bytes 1572872 | tf_op jit(solution)/shard_map/ppermute | solution.py:25
  84.9 28.1 %collective-permute-start.5 = (bf16[2,256,512]{2,1,0:T(8,128)(2,1)}, bf16[2,256,512]{2,1,0:T(8,128)(2,1)}, u32[]{:S(2)}, u32[]{:S(2)}) collective-permute-start(bf16[2,256,512]{2,1,0:T(8,128)(2,1)} %collective-permute-done.4.refs_4_), channel_id=1, source_target_pairs={{0,8},{2,10},{4,12},{6,14},{8,16},{10,18},{12,20},{14,22},{16,24},... | collective-permute-start | bytes 1572872 | tf_op jit(solution)/shard_map/ppermute | solution.py:25
  86.9 27.1 %collective-permute-start.11 = (bf16[2,256,512]{2,1,0:T(8,128)(2,1)S(1)}, bf16[2,256,512]{2,1,0:T(8,128)(2,1)}, u32[]{:S(2)}, u32[]{:S(2)}) collective-permute-start(bf16[2,256,512]{2,1,0:T(8,128)(2,1)S(1)} %get-tuple-element.31.refs_0_.refs_1_), channel_id=1, source_target_pairs={{64,0},{66,2},{68,4},{70,6},{72,8},{74,10},{76,12},{78,14},{80,16}... | collective-permute-start | bytes 1572872 | tf_op jit(solution)/shard_map/ppermute | solution.py:25
  90.1 25.8 %collective-permute-start.9 = (bf16[2,256,512]{2,1,0:T(8,128)(2,1)}, bf16[2,256,512]{2,1,0:T(8,128)(2,1)}, u32[]{:S(2)}, u32[]{:S(2)}) collective-permute-start(bf16[2,256,512]{2,1,0:T(8,128)(2,1)} %copy-done.1), channel_id=1, source_target_pairs={{0,64},{2,66},{4,68},{6,70},{8,72},{10,74},{12,76},{14,78},{16,80}... | collective-permute-start | bytes 1572872 | tf_op jit(solution)/shard_map/ppermute | solution.py:25
  92.2 23.7 %collective-permute-start.8 = (bf16[2,256,512]{2,1,0:T(8,128)(2,1)}, bf16[2,256,512]{2,1,0:T(8,128)(2,1)}, u32[]{:S(2)}, u32[]{:S(2)}) collective-permute-start(bf16[2,256,512]{2,1,0:T(8,128)(2,1)} %broadcast_select_fusion.1), channel_id=1, source_target_pairs={{0,32},{2,34},{4,36},{6,38},{8,40},{10,42},{12,44},{14,46},{16,48}... | collective-permute-start | bytes 1572872 | tf_op jit(solution)/shard_map/ppermute | solution.py:300
  113.9 2.3 %collective-permute-start.7 = (bf16[2,256,512]{2,1,0:T(8,128)(2,1)}, bf16[2,256,512]{2,1,0:T(8,128)(2,1)}, u32[]{:S(2)}, u32[]{:S(2)}) collective-permute-start(bf16[2,256,512]{2,1,0:T(8,128)(2,1)} %broadcast_select_fusion.3), channel_id=1, source_target_pairs={{0,2},{2,0},{4,6},{6,4},{8,10},{10,8},{12,14},{14,12},{16,18},{18,... | collective-permute-start | bytes 1572872 | tf_op jit(solution)/shard_map/ppermute | solution.py:300
  113.9 2.3 %copy-start.2 = (bf16[2,256,512]{2,1,0:T(8,128)(2,1)S(1)}, bf16[2,256,512]{2,1,0:T(8,128)(2,1)}, u32[]{:S(2)}) copy-start(bf16[2,256,512]{2,1,0:T(8,128)(2,1)} %copy-done.1) | copy-start | bytes 1572868
  113.9 2.3 %copy-start.4 = (bf16[2,256,512]{2,1,0:T(8,128)(2,1)S(1)}, bf16[2,256,512]{2,1,0:T(8,128)(2,1)}, u32[]{:S(2)}) copy-start(bf16[2,256,512]{2,1,0:T(8,128)(2,1)} %copy-done.3) | copy-start | bytes 1572868
  115.3 14.3 %collective-permute-start.12 = (bf16[2,256,512]{2,1,0:T(8,128)(2,1)S(1)}, bf16[2,256,512]{2,1,0:T(8,128)(2,1)S(1)}, u32[]{:S(2)}, u32[]{:S(2)}) collective-permute-start(bf16[2,256,512]{2,1,0:T(8,128)(2,1)S(1)} %get-tuple-element.58), channel_id=1, source_target_pairs={{0,32},{2,34},{4,36},{6,38},{8,40},{10,42},{12,44},{14,46},{16,48}... | collective-permute-start | bytes 1572872 | tf_op jit(solution)/shard_map/ppermute | solution.py:300
  115.4 9.1 %copy-start.8 = (bf16[512,2048]{1,0:T(8,128)(2,1)S(1)}, bf16[512,2048]{1,0:T(8,128)(2,1)}, u32[]{:S(2)}) copy-start(bf16[512,2048]{1,0:T(8,128)(2,1)} %param.12) | copy-start | bytes 6291460
  115.4 14.2 %collective-permute-start.10 = (bf16[2,256,512]{2,1,0:T(8,128)(2,1)S(1)}, bf16[2,256,512]{2,1,0:T(8,128)(2,1)S(1)}, u32[]{:S(2)}, u32[]{:S(2)}) collective-permute-start(bf16[2,256,512]{2,1,0:T(8,128)(2,1)S(1)} %get-tuple-element.59), channel_id=1, source_target_pairs={{0,2},{2,0},{4,6},{6,4},{8,10},{10,8},{12,14},{14,12},{16,18},{18,... | collective-permute-start | bytes 1572872 | tf_op jit(solution)/shard_map/ppermute | solution.py:300
  125.7 16.6 %collective-permute-start.14 = (bf16[128,2048]{1,0:T(8,128)(2,1)}, bf16[128,2048]{1,0:T(8,128)(2,1)}, u32[]{:S(2)}, u32[]{:S(2)}) collective-permute-start(bf16[128,2048]{1,0:T(8,128)(2,1)} %convolution_convert_fusion), channel_id=1, source_target_pairs={{0,1},{1,0},{2,3},{3,2},{4,5},{5,4},{6,7},{7,6},{8,9},{9,8},{10,11... | collective-permute-start | bytes 1572872 | tf_op jit(solution)/shard_map/ppermute | solution.py:29
  129.6 0.8 copy-start.15
  129.6 3.2 %copy-start.16 = (bf16[2,256,512]{2,1,0:T(8,128)(2,1)}, bf16[2,256,512]{2,1,0:T(8,128)(2,1)S(1)}, u32[]{:S(2)}) copy-start(bf16[2,256,512]{2,1,0:T(8,128)(2,1)S(1)} %collective-permute-done.10.refs_3_) | copy-start | bytes 1572868
  130.4 8.7 %collective-permute-start.16 = (f32[4,2,256]{2,1,0:T(2,128)S(1)}, f32[4,2,256]{2,1,0:T(2,128)S(1)}, u32[]{:S(2)}, u32[]{:S(2)}) collective-permute-start(f32[4,2,256]{2,1,0:T(2,128)S(1)} %get-tuple-element.54.refs_2_), channel_id=1, source_target_pairs={{64,0},{66,2},{68,4},{70,6},{72,8},{74,10},{76,12},{78,14},{80,16}... | collective-permute-start | bytes 24584 | tf_op jit(solution)/shard_map/ppermute | solution.py:25
  132.8 9.6 %collective-permute-start.13 = (f32[4,2,256]{2,1,0:T(2,128)S(1)}, f32[4,2,256]{2,1,0:T(2,128)S(1)}, u32[]{:S(2)}, u32[]{:S(2)}) collective-permute-start(f32[4,2,256]{2,1,0:T(2,128)S(1)} %get-tuple-element.54.refs_2_), channel_id=1, source_target_pairs={{4,0},{6,2},{8,4},{10,6},{12,8},{14,10},{16,12},{18,14},{20,16},{2... | collective-permute-start | bytes 24584 | tf_op jit(solution)/shard_map/ppermute | solution.py:25
  134.8 28.1 %collective-permute-start.19 = (bf16[2,256,512]{2,1,0:T(8,128)(2,1)}, bf16[2,256,512]{2,1,0:T(8,128)(2,1)S(1)}, u32[]{:S(2)}, u32[]{:S(2)}) collective-permute-start(bf16[2,256,512]{2,1,0:T(8,128)(2,1)} %get-tuple-element.56), channel_id=1, source_target_pairs={{16,0},{18,2},{20,4},{22,6},{24,8},{26,10},{28,12},{30,14},{32,16}... | collective-permute-start | bytes 1572872 | tf_op jit(solution)/shard_map/ppermute | solution.py:25
  136.7 26.2 %collective-permute-start.20 = (bf16[2,256,512]{2,1,0:T(8,128)(2,1)}, bf16[2,256,512]{2,1,0:T(8,128)(2,1)S(1)}, u32[]{:S(2)}, u32[]{:S(2)}) collective-permute-start(bf16[2,256,512]{2,1,0:T(8,128)(2,1)} %get-tuple-element.57), channel_id=1, source_target_pairs={{128,0},{130,2},{132,4},{134,6},{136,8},{138,10},{140,12},{142,14}... | collective-permute-start | bytes 1572872 | tf_op jit(solution)/shard_map/ppermute | solution.py:25
  139.1 10.9 %collective-permute-start.17 = (f32[4,2,256]{2,1,0:T(2,128)S(1)}, f32[4,2,256]{2,1,0:T(2,128)S(1)}, u32[]{:S(2)}, u32[]{:S(2)}) collective-permute-start(f32[4,2,256]{2,1,0:T(2,128)S(1)} %get-tuple-element.54.refs_2_), channel_id=1, source_target_pairs={{8,0},{10,2},{12,4},{14,6},{16,8},{18,10},{20,12},{22,14},{24,16},... | collective-permute-start | bytes 24584 | tf_op jit(solution)/shard_map/ppermute | solution.py:25
  142.4 20.5 %collective-permute-start.18 = (f32[4,2,256]{2,1,0:T(2,128)S(1)}, f32[4,2,256]{2,1,0:T(2,128)S(1)}, u32[]{:S(2)}, u32[]{:S(2)}) collective-permute-start(f32[4,2,256]{2,1,0:T(2,128)S(1)} %bitcast.79), channel_id=1, source_target_pairs={{0,32},{2,34},{4,36},{6,38},{8,40},{10,42},{12,44},{14,46},{16,48}... | collective-permute-start | bytes 24584 | tf_op jit(solution)/shard_map/ppermute | solution.py:300
  146.8 16.1 %collective-permute-start.15 = (f32[4,2,256]{2,1,0:T(2,128)S(1)}, f32[4,2,256]{2,1,0:T(2,128)S(1)}, u32[]{:S(2)}, u32[]{:S(2)}) collective-permute-start(f32[4,2,256]{2,1,0:T(2,128)S(1)} %bitcast.78), channel_id=1, source_target_pairs={{0,2},{2,0},{4,6},{6,4},{8,10},{10,8},{12,14},{14,12},{16,18},{18,... | collective-permute-start | bytes 24584 | tf_op jit(solution)/shard_map/ppermute | solution.py:300
  149.2 18.0 %copy-start.11 = (bf16[2048,512]{1,0:T(8,128)(2,1)S(1)}, bf16[2048,512]{1,0:T(8,128)(2,1)}, u32[]{:S(2)}) copy-start(bf16[2048,512]{1,0:T(8,128)(2,1)} %param.10) | copy-start | bytes 6291460
  168.1 2.9 %copy-start.9 = (bf16[512,2048]{1,0:T(8,128)(2,1)S(1)}, bf16[512,2048]{1,0:T(8,128)(2,1)}, u32[]{:S(2)}) copy-start(bf16[512,2048]{1,0:T(8,128)(2,1)} %param.12) | copy-start | bytes 6291460
  168.1 2.9 %copy-start.13 = (bf16[128,2048]{1,0:T(8,128)(2,1)S(1)}, bf16[128,2048]{1,0:T(8,128)(2,1)}, u32[]{:S(2)}) copy-start(bf16[128,2048]{1,0:T(8,128)(2,1)} %series_ref.1) | copy-start | bytes 1572868
  168.9 13.6 %collective-permute-start.21 = (bf16[128,2048]{1,0:T(8,128)(2,1)S(1)}, bf16[128,2048]{1,0:T(8,128)(2,1)S(1)}, u32[]{:S(2)}, u32[]{:S(2)}) collective-permute-start(bf16[128,2048]{1,0:T(8,128)(2,1)S(1)} %fusion.18), channel_id=1, source_target_pairs={{0,1},{1,0},{2,3},{3,2},{4,5},{5,4},{6,7},{7,6},{8,9},{9,8},{10,11... | collective-permute-start | bytes 1572872 | tf_op jit(solution)/shard_map/ppermute | solution.py:29
  177.6 4.9 %copy-start.6 = (f32[2048]{0:T(1024)S(1)}, f32[2048]{0:T(1024)}, u32[]{:S(2)}) copy-start(f32[2048]{0:T(1024)} %param.8) | copy-start | bytes 24580
  178.4 5.1 %copy-start.14 = (bf16[128,2048]{1,0:T(8,128)(2,1)S(1)}, bf16[128,2048]{1,0:T(8,128)(2,1)}, u32[]{:S(2)}) copy-start(bf16[128,2048]{1,0:T(8,128)(2,1)} %grad_ref.1) | copy-start | bytes 1572868

commit v12 on v10

--- a/solution.py
+++ b/solution.py
@@ -207,7 +207,7 @@
     row_out = jax.ShapeDtypeStruct((rows, width), BF16)
     stat_out = jax.ShapeDtypeStruct((heads, 2, rows), F32)
     back_out = jax.ShapeDtypeStruct((2, rows, width), BF16)
-    outs = [row_out, row_out, stat_out] + [back_out] * n_back
+    outs = [row_out, pltpu.HBM(row_out.shape, BF16), stat_out] + [back_out] * n_back
     return call(
         functools.partial(query_kernel, tuple(len(f) for f in fetched), n_back),
         where,
@@ -304,19 +304,14 @@
     two, far = lax.optimization_barrier((two, far))
     two_q, far_q = lax.optimization_barrier((two_q, far_q))
     four, four_q = shifted(two, 2), shifted(two_q, -2)
+    one, sixteen = swapped(keys, two, 1, 1), swapped(keys, far, 16, 1)
+    one_q, sixteen_q = swapped(queries, two_q, 1, -1), swapped(queries, far_q, 16, -1)
+    four, one, sixteen = lax.optimization_barrier((four, one, sixteen))
+    four_q, one_q, sixteen_q = lax.optimization_barrier((four_q, one_q, sixteen_q))
     eight, eight_q = shifted(four, 4), shifted(four_q, -4)
-    last, last_q = shifted(far, 32), shifted(far_q, -32)
-    sixteen = swapped(keys, far, 16, 1)
-    sixteen_q = swapped(queries, far_q, 16, -1)
-    keys_late, two_late, eight, last_q, sixteen_q = lax.optimization_barrier(
-        (keys, two, eight, last_q, sixteen_q)
-    )
-    one = swapped(keys_late, two_late, 1, 1)
-    queries_late, two_q_late, eight_q = lax.optimization_barrier((queries, two_q, eight_q))
-    one_q = swapped(queries_late, two_q_late, 1, -1)
     return (
-        [one, two, four, eight, sixteen, far, last],
-        [one_q, two_q, four_q, eight_q, sixteen_q, far_q, last_q],
+        [one, two, four, eight, sixteen, far, shifted(far, 32)],
+        [one_q, two_q, four_q, eight_q, sixteen_q, far_q, shifted(far_q, -32)],
     )
 
 

time: 173 us -> 175 us (1.012)
  waiting for transfers between devices: 48.3 us -> 51.8 us
  other arithmetic: 6.17 us -> 3.86 us
    ppermute x6, waiting for transfers between devices: 0.68 us -> 8.31 us  [swapped(): return lax.ppermute(sent, 'seq', [(i, i ^ bit) for i in range(size)])]
    ppermute x15, waiting for transfers between devices: 24.7 us -> 17.8 us  [shifted(): return lax.ppermute(value, 'seq', pairs)]
    ppermute x3, waiting for transfers between devices: 22.9 us -> 25.7 us  [swap_tp(): return lax.ppermute(value, 'tp', [(0, 1), (1, 0)])]
    unnamed x32 -> x34, local copies, waits for them, and re-layouts: 4.85 us -> 5.98 us
  transfers between devices with their start and end apart: 24 -> 24, of which waited for: 7 -> 7; matrix products, arithmetic and copies ran while one was open for 9% -> 8% of each run, Pallas kernels for 6% -> 7%
where the time goes in v12:
time: 175 us; the launch traced here: 174 us
  starting transfers between devices  76.7 us (44%)
  waiting for transfers between devices  51.8 us (30%)
  Pallas kernels  18.9 us (11%)
  matrix products  15.7 us (9%)
  local copies, waits for them, and re-layouts  5.98 us (3%)
  other arithmetic  3.86 us (2%)
    ppermute x15, starting transfers between devices, shifted(): return lax.ppermute(value, 'seq', pairs)  67.4 us
    ppermute x3, waiting for transfers between devices, swap_tp(): return lax.ppermute(value, 'tp', [(0, 1), (1, 0)])  25.7 us
    ppermute x15, waiting for transfers between devices, shifted(): return lax.ppermute(value, 'seq', pairs)  17.8 us
    pallas_call x3, Pallas kernels, call(): pl.pallas_call(kernel, out_shape=outs, grid_spec=pltpu.PrefetchScalarGrid...  16.3 us
    dot_general x7, matrix products, matmul_t(): return lax.dot_general(a, b, NT, preferred_element_type=F32)  9.32 us
    ppermute x6, waiting for transfers between devices, swapped(): return lax.ppermute(sent, 'seq', [(i, i ^ bit) for i in range(size)])  8.31 us
    ppermute x3, starting transfers between devices, swap_tp(): return lax.ppermute(value, 'tp', [(0, 1), (1, 0)])  7.14 us
    dot_general x8, matrix products, matmul(): return jnp.dot(a, b, preferred_element_type=F32)  6.39 us
  transfers between devices with their start and end apart: 24, of which 7 were waited for; matrix products, arithmetic and copies ran while one was open for 8% of the time, Pallas kernels for 7%

profile of v12, /device:TPU:24, one launch (start us, length us, event | category | flops | bytes accessed | tf_op | source)
XLA Modules:
  0.0 174.2 jit_solution(16760384777722393197)
XLA Ops:
  0.6 0.0 copy-start
  0.6 0.0 copy-start.5
  0.7 0.8 copy-done.5
  1.5 2.6 %normalize.1 = (bf16[2,128,2048]{2,1,0:T(8,128)(2,1)S(1)}, f32[128,1]{1,0:T(8,128)S(1)}) custom-call(bf16[128,2048]{1,0:T(8,128)(2,1)} %series_ref.1, f32[1,2048]{1,0:T(1,128)S(1)} %bitcast.77, bf16[128,2048]{1,0:T(8,128)(2,1)} %grad_ref.1), custom_call_target="tpu_custom_call" | custom-call | tf_op jit(solution)/shard_map/normalize/pallas_call | solution.py:269
  4.1 3.1 %collective-permute-start = (bf16[2,128,2048]{2,1,0:T(8,128)(2,1)S(1)}, bf16[2,128,2048]{2,1,0:T(8,128)(2,1)S(1)}, u32[]{:S(2)}, u32[]{:S(2)}) collective-permute-start(bf16[2,128,2048]{2,1,0:T(8,128)(2,1)S(1)} %get-tuple-element.29), channel_id=1, source_target_pairs={{0,1},{1,0},{2,3},{3,2},{4,5},{5,4},{6,7},{7,6},{8,9},{9,8},{10,11... | collective-permute-start | bytes 3145736 | tf_op jit(solution)/shard_map/ppermute | solution.py:29
  7.2 2.6 %fusion.9 = bf16[1,128,512]{2,1,0:T(8,128)(2,1)S(1)} fusion(bf16[128,2048]{1,0:T(8,128)(2,1)} %grad_ref.1, bf16[512,2048]{1,0:T(8,128)(2,1)} %param.12), kind=kOutput, calls=%fused_computation.20 | convolution fusion | flops 268500992 | bytes 2752512 | tf_op jit(solution)/shard_map/dot_general | solution.py:291
  9.9 0.0 copy-start.10
  9.9 0.4 fusion.8
  10.3 0.5 fusion.5
  10.8 0.6 copy-done.10
  11.5 0.4 fusion.4
  11.9 18.7 %collective-permute-done = bf16[2,128,2048]{2,1,0:T(8,128)(2,1)S(1)} collective-permute-done((bf16[2,128,2048]{2,1,0:T(8,128)(2,1)S(1)}, bf16[2,128,2048]{2,1,0:T(8,128)(2,1)S(1)}, u32[]{:S(2)}, u32[]{:S(2)}) %collective-permute-start) | collective-permute-done | bytes 1048608 | tf_op jit(solution)/shard_map/ppermute | solution.py:29
  30.6 0.4 fusion.7
  31.1 0.5 fusion.10
  31.6 0.9 fusion.11
  32.4 0.5 fusion.6
  32.9 0.1 maximum_maximum_fusion
  33.0 1.3 collective-permute-start.2
  34.3 3.8 %collective-permute-start.1 = (bf16[2,256,512]{2,1,0:T(8,128)(2,1)S(1)}, bf16[2,256,512]{2,1,0:T(8,128)(2,1)}, u32[]{:S(2)}, u32[]{:S(2)}) collective-permute-start(bf16[2,256,512]{2,1,0:T(8,128)(2,1)S(1)} %get-tuple-element.31.refs_1_.refs_0_), channel_id=1, source_target_pairs={{0,4},{2,6},{4,8},{6,10},{8,12},{10,14},{12,16},{14,18},{16,20},{1... | collective-permute-start | bytes 1572872 | tf_op jit(solution)/shard_map/ppermute | solution.py:25
  38.2 5.3 %collective-permute-start.9 = (bf16[2,256,512]{2,1,0:T(8,128)(2,1)S(1)}, bf16[2,256,512]{2,1,0:T(8,128)(2,1)}, u32[]{:S(2)}, u32[]{:S(2)}) collective-permute-start(bf16[2,256,512]{2,1,0:T(8,128)(2,1)S(1)} %get-tuple-element.30.refs_0_.refs_1_), channel_id=1, source_target_pairs={{64,0},{66,2},{68,4},{70,6},{72,8},{74,10},{76,12},{78,14},{80,16}... | collective-permute-start | bytes 1572872 | tf_op jit(solution)/shard_map/ppermute | solution.py:25
  43.5 6.2 %collective-permute-start.8 = (bf16[2,256,512]{2,1,0:T(8,128)(2,1)S(1)}, bf16[2,256,512]{2,1,0:T(8,128)(2,1)}, u32[]{:S(2)}, u32[]{:S(2)}) collective-permute-start(bf16[2,256,512]{2,1,0:T(8,128)(2,1)S(1)} %get-tuple-element.30.refs_0_.refs_1_), channel_id=1, source_target_pairs={{4,0},{6,2},{8,4},{10,6},{12,8},{14,10},{16,12},{18,14},{20,16},{2... | collective-permute-start | bytes 1572872 | tf_op jit(solution)/shard_map/ppermute | solution.py:25
  49.7 9.3 %collective-permute-done.2.refs_7_ = bf16[2,256,512]{2,1,0:T(8,128)(2,1)} collective-permute-done((bf16[2,256,512]{2,1,0:T(8,128)(2,1)S(1)}, bf16[2,256,512]{2,1,0:T(8,128)(2,1)}, u32[]{:S(2)}, u32[]{:S(2)}) %collective-permute-start.2) | collective-permute-done | bytes 524320 | tf_op jit(solution)/shard_map/ppermute | solution.py:25
  59.0 1.9 %collective-permute-start.3 = (bf16[2,256,512]{2,1,0:T(8,128)(2,1)}, bf16[2,256,512]{2,1,0:T(8,128)(2,1)}, u32[]{:S(2)}, u32[]{:S(2)}) collective-permute-start(bf16[2,256,512]{2,1,0:T(8,128)(2,1)} %collective-permute-done.1.refs_3_), channel_id=1, source_target_pairs={{0,4},{2,6},{4,8},{6,10},{8,12},{10,14},{12,16},{14,18},{16,20},{1... | collective-permute-start | bytes 1572872 | tf_op jit(solution)/shard_map/ppermute | solution.py:25
  60.9 0.1 broadcast_select_fusion.1
  61.1 0.1 collective-permute-start.5
  61.2 0.1 collective-permute-start.4
  61.3 11.5 %collective-permute-start.10 = (bf16[2,256,512]{2,1,0:T(8,128)(2,1)}, bf16[2,256,512]{2,1,0:T(8,128)(2,1)}, u32[]{:S(2)}, u32[]{:S(2)}) collective-permute-start(bf16[2,256,512]{2,1,0:T(8,128)(2,1)} %collective-permute-done.8.refs_4_), channel_id=1, source_target_pairs={{4,0},{6,2},{8,4},{10,6},{12,8},{14,10},{16,12},{18,14},{20,16},{2... | collective-permute-start | bytes 1572872 | tf_op jit(solution)/shard_map/ppermute | solution.py:25
  72.8 2.3 %broadcast_select_fusion = (bf16[2,256,512]{2,1,0:T(8,128)(2,1)}, bf16[2,256,512]{2,1,0:T(8,128)(2,1)}) fusion(bf16[2,256,512]{2,1,0:T(8,128)(2,1)S(1)} %get-tuple-element.30.refs_0_.refs_1_, bf16[2,256,512]{2,1,0:T(8,128)(2,1)} %collective-permute-done.9.refs_8_, pred[]{:T(512)S(6)} %eq.18, bf16[2,256,512]{2,1,0:T(8,128)(2,1)} %collective-permute-done.8.refs_4_, ...), kind=kLoop, calls=%fused_computation.42 | loop fusion | flops 524288 | bytes 2621442 | tf_op jit(solution)/shard_map/jit(_where)/select_n | solution.py:297
  75.1 1.1 collective-permute-done.3.refs_4_
  76.2 3.7 %collective-permute-done.5.refs_6_ = bf16[2,256,512]{2,1,0:T(8,128)(2,1)S(1)} collective-permute-done((bf16[2,256,512]{2,1,0:T(8,128)(2,1)S(1)}, bf16[2,256,512]{2,1,0:T(8,128)(2,1)S(1)}, u32[]{:S(2)}, u32[]{:S(2)}) %collective-permute-start.5) | collective-permute-done | bytes 524320 | tf_op jit(solution)/shard_map/ppermute | solution.py:298
  79.9 0.8 copy-done.1
  80.7 1.3 collective-permute-start.7
  82.0 0.8 copy-done.3
  82.8 1.9 %collective-permute-start.6 = (bf16[2,256,512]{2,1,0:T(8,128)(2,1)}, bf16[2,256,512]{2,1,0:T(8,128)(2,1)}, u32[]{:S(2)}, u32[]{:S(2)}) collective-permute-start(bf16[2,256,512]{2,1,0:T(8,128)(2,1)} %collective-permute-done.3.refs_4_), channel_id=1, source_target_pairs={{0,8},{2,10},{4,12},{6,14},{8,16},{10,18},{12,20},{14,22},{16,24},... | collective-permute-start | bytes 1572872 | tf_op jit(solution)/shard_map/ppermute | solution.py:25
  84.7 0.1 pad_add_fusion.where_ref
  84.8 10.6 %collective-permute-start.14 = (bf16[2,256,512]{2,1,0:T(8,128)(2,1)}, bf16[2,256,512]{2,1,0:T(8,128)(2,1)S(1)}, u32[]{:S(2)}, u32[]{:S(2)}) collective-permute-start(bf16[2,256,512]{2,1,0:T(8,128)(2,1)} %collective-permute-done.9.refs_8_), channel_id=1, source_target_pairs={{64,0},{66,2},{68,4},{70,6},{72,8},{74,10},{76,12},{78,14},{80,16}... | collective-permute-start | bytes 1572872 | tf_op jit(solution)/shard_map/ppermute | solution.py:25
  95.4 4.6 %collective-permute-done.12.refs_7_ = bf16[2,256,512]{2,1,0:T(8,128)(2,1)} collective-permute-done((bf16[2,256,512]{2,1,0:T(8,128)(2,1)}, bf16[2,256,512]{2,1,0:T(8,128)(2,1)}, u32[]{:S(2)}, u32[]{:S(2)}) %collective-permute-start.12) | collective-permute-done | bytes 524320 | tf_op jit(solution)/shard_map/ppermute | solution.py:298
  100.1 3.2 %collective-permute-start.13 = (bf16[2,256,512]{2,1,0:T(8,128)(2,1)}, bf16[2,256,512]{2,1,0:T(8,128)(2,1)S(1)}, u32[]{:S(2)}, u32[]{:S(2)}) collective-permute-start(bf16[2,256,512]{2,1,0:T(8,128)(2,1)} %collective-permute-done.10.refs_5_), channel_id=1, source_target_pairs={{8,0},{10,2},{12,4},{14,6},{16,8},{18,10},{20,12},{22,14},{24,16},... | collective-permute-start | bytes 1572872 | tf_op jit(solution)/shard_map/ppermute | solution.py:25
  103.2 7.4 %collective-permute-done.7.refs_8_ = bf16[2,256,512]{2,1,0:T(8,128)(2,1)} collective-permute-done((bf16[2,256,512]{2,1,0:T(8,128)(2,1)}, bf16[2,256,512]{2,1,0:T(8,128)(2,1)}, u32[]{:S(2)}, u32[]{:S(2)}) %collective-permute-start.7) | collective-permute-done | bytes 524320 | tf_op jit(solution)/shard_map/ppermute | solution.py:25
  110.6 1.0 copy-done.2
  111.6 1.0 copy-done.4
  112.7 6.9 %query_side.1 = (bf16[256,512]{1,0:T(8,128)(2,1)S(1)}, bf16[256,512]{1,0:T(8,128)(2,1)}, f32[4,2,256]{2,1,0:T(2,128)S(1)}) custom-call(s32[2]{0:T(128)S(1)} %pad_add_fusion.where_ref, bf16[2,256,512]{2,1,0:T(8,128)(2,1)S(1)} %get-tuple-element.30.refs_0_.refs_1_, bf16[2,256,512]{2,1,0:T(8,128)(2,1)S(1)} %get-tuple-element.31.refs_1_.refs_0_, ...), custom_call_target="tpu_custom_call" | custom-call | flops 163840 | bytes 65536 | tf_op jit(solution)/shard_map/query_side/pallas_call | solution.py:188
  119.6 1.3 convolution_convert_fusion
  120.8 3.0 %collective-permute-start.16 = (bf16[128,2048]{1,0:T(8,128)(2,1)}, bf16[128,2048]{1,0:T(8,128)(2,1)}, u32[]{:S(2)}, u32[]{:S(2)}) collective-permute-start(bf16[128,2048]{1,0:T(8,128)(2,1)} %convolution_convert_fusion), channel_id=1, source_target_pairs={{0,1},{1,0},{2,3},{3,2},{4,5},{5,4},{6,7},{7,6},{8,9},{9,8},{10,11... | collective-permute-start | bytes 1572872 | tf_op jit(solution)/shard_map/ppermute | solution.py:29
  123.9 0.8 copy-done.15
  124.6 6.6 %collective-permute-start.15 = (f32[4,2,256]{2,1,0:T(2,128)S(1)}, f32[4,2,256]{2,1,0:T(2,128)S(1)}, u32[]{:S(2)}, u32[]{:S(2)}) collective-permute-start(f32[4,2,256]{2,1,0:T(2,128)S(1)} %get-tuple-element.44.refs_2_), channel_id=1, source_target_pairs={{4,0},{6,2},{8,4},{10,6},{12,8},{14,10},{16,12},{18,14},{20,16},{2... | collective-permute-start | bytes 24584 | tf_op jit(solution)/shard_map/ppermute | solution.py:25
  131.3 5.7 %collective-permute-start.20 = (f32[4,2,256]{2,1,0:T(2,128)S(1)}, f32[4,2,256]{2,1,0:T(2,128)S(1)}, u32[]{:S(2)}, u32[]{:S(2)}) collective-permute-start(f32[4,2,256]{2,1,0:T(2,128)S(1)} %get-tuple-element.44.refs_2_), channel_id=1, source_target_pairs={{64,0},{66,2},{68,4},{70,6},{72,8},{74,10},{76,12},{78,14},{80,16}... | collective-permute-start | bytes 24584 | tf_op jit(solution)/shard_map/ppermute | solution.py:25
  137.0 0.1 reduce
  137.1 1.3 collective-permute-start.22
  138.4 1.9 %collective-permute-start.19 = (f32[4,2,256]{2,1,0:T(2,128)S(1)}, f32[4,2,256]{2,1,0:T(2,128)S(1)}, u32[]{:S(2)}, u32[]{:S(2)}) collective-permute-start(f32[4,2,256]{2,1,0:T(2,128)S(1)} %get-tuple-element.44.refs_2_), channel_id=1, source_target_pairs={{16,0},{18,2},{20,4},{22,6},{24,8},{26,10},{28,12},{30,14},{32,16}... | collective-permute-start | bytes 24584 | tf_op jit(solution)/shard_map/ppermute | solution.py:25
  140.4 4.7 %collective-permute-start.18 = (f32[4,2,256]{2,1,0:T(2,128)S(1)}, f32[4,2,256]{2,1,0:T(2,128)S(1)}, u32[]{:S(2)}, u32[]{:S(2)}) collective-permute-start(f32[4,2,256]{2,1,0:T(2,128)S(1)} %get-tuple-element.44.refs_2_), channel_id=1, source_target_pairs={{8,0},{10,2},{12,4},{14,6},{16,8},{18,10},{20,12},{22,14},{24,16},... | collective-permute-start | bytes 24584 | tf_op jit(solution)/shard_map/ppermute | solution.py:25
  145.1 2.0 %collective-permute-start.21 = (f32[4,2,256]{2,1,0:T(2,128)S(1)}, f32[4,2,256]{2,1,0:T(2,128)S(1)}, u32[]{:S(2)}, u32[]{:S(2)}) collective-permute-start(f32[4,2,256]{2,1,0:T(2,128)S(1)} %bitcast.79), channel_id=1, source_target_pairs={{0,32},{2,34},{4,36},{6,38},{8,40},{10,42},{12,44},{14,46},{16,48}... | collective-permute-start | bytes 24584 | tf_op jit(solution)/shard_map/ppermute | solution.py:298
  147.2 2.4 %fusion.34 = f32[256,2048]{1,0:T(8,128)S(1)} fusion(bf16[256,512]{1,0:T(8,128)(2,1)} %get-tuple-element.47, bf16[2048,512]{1,0:T(8,128)(2,1)} %param.9), kind=kOutput, calls=%fused_computation.63 | convolution fusion | flops 536870912 | bytes 4456448 | tf_op jit(solution)/shard_map/dot_general | solution.py:291
  149.7 4.7 %key_side.3 = bf16[2,128,512]{2,1,0:T(8,128)(2,1)S(1)} custom-call(s32[2]{0:T(128)S(1)} %pad_add_fusion.where_ref, bf16[2,256,512]{2,1,0:T(8,128)(2,1)S(1)} %get-tuple-element.31.refs_1_.refs_0_, bf16[2,256,512]{2,1,0:T(8,128)(2,1)S(1)} %get-tuple-element.30.refs_0_.refs_1_, f32[4,2,256]{2,1,0:T(2,128)S(1)} %get-tuple-element.44.refs_2_, ...), custom_call_target="tpu_custom_call" | custom-call | flops 81920 | bytes 65536 | tf_op jit(solution)/shard_map/key_side/pallas_call | solution.py:188
  154.4 0.8 fusion.29
  155.2 0.0 copy-start.9
  155.2 0.8 fusion.18
  156.1 1.0 collective-permute-start.23
  157.1 2.4 %fusion.1 = bf16[128,2048]{1,0:T(8,128)(2,1)} fusion(bf16[512,2048]{1,0:T(8,128)(2,1)S(1)} %copy-done.9, bf16[128,2048]{1,0:T(8,128)(2,1)S(1)} %copy-done.13, bf16[128,2048]{1,0:T(8,128)(2,1)} %collective-permute-done.16, bf16[256,512]{1,0:T(8,128)(2,1)S(1)} %get-tuple-element.37), kind=kOutput, calls=%fused_computation.2 | convolution fusion | flops 269746176 | bytes 3801088 | tf_op jit(solution)/shard_map/dot_general | solution.py:287
  159.4 4.7 %key_side.2 = bf16[2,128,512]{2,1,0:T(8,128)(2,1)S(1)} custom-call(s32[2]{0:T(128)S(1)} %pad_add_fusion.where_ref, bf16[2,256,512]{2,1,0:T(8,128)(2,1)S(1)} %get-tuple-element.31.refs_1_.refs_0_, bf16[2,256,512]{2,1,0:T(8,128)(2,1)S(1)} %get-tuple-element.30.refs_0_.refs_1_, f32[4,2,256]{2,1,0:T(2,128)S(1)} %get-tuple-element.44.refs_2_, ...), custom_call_target="tpu_custom_call" | custom-call | flops 81920 | bytes 65536 | tf_op jit(solution)/shard_map/key_side/pallas_call | solution.py:188
  164.1 0.8 fusion.31
  165.0 7.0 %collective-permute-done.23 = bf16[128,2048]{1,0:T(8,128)(2,1)S(1)} collective-permute-done((bf16[128,2048]{1,0:T(8,128)(2,1)S(1)}, bf16[128,2048]{1,0:T(8,128)(2,1)S(1)}, u32[]{:S(2)}, u32[]{:S(2)}) %collective-permute-start.23) | collective-permute-done | bytes 524320 | tf_op jit(solution)/shard_map/ppermute | solution.py:29
  172.0 1.0 fusion.12
  173.0 1.2 fusion.16
  (45 shorter events, 0.1 us)
Async XLA Ops:
  0.6 9.7 %copy-start = (bf16[2048,512]{1,0:T(8,128)(2,1)S(1)}, bf16[2048,512]{1,0:T(8,128)(2,1)}, u32[]{:S(2)}) copy-start(bf16[2048,512]{1,0:T(8,128)(2,1)} %param.11) | copy-start | bytes 6291460
  0.6 0.8 copy-start.5
  1.5 8.4 %copy-start.12 = (bf16[2048,512]{1,0:T(8,128)(2,1)S(1)}, bf16[2048,512]{1,0:T(8,128)(2,1)}, u32[]{:S(2)}) copy-start(bf16[2048,512]{1,0:T(8,128)(2,1)} %param.9) | copy-start | bytes 6291460
  4.1 26.5 %collective-permute-start = (bf16[2,128,2048]{2,1,0:T(8,128)(2,1)S(1)}, bf16[2,128,2048]{2,1,0:T(8,128)(2,1)S(1)}, u32[]{:S(2)}, u32[]{:S(2)}) collective-permute-start(bf16[2,128,2048]{2,1,0:T(8,128)(2,1)S(1)} %get-tuple-element.29), channel_id=1, source_target_pairs={{0,1},{1,0},{2,3},{3,2},{4,5},{5,4},{6,7},{7,6},{8,9},{9,8},{10,11... | collective-permute-start | bytes 3145736 | tf_op jit(solution)/shard_map/ppermute | solution.py:29
  9.9 1.6 copy-start.10
  11.9 19.6 %copy-start.7 = (bf16[512,2048]{1,0:T(8,128)(2,1)S(1)}, bf16[512,2048]{1,0:T(8,128)(2,1)}, u32[]{:S(2)}) copy-start(bf16[512,2048]{1,0:T(8,128)(2,1)} %param.12) | copy-start | bytes 6291460
  33.0 26.0 %collective-permute-start.2 = (bf16[2,256,512]{2,1,0:T(8,128)(2,1)S(1)}, bf16[2,256,512]{2,1,0:T(8,128)(2,1)}, u32[]{:S(2)}, u32[]{:S(2)}) collective-permute-start(bf16[2,256,512]{2,1,0:T(8,128)(2,1)S(1)} %get-tuple-element.31.refs_1_.refs_0_), channel_id=1, source_target_pairs={{0,64},{2,66},{4,68},{6,70},{8,72},{10,74},{12,76},{14,78},{16,80}... | collective-permute-start | bytes 1572872 | tf_op jit(solution)/shard_map/ppermute | solution.py:25
  34.3 24.7 %collective-permute-start.1 = (bf16[2,256,512]{2,1,0:T(8,128)(2,1)S(1)}, bf16[2,256,512]{2,1,0:T(8,128)(2,1)}, u32[]{:S(2)}, u32[]{:S(2)}) collective-permute-start(bf16[2,256,512]{2,1,0:T(8,128)(2,1)S(1)} %get-tuple-element.31.refs_1_.refs_0_), channel_id=1, source_target_pairs={{0,4},{2,6},{4,8},{6,10},{8,12},{10,14},{12,16},{14,18},{16,20},{1... | collective-permute-start | bytes 1572872 | tf_op jit(solution)/shard_map/ppermute | solution.py:25
  38.2 23.1 %collective-permute-start.9 = (bf16[2,256,512]{2,1,0:T(8,128)(2,1)S(1)}, bf16[2,256,512]{2,1,0:T(8,128)(2,1)}, u32[]{:S(2)}, u32[]{:S(2)}) collective-permute-start(bf16[2,256,512]{2,1,0:T(8,128)(2,1)S(1)} %get-tuple-element.30.refs_0_.refs_1_), channel_id=1, source_target_pairs={{64,0},{66,2},{68,4},{70,6},{72,8},{74,10},{76,12},{78,14},{80,16}... | collective-permute-start | bytes 1572872 | tf_op jit(solution)/shard_map/ppermute | solution.py:25
  43.5 17.8 %collective-permute-start.8 = (bf16[2,256,512]{2,1,0:T(8,128)(2,1)S(1)}, bf16[2,256,512]{2,1,0:T(8,128)(2,1)}, u32[]{:S(2)}, u32[]{:S(2)}) collective-permute-start(bf16[2,256,512]{2,1,0:T(8,128)(2,1)S(1)} %get-tuple-element.30.refs_0_.refs_1_), channel_id=1, source_target_pairs={{4,0},{6,2},{8,4},{10,6},{12,8},{14,10},{16,12},{18,14},{20,16},{2... | collective-permute-start | bytes 1572872 | tf_op jit(solution)/shard_map/ppermute | solution.py:25
  59.0 17.2 %collective-permute-start.3 = (bf16[2,256,512]{2,1,0:T(8,128)(2,1)}, bf16[2,256,512]{2,1,0:T(8,128)(2,1)}, u32[]{:S(2)}, u32[]{:S(2)}) collective-permute-start(bf16[2,256,512]{2,1,0:T(8,128)(2,1)} %collective-permute-done.1.refs_3_), channel_id=1, source_target_pairs={{0,4},{2,6},{4,8},{6,10},{8,12},{10,14},{12,16},{14,18},{16,20},{1... | collective-permute-start | bytes 1572872 | tf_op jit(solution)/shard_map/ppermute | solution.py:25
  61.1 18.8 %collective-permute-start.5 = (bf16[2,256,512]{2,1,0:T(8,128)(2,1)S(1)}, bf16[2,256,512]{2,1,0:T(8,128)(2,1)S(1)}, u32[]{:S(2)}, u32[]{:S(2)}) collective-permute-start(bf16[2,256,512]{2,1,0:T(8,128)(2,1)S(1)} %get-tuple-element.58), channel_id=1, source_target_pairs={{0,32},{2,34},{4,36},{6,38},{8,40},{10,42},{12,44},{14,46},{16,48}... | collective-permute-start | bytes 1572872 | tf_op jit(solution)/shard_map/ppermute | solution.py:298
  61.2 20.8 %collective-permute-start.4 = (bf16[2,256,512]{2,1,0:T(8,128)(2,1)S(1)}, bf16[2,256,512]{2,1,0:T(8,128)(2,1)S(1)}, u32[]{:S(2)}, u32[]{:S(2)}) collective-permute-start(bf16[2,256,512]{2,1,0:T(8,128)(2,1)S(1)} %get-tuple-element.59), channel_id=1, source_target_pairs={{0,2},{2,0},{4,6},{6,4},{8,10},{10,8},{12,14},{14,12},{16,18},{18,... | collective-permute-start | bytes 1572872 | tf_op jit(solution)/shard_map/ppermute | solution.py:298
  61.3 23.5 %collective-permute-start.10 = (bf16[2,256,512]{2,1,0:T(8,128)(2,1)}, bf16[2,256,512]{2,1,0:T(8,128)(2,1)}, u32[]{:S(2)}, u32[]{:S(2)}) collective-permute-start(bf16[2,256,512]{2,1,0:T(8,128)(2,1)} %collective-permute-done.8.refs_4_), channel_id=1, source_target_pairs={{4,0},{6,2},{8,4},{10,6},{12,8},{14,10},{16,12},{18,14},{20,16},{2... | collective-permute-start | bytes 1572872 | tf_op jit(solution)/shard_map/ppermute | solution.py:25
  75.1 25.0 %collective-permute-start.12 = (bf16[2,256,512]{2,1,0:T(8,128)(2,1)}, bf16[2,256,512]{2,1,0:T(8,128)(2,1)}, u32[]{:S(2)}, u32[]{:S(2)}) collective-permute-start(bf16[2,256,512]{2,1,0:T(8,128)(2,1)} %get-tuple-element.56), channel_id=1, source_target_pairs={{0,32},{2,34},{4,36},{6,38},{8,40},{10,42},{12,44},{14,46},{16,48}... | collective-permute-start | bytes 1572872 | tf_op jit(solution)/shard_map/ppermute | solution.py:298
  76.2 23.8 %collective-permute-start.11 = (bf16[2,256,512]{2,1,0:T(8,128)(2,1)}, bf16[2,256,512]{2,1,0:T(8,128)(2,1)}, u32[]{:S(2)}, u32[]{:S(2)}) collective-permute-start(bf16[2,256,512]{2,1,0:T(8,128)(2,1)} %get-tuple-element.57), channel_id=1, source_target_pairs={{0,2},{2,0},{4,6},{6,4},{8,10},{10,8},{12,14},{14,12},{16,18},{18,... | collective-permute-start | bytes 1572872 | tf_op jit(solution)/shard_map/ppermute | solution.py:298
  79.9 0.8 copy-start.1
  80.7 29.9 %collective-permute-start.7 = (bf16[2,256,512]{2,1,0:T(8,128)(2,1)}, bf16[2,256,512]{2,1,0:T(8,128)(2,1)}, u32[]{:S(2)}, u32[]{:S(2)}) collective-permute-start(bf16[2,256,512]{2,1,0:T(8,128)(2,1)} %collective-permute-done.2.refs_7_), channel_id=1, source_target_pairs={{0,64},{2,66},{4,68},{6,70},{8,72},{10,74},{12,76},{14,78},{16,80}... | collective-permute-start | bytes 1572872 | tf_op jit(solution)/shard_map/ppermute | solution.py:25
  82.0 0.8 copy-start.3
  82.8 27.8 %collective-permute-start.6 = (bf16[2,256,512]{2,1,0:T(8,128)(2,1)}, bf16[2,256,512]{2,1,0:T(8,128)(2,1)}, u32[]{:S(2)}, u32[]{:S(2)}) collective-permute-start(bf16[2,256,512]{2,1,0:T(8,128)(2,1)} %collective-permute-done.3.refs_4_), channel_id=1, source_target_pairs={{0,8},{2,10},{4,12},{6,14},{8,16},{10,18},{12,20},{14,22},{16,24},... | collective-permute-start | bytes 1572872 | tf_op jit(solution)/shard_map/ppermute | solution.py:25
  84.8 39.1 %collective-permute-start.14 = (bf16[2,256,512]{2,1,0:T(8,128)(2,1)}, bf16[2,256,512]{2,1,0:T(8,128)(2,1)S(1)}, u32[]{:S(2)}, u32[]{:S(2)}) collective-permute-start(bf16[2,256,512]{2,1,0:T(8,128)(2,1)} %collective-permute-done.9.refs_8_), channel_id=1, source_target_pairs={{64,0},{66,2},{68,4},{70,6},{72,8},{74,10},{76,12},{78,14},{80,16}... | collective-permute-start | bytes 1572872 | tf_op jit(solution)/shard_map/ppermute | solution.py:25
  100.1 23.8 %collective-permute-start.13 = (bf16[2,256,512]{2,1,0:T(8,128)(2,1)}, bf16[2,256,512]{2,1,0:T(8,128)(2,1)S(1)}, u32[]{:S(2)}, u32[]{:S(2)}) collective-permute-start(bf16[2,256,512]{2,1,0:T(8,128)(2,1)} %collective-permute-done.10.refs_5_), channel_id=1, source_target_pairs={{8,0},{10,2},{12,4},{14,6},{16,8},{18,10},{20,12},{22,14},{24,16},... | collective-permute-start | bytes 1572872 | tf_op jit(solution)/shard_map/ppermute | solution.py:25
  110.6 1.0 copy-start.2
  111.6 1.0 copy-start.4
  112.7 6.9 %copy-start.8 = (bf16[512,2048]{1,0:T(8,128)(2,1)S(1)}, bf16[512,2048]{1,0:T(8,128)(2,1)}, u32[]{:S(2)}) copy-start(bf16[512,2048]{1,0:T(8,128)(2,1)} %param.12) | copy-start | bytes 6291460
  120.8 24.3 %collective-permute-start.16 = (bf16[128,2048]{1,0:T(8,128)(2,1)}, bf16[128,2048]{1,0:T(8,128)(2,1)}, u32[]{:S(2)}, u32[]{:S(2)}) collective-permute-start(bf16[128,2048]{1,0:T(8,128)(2,1)} %convolution_convert_fusion), channel_id=1, source_target_pairs={{0,1},{1,0},{2,3},{3,2},{4,5},{5,4},{6,7},{7,6},{8,9},{9,8},{10,11... | collective-permute-start | bytes 1572872 | tf_op jit(solution)/shard_map/ppermute | solution.py:29
  123.9 0.8 copy-start.15
  123.9 7.4 %copy-start.16 = (bf16[2,256,512]{2,1,0:T(8,128)(2,1)}, bf16[2,256,512]{2,1,0:T(8,128)(2,1)S(1)}, u32[]{:S(2)}) copy-start(bf16[2,256,512]{2,1,0:T(8,128)(2,1)S(1)} %collective-permute-done.13.refs_6_) | copy-start | bytes 1572868
  124.6 15.7 %collective-permute-start.15 = (f32[4,2,256]{2,1,0:T(2,128)S(1)}, f32[4,2,256]{2,1,0:T(2,128)S(1)}, u32[]{:S(2)}, u32[]{:S(2)}) collective-permute-start(f32[4,2,256]{2,1,0:T(2,128)S(1)} %get-tuple-element.44.refs_2_), channel_id=1, source_target_pairs={{4,0},{6,2},{8,4},{10,6},{12,8},{14,10},{16,12},{18,14},{20,16},{2... | collective-permute-start | bytes 24584 | tf_op jit(solution)/shard_map/ppermute | solution.py:25
  131.3 13.8 %collective-permute-start.20 = (f32[4,2,256]{2,1,0:T(2,128)S(1)}, f32[4,2,256]{2,1,0:T(2,128)S(1)}, u32[]{:S(2)}, u32[]{:S(2)}) collective-permute-start(f32[4,2,256]{2,1,0:T(2,128)S(1)} %get-tuple-element.44.refs_2_), channel_id=1, source_target_pairs={{64,0},{66,2},{68,4},{70,6},{72,8},{74,10},{76,12},{78,14},{80,16}... | collective-permute-start | bytes 24584 | tf_op jit(solution)/shard_map/ppermute | solution.py:25
  137.1 12.5 %collective-permute-start.22 = (f32[4,2,256]{2,1,0:T(2,128)S(1)}, f32[4,2,256]{2,1,0:T(2,128)S(1)}, u32[]{:S(2)}, u32[]{:S(2)}) collective-permute-start(f32[4,2,256]{2,1,0:T(2,128)S(1)} %get-tuple-element.44.refs_2_), channel_id=1, source_target_pairs={{128,0},{130,2},{132,4},{134,6},{136,8},{138,10},{140,12},{142,14}... | collective-permute-start | bytes 24584 | tf_op jit(solution)/shard_map/ppermute | solution.py:25
  138.4 11.2 %collective-permute-start.19 = (f32[4,2,256]{2,1,0:T(2,128)S(1)}, f32[4,2,256]{2,1,0:T(2,128)S(1)}, u32[]{:S(2)}, u32[]{:S(2)}) collective-permute-start(f32[4,2,256]{2,1,0:T(2,128)S(1)} %get-tuple-element.44.refs_2_), channel_id=1, source_target_pairs={{16,0},{18,2},{20,4},{22,6},{24,8},{26,10},{28,12},{30,14},{32,16}... | collective-permute-start | bytes 24584 | tf_op jit(solution)/shard_map/ppermute | solution.py:25
  140.4 9.3 %collective-permute-start.18 = (f32[4,2,256]{2,1,0:T(2,128)S(1)}, f32[4,2,256]{2,1,0:T(2,128)S(1)}, u32[]{:S(2)}, u32[]{:S(2)}) collective-permute-start(f32[4,2,256]{2,1,0:T(2,128)S(1)} %get-tuple-element.44.refs_2_), channel_id=1, source_target_pairs={{8,0},{10,2},{12,4},{14,6},{16,8},{18,10},{20,12},{22,14},{24,16},... | collective-permute-start | bytes 24584 | tf_op jit(solution)/shard_map/ppermute | solution.py:25
  145.1 4.5 %collective-permute-start.21 = (f32[4,2,256]{2,1,0:T(2,128)S(1)}, f32[4,2,256]{2,1,0:T(2,128)S(1)}, u32[]{:S(2)}, u32[]{:S(2)}) collective-permute-start(f32[4,2,256]{2,1,0:T(2,128)S(1)} %bitcast.79), channel_id=1, source_target_pairs={{0,32},{2,34},{4,36},{6,38},{8,40},{10,42},{12,44},{14,46},{16,48}... | collective-permute-start | bytes 24584 | tf_op jit(solution)/shard_map/ppermute | solution.py:298
  147.2 2.5 %collective-permute-start.17 = (f32[4,2,256]{2,1,0:T(2,128)S(1)}, f32[4,2,256]{2,1,0:T(2,128)S(1)}, u32[]{:S(2)}, u32[]{:S(2)}) collective-permute-start(f32[4,2,256]{2,1,0:T(2,128)S(1)} %bitcast.78), channel_id=1, source_target_pairs={{0,2},{2,0},{4,6},{6,4},{8,10},{10,8},{12,14},{14,12},{16,18},{18,... | collective-permute-start | bytes 24584 | tf_op jit(solution)/shard_map/ppermute | solution.py:298
  149.6 4.8 %copy-start.11 = (bf16[2048,512]{1,0:T(8,128)(2,1)S(1)}, bf16[2048,512]{1,0:T(8,128)(2,1)}, u32[]{:S(2)}) copy-start(bf16[2048,512]{1,0:T(8,128)(2,1)} %param.10) | copy-start | bytes 6291460
  155.2 1.9 %copy-start.9 = (bf16[512,2048]{1,0:T(8,128)(2,1)S(1)}, bf16[512,2048]{1,0:T(8,128)(2,1)}, u32[]{:S(2)}) copy-start(bf16[512,2048]{1,0:T(8,128)(2,1)} %param.12) | copy-start | bytes 6291460
  155.2 1.8 %copy-start.13 = (bf16[128,2048]{1,0:T(8,128)(2,1)S(1)}, bf16[128,2048]{1,0:T(8,128)(2,1)}, u32[]{:S(2)}) copy-start(bf16[128,2048]{1,0:T(8,128)(2,1)} %series_ref.1) | copy-start | bytes 1572868
  156.1 15.9 %collective-permute-start.23 = (bf16[128,2048]{1,0:T(8,128)(2,1)S(1)}, bf16[128,2048]{1,0:T(8,128)(2,1)S(1)}, u32[]{:S(2)}, u32[]{:S(2)}) collective-permute-start(bf16[128,2048]{1,0:T(8,128)(2,1)S(1)} %fusion.18), channel_id=1, source_target_pairs={{0,1},{1,0},{2,3},{3,2},{4,5},{5,4},{6,7},{7,6},{8,9},{9,8},{10,11... | collective-permute-start | bytes 1572872 | tf_op jit(solution)/shard_map/ppermute | solution.py:29
  164.1 7.8 %copy-start.6 = (f32[2048]{0:T(1024)S(1)}, f32[2048]{0:T(1024)}, u32[]{:S(2)}) copy-start(f32[2048]{0:T(1024)} %param.8) | copy-start | bytes 24580
  165.0 8.0 %copy-start.14 = (bf16[128,2048]{1,0:T(8,128)(2,1)S(1)}, bf16[128,2048]{1,0:T(8,128)(2,1)}, u32[]{:S(2)}) copy-start(bf16[128,2048]{1,0:T(8,128)(2,1)} %grad_ref.1) | copy-start | bytes 1572868

commit v13 on v9

--- a/solution.py
+++ b/solution.py
@@ -17,6 +17,7 @@
 NT = (((1,), (1,)), ((), ()))
 TN = (((0,), (0,)), ((), ()))
 NEAR = (1, 2, 4)
+GROUP = 2
 
 
 def shifted(value, by):
@@ -174,24 +175,40 @@
 
 
 def head_spec(a):
-    if a.ndim == 2:
-        return pl.BlockSpec((a.shape[0], HD), lambda h, w: (0, h))
-    return pl.BlockSpec((a.shape[0], a.shape[1], HD), lambda h, w: (0, 0, h))
+    if len(a.shape) == 2:
+        return pl.BlockSpec((a.shape[0], GROUP * HD), lambda h, w: (0, h))
+    return pl.BlockSpec((a.shape[0], a.shape[1], GROUP * HD), lambda h, w: (0, 0, h))
 
 
 def stat_spec(a):
-    return pl.BlockSpec((1,) + a.shape[1:], lambda h, w: (h, 0, 0))
+    return pl.BlockSpec((GROUP,) + a.shape[1:], lambda h, w: (h, 0, 0))
+
+
+def each_head(kernel):
+    def run(where_ref, *refs):
+        for head in range(GROUP):
+            columns = slice(head * HD, (head + 1) * HD)
+            kernel(
+                where_ref,
+                *[
+                    r.at[head : head + 1] if r.dtype == F32
+                    else r.at[..., columns]
+                    for r in refs
+                ],
+            )
+
+    return run
 
 
 def call(kernel, where, operands, in_specs, outs, out_specs, heads, keys, name):
     rows = outs[0].shape[-2]
     return pl.pallas_call(
-        kernel,
+        each_head(kernel),
         out_shape=outs,
         grid_spec=pltpu.PrefetchScalarGridSpec(
-            num_scalar_prefetch=1, grid=(heads,), in_specs=in_specs, out_specs=out_specs
+            num_scalar_prefetch=1, grid=(heads // GROUP,), in_specs=in_specs, out_specs=out_specs
         ),
-        compiler_params=pltpu.CompilerParams(vmem_limit_bytes=6 * 2**20),
+        compiler_params=pltpu.CompilerParams(vmem_limit_bytes=14 * 2**20),
         cost_estimate=pl.CostEstimate(
             flops=rows * keys, bytes_accessed=2**16, transcendentals=0
         ),
@@ -207,7 +224,7 @@
     row_out = jax.ShapeDtypeStruct((rows, width), BF16)
     stat_out = jax.ShapeDtypeStruct((heads, 2, rows), F32)
     back_out = jax.ShapeDtypeStruct((2, rows, width), BF16)
-    outs = [row_out, row_out, stat_out] + [back_out] * n_back
+    outs = [row_out, pltpu.HBM(row_out.shape, BF16), stat_out] + [back_out] * n_back
     return call(
         functools.partial(query_kernel, tuple(len(f) for f in fetched), n_back),
         where,
@@ -224,7 +241,7 @@
 def key_side(half, where, kv, qg, stat, later, later_stats):
     rows, width = kv.shape[1] // 2, kv.shape[2]
     heads = width // HD
-    half_of_whole = pl.BlockSpec((2, rows, HD), lambda h, w: (0, half, h))
+    half_of_whole = pl.BlockSpec((2, rows, GROUP * HD), lambda h, w: (0, half, h))
     far = [f[-1] if len(f) == 1 else f[half] for f in later[1:]]
     first, *far = [pltpu.with_memory_space_constraint(a, pltpu.HBM) for a in (*later[0], *far)]
     operands = [kv, qg, stat, first, *far, *later_stats]
@@ -251,33 +268,29 @@
     return result
 
 
-def norm_kernel(series_ref, gain_ref, grad_ref, sent_ref, inv_ref):
+def norm_kernel(series_ref, gain_ref, normed_ref, inv_ref):
     rows = series_ref[...].astype(F32)
     inv_rms = lax.rsqrt(jnp.mean(rows * rows, axis=-1, keepdims=True) + EPS)
     inv_ref[...] = inv_rms
-    sent_ref[0] = (rows * inv_rms * gain_ref[...]).astype(BF16)
-    sent_ref[1] = grad_ref[...]
-
-
-def normalize(series, gain, out_grad):
+    normed_ref[...] = (rows * inv_rms * gain_ref[...]).astype(BF16)
+
+
+def normalize(series, gain):
     rows, width = series.shape
-    step = rows // 4
+    step = rows // 2
     row_spec = pl.BlockSpec((step, width), lambda i: (i, 0))
     return pl.pallas_call(
         norm_kernel,
         out_shape=[
-            jax.ShapeDtypeStruct((2, rows, width), BF16),
+            jax.ShapeDtypeStruct((rows, width), BF16),
             jax.ShapeDtypeStruct((rows, 1), F32),
         ],
-        grid=(4,),
-        in_specs=[row_spec, pl.BlockSpec((1, width), lambda i: (0, 0)), row_spec],
-        out_specs=[
-            pl.BlockSpec((2, step, width), lambda i: (0, i, 0)),
-            pl.BlockSpec((step, 1), lambda i: (i, 0)),
-        ],
-        compiler_params=pltpu.CompilerParams(vmem_limit_bytes=6 * 2**20),
+        grid=(2,),
+        in_specs=[row_spec, pl.BlockSpec((1, width), lambda i: (0, 0))],
+        out_specs=[row_spec, pl.BlockSpec((step, 1), lambda i: (i, 0))],
+        compiler_params=pltpu.CompilerParams(vmem_limit_bytes=10 * 2**20),
         name="normalize",
-    )(series, gain[None], out_grad)
+    )(pltpu.with_memory_space_constraint(series, pltpu.HBM), gain[None])
 
 
 def matmul(a, b):
@@ -323,10 +336,9 @@
     seq_index = lax.axis_index("seq").astype(jnp.int32)
     where = jnp.stack([tp_index, seq_index * blocks])
     series_f = series.astype(F32)
-    sent, inv_rms = normalize(series, norm_gain, out_grad)
-    normed = sent[0]
+    normed, inv_rms = normalize(series, norm_gain)
     unit_rows = series_f * inv_rms
-    normed_other, out_grad_other = swap_tp(sent)
+    normed_other, out_grad_other = lax.optimization_barrier((swap_tp(normed), swap_tp(out_grad)))
 
     def key_value(rows):
         return jnp.stack([matmul(rows, w_key).astype(BF16), matmul(rows, w_value).astype(BF16)])
@@ -351,13 +363,11 @@
     attn_rows = matmul(mixed[:half], w_out) + attn_other.astype(F32)
     layer_out = (series_f + attn_rows).astype(BF16)
 
-    grad_queries = lax.optimization_barrier(matmul_t(grad_query, w_query))
-
     def back(at):
         grad_kv = key_side(at, where, kv_all, qg_all, stat, later, later_stats)
         rows = slice(at * half, (at + 1) * half)
         return (
-            grad_queries[rows]
+            matmul_t(grad_query[rows], w_query)
             + matmul_t(grad_kv[0], w_key)
             + matmul_t(grad_kv[1], w_value)
         )

time: 166 us -> 167 us (level)
  waiting for transfers between devices: 59.5 us -> 62.1 us
  local copies, waits for them, and re-layouts: 5.12 us -> 2.62 us
    ppermute x3 -> x4, waiting for transfers between devices: 23.4 us -> 25.9 us  [swap_tp(): return lax.ppermute(value, 'tp', [(0, 1), (1, 0)])]
    unnamed x44 -> x40, local copies, waits for them, and re-layouts: 5.12 us -> 2.62 us
    dot_general x7 -> x8, matrix products: 9.16 us -> 6.7 us  [matmul_t(): return lax.dot_general(a, b, NT, preferred_element_type=F32)]
    dot_general x8, matrix products: 6.37 us -> 8.79 us  [matmul(): return jnp.dot(a, b, preferred_element_type=F32)]
    ppermute x3 -> x4, starting transfers between devices: 8.69 us -> 9.14 us  [swap_tp(): return lax.ppermute(value, 'tp', [(0, 1), (1, 0)])]
  transfers between devices with their start and end apart: 24 -> 25, of which waited for: 7 -> 8; matrix products, arithmetic and copies ran while one was open for 7% -> 7% of each run, Pallas kernels for 7% -> 6%
where the time goes in v13:
time: 167 us; the launch traced here: 166 us
  starting transfers between devices  65.8 us (39%)
  waiting for transfers between devices  62.1 us (37%)
  Pallas kernels  15.9 us (10%)
  matrix products  15.5 us (9%)
  other arithmetic  2.74 us (2%)
  local copies, waits for them, and re-layouts  2.62 us (2%)
    ppermute x15, starting transfers between devices, shifted(): return lax.ppermute(value, 'seq', pairs)  53 us
    ppermute x15, waiting for transfers between devices, shifted(): return lax.ppermute(value, 'seq', pairs)  36.2 us
    ppermute x4, waiting for transfers between devices, swap_tp(): return lax.ppermute(value, 'tp', [(0, 1), (1, 0)])  25.9 us
    pallas_call x3, Pallas kernels, call(): pl.pallas_call(each_head(kernel), out_shape=outs, grid_spec=pltpu.Prefetc...  14.4 us
    ppermute x4, starting transfers between devices, swap_tp(): return lax.ppermute(value, 'tp', [(0, 1), (1, 0)])  9.14 us
    dot_general x8, matrix products, matmul(): return jnp.dot(a, b, preferred_element_type=F32)  8.79 us
    dot_general x8, matrix products, matmul_t(): return lax.dot_general(a, b, NT, preferred_element_type=F32)  6.7 us
    ppermute x6, starting transfers between devices, swapped(): return lax.ppermute(sent, 'seq', [(i, i ^ bit) for i in range(size)])  3.63 us
  transfers between devices with their start and end apart: 25, of which 8 were waited for; matrix products, arithmetic and copies ran while one was open for 7% of the time, Pallas kernels for 6%

profile of v13, /device:TPU:24, one launch (start us, length us, event | category | flops | bytes accessed | tf_op | source)
XLA Modules:
  0.0 165.9 jit_solution(5459152222855940141)
XLA Ops:
  0.7 0.8 copy-done.3
  1.5 1.5 normalize.1
  3.0 3.1 %collective-permute-start = (bf16[128,2048]{1,0:T(8,128)(2,1)S(1)}, bf16[128,2048]{1,0:T(8,128)(2,1)S(1)}, u32[]{:S(2)}, u32[]{:S(2)}) collective-permute-start(bf16[128,2048]{1,0:T(8,128)(2,1)S(1)} %get-tuple-element.27), channel_id=1, source_target_pairs={{0,1},{1,0},{2,3},{3,2},{4,5},{5,4},{6,7},{7,6},{8,9},{9,8},{10,11... | collective-permute-start | bytes 1572872 | tf_op jit(solution)/shard_map/ppermute | solution.py:30
  6.1 0.5 collective-permute-start.1
  6.6 2.0 %fusion.10 = bf16[1,128,512]{2,1,0:T(8,128)(2,1)S(1)} fusion(bf16[128,2048]{1,0:T(8,128)(2,1)S(1)} %get-tuple-element.27, bf16[2048,512]{1,0:T(8,128)(2,1)} %param.11), kind=kOutput, calls=%fused_computation.23 | convolution fusion | flops 268500992 | bytes 2752512 | tf_op jit(solution)/shard_map/dot_general | solution.py:297
  8.7 0.5 fusion.9
  9.2 0.8 fusion.14
  10.0 0.5 fusion.13
  10.5 8.9 %collective-permute-done = bf16[128,2048]{1,0:T(8,128)(2,1)S(1)} collective-permute-done((bf16[128,2048]{1,0:T(8,128)(2,1)S(1)}, bf16[128,2048]{1,0:T(8,128)(2,1)S(1)}, u32[]{:S(2)}, u32[]{:S(2)}) %collective-permute-start) | collective-permute-done | bytes 524320 | tf_op jit(solution)/shard_map/ppermute | solution.py:30
  19.4 10.1 %collective-permute-done.1 = bf16[128,2048]{1,0:T(8,128)(2,1)S(1)} collective-permute-done((bf16[128,2048]{1,0:T(8,128)(2,1)}, bf16[128,2048]{1,0:T(8,128)(2,1)S(1)}, u32[]{:S(2)}, u32[]{:S(2)}) %collective-permute-start.1) | collective-permute-done | bytes 524320 | tf_op jit(solution)/shard_map/ppermute | solution.py:30
  29.5 0.5 fusion.12
  30.0 0.5 fusion.11
  30.4 0.5 fusion.15
  30.9 0.8 fusion.16
  31.7 0.1 maximum_maximum_fusion
  31.8 3.8 %collective-permute-start.2 = (bf16[2,256,512]{2,1,0:T(8,128)(2,1)S(1)}, bf16[2,256,512]{2,1,0:T(8,128)(2,1)S(1)}, u32[]{:S(2)}, u32[]{:S(2)}) collective-permute-start(bf16[2,256,512]{2,1,0:T(8,128)(2,1)S(1)} %get-tuple-element.33.refs_1_.refs_0_), channel_id=1, source_target_pairs={{0,4},{2,6},{4,8},{6,10},{8,12},{10,14},{12,16},{14,18},{16,20},{1... | collective-permute-start | bytes 1572872 | tf_op jit(solution)/shard_map/ppermute | solution.py:26
  35.7 7.0 %collective-permute-start.9 = (bf16[2,256,512]{2,1,0:T(8,128)(2,1)S(1)}, bf16[2,256,512]{2,1,0:T(8,128)(2,1)}, u32[]{:S(2)}, u32[]{:S(2)}) collective-permute-start(bf16[2,256,512]{2,1,0:T(8,128)(2,1)S(1)} %get-tuple-element.37.refs_0_.refs_1_), channel_id=1, source_target_pairs={{4,0},{6,2},{8,4},{10,6},{12,8},{14,10},{16,12},{18,14},{20,16},{2... | collective-permute-start | bytes 1572872 | tf_op jit(solution)/shard_map/ppermute | solution.py:26
  42.6 9.1 %collective-permute-done.2.refs_3_ = bf16[2,256,512]{2,1,0:T(8,128)(2,1)S(1)} collective-permute-done((bf16[2,256,512]{2,1,0:T(8,128)(2,1)S(1)}, bf16[2,256,512]{2,1,0:T(8,128)(2,1)S(1)}, u32[]{:S(2)}, u32[]{:S(2)}) %collective-permute-start.2) | collective-permute-done | bytes 524320 | tf_op jit(solution)/shard_map/ppermute | solution.py:26
  51.7 1.9 %collective-permute-start.3 = (bf16[2,256,512]{2,1,0:T(8,128)(2,1)S(1)}, bf16[2,256,512]{2,1,0:T(8,128)(2,1)}, u32[]{:S(2)}, u32[]{:S(2)}) collective-permute-start(bf16[2,256,512]{2,1,0:T(8,128)(2,1)S(1)} %collective-permute-done.2.refs_3_), channel_id=1, source_target_pairs={{0,4},{2,6},{4,8},{6,10},{8,12},{10,14},{12,16},{14,18},{16,20},{1... | collective-permute-start | bytes 1572872 | tf_op jit(solution)/shard_map/ppermute | solution.py:26
  53.7 1.3 collective-permute-start.6
  55.0 7.6 %collective-permute-start.10 = (bf16[2,256,512]{2,1,0:T(8,128)(2,1)}, bf16[2,256,512]{2,1,0:T(8,128)(2,1)}, u32[]{:S(2)}, u32[]{:S(2)}) collective-permute-start(bf16[2,256,512]{2,1,0:T(8,128)(2,1)} %collective-permute-done.9.refs_4_), channel_id=1, source_target_pairs={{4,0},{6,2},{8,4},{10,6},{12,8},{14,10},{16,12},{18,14},{20,16},{2... | collective-permute-start | bytes 1572872 | tf_op jit(solution)/shard_map/ppermute | solution.py:26
  62.5 6.5 %collective-permute-done.3.refs_4_ = bf16[2,256,512]{2,1,0:T(8,128)(2,1)} collective-permute-done((bf16[2,256,512]{2,1,0:T(8,128)(2,1)S(1)}, bf16[2,256,512]{2,1,0:T(8,128)(2,1)}, u32[]{:S(2)}, u32[]{:S(2)}) %collective-permute-start.3) | collective-permute-done | bytes 524320 | tf_op jit(solution)/shard_map/ppermute | solution.py:26
  69.0 1.9 %collective-permute-start.4 = (bf16[2,256,512]{2,1,0:T(8,128)(2,1)}, bf16[2,256,512]{2,1,0:T(8,128)(2,1)}, u32[]{:S(2)}, u32[]{:S(2)}) collective-permute-start(bf16[2,256,512]{2,1,0:T(8,128)(2,1)} %collective-permute-done.3.refs_4_), channel_id=1, source_target_pairs={{0,8},{2,10},{4,12},{6,14},{8,16},{10,18},{12,20},{14,22},{16,24},... | collective-permute-start | bytes 1572872 | tf_op jit(solution)/shard_map/ppermute | solution.py:26
  71.0 0.1 pad_add_fusion.where_ref
  71.0 2.4 %collective-permute-start.13 = (bf16[2,256,512]{2,1,0:T(8,128)(2,1)S(1)}, bf16[2,256,512]{2,1,0:T(8,128)(2,1)S(1)}, u32[]{:S(2)}, u32[]{:S(2)}) collective-permute-start(bf16[2,256,512]{2,1,0:T(8,128)(2,1)S(1)} %get-tuple-element.37.refs_0_.refs_1_), channel_id=1, source_target_pairs={{64,0},{66,2},{68,4},{70,6},{72,8},{74,10},{76,12},{78,14},{80,16}... | collective-permute-start | bytes 1572872 | tf_op jit(solution)/shard_map/ppermute | solution.py:26
  73.4 7.1 %collective-permute-done.6.refs_7_ = bf16[2,256,512]{2,1,0:T(8,128)(2,1)} collective-permute-done((bf16[2,256,512]{2,1,0:T(8,128)(2,1)S(1)}, bf16[2,256,512]{2,1,0:T(8,128)(2,1)}, u32[]{:S(2)}, u32[]{:S(2)}) %collective-permute-start.6) | collective-permute-done | bytes 524320 | tf_op jit(solution)/shard_map/ppermute | solution.py:26
  80.5 0.1 broadcast_select_fusion.1
  80.6 0.1 collective-permute-start.7
  80.7 1.4 collective-permute-start.8
  82.1 4.0 %collective-permute-start.11 = (bf16[2,256,512]{2,1,0:T(8,128)(2,1)}, bf16[2,256,512]{2,1,0:T(8,128)(2,1)S(1)}, u32[]{:S(2)}, u32[]{:S(2)}) collective-permute-start(bf16[2,256,512]{2,1,0:T(8,128)(2,1)} %collective-permute-done.10.refs_5_), channel_id=1, source_target_pairs={{8,0},{10,2},{12,4},{14,6},{16,8},{18,10},{20,12},{22,14},{24,16},... | collective-permute-start | bytes 1572872 | tf_op jit(solution)/shard_map/ppermute | solution.py:26
  86.1 8.8 %collective-permute-done.4.refs_5_ = bf16[2,256,512]{2,1,0:T(8,128)(2,1)} collective-permute-done((bf16[2,256,512]{2,1,0:T(8,128)(2,1)}, bf16[2,256,512]{2,1,0:T(8,128)(2,1)}, u32[]{:S(2)}, u32[]{:S(2)}) %collective-permute-start.4) | collective-permute-done | bytes 524320 | tf_op jit(solution)/shard_map/ppermute | solution.py:26
  94.9 0.1 broadcast_select_fusion.3
  95.0 0.1 collective-permute-start.5
  95.2 0.2 collective-permute-start.14
  95.4 4.7 %collective-permute-done.11.refs_6_ = bf16[2,256,512]{2,1,0:T(8,128)(2,1)S(1)} collective-permute-done((bf16[2,256,512]{2,1,0:T(8,128)(2,1)}, bf16[2,256,512]{2,1,0:T(8,128)(2,1)S(1)}, u32[]{:S(2)}, u32[]{:S(2)}) %collective-permute-start.11) | collective-permute-done | bytes 524320 | tf_op jit(solution)/shard_map/ppermute | solution.py:26
  100.1 4.3 %collective-permute-start.15 = (bf16[2,256,512]{2,1,0:T(8,128)(2,1)S(1)}, bf16[2,256,512]{2,1,0:T(8,128)(2,1)S(1)}, u32[]{:S(2)}, u32[]{:S(2)}) collective-permute-start(bf16[2,256,512]{2,1,0:T(8,128)(2,1)S(1)} %collective-permute-done.13.refs_8_), channel_id=1, source_target_pairs={{64,0},{66,2},{68,4},{70,6},{72,8},{74,10},{76,12},{78,14},{80,16}... | collective-permute-start | bytes 1572872 | tf_op jit(solution)/shard_map/ppermute | solution.py:26
  104.4 1.1 broadcast_select_fusion.2
  105.5 0.1 collective-permute-start.12
  105.7 6.4 %query_side.1 = (bf16[256,512]{1,0:T(8,128)(2,1)S(1)}, bf16[256,512]{1,0:T(8,128)(2,1)}, f32[4,2,256]{2,1,0:T(2,128)S(1)}) custom-call(s32[2]{0:T(128)S(1)} %pad_add_fusion.where_ref, bf16[2,256,512]{2,1,0:T(8,128)(2,1)S(1)} %get-tuple-element.37.refs_0_.refs_1_, bf16[2,256,512]{2,1,0:T(8,128)(2,1)S(1)} %get-tuple-element.33.refs_1_.refs_0_, ...), custom_call_target="tpu_custom_call" | custom-call | flops 163840 | bytes 65536 | tf_op jit(solution)/shard_map/query_side/pallas_call | solution.py:205
  112.1 1.3 convolution_convert_fusion
  113.4 2.7 %collective-permute-start.17 = (bf16[128,2048]{1,0:T(8,128)(2,1)}, bf16[128,2048]{1,0:T(8,128)(2,1)}, u32[]{:S(2)}, u32[]{:S(2)}) collective-permute-start(bf16[128,2048]{1,0:T(8,128)(2,1)} %convolution_convert_fusion), channel_id=1, source_target_pairs={{0,1},{1,0},{2,3},{3,2},{4,5},{5,4},{6,7},{7,6},{8,9},{9,8},{10,11... | collective-permute-start | bytes 1572872 | tf_op jit(solution)/shard_map/ppermute | solution.py:30
  116.1 0.8 copy-done.16
  116.9 7.3 %collective-permute-start.16 = (f32[4,2,256]{2,1,0:T(2,128)S(1)}, f32[4,2,256]{2,1,0:T(2,128)S(1)}, u32[]{:S(2)}, u32[]{:S(2)}) collective-permute-start(f32[4,2,256]{2,1,0:T(2,128)S(1)} %get-tuple-element.40.refs_2_), channel_id=1, source_target_pairs={{4,0},{6,2},{8,4},{10,6},{12,8},{14,10},{16,12},{18,14},{20,16},{2... | collective-permute-start | bytes 24584 | tf_op jit(solution)/shard_map/ppermute | solution.py:26
  124.3 2.4 %collective-permute-start.21 = (f32[4,2,256]{2,1,0:T(2,128)S(1)}, f32[4,2,256]{2,1,0:T(2,128)S(1)}, u32[]{:S(2)}, u32[]{:S(2)}) collective-permute-start(f32[4,2,256]{2,1,0:T(2,128)S(1)} %get-tuple-element.40.refs_2_), channel_id=1, source_target_pairs={{64,0},{66,2},{68,4},{70,6},{72,8},{74,10},{76,12},{78,14},{80,16}... | collective-permute-start | bytes 24584 | tf_op jit(solution)/shard_map/ppermute | solution.py:26
  126.7 0.1 reduce
  126.8 2.6 %collective-permute-start.19 = (f32[4,2,256]{2,1,0:T(2,128)S(1)}, f32[4,2,256]{2,1,0:T(2,128)S(1)}, u32[]{:S(2)}, u32[]{:S(2)}) collective-permute-start(f32[4,2,256]{2,1,0:T(2,128)S(1)} %get-tuple-element.40.refs_2_), channel_id=1, source_target_pairs={{8,0},{10,2},{12,4},{14,6},{16,8},{18,10},{20,12},{22,14},{24,16},... | collective-permute-start | bytes 24584 | tf_op jit(solution)/shard_map/ppermute | solution.py:26
  129.4 3.3 %collective-permute-start.20 = (f32[4,2,256]{2,1,0:T(2,128)S(1)}, f32[4,2,256]{2,1,0:T(2,128)S(1)}, u32[]{:S(2)}, u32[]{:S(2)}) collective-permute-start(f32[4,2,256]{2,1,0:T(2,128)S(1)} %get-tuple-element.40.refs_2_), channel_id=1, source_target_pairs={{16,0},{18,2},{20,4},{22,6},{24,8},{26,10},{28,12},{30,14},{32,16}... | collective-permute-start | bytes 24584 | tf_op jit(solution)/shard_map/ppermute | solution.py:26
  132.7 1.8 %collective-permute-start.23 = (f32[4,2,256]{2,1,0:T(2,128)S(1)}, f32[4,2,256]{2,1,0:T(2,128)S(1)}, u32[]{:S(2)}, u32[]{:S(2)}) collective-permute-start(f32[4,2,256]{2,1,0:T(2,128)S(1)} %get-tuple-element.40.refs_2_), channel_id=1, source_target_pairs={{128,0},{130,2},{132,4},{134,6},{136,8},{138,10},{140,12},{142,14}... | collective-permute-start | bytes 24584 | tf_op jit(solution)/shard_map/ppermute | solution.py:26
  134.6 0.1 collective-permute-start.18
  134.7 3.0 %collective-permute-start.22 = (f32[4,2,256]{2,1,0:T(2,128)S(1)}, f32[4,2,256]{2,1,0:T(2,128)S(1)}, u32[]{:S(2)}, u32[]{:S(2)}) collective-permute-start(f32[4,2,256]{2,1,0:T(2,128)S(1)} %bitcast.64), channel_id=1, source_target_pairs={{0,32},{2,34},{4,36},{6,38},{8,40},{10,42},{12,44},{14,46},{16,48}... | collective-permute-start | bytes 24584 | tf_op jit(solution)/shard_map/ppermute | solution.py:308
  137.8 3.2 %fusion.5 = bf16[128,2048]{1,0:T(8,128)(2,1)} fusion(bf16[512,2048]{1,0:T(8,128)(2,1)} %param.12, bf16[128,2048]{1,0:T(8,128)(2,1)} %series_ref.1, bf16[128,2048]{1,0:T(8,128)(2,1)} %collective-permute-done.17, bf16[256,512]{1,0:T(8,128)(2,1)S(1)} %get-tuple-element.35), kind=kOutput, calls=%fused_computation.8 | convolution fusion | flops 269746176 | bytes 3801088 | tf_op jit(solution)/shard_map/dot_general | solution.py:297
  141.0 4.0 %key_side.3 = bf16[2,128,512]{2,1,0:T(8,128)(2,1)S(1)} custom-call(s32[2]{0:T(128)S(1)} %pad_add_fusion.where_ref, bf16[2,256,512]{2,1,0:T(8,128)(2,1)S(1)} %get-tuple-element.33.refs_1_.refs_0_, bf16[2,256,512]{2,1,0:T(8,128)(2,1)S(1)} %get-tuple-element.37.refs_0_.refs_1_, f32[4,2,256]{2,1,0:T(2,128)S(1)} %get-tuple-element.40.refs_2_, ...), custom_call_target="tpu_custom_call" | custom-call | flops 81920 | bytes 65536 | tf_op jit(solution)/shard_map/key_side/pallas_call | solution.py:205
  145.0 0.8 fusion.22
  145.8 0.8 copy-done.10
  146.6 0.8 fusion.23
  147.4 0.1 copy-done.19
  147.5 0.8 fusion.6
  148.4 2.8 %collective-permute-start.24 = (bf16[128,2048]{1,0:T(8,128)(2,1)S(1)}, bf16[128,2048]{1,0:T(8,128)(2,1)S(1)}, u32[]{:S(2)}, u32[]{:S(2)}) collective-permute-start(bf16[128,2048]{1,0:T(8,128)(2,1)S(1)} %fusion.6), channel_id=1, source_target_pairs={{0,1},{1,0},{2,3},{3,2},{4,5},{5,4},{6,7},{7,6},{8,9},{9,8},{10,11... | collective-permute-start | bytes 1572872 | tf_op jit(solution)/shard_map/ppermute | solution.py:30
  151.2 4.0 %key_side.2 = bf16[2,128,512]{2,1,0:T(8,128)(2,1)S(1)} custom-call(s32[2]{0:T(128)S(1)} %pad_add_fusion.where_ref, bf16[2,256,512]{2,1,0:T(8,128)(2,1)S(1)} %get-tuple-element.33.refs_1_.refs_0_, bf16[2,256,512]{2,1,0:T(8,128)(2,1)S(1)} %get-tuple-element.37.refs_0_.refs_1_, f32[4,2,256]{2,1,0:T(2,128)S(1)} %get-tuple-element.40.refs_2_, ...), custom_call_target="tpu_custom_call" | custom-call | flops 81920 | bytes 65536 | tf_op jit(solution)/shard_map/key_side/pallas_call | solution.py:205
  155.1 0.8 fusion.24
  156.0 0.8 fusion.25
  156.8 6.9 %collective-permute-done.24 = bf16[128,2048]{1,0:T(8,128)(2,1)S(1)} collective-permute-done((bf16[128,2048]{1,0:T(8,128)(2,1)S(1)}, bf16[128,2048]{1,0:T(8,128)(2,1)S(1)}, u32[]{:S(2)}, u32[]{:S(2)}) %collective-permute-start.24) | collective-permute-done | bytes 524320 | tf_op jit(solution)/shard_map/ppermute | solution.py:30
  163.7 1.0 fusion.17
  164.7 1.2 fusion.21
  (56 shorter events, 0.2 us)
Async XLA Ops:
  0.6 9.4 %copy-start = (bf16[2048,512]{1,0:T(8,128)(2,1)S(1)}, bf16[2048,512]{1,0:T(8,128)(2,1)}, u32[]{:S(2)}) copy-start(bf16[2048,512]{1,0:T(8,128)(2,1)} %param.9) | copy-start | bytes 6291460
  0.6 0.8 copy-start.3
  1.5 7.2 %copy-start.9 = (bf16[2048,512]{1,0:T(8,128)(2,1)S(1)}, bf16[2048,512]{1,0:T(8,128)(2,1)}, u32[]{:S(2)}) copy-start(bf16[2048,512]{1,0:T(8,128)(2,1)} %param.10) | copy-start | bytes 6291460
  3.0 6.2 %copy-start.5 = (bf16[512,2048]{1,0:T(8,128)(2,1)S(1)}, bf16[512,2048]{1,0:T(8,128)(2,1)}, u32[]{:S(2)}) copy-start(bf16[512,2048]{1,0:T(8,128)(2,1)} %param.12) | copy-start | bytes 6291460
  3.0 6.2 %copy-start.13 = (bf16[128,2048]{1,0:T(8,128)(2,1)S(1)}, bf16[128,2048]{1,0:T(8,128)(2,1)}, u32[]{:S(2)}) copy-start(bf16[128,2048]{1,0:T(8,128)(2,1)} %param.13) | copy-start | bytes 1572868
  3.0 16.4 %collective-permute-start = (bf16[128,2048]{1,0:T(8,128)(2,1)S(1)}, bf16[128,2048]{1,0:T(8,128)(2,1)S(1)}, u32[]{:S(2)}, u32[]{:S(2)}) collective-permute-start(bf16[128,2048]{1,0:T(8,128)(2,1)S(1)} %get-tuple-element.27), channel_id=1, source_target_pairs={{0,1},{1,0},{2,3},{3,2},{4,5},{5,4},{6,7},{7,6},{8,9},{9,8},{10,11... | collective-permute-start | bytes 1572872 | tf_op jit(solution)/shard_map/ppermute | solution.py:30
  6.1 23.4 %collective-permute-start.1 = (bf16[128,2048]{1,0:T(8,128)(2,1)}, bf16[128,2048]{1,0:T(8,128)(2,1)S(1)}, u32[]{:S(2)}, u32[]{:S(2)}) collective-permute-start(bf16[128,2048]{1,0:T(8,128)(2,1)} %param.13), channel_id=1, source_target_pairs={{0,1},{1,0},{2,3},{3,2},{4,5},{5,4},{6,7},{7,6},{8,9},{9,8},{10,11... | collective-permute-start | bytes 1572872 | tf_op jit(solution)/shard_map/ppermute | solution.py:30
  9.2 20.3 %copy-start.7 = (bf16[2048,512]{1,0:T(8,128)(2,1)S(1)}, bf16[2048,512]{1,0:T(8,128)(2,1)}, u32[]{:S(2)}) copy-start(bf16[2048,512]{1,0:T(8,128)(2,1)} %param.11) | copy-start | bytes 6291460
  31.8 19.9 %collective-permute-start.2 = (bf16[2,256,512]{2,1,0:T(8,128)(2,1)S(1)}, bf16[2,256,512]{2,1,0:T(8,128)(2,1)S(1)}, u32[]{:S(2)}, u32[]{:S(2)}) collective-permute-start(bf16[2,256,512]{2,1,0:T(8,128)(2,1)S(1)} %get-tuple-element.33.refs_1_.refs_0_), channel_id=1, source_target_pairs={{0,4},{2,6},{4,8},{6,10},{8,12},{10,14},{12,16},{14,18},{16,20},{1... | collective-permute-start | bytes 1572872 | tf_op jit(solution)/shard_map/ppermute | solution.py:26
  35.7 19.3 %collective-permute-start.9 = (bf16[2,256,512]{2,1,0:T(8,128)(2,1)S(1)}, bf16[2,256,512]{2,1,0:T(8,128)(2,1)}, u32[]{:S(2)}, u32[]{:S(2)}) collective-permute-start(bf16[2,256,512]{2,1,0:T(8,128)(2,1)S(1)} %get-tuple-element.37.refs_0_.refs_1_), channel_id=1, source_target_pairs={{4,0},{6,2},{8,4},{10,6},{12,8},{14,10},{16,12},{18,14},{20,16},{2... | collective-permute-start | bytes 1572872 | tf_op jit(solution)/shard_map/ppermute | solution.py:26
  51.7 3.2 %copy-start.1 = (bf16[2,256,512]{2,1,0:T(8,128)(2,1)}, bf16[2,256,512]{2,1,0:T(8,128)(2,1)S(1)}, u32[]{:S(2)}) copy-start(bf16[2,256,512]{2,1,0:T(8,128)(2,1)S(1)} %collective-permute-done.2.refs_3_) | copy-start | bytes 1572868
  51.7 17.3 %collective-permute-start.3 = (bf16[2,256,512]{2,1,0:T(8,128)(2,1)S(1)}, bf16[2,256,512]{2,1,0:T(8,128)(2,1)}, u32[]{:S(2)}, u32[]{:S(2)}) collective-permute-start(bf16[2,256,512]{2,1,0:T(8,128)(2,1)S(1)} %collective-permute-done.2.refs_3_), channel_id=1, source_target_pairs={{0,4},{2,6},{4,8},{6,10},{8,12},{10,14},{12,16},{14,18},{16,20},{1... | collective-permute-start | bytes 1572872 | tf_op jit(solution)/shard_map/ppermute | solution.py:26
  53.7 26.8 %collective-permute-start.6 = (bf16[2,256,512]{2,1,0:T(8,128)(2,1)S(1)}, bf16[2,256,512]{2,1,0:T(8,128)(2,1)}, u32[]{:S(2)}, u32[]{:S(2)}) collective-permute-start(bf16[2,256,512]{2,1,0:T(8,128)(2,1)S(1)} %get-tuple-element.33.refs_1_.refs_0_), channel_id=1, source_target_pairs={{0,64},{2,66},{4,68},{6,70},{8,72},{10,74},{12,76},{14,78},{16,80}... | collective-permute-start | bytes 1572872 | tf_op jit(solution)/shard_map/ppermute | solution.py:26
  55.0 27.1 %collective-permute-start.10 = (bf16[2,256,512]{2,1,0:T(8,128)(2,1)}, bf16[2,256,512]{2,1,0:T(8,128)(2,1)}, u32[]{:S(2)}, u32[]{:S(2)}) collective-permute-start(bf16[2,256,512]{2,1,0:T(8,128)(2,1)} %collective-permute-done.9.refs_4_), channel_id=1, source_target_pairs={{4,0},{6,2},{8,4},{10,6},{12,8},{14,10},{16,12},{18,14},{20,16},{2... | collective-permute-start | bytes 1572872 | tf_op jit(solution)/shard_map/ppermute | solution.py:26
  69.0 25.9 %collective-permute-start.4 = (bf16[2,256,512]{2,1,0:T(8,128)(2,1)}, bf16[2,256,512]{2,1,0:T(8,128)(2,1)}, u32[]{:S(2)}, u32[]{:S(2)}) collective-permute-start(bf16[2,256,512]{2,1,0:T(8,128)(2,1)} %collective-permute-done.3.refs_4_), channel_id=1, source_target_pairs={{0,8},{2,10},{4,12},{6,14},{8,16},{10,18},{12,20},{14,22},{16,24},... | collective-permute-start | bytes 1572872 | tf_op jit(solution)/shard_map/ppermute | solution.py:26
  71.0 24.0 %collective-permute-start.13 = (bf16[2,256,512]{2,1,0:T(8,128)(2,1)S(1)}, bf16[2,256,512]{2,1,0:T(8,128)(2,1)S(1)}, u32[]{:S(2)}, u32[]{:S(2)}) collective-permute-start(bf16[2,256,512]{2,1,0:T(8,128)(2,1)S(1)} %get-tuple-element.37.refs_0_.refs_1_), channel_id=1, source_target_pairs={{64,0},{66,2},{68,4},{70,6},{72,8},{74,10},{76,12},{78,14},{80,16}... | collective-permute-start | bytes 1572872 | tf_op jit(solution)/shard_map/ppermute | solution.py:26
  80.6 25.1 %copy-start.2 = (bf16[2,256,512]{2,1,0:T(8,128)(2,1)S(1)}, bf16[2,256,512]{2,1,0:T(8,128)(2,1)}, u32[]{:S(2)}) copy-start(bf16[2,256,512]{2,1,0:T(8,128)(2,1)} %copy-done.1) | copy-start | bytes 1572868
  80.6 24.9 %collective-permute-start.7 = (bf16[2,256,512]{2,1,0:T(8,128)(2,1)S(1)}, bf16[2,256,512]{2,1,0:T(8,128)(2,1)S(1)}, u32[]{:S(2)}, u32[]{:S(2)}) collective-permute-start(bf16[2,256,512]{2,1,0:T(8,128)(2,1)S(1)} %broadcast_select_fusion.1), channel_id=1, source_target_pairs={{0,32},{2,34},{4,36},{6,38},{8,40},{10,42},{12,44},{14,46},{16,48}... | collective-permute-start | bytes 1572872 | tf_op jit(solution)/shard_map/ppermute | solution.py:308
  80.7 25.0 %collective-permute-start.8 = (bf16[2,256,512]{2,1,0:T(8,128)(2,1)}, bf16[2,256,512]{2,1,0:T(8,128)(2,1)S(1)}, u32[]{:S(2)}, u32[]{:S(2)}) collective-permute-start(bf16[2,256,512]{2,1,0:T(8,128)(2,1)} %collective-permute-done.6.refs_7_), channel_id=1, source_target_pairs={{0,64},{2,66},{4,68},{6,70},{8,72},{10,74},{12,76},{14,78},{16,80}... | collective-permute-start | bytes 1572872 | tf_op jit(solution)/shard_map/ppermute | solution.py:26
  82.1 18.0 %collective-permute-start.11 = (bf16[2,256,512]{2,1,0:T(8,128)(2,1)}, bf16[2,256,512]{2,1,0:T(8,128)(2,1)S(1)}, u32[]{:S(2)}, u32[]{:S(2)}) collective-permute-start(bf16[2,256,512]{2,1,0:T(8,128)(2,1)} %collective-permute-done.10.refs_5_), channel_id=1, source_target_pairs={{8,0},{10,2},{12,4},{14,6},{16,8},{18,10},{20,12},{22,14},{24,16},... | collective-permute-start | bytes 1572872 | tf_op jit(solution)/shard_map/ppermute | solution.py:26
  95.0 10.7 %collective-permute-start.5 = (bf16[2,256,512]{2,1,0:T(8,128)(2,1)S(1)}, bf16[2,256,512]{2,1,0:T(8,128)(2,1)S(1)}, u32[]{:S(2)}, u32[]{:S(2)}) collective-permute-start(bf16[2,256,512]{2,1,0:T(8,128)(2,1)S(1)} %broadcast_select_fusion.3), channel_id=1, source_target_pairs={{0,2},{2,0},{4,6},{6,4},{8,10},{10,8},{12,14},{14,12},{16,18},{18,... | collective-permute-start | bytes 1572872 | tf_op jit(solution)/shard_map/ppermute | solution.py:308
  95.1 17.0 %copy-start.12 = (bf16[2,256,512]{2,1,0:T(8,128)(2,1)}, bf16[2,256,512]{2,1,0:T(8,128)(2,1)S(1)}, u32[]{:S(2)}) copy-start(bf16[2,256,512]{2,1,0:T(8,128)(2,1)S(1)} %collective-permute-done.13.refs_8_) | copy-start | bytes 1572868
  95.2 20.9 %collective-permute-start.14 = (bf16[2,256,512]{2,1,0:T(8,128)(2,1)S(1)}, bf16[2,256,512]{2,1,0:T(8,128)(2,1)S(1)}, u32[]{:S(2)}, u32[]{:S(2)}) collective-permute-start(bf16[2,256,512]{2,1,0:T(8,128)(2,1)S(1)} %broadcast_select_fusion), channel_id=1, source_target_pairs={{0,32},{2,34},{4,36},{6,38},{8,40},{10,42},{12,44},{14,46},{16,48}... | collective-permute-start | bytes 1572872 | tf_op jit(solution)/shard_map/ppermute | solution.py:308
  100.1 4.3 %copy-start.15 = (bf16[2,256,512]{2,1,0:T(8,128)(2,1)}, bf16[2,256,512]{2,1,0:T(8,128)(2,1)S(1)}, u32[]{:S(2)}) copy-start(bf16[2,256,512]{2,1,0:T(8,128)(2,1)S(1)} %collective-permute-done.11.refs_6_) | copy-start | bytes 1572868
  100.1 16.0 %collective-permute-start.15 = (bf16[2,256,512]{2,1,0:T(8,128)(2,1)S(1)}, bf16[2,256,512]{2,1,0:T(8,128)(2,1)S(1)}, u32[]{:S(2)}, u32[]{:S(2)}) collective-permute-start(bf16[2,256,512]{2,1,0:T(8,128)(2,1)S(1)} %collective-permute-done.13.refs_8_), channel_id=1, source_target_pairs={{64,0},{66,2},{68,4},{70,6},{72,8},{74,10},{76,12},{78,14},{80,16}... | collective-permute-start | bytes 1572872 | tf_op jit(solution)/shard_map/ppermute | solution.py:26
  105.5 6.6 %copy-start.6 = (bf16[512,2048]{1,0:T(8,128)(2,1)S(1)}, bf16[512,2048]{1,0:T(8,128)(2,1)}, u32[]{:S(2)}) copy-start(bf16[512,2048]{1,0:T(8,128)(2,1)} %param.12) | copy-start | bytes 6291460
  105.5 10.6 %collective-permute-start.12 = (bf16[2,256,512]{2,1,0:T(8,128)(2,1)S(1)}, bf16[2,256,512]{2,1,0:T(8,128)(2,1)S(1)}, u32[]{:S(2)}, u32[]{:S(2)}) collective-permute-start(bf16[2,256,512]{2,1,0:T(8,128)(2,1)S(1)} %broadcast_select_fusion.2), channel_id=1, source_target_pairs={{0,2},{2,0},{4,6},{6,4},{8,10},{10,8},{12,14},{14,12},{16,18},{18,... | collective-permute-start | bytes 1572872 | tf_op jit(solution)/shard_map/ppermute | solution.py:308
  113.4 21.2 %collective-permute-start.17 = (bf16[128,2048]{1,0:T(8,128)(2,1)}, bf16[128,2048]{1,0:T(8,128)(2,1)}, u32[]{:S(2)}, u32[]{:S(2)}) collective-permute-start(bf16[128,2048]{1,0:T(8,128)(2,1)} %convolution_convert_fusion), channel_id=1, source_target_pairs={{0,1},{1,0},{2,3},{3,2},{4,5},{5,4},{6,7},{7,6},{8,9},{9,8},{10,11... | collective-permute-start | bytes 1572872 | tf_op jit(solution)/shard_map/ppermute | solution.py:30
  116.1 0.8 copy-start.16
  116.1 8.2 %copy-start.17 = (bf16[2,256,512]{2,1,0:T(8,128)(2,1)}, bf16[2,256,512]{2,1,0:T(8,128)(2,1)S(1)}, u32[]{:S(2)}) copy-start(bf16[2,256,512]{2,1,0:T(8,128)(2,1)S(1)} %collective-permute-done.15.refs_9_) | copy-start | bytes 1572868
  116.1 10.5 %copy-start.18 = (bf16[2,256,512]{2,1,0:T(8,128)(2,1)}, bf16[2,256,512]{2,1,0:T(8,128)(2,1)S(1)}, u32[]{:S(2)}) copy-start(bf16[2,256,512]{2,1,0:T(8,128)(2,1)S(1)} %collective-permute-done.12.refs_3_) | copy-start | bytes 1572868
  116.9 15.8 %collective-permute-start.16 = (f32[4,2,256]{2,1,0:T(2,128)S(1)}, f32[4,2,256]{2,1,0:T(2,128)S(1)}, u32[]{:S(2)}, u32[]{:S(2)}) collective-permute-start(f32[4,2,256]{2,1,0:T(2,128)S(1)} %get-tuple-element.40.refs_2_), channel_id=1, source_target_pairs={{4,0},{6,2},{8,4},{10,6},{12,8},{14,10},{16,12},{18,14},{20,16},{2... | collective-permute-start | bytes 24584 | tf_op jit(solution)/shard_map/ppermute | solution.py:26
  124.3 10.3 %collective-permute-start.21 = (f32[4,2,256]{2,1,0:T(2,128)S(1)}, f32[4,2,256]{2,1,0:T(2,128)S(1)}, u32[]{:S(2)}, u32[]{:S(2)}) collective-permute-start(f32[4,2,256]{2,1,0:T(2,128)S(1)} %get-tuple-element.40.refs_2_), channel_id=1, source_target_pairs={{64,0},{66,2},{68,4},{70,6},{72,8},{74,10},{76,12},{78,14},{80,16}... | collective-permute-start | bytes 24584 | tf_op jit(solution)/shard_map/ppermute | solution.py:26
  126.8 14.2 %collective-permute-start.19 = (f32[4,2,256]{2,1,0:T(2,128)S(1)}, f32[4,2,256]{2,1,0:T(2,128)S(1)}, u32[]{:S(2)}, u32[]{:S(2)}) collective-permute-start(f32[4,2,256]{2,1,0:T(2,128)S(1)} %get-tuple-element.40.refs_2_), channel_id=1, source_target_pairs={{8,0},{10,2},{12,4},{14,6},{16,8},{18,10},{20,12},{22,14},{24,16},... | collective-permute-start | bytes 24584 | tf_op jit(solution)/shard_map/ppermute | solution.py:26
  129.4 11.5 %collective-permute-start.20 = (f32[4,2,256]{2,1,0:T(2,128)S(1)}, f32[4,2,256]{2,1,0:T(2,128)S(1)}, u32[]{:S(2)}, u32[]{:S(2)}) collective-permute-start(f32[4,2,256]{2,1,0:T(2,128)S(1)} %get-tuple-element.40.refs_2_), channel_id=1, source_target_pairs={{16,0},{18,2},{20,4},{22,6},{24,8},{26,10},{28,12},{30,14},{32,16}... | collective-permute-start | bytes 24584 | tf_op jit(solution)/shard_map/ppermute | solution.py:26
  132.7 8.2 %collective-permute-start.23 = (f32[4,2,256]{2,1,0:T(2,128)S(1)}, f32[4,2,256]{2,1,0:T(2,128)S(1)}, u32[]{:S(2)}, u32[]{:S(2)}) collective-permute-start(f32[4,2,256]{2,1,0:T(2,128)S(1)} %get-tuple-element.40.refs_2_), channel_id=1, source_target_pairs={{128,0},{130,2},{132,4},{134,6},{136,8},{138,10},{140,12},{142,14}... | collective-permute-start | bytes 24584 | tf_op jit(solution)/shard_map/ppermute | solution.py:26
  134.6 6.3 %collective-permute-start.18 = (f32[4,2,256]{2,1,0:T(2,128)S(1)}, f32[4,2,256]{2,1,0:T(2,128)S(1)}, u32[]{:S(2)}, u32[]{:S(2)}) collective-permute-start(f32[4,2,256]{2,1,0:T(2,128)S(1)} %bitcast.65), channel_id=1, source_target_pairs={{0,2},{2,0},{4,6},{6,4},{8,10},{10,8},{12,14},{14,12},{16,18},{18,... | collective-permute-start | bytes 24584 | tf_op jit(solution)/shard_map/ppermute | solution.py:308
  134.7 6.2 %collective-permute-start.22 = (f32[4,2,256]{2,1,0:T(2,128)S(1)}, f32[4,2,256]{2,1,0:T(2,128)S(1)}, u32[]{:S(2)}, u32[]{:S(2)}) collective-permute-start(f32[4,2,256]{2,1,0:T(2,128)S(1)} %bitcast.64), channel_id=1, source_target_pairs={{0,32},{2,34},{4,36},{6,38},{8,40},{10,42},{12,44},{14,46},{16,48}... | collective-permute-start | bytes 24584 | tf_op jit(solution)/shard_map/ppermute | solution.py:308
  140.9 4.0 %copy-start.8 = (bf16[2048,512]{1,0:T(8,128)(2,1)S(1)}, bf16[2048,512]{1,0:T(8,128)(2,1)}, u32[]{:S(2)}) copy-start(bf16[2048,512]{1,0:T(8,128)(2,1)} %param.11) | copy-start | bytes 6291460
  145.0 1.6 copy-start.10
  146.6 0.9 copy-start.19
  148.4 15.4 %collective-permute-start.24 = (bf16[128,2048]{1,0:T(8,128)(2,1)S(1)}, bf16[128,2048]{1,0:T(8,128)(2,1)S(1)}, u32[]{:S(2)}, u32[]{:S(2)}) collective-permute-start(bf16[128,2048]{1,0:T(8,128)(2,1)S(1)} %fusion.6), channel_id=1, source_target_pairs={{0,1},{1,0},{2,3},{3,2},{4,5},{5,4},{6,7},{7,6},{8,9},{9,8},{10,11... | collective-permute-start | bytes 1572872 | tf_op jit(solution)/shard_map/ppermute | solution.py:30
  156.0 7.8 %copy-start.4 = (f32[2048]{0:T(1024)S(1)}, f32[2048]{0:T(1024)}, u32[]{:S(2)}) copy-start(f32[2048]{0:T(1024)} %param.8) | copy-start | bytes 24580
  156.0 7.8 %copy-start.11 = (bf16[128,2048]{1,0:T(8,128)(2,1)S(1)}, bf16[128,2048]{1,0:T(8,128)(2,1)}, u32[]{:S(2)}) copy-start(bf16[128,2048]{1,0:T(8,128)(2,1)} %series_ref.1) | copy-start | bytes 1572868
  156.8 7.9 %copy-start.14 = (bf16[128,2048]{1,0:T(8,128)(2,1)S(1)}, bf16[128,2048]{1,0:T(8,128)(2,1)}, u32[]{:S(2)}) copy-start(bf16[128,2048]{1,0:T(8,128)(2,1)} %param.13) | copy-start | bytes 1572868

commit v14 on v13

--- a/solution.py
+++ b/solution.py
@@ -308,15 +308,22 @@
     return lax.ppermute(sent, "seq", [(i, i ^ bit) for i in range(size)])
 
 
-def exchange(rows, sign):
-    two = shifted(rows, sign * 2)
-    far = shifted(rows, sign * 32)
-    four = shifted(two, sign * 2)
-    eight = shifted(four, sign * 4)
-    sixteen = swapped(rows, far, 16, sign)
-    rows_last, two_last, eight = lax.optimization_barrier((rows, two, eight))
-    one = swapped(rows_last, two_last, 1, sign)
-    return [one, two, four, eight, sixteen, far, shifted(far, sign * 32)]
+def exchange(keys, queries):
+    two, two_q = shifted(keys, 2), shifted(queries, -2)
+    far, far_q = shifted(keys, 32), shifted(queries, -32)
+    two, far = lax.optimization_barrier((two, far))
+    two_q, far_q = lax.optimization_barrier((two_q, far_q))
+    four, four_q = shifted(two, 2), shifted(two_q, -2)
+    one, sixteen = swapped(keys, two, 1, 1), swapped(keys, far, 16, 1)
+    one_q, sixteen_q = swapped(queries, two_q, 1, -1), swapped(queries, far_q, 16, -1)
+    last = shifted(far, 32)
+    four, one = lax.optimization_barrier((four, one))
+    four_q, one_q, last = lax.optimization_barrier((four_q, one_q, last))
+    eight, eight_q = shifted(four, 4), shifted(four_q, -4)
+    return (
+        [one, two, four, eight, sixteen, far, last],
+        [one_q, two_q, four_q, eight_q, sixteen_q, far_q, shifted(far_q, -32)],
+    )
 
 
 def exchange_stats(stat, attn_other):
@@ -353,16 +360,12 @@
     kv_all, qg_all = lax.optimization_barrier(
         (jnp.concatenate(kv, axis=1), jnp.concatenate(qg, axis=1))
     )
-    fetched = exchange(kv_all, 1)
-    later = exchange(qg_all, -1)
+    fetched, later = exchange(kv_all, qg_all)
     mixed, grad_query, stat = query_side(where, qg_all, kv_all, [(f,) for f in fetched], 0)
     stat, later = lax.optimization_barrier((stat, later))
     later = [(f,) for f in later]
     attn_other = swap_tp(matmul(mixed[half:], w_out).astype(BF16))
     attn_other, later_stats = exchange_stats(stat, attn_other)
-    attn_rows = matmul(mixed[:half], w_out) + attn_other.astype(F32)
-    layer_out = (series_f + attn_rows).astype(BF16)
-
     def back(at):
         grad_kv = key_side(at, where, kv_all, qg_all, stat, later, later_stats)
         rows = slice(at * half, (at + 1) * half)
@@ -372,7 +375,10 @@
             + matmul_t(grad_kv[1], w_value)
         )
 
-    normed_grad_other = swap_tp(back(1).astype(BF16))
+    partial, attn_other = lax.optimization_barrier((back(1).astype(BF16), attn_other))
+    normed_grad_other = swap_tp(partial)
+    attn_rows = matmul(mixed[:half], w_out) + attn_other.astype(F32)
+    layer_out = (series_f + attn_rows).astype(BF16)
     normed_grad = back(0) + normed_grad_other.astype(F32)
     scaled = normed_grad * norm_gain
     series_grad = out_grad.astype(F32) + inv_rms * (

time: 167 us -> 160 us (0.958)
  waiting for transfers between devices: 62.1 us -> 49.5 us
  local copies, waits for them, and re-layouts: 2.62 us -> 5.75 us
  starting transfers between devices: 65.8 us -> 68.4 us
  other arithmetic: 2.74 us -> 5.27 us
  matrix products: 15.5 us -> 13 us
    ppermute x4, waiting for transfers between devices: 25.9 us -> 17.9 us  [swap_tp(): return lax.ppermute(value, 'tp', [(0, 1), (1, 0)])]
    ppermute x15, starting transfers between devices: 53 us -> 57.8 us  [shifted(): return lax.ppermute(value, 'seq', pairs)]
    ppermute x15, waiting for transfers between devices: 36.2 us -> 31.5 us  [shifted(): return lax.ppermute(value, 'seq', pairs)]
    dot_general x8, matrix products: 8.79 us -> 4.56 us  [matmul(): return jnp.dot(a, b, preferred_element_type=F32)]
    unnamed x40, local copies, waits for them, and re-layouts: 2.62 us -> 5.75 us
    ppermute x6, starting transfers between devices: 3.63 us -> 0.98 us  [swapped(): return lax.ppermute(sent, 'seq', [(i, i ^ bit) for i in range(size)])]
    dot_general x8, matrix products: 6.7 us -> 8.46 us  [matmul_t(): return lax.dot_general(a, b, NT, preferred_element_type=F32)]
    select_n x3 -> x2, other arithmetic: 1.17 us -> 2.91 us  [swapped(): jnp.where(high, own, passed)]
  transfers between devices with their start and end apart: 25 -> 25, of which waited for: 8 -> 8; matrix products, arithmetic and copies ran while one was open for 7% -> 7% of each run, Pallas kernels for 6% -> 8%
where the time goes in v14:
time: 160 us; the launch traced here: 159 us
  starting transfers between devices  68.4 us (43%)
  waiting for transfers between devices  49.5 us (31%)
  Pallas kernels  15.9 us (10%)
  matrix products  13 us (8%)
  local copies, waits for them, and re-layouts  5.75 us (4%)
  other arithmetic  5.27 us (3%)
    ppermute x15, starting transfers between devices, shifted(): return lax.ppermute(value, 'seq', pairs)  57.8 us
    ppermute x15, waiting for transfers between devices, shifted(): return lax.ppermute(value, 'seq', pairs)  31.5 us
    ppermute x4, waiting for transfers between devices, swap_tp(): return lax.ppermute(value, 'tp', [(0, 1), (1, 0)])  17.9 us
    pallas_call x3, Pallas kernels, call(): pl.pallas_call(each_head(kernel), out_shape=outs, grid_spec=pltpu.Prefetc...  14.6 us
    ppermute x4, starting transfers between devices, swap_tp(): return lax.ppermute(value, 'tp', [(0, 1), (1, 0)])  9.62 us
    dot_general x8, matrix products, matmul_t(): return lax.dot_general(a, b, NT, preferred_element_type=F32)  8.46 us
    unnamed x40, local copies, waits for them, and re-layouts  5.75 us
    dot_general x8, matrix products, matmul(): return jnp.dot(a, b, preferred_element_type=F32)  4.56 us
  transfers between devices with their start and end apart: 25, of which 8 were waited for; matrix products, arithmetic and copies ran while one was open for 7% of the time, Pallas kernels for 8%

profile of v14, /device:TPU:24, one launch (start us, length us, event | category | flops | bytes accessed | tf_op | source)
XLA Modules:
  0.0 159.1 jit_solution(8332342582778302546)
XLA Ops:
  0.6 3.1 %collective-permute-start.1 = (bf16[128,2048]{1,0:T(8,128)(2,1)}, bf16[128,2048]{1,0:T(8,128)(2,1)S(1)}, u32[]{:S(2)}, u32[]{:S(2)}) collective-permute-start(bf16[128,2048]{1,0:T(8,128)(2,1)} %param.13), channel_id=1, source_target_pairs={{0,1},{1,0},{2,3},{3,2},{4,5},{5,4},{6,7},{7,6},{8,9},{9,8},{10,11... | collective-permute-start | bytes 1572872 | tf_op jit(solution)/shard_map/ppermute | solution.py:30
  3.8 0.7 copy-done.3
  4.5 1.3 normalize.1
  5.8 0.6 collective-permute-start
  6.4 2.6 %fusion.14 = bf16[1,128,512]{2,1,0:T(8,128)(2,1)S(1)} fusion(bf16[128,2048]{1,0:T(8,128)(2,1)} %param.13, bf16[512,2048]{1,0:T(8,128)(2,1)} %param.12), kind=kOutput, calls=%fused_computation.27 | convolution fusion | flops 268500992 | bytes 2752512 | tf_op jit(solution)/shard_map/dot_general | solution.py:301
  9.0 0.4 fusion.13
  9.5 0.5 fusion.10
  10.0 0.6 copy-done.7
  10.6 0.4 fusion.9
  11.1 6.2 %collective-permute-done.1 = bf16[128,2048]{1,0:T(8,128)(2,1)S(1)} collective-permute-done((bf16[128,2048]{1,0:T(8,128)(2,1)}, bf16[128,2048]{1,0:T(8,128)(2,1)S(1)}, u32[]{:S(2)}, u32[]{:S(2)}) %collective-permute-start.1) | collective-permute-done | bytes 524320 | tf_op jit(solution)/shard_map/ppermute | solution.py:30
  17.3 10.1 %collective-permute-done = bf16[128,2048]{1,0:T(8,128)(2,1)S(1)} collective-permute-done((bf16[128,2048]{1,0:T(8,128)(2,1)S(1)}, bf16[128,2048]{1,0:T(8,128)(2,1)S(1)}, u32[]{:S(2)}, u32[]{:S(2)}) %collective-permute-start) | collective-permute-done | bytes 524320 | tf_op jit(solution)/shard_map/ppermute | solution.py:30
  27.3 0.4 fusion.15
  27.8 0.5 fusion.12
  28.3 0.5 fusion.11
  28.8 0.6 copy-done.9
  29.4 0.8 fusion.16
  30.3 1.3 collective-permute-start.3
  31.6 3.8 %collective-permute-start.2 = (bf16[2,256,512]{2,1,0:T(8,128)(2,1)S(1)}, bf16[2,256,512]{2,1,0:T(8,128)(2,1)}, u32[]{:S(2)}, u32[]{:S(2)}) collective-permute-start(bf16[2,256,512]{2,1,0:T(8,128)(2,1)S(1)} %get-tuple-element.36.refs_1_.refs_0_), channel_id=1, source_target_pairs={{0,4},{2,6},{4,8},{6,10},{8,12},{10,14},{12,16},{14,18},{16,20},{1... | collective-permute-start | bytes 1572872 | tf_op jit(solution)/shard_map/ppermute | solution.py:26
  35.5 5.4 %collective-permute-start.9 = (bf16[2,256,512]{2,1,0:T(8,128)(2,1)S(1)}, bf16[2,256,512]{2,1,0:T(8,128)(2,1)}, u32[]{:S(2)}, u32[]{:S(2)}) collective-permute-start(bf16[2,256,512]{2,1,0:T(8,128)(2,1)S(1)} %get-tuple-element.35.refs_0_.refs_1_), channel_id=1, source_target_pairs={{64,0},{66,2},{68,4},{70,6},{72,8},{74,10},{76,12},{78,14},{80,16}... | collective-permute-start | bytes 1572872 | tf_op jit(solution)/shard_map/ppermute | solution.py:26
  40.8 6.2 %collective-permute-start.8 = (bf16[2,256,512]{2,1,0:T(8,128)(2,1)S(1)}, bf16[2,256,512]{2,1,0:T(8,128)(2,1)}, u32[]{:S(2)}, u32[]{:S(2)}) collective-permute-start(bf16[2,256,512]{2,1,0:T(8,128)(2,1)S(1)} %get-tuple-element.35.refs_0_.refs_1_), channel_id=1, source_target_pairs={{4,0},{6,2},{8,4},{10,6},{12,8},{14,10},{16,12},{18,14},{20,16},{2... | collective-permute-start | bytes 1572872 | tf_op jit(solution)/shard_map/ppermute | solution.py:26
  47.0 9.3 %collective-permute-done.3.refs_7_ = bf16[2,256,512]{2,1,0:T(8,128)(2,1)} collective-permute-done((bf16[2,256,512]{2,1,0:T(8,128)(2,1)S(1)}, bf16[2,256,512]{2,1,0:T(8,128)(2,1)}, u32[]{:S(2)}, u32[]{:S(2)}) %collective-permute-start.3) | collective-permute-done | bytes 524320 | tf_op jit(solution)/shard_map/ppermute | solution.py:26
  56.3 1.9 %collective-permute-start.4 = (bf16[2,256,512]{2,1,0:T(8,128)(2,1)}, bf16[2,256,512]{2,1,0:T(8,128)(2,1)}, u32[]{:S(2)}, u32[]{:S(2)}) collective-permute-start(bf16[2,256,512]{2,1,0:T(8,128)(2,1)} %collective-permute-done.2.refs_3_), channel_id=1, source_target_pairs={{0,4},{2,6},{4,8},{6,10},{8,12},{10,14},{12,16},{14,18},{16,20},{1... | collective-permute-start | bytes 1572872 | tf_op jit(solution)/shard_map/ppermute | solution.py:26
  58.3 0.9 broadcast_select_fusion.1
  59.2 1.3 collective-permute-start.12
  60.5 9.6 %collective-permute-start.10 = (bf16[2,256,512]{2,1,0:T(8,128)(2,1)}, bf16[2,256,512]{2,1,0:T(8,128)(2,1)}, u32[]{:S(2)}, u32[]{:S(2)}) collective-permute-start(bf16[2,256,512]{2,1,0:T(8,128)(2,1)} %collective-permute-done.8.refs_4_), channel_id=1, source_target_pairs={{4,0},{6,2},{8,4},{10,6},{12,8},{14,10},{16,12},{18,14},{20,16},{2... | collective-permute-start | bytes 1572872 | tf_op jit(solution)/shard_map/ppermute | solution.py:26
  70.1 2.3 %broadcast_select_fusion = (bf16[2,256,512]{2,1,0:T(8,128)(2,1)}, bf16[2,256,512]{2,1,0:T(8,128)(2,1)}) fusion(bf16[2,256,512]{2,1,0:T(8,128)(2,1)S(1)} %get-tuple-element.35.refs_0_.refs_1_, bf16[2,256,512]{2,1,0:T(8,128)(2,1)} %collective-permute-done.9.refs_8_, pred[]{:T(512)S(6)} %eq.18, bf16[2,256,512]{2,1,0:T(8,128)(2,1)} %collective-permute-done.8.refs_4_, ...), kind=kLoop, calls=%fused_computation.37 | loop fusion | flops 524288 | bytes 2621442 | tf_op jit(solution)/shard_map/jit(_where)/select_n | solution.py:307
  72.4 1.2 collective-permute-done.4.refs_4_
  73.5 0.8 copy-done.1
  74.3 1.9 %collective-permute-start.6 = (bf16[2,256,512]{2,1,0:T(8,128)(2,1)}, bf16[2,256,512]{2,1,0:T(8,128)(2,1)}, u32[]{:S(2)}, u32[]{:S(2)}) collective-permute-start(bf16[2,256,512]{2,1,0:T(8,128)(2,1)} %collective-permute-done.4.refs_4_), channel_id=1, source_target_pairs={{0,8},{2,10},{4,12},{6,14},{8,16},{10,18},{12,20},{14,22},{16,24},... | collective-permute-start | bytes 1572872 | tf_op jit(solution)/shard_map/ppermute | solution.py:26
  76.3 4.9 %collective-permute-done.10.refs_5_ = bf16[2,256,512]{2,1,0:T(8,128)(2,1)} collective-permute-done((bf16[2,256,512]{2,1,0:T(8,128)(2,1)}, bf16[2,256,512]{2,1,0:T(8,128)(2,1)}, u32[]{:S(2)}, u32[]{:S(2)}) %collective-permute-start.10) | collective-permute-done | bytes 524320 | tf_op jit(solution)/shard_map/ppermute | solution.py:26
  81.3 3.7 %collective-permute-start.15 = (bf16[2,256,512]{2,1,0:T(8,128)(2,1)}, bf16[2,256,512]{2,1,0:T(8,128)(2,1)S(1)}, u32[]{:S(2)}, u32[]{:S(2)}) collective-permute-start(bf16[2,256,512]{2,1,0:T(8,128)(2,1)} %collective-permute-done.9.refs_8_), channel_id=1, source_target_pairs={{64,0},{66,2},{68,4},{70,6},{72,8},{74,10},{76,12},{78,14},{80,16}... | collective-permute-start | bytes 1572872 | tf_op jit(solution)/shard_map/ppermute | solution.py:26
  84.9 0.1 collective-permute-start.14
  85.1 4.0 %collective-permute-start.13 = (bf16[2,256,512]{2,1,0:T(8,128)(2,1)}, bf16[2,256,512]{2,1,0:T(8,128)(2,1)S(1)}, u32[]{:S(2)}, u32[]{:S(2)}) collective-permute-start(bf16[2,256,512]{2,1,0:T(8,128)(2,1)} %collective-permute-done.10.refs_5_), channel_id=1, source_target_pairs={{8,0},{10,2},{12,4},{14,6},{16,8},{18,10},{20,12},{22,14},{24,16},... | collective-permute-start | bytes 1572872 | tf_op jit(solution)/shard_map/ppermute | solution.py:26
  89.1 12.3 %collective-permute-done.6.refs_5_ = bf16[2,256,512]{2,1,0:T(8,128)(2,1)} collective-permute-done((bf16[2,256,512]{2,1,0:T(8,128)(2,1)}, bf16[2,256,512]{2,1,0:T(8,128)(2,1)}, u32[]{:S(2)}, u32[]{:S(2)}) %collective-permute-start.6) | collective-permute-done | bytes 524320 | tf_op jit(solution)/shard_map/ppermute | solution.py:26
  101.4 1.0 copy-done.2
  102.4 6.7 %query_side.1 = (bf16[256,512]{1,0:T(8,128)(2,1)S(1)}, bf16[256,512]{1,0:T(8,128)(2,1)}, f32[4,2,256]{2,1,0:T(2,128)S(1)}) custom-call(s32[2]{0:T(128)S(1)} %pad_add_fusion.where_ref, bf16[2,256,512]{2,1,0:T(8,128)(2,1)S(1)} %get-tuple-element.35.refs_0_.refs_1_, bf16[2,256,512]{2,1,0:T(8,128)(2,1)S(1)} %get-tuple-element.36.refs_1_.refs_0_, ...), custom_call_target="tpu_custom_call" | custom-call | flops 163840 | bytes 65536 | tf_op jit(solution)/shard_map/query_side/pallas_call | solution.py:205
  109.1 0.5 convolution_convert_fusion
  109.6 2.8 %collective-permute-start.17 = (bf16[128,2048]{1,0:T(8,128)(2,1)S(1)}, bf16[128,2048]{1,0:T(8,128)(2,1)S(1)}, u32[]{:S(2)}, u32[]{:S(2)}) collective-permute-start(bf16[128,2048]{1,0:T(8,128)(2,1)S(1)} %convolution_convert_fusion), channel_id=1, source_target_pairs={{0,1},{1,0},{2,3},{3,2},{4,5},{5,4},{6,7},{7,6},{8,9},{9,8},{10,11... | collective-permute-start | bytes 1572872 | tf_op jit(solution)/shard_map/ppermute | solution.py:30
  112.4 10.2 %collective-permute-start.16 = (f32[4,2,256]{2,1,0:T(2,128)S(1)}, f32[4,2,256]{2,1,0:T(2,128)S(1)}, u32[]{:S(2)}, u32[]{:S(2)}) collective-permute-start(f32[4,2,256]{2,1,0:T(2,128)S(1)} %get-tuple-element.49.refs_2_), channel_id=1, source_target_pairs={{4,0},{6,2},{8,4},{10,6},{12,8},{14,10},{16,12},{18,14},{20,16},{2... | collective-permute-start | bytes 24584 | tf_op jit(solution)/shard_map/ppermute | solution.py:26
  122.6 3.4 %collective-permute-start.21 = (f32[4,2,256]{2,1,0:T(2,128)S(1)}, f32[4,2,256]{2,1,0:T(2,128)S(1)}, u32[]{:S(2)}, u32[]{:S(2)}) collective-permute-start(f32[4,2,256]{2,1,0:T(2,128)S(1)} %get-tuple-element.49.refs_2_), channel_id=1, source_target_pairs={{64,0},{66,2},{68,4},{70,6},{72,8},{74,10},{76,12},{78,14},{80,16}... | collective-permute-start | bytes 24584 | tf_op jit(solution)/shard_map/ppermute | solution.py:26
  126.0 1.3 collective-permute-start.23
  127.3 1.9 %collective-permute-start.20 = (f32[4,2,256]{2,1,0:T(2,128)S(1)}, f32[4,2,256]{2,1,0:T(2,128)S(1)}, u32[]{:S(2)}, u32[]{:S(2)}) collective-permute-start(f32[4,2,256]{2,1,0:T(2,128)S(1)} %get-tuple-element.49.refs_2_), channel_id=1, source_target_pairs={{16,0},{18,2},{20,4},{22,6},{24,8},{26,10},{28,12},{30,14},{32,16}... | collective-permute-start | bytes 24584 | tf_op jit(solution)/shard_map/ppermute | solution.py:26
  129.3 1.9 %collective-permute-start.19 = (f32[4,2,256]{2,1,0:T(2,128)S(1)}, f32[4,2,256]{2,1,0:T(2,128)S(1)}, u32[]{:S(2)}, u32[]{:S(2)}) collective-permute-start(f32[4,2,256]{2,1,0:T(2,128)S(1)} %get-tuple-element.49.refs_2_), channel_id=1, source_target_pairs={{8,0},{10,2},{12,4},{14,6},{16,8},{18,10},{20,12},{22,14},{24,16},... | collective-permute-start | bytes 24584 | tf_op jit(solution)/shard_map/ppermute | solution.py:26
  131.2 0.6 broadcast_select_fusion.4
  131.9 0.9 collective-permute-start.22
  132.8 0.1 reduce
  132.9 3.9 %collective-permute-done.20.refs_13_ = f32[4,2,256]{2,1,0:T(2,128)S(1)} collective-permute-done((f32[4,2,256]{2,1,0:T(2,128)S(1)}, f32[4,2,256]{2,1,0:T(2,128)S(1)}, u32[]{:S(2)}, u32[]{:S(2)}) %collective-permute-start.20) | collective-permute-done | bytes 8224 | tf_op jit(solution)/shard_map/ppermute | solution.py:26
  136.8 4.0 %key_side.2 = bf16[2,128,512]{2,1,0:T(8,128)(2,1)S(1)} custom-call(s32[2]{0:T(128)S(1)} %pad_add_fusion.where_ref, bf16[2,256,512]{2,1,0:T(8,128)(2,1)S(1)} %get-tuple-element.36.refs_1_.refs_0_, bf16[2,256,512]{2,1,0:T(8,128)(2,1)S(1)} %get-tuple-element.35.refs_0_.refs_1_, f32[4,2,256]{2,1,0:T(2,128)S(1)} %get-tuple-element.49.refs_2_, ...), custom_call_target="tpu_custom_call" | custom-call | flops 81920 | bytes 65536 | tf_op jit(solution)/shard_map/key_side/pallas_call | solution.py:205
  140.8 0.8 fusion.24
  141.6 0.8 copy-done.8
  142.4 0.8 fusion.25
  143.2 0.1 copy-done.19
  143.3 0.8 fusion.6
  144.2 3.1 %collective-permute-start.24 = (bf16[128,2048]{1,0:T(8,128)(2,1)S(1)}, bf16[128,2048]{1,0:T(8,128)(2,1)S(1)}, u32[]{:S(2)}, u32[]{:S(2)}) collective-permute-start(bf16[128,2048]{1,0:T(8,128)(2,1)S(1)} %fusion.6), channel_id=1, source_target_pairs={{0,1},{1,0},{2,3},{3,2},{4,5},{5,4},{6,7},{7,6},{8,9},{9,8},{10,11... | collective-permute-start | bytes 1572872 | tf_op jit(solution)/shard_map/ppermute | solution.py:30
  147.3 4.0 %key_side.3 = bf16[2,128,512]{2,1,0:T(8,128)(2,1)S(1)} custom-call(s32[2]{0:T(128)S(1)} %pad_add_fusion.where_ref, bf16[2,256,512]{2,1,0:T(8,128)(2,1)S(1)} %get-tuple-element.36.refs_1_.refs_0_, bf16[2,256,512]{2,1,0:T(8,128)(2,1)S(1)} %get-tuple-element.35.refs_0_.refs_1_, f32[4,2,256]{2,1,0:T(2,128)S(1)} %get-tuple-element.49.refs_2_, ...), custom_call_target="tpu_custom_call" | custom-call | flops 81920 | bytes 65536 | tf_op jit(solution)/shard_map/key_side/pallas_call | solution.py:205
  151.2 0.8 fusion.22
  152.1 0.8 fusion.23
  152.9 0.7 copy-done.11
  153.7 0.1 copy-done.12
  153.7 0.2 copy-done.18
  153.9 1.3 fusion.5
  155.2 1.6 %collective-permute-done.24 = bf16[128,2048]{1,0:T(8,128)(2,1)S(1)} collective-permute-done((bf16[128,2048]{1,0:T(8,128)(2,1)S(1)}, bf16[128,2048]{1,0:T(8,128)(2,1)S(1)}, u32[]{:S(2)}, u32[]{:S(2)}) %collective-permute-start.24) | collective-permute-done | bytes 524320 | tf_op jit(solution)/shard_map/ppermute | solution.py:30
  156.9 1.0 fusion.17
  157.9 1.2 fusion.21
  (54 shorter events, 0.3 us)
Async XLA Ops:
  0.6 8.4 %copy-start = (bf16[2048,512]{1,0:T(8,128)(2,1)S(1)}, bf16[2048,512]{1,0:T(8,128)(2,1)}, u32[]{:S(2)}) copy-start(bf16[2048,512]{1,0:T(8,128)(2,1)} %param.9) | copy-start | bytes 6291460
  0.6 16.6 %collective-permute-start.1 = (bf16[128,2048]{1,0:T(8,128)(2,1)}, bf16[128,2048]{1,0:T(8,128)(2,1)S(1)}, u32[]{:S(2)}, u32[]{:S(2)}) collective-permute-start(bf16[128,2048]{1,0:T(8,128)(2,1)} %param.13), channel_id=1, source_target_pairs={{0,1},{1,0},{2,3},{3,2},{4,5},{5,4},{6,7},{7,6},{8,9},{9,8},{10,11... | collective-permute-start | bytes 1572872 | tf_op jit(solution)/shard_map/ppermute | solution.py:30
  3.8 0.7 copy-start.3
  5.8 3.7 %copy-start.5 = (bf16[2048,512]{1,0:T(8,128)(2,1)S(1)}, bf16[2048,512]{1,0:T(8,128)(2,1)}, u32[]{:S(2)}) copy-start(bf16[2048,512]{1,0:T(8,128)(2,1)} %param.11) | copy-start | bytes 6291460
  5.8 21.6 %collective-permute-start = (bf16[128,2048]{1,0:T(8,128)(2,1)S(1)}, bf16[128,2048]{1,0:T(8,128)(2,1)S(1)}, u32[]{:S(2)}, u32[]{:S(2)}) collective-permute-start(bf16[128,2048]{1,0:T(8,128)(2,1)S(1)} %get-tuple-element.32), channel_id=1, source_target_pairs={{0,1},{1,0},{2,3},{3,2},{4,5},{5,4},{6,7},{7,6},{8,9},{9,8},{10,11... | collective-permute-start | bytes 1572872 | tf_op jit(solution)/shard_map/ppermute | solution.py:30
  9.0 1.6 %copy-start.7 = (bf16[2048,512]{1,0:T(8,128)(2,1)S(1)}, bf16[2048,512]{1,0:T(8,128)(2,1)}, u32[]{:S(2)}) copy-start(bf16[2048,512]{1,0:T(8,128)(2,1)} %param.10) | copy-start | bytes 6291460
  27.8 1.6 %copy-start.9 = (bf16[512,2048]{1,0:T(8,128)(2,1)S(1)}, bf16[512,2048]{1,0:T(8,128)(2,1)}, u32[]{:S(2)}) copy-start(bf16[512,2048]{1,0:T(8,128)(2,1)} %param.12) | copy-start | bytes 6291460
  30.3 26.0 %collective-permute-start.3 = (bf16[2,256,512]{2,1,0:T(8,128)(2,1)S(1)}, bf16[2,256,512]{2,1,0:T(8,128)(2,1)}, u32[]{:S(2)}, u32[]{:S(2)}) collective-permute-start(bf16[2,256,512]{2,1,0:T(8,128)(2,1)S(1)} %get-tuple-element.36.refs_1_.refs_0_), channel_id=1, source_target_pairs={{0,64},{2,66},{4,68},{6,70},{8,72},{10,74},{12,76},{14,78},{16,80}... | collective-permute-start | bytes 1572872 | tf_op jit(solution)/shard_map/ppermute | solution.py:26
  31.6 24.7 %collective-permute-start.2 = (bf16[2,256,512]{2,1,0:T(8,128)(2,1)S(1)}, bf16[2,256,512]{2,1,0:T(8,128)(2,1)}, u32[]{:S(2)}, u32[]{:S(2)}) collective-permute-start(bf16[2,256,512]{2,1,0:T(8,128)(2,1)S(1)} %get-tuple-element.36.refs_1_.refs_0_), channel_id=1, source_target_pairs={{0,4},{2,6},{4,8},{6,10},{8,12},{10,14},{12,16},{14,18},{16,20},{1... | collective-permute-start | bytes 1572872 | tf_op jit(solution)/shard_map/ppermute | solution.py:26
  35.5 25.0 %collective-permute-start.9 = (bf16[2,256,512]{2,1,0:T(8,128)(2,1)S(1)}, bf16[2,256,512]{2,1,0:T(8,128)(2,1)}, u32[]{:S(2)}, u32[]{:S(2)}) collective-permute-start(bf16[2,256,512]{2,1,0:T(8,128)(2,1)S(1)} %get-tuple-element.35.refs_0_.refs_1_), channel_id=1, source_target_pairs={{64,0},{66,2},{68,4},{70,6},{72,8},{74,10},{76,12},{78,14},{80,16}... | collective-permute-start | bytes 1572872 | tf_op jit(solution)/shard_map/ppermute | solution.py:26
  40.8 19.6 %collective-permute-start.8 = (bf16[2,256,512]{2,1,0:T(8,128)(2,1)S(1)}, bf16[2,256,512]{2,1,0:T(8,128)(2,1)}, u32[]{:S(2)}, u32[]{:S(2)}) collective-permute-start(bf16[2,256,512]{2,1,0:T(8,128)(2,1)S(1)} %get-tuple-element.35.refs_0_.refs_1_), channel_id=1, source_target_pairs={{4,0},{6,2},{8,4},{10,6},{12,8},{14,10},{16,12},{18,14},{20,16},{2... | collective-permute-start | bytes 1572872 | tf_op jit(solution)/shard_map/ppermute | solution.py:26
  56.3 17.2 %collective-permute-start.4 = (bf16[2,256,512]{2,1,0:T(8,128)(2,1)}, bf16[2,256,512]{2,1,0:T(8,128)(2,1)}, u32[]{:S(2)}, u32[]{:S(2)}) collective-permute-start(bf16[2,256,512]{2,1,0:T(8,128)(2,1)} %collective-permute-done.2.refs_3_), channel_id=1, source_target_pairs={{0,4},{2,6},{4,8},{6,10},{8,12},{10,14},{12,16},{14,18},{16,20},{1... | collective-permute-start | bytes 1572872 | tf_op jit(solution)/shard_map/ppermute | solution.py:26
  59.2 14.4 %collective-permute-start.5 = (bf16[2,256,512]{2,1,0:T(8,128)(2,1)S(1)}, bf16[2,256,512]{2,1,0:T(8,128)(2,1)S(1)}, u32[]{:S(2)}, u32[]{:S(2)}) collective-permute-start(bf16[2,256,512]{2,1,0:T(8,128)(2,1)S(1)} %get-tuple-element.65), channel_id=1, source_target_pairs={{0,2},{2,0},{4,6},{6,4},{8,10},{10,8},{12,14},{14,12},{16,18},{18,... | collective-permute-start | bytes 1572872 | tf_op jit(solution)/shard_map/ppermute | solution.py:308
  59.2 25.8 %collective-permute-start.12 = (bf16[2,256,512]{2,1,0:T(8,128)(2,1)}, bf16[2,256,512]{2,1,0:T(8,128)(2,1)}, u32[]{:S(2)}, u32[]{:S(2)}) collective-permute-start(bf16[2,256,512]{2,1,0:T(8,128)(2,1)} %collective-permute-done.3.refs_7_), channel_id=1, source_target_pairs={{0,64},{2,66},{4,68},{6,70},{8,72},{10,74},{12,76},{14,78},{16,80}... | collective-permute-start | bytes 1572872 | tf_op jit(solution)/shard_map/ppermute | solution.py:26
  60.5 20.8 %collective-permute-start.10 = (bf16[2,256,512]{2,1,0:T(8,128)(2,1)}, bf16[2,256,512]{2,1,0:T(8,128)(2,1)}, u32[]{:S(2)}, u32[]{:S(2)}) collective-permute-start(bf16[2,256,512]{2,1,0:T(8,128)(2,1)} %collective-permute-done.8.refs_4_), channel_id=1, source_target_pairs={{4,0},{6,2},{8,4},{10,6},{12,8},{14,10},{16,12},{18,14},{20,16},{2... | collective-permute-start | bytes 1572872 | tf_op jit(solution)/shard_map/ppermute | solution.py:26
  72.4 12.7 %collective-permute-start.11 = (bf16[2,256,512]{2,1,0:T(8,128)(2,1)}, bf16[2,256,512]{2,1,0:T(8,128)(2,1)}, u32[]{:S(2)}, u32[]{:S(2)}) collective-permute-start(bf16[2,256,512]{2,1,0:T(8,128)(2,1)} %get-tuple-element.63), channel_id=1, source_target_pairs={{0,2},{2,0},{4,6},{6,4},{8,10},{10,8},{12,14},{14,12},{16,18},{18,... | collective-permute-start | bytes 1572872 | tf_op jit(solution)/shard_map/ppermute | solution.py:308
  73.5 15.6 %collective-permute-start.7 = (bf16[2,256,512]{2,1,0:T(8,128)(2,1)}, bf16[2,256,512]{2,1,0:T(8,128)(2,1)}, u32[]{:S(2)}, u32[]{:S(2)}) collective-permute-start(bf16[2,256,512]{2,1,0:T(8,128)(2,1)} %get-tuple-element.64), channel_id=1, source_target_pairs={{0,32},{2,34},{4,36},{6,38},{8,40},{10,42},{12,44},{14,46},{16,48}... | collective-permute-start | bytes 1572872 | tf_op jit(solution)/shard_map/ppermute | solution.py:308
  73.5 0.8 copy-start.1
  74.3 27.0 %collective-permute-start.6 = (bf16[2,256,512]{2,1,0:T(8,128)(2,1)}, bf16[2,256,512]{2,1,0:T(8,128)(2,1)}, u32[]{:S(2)}, u32[]{:S(2)}) collective-permute-start(bf16[2,256,512]{2,1,0:T(8,128)(2,1)} %collective-permute-done.4.refs_4_), channel_id=1, source_target_pairs={{0,8},{2,10},{4,12},{6,14},{8,16},{10,18},{12,20},{14,22},{16,24},... | collective-permute-start | bytes 1572872 | tf_op jit(solution)/shard_map/ppermute | solution.py:26
  81.3 31.1 %collective-permute-start.15 = (bf16[2,256,512]{2,1,0:T(8,128)(2,1)}, bf16[2,256,512]{2,1,0:T(8,128)(2,1)S(1)}, u32[]{:S(2)}, u32[]{:S(2)}) collective-permute-start(bf16[2,256,512]{2,1,0:T(8,128)(2,1)} %collective-permute-done.9.refs_8_), channel_id=1, source_target_pairs={{64,0},{66,2},{68,4},{70,6},{72,8},{74,10},{76,12},{78,14},{80,16}... | collective-permute-start | bytes 1572872 | tf_op jit(solution)/shard_map/ppermute | solution.py:26
  84.9 27.4 %collective-permute-start.14 = (bf16[2,256,512]{2,1,0:T(8,128)(2,1)}, bf16[2,256,512]{2,1,0:T(8,128)(2,1)S(1)}, u32[]{:S(2)}, u32[]{:S(2)}) collective-permute-start(bf16[2,256,512]{2,1,0:T(8,128)(2,1)} %get-tuple-element.62), channel_id=1, source_target_pairs={{0,32},{2,34},{4,36},{6,38},{8,40},{10,42},{12,44},{14,46},{16,48}... | collective-permute-start | bytes 1572872 | tf_op jit(solution)/shard_map/ppermute | solution.py:308
  85.1 27.3 %collective-permute-start.13 = (bf16[2,256,512]{2,1,0:T(8,128)(2,1)}, bf16[2,256,512]{2,1,0:T(8,128)(2,1)S(1)}, u32[]{:S(2)}, u32[]{:S(2)}) collective-permute-start(bf16[2,256,512]{2,1,0:T(8,128)(2,1)} %collective-permute-done.10.refs_5_), channel_id=1, source_target_pairs={{8,0},{10,2},{12,4},{14,6},{16,8},{18,10},{20,12},{22,14},{24,16},... | collective-permute-start | bytes 1572872 | tf_op jit(solution)/shard_map/ppermute | solution.py:26
  101.4 1.0 copy-start.2
  102.4 6.7 %copy-start.10 = (bf16[512,2048]{1,0:T(8,128)(2,1)S(1)}, bf16[512,2048]{1,0:T(8,128)(2,1)}, u32[]{:S(2)}) copy-start(bf16[512,2048]{1,0:T(8,128)(2,1)} %param.12) | copy-start | bytes 6291460
  109.6 21.6 %collective-permute-start.17 = (bf16[128,2048]{1,0:T(8,128)(2,1)S(1)}, bf16[128,2048]{1,0:T(8,128)(2,1)S(1)}, u32[]{:S(2)}, u32[]{:S(2)}) collective-permute-start(bf16[128,2048]{1,0:T(8,128)(2,1)S(1)} %convolution_convert_fusion), channel_id=1, source_target_pairs={{0,1},{1,0},{2,3},{3,2},{4,5},{5,4},{6,7},{7,6},{8,9},{9,8},{10,11... | collective-permute-start | bytes 1572872 | tf_op jit(solution)/shard_map/ppermute | solution.py:30
  112.4 20.4 %copy-start.14 = (bf16[2,256,512]{2,1,0:T(8,128)(2,1)}, bf16[2,256,512]{2,1,0:T(8,128)(2,1)S(1)}, u32[]{:S(2)}) copy-start(bf16[2,256,512]{2,1,0:T(8,128)(2,1)S(1)} %collective-permute-done.15.refs_9_) | copy-start | bytes 1572868
  112.4 20.4 %copy-start.15 = (bf16[2,256,512]{2,1,0:T(8,128)(2,1)}, bf16[2,256,512]{2,1,0:T(8,128)(2,1)S(1)}, u32[]{:S(2)}) copy-start(bf16[2,256,512]{2,1,0:T(8,128)(2,1)S(1)} %collective-permute-done.14.refs_7_) | copy-start | bytes 1572868
  112.4 20.4 %copy-start.16 = (bf16[2,256,512]{2,1,0:T(8,128)(2,1)}, bf16[2,256,512]{2,1,0:T(8,128)(2,1)S(1)}, u32[]{:S(2)}) copy-start(bf16[2,256,512]{2,1,0:T(8,128)(2,1)S(1)} %collective-permute-done.13.refs_6_) | copy-start | bytes 1572868
  112.4 16.8 %collective-permute-start.16 = (f32[4,2,256]{2,1,0:T(2,128)S(1)}, f32[4,2,256]{2,1,0:T(2,128)S(1)}, u32[]{:S(2)}, u32[]{:S(2)}) collective-permute-start(f32[4,2,256]{2,1,0:T(2,128)S(1)} %get-tuple-element.49.refs_2_), channel_id=1, source_target_pairs={{4,0},{6,2},{8,4},{10,6},{12,8},{14,10},{16,12},{18,14},{20,16},{2... | collective-permute-start | bytes 24584 | tf_op jit(solution)/shard_map/ppermute | solution.py:26
  122.6 8.6 %collective-permute-start.21 = (f32[4,2,256]{2,1,0:T(2,128)S(1)}, f32[4,2,256]{2,1,0:T(2,128)S(1)}, u32[]{:S(2)}, u32[]{:S(2)}) collective-permute-start(f32[4,2,256]{2,1,0:T(2,128)S(1)} %get-tuple-element.49.refs_2_), channel_id=1, source_target_pairs={{64,0},{66,2},{68,4},{70,6},{72,8},{74,10},{76,12},{78,14},{80,16}... | collective-permute-start | bytes 24584 | tf_op jit(solution)/shard_map/ppermute | solution.py:26
  126.0 6.9 %collective-permute-start.23 = (f32[4,2,256]{2,1,0:T(2,128)S(1)}, f32[4,2,256]{2,1,0:T(2,128)S(1)}, u32[]{:S(2)}, u32[]{:S(2)}) collective-permute-start(f32[4,2,256]{2,1,0:T(2,128)S(1)} %get-tuple-element.49.refs_2_), channel_id=1, source_target_pairs={{128,0},{130,2},{132,4},{134,6},{136,8},{138,10},{140,12},{142,14}... | collective-permute-start | bytes 24584 | tf_op jit(solution)/shard_map/ppermute | solution.py:26
  127.3 9.5 %collective-permute-start.20 = (f32[4,2,256]{2,1,0:T(2,128)S(1)}, f32[4,2,256]{2,1,0:T(2,128)S(1)}, u32[]{:S(2)}, u32[]{:S(2)}) collective-permute-start(f32[4,2,256]{2,1,0:T(2,128)S(1)} %get-tuple-element.49.refs_2_), channel_id=1, source_target_pairs={{16,0},{18,2},{20,4},{22,6},{24,8},{26,10},{28,12},{30,14},{32,16}... | collective-permute-start | bytes 24584 | tf_op jit(solution)/shard_map/ppermute | solution.py:26
  129.3 7.5 %collective-permute-start.19 = (f32[4,2,256]{2,1,0:T(2,128)S(1)}, f32[4,2,256]{2,1,0:T(2,128)S(1)}, u32[]{:S(2)}, u32[]{:S(2)}) collective-permute-start(f32[4,2,256]{2,1,0:T(2,128)S(1)} %get-tuple-element.49.refs_2_), channel_id=1, source_target_pairs={{8,0},{10,2},{12,4},{14,6},{16,8},{18,10},{20,12},{22,14},{24,16},... | collective-permute-start | bytes 24584 | tf_op jit(solution)/shard_map/ppermute | solution.py:26
  131.2 1.6 copy-start.17
  131.9 4.9 %collective-permute-start.22 = (f32[4,2,256]{2,1,0:T(2,128)}, f32[4,2,256]{2,1,0:T(2,128)S(1)}, u32[]{:S(2)}, u32[]{:S(2)}) collective-permute-start(f32[4,2,256]{2,1,0:T(2,128)} %bitcast.58), channel_id=1, source_target_pairs={{0,32},{2,34},{4,36},{6,38},{8,40},{10,42},{12,44},{14,46},{16,48}... | collective-permute-start | bytes 24584 | tf_op jit(solution)/shard_map/ppermute | solution.py:308
  132.7 4.0 %collective-permute-start.18 = (f32[4,2,256]{2,1,0:T(2,128)S(1)}, f32[4,2,256]{2,1,0:T(2,128)S(1)}, u32[]{:S(2)}, u32[]{:S(2)}) collective-permute-start(f32[4,2,256]{2,1,0:T(2,128)S(1)} %bitcast.64), channel_id=1, source_target_pairs={{0,2},{2,0},{4,6},{6,4},{8,10},{10,8},{12,14},{14,12},{16,18},{18,... | collective-permute-start | bytes 24584 | tf_op jit(solution)/shard_map/ppermute | solution.py:308
  132.9 7.9 %copy-start.6 = (bf16[2048,512]{1,0:T(8,128)(2,1)S(1)}, bf16[2048,512]{1,0:T(8,128)(2,1)}, u32[]{:S(2)}) copy-start(bf16[2048,512]{1,0:T(8,128)(2,1)} %param.11) | copy-start | bytes 6291460
  140.8 1.6 %copy-start.8 = (bf16[2048,512]{1,0:T(8,128)(2,1)S(1)}, bf16[2048,512]{1,0:T(8,128)(2,1)}, u32[]{:S(2)}) copy-start(bf16[2048,512]{1,0:T(8,128)(2,1)} %param.10) | copy-start | bytes 6291460
  142.4 0.9 copy-start.19
  144.2 12.7 %collective-permute-start.24 = (bf16[128,2048]{1,0:T(8,128)(2,1)S(1)}, bf16[128,2048]{1,0:T(8,128)(2,1)S(1)}, u32[]{:S(2)}, u32[]{:S(2)}) collective-permute-start(bf16[128,2048]{1,0:T(8,128)(2,1)S(1)} %fusion.6), channel_id=1, source_target_pairs={{0,1},{1,0},{2,3},{3,2},{4,5},{5,4},{6,7},{7,6},{8,9},{9,8},{10,11... | collective-permute-start | bytes 1572872 | tf_op jit(solution)/shard_map/ppermute | solution.py:30
  152.1 1.6 %copy-start.11 = (bf16[512,2048]{1,0:T(8,128)(2,1)S(1)}, bf16[512,2048]{1,0:T(8,128)(2,1)}, u32[]{:S(2)}) copy-start(bf16[512,2048]{1,0:T(8,128)(2,1)} %param.12) | copy-start | bytes 6291460
  152.1 1.7 %copy-start.12 = (bf16[128,2048]{1,0:T(8,128)(2,1)S(1)}, bf16[128,2048]{1,0:T(8,128)(2,1)}, u32[]{:S(2)}) copy-start(bf16[128,2048]{1,0:T(8,128)(2,1)} %series_ref.1) | copy-start | bytes 1572868
  152.1 1.8 %copy-start.18 = (bf16[128,2048]{1,0:T(8,128)(2,1)S(1)}, bf16[128,2048]{1,0:T(8,128)(2,1)}, u32[]{:S(2)}) copy-start(bf16[128,2048]{1,0:T(8,128)(2,1)} %copy-done.17) | copy-start | bytes 1572868
  153.9 3.0 %copy-start.4 = (f32[2048]{0:T(1024)S(1)}, f32[2048]{0:T(1024)}, u32[]{:S(2)}) copy-start(f32[2048]{0:T(1024)} %param.8) | copy-start | bytes 24580
  155.2 2.6 %copy-start.13 = (bf16[128,2048]{1,0:T(8,128)(2,1)S(1)}, bf16[128,2048]{1,0:T(8,128)(2,1)}, u32[]{:S(2)}) copy-start(bf16[128,2048]{1,0:T(8,128)(2,1)} %param.13) | copy-start | bytes 1572868

commit v15 on v14

--- a/solution.py
+++ b/solution.py
@@ -308,20 +308,22 @@
     return lax.ppermute(sent, "seq", [(i, i ^ bit) for i in range(size)])
 
 
-def exchange(keys, queries):
+def exchange(keys, keys_other, queries):
     two, two_q = shifted(keys, 2), shifted(queries, -2)
     far, far_q = shifted(keys, 32), shifted(queries, -32)
     two, far = lax.optimization_barrier((two, far))
     two_q, far_q = lax.optimization_barrier((two_q, far_q))
     four, four_q = shifted(two, 2), shifted(two_q, -2)
+    eight_other = shifted(keys_other, 8)
     one, sixteen = swapped(keys, two, 1, 1), swapped(keys, far, 16, 1)
     one_q, sixteen_q = swapped(queries, two_q, 1, -1), swapped(queries, far_q, 16, -1)
     last = shifted(far, 32)
-    four, one = lax.optimization_barrier((four, one))
+    four, one, eight_other = lax.optimization_barrier((four, one, eight_other))
     four_q, one_q, last = lax.optimization_barrier((four_q, one_q, last))
-    eight, eight_q = shifted(four, 4), shifted(four_q, -4)
+    eight_own, eight_q = shifted(four[:, : four.shape[1] // 2], 4), shifted(four_q, -4)
+    whole = [(one,), (two,), (four,), (sixteen,), (far,), (last,)]
     return (
-        [one, two, four, eight, sixteen, far, last],
+        whole[:3] + [(eight_own, eight_other)] + whole[3:],
         [one_q, two_q, four_q, eight_q, sixteen_q, far_q, shifted(far_q, -32)],
     )
 
@@ -360,8 +362,8 @@
     kv_all, qg_all = lax.optimization_barrier(
         (jnp.concatenate(kv, axis=1), jnp.concatenate(qg, axis=1))
     )
-    fetched, later = exchange(kv_all, qg_all)
-    mixed, grad_query, stat = query_side(where, qg_all, kv_all, [(f,) for f in fetched], 0)
+    fetched, later = exchange(kv_all, kv[1], qg_all)
+    mixed, grad_query, stat = query_side(where, qg_all, kv_all, fetched, 0)
     stat, later = lax.optimization_barrier((stat, later))
     later = [(f,) for f in later]
     attn_other = swap_tp(matmul(mixed[half:], w_out).astype(BF16))

time: 160 us -> 167 us (1.044)
  waiting for transfers between devices: 49.5 us -> 54.4 us
  local copies, waits for them, and re-layouts: 5.75 us -> 8.38 us
    ppermute x4, waiting for transfers between devices: 17.9 us -> 20.2 us  [swap_tp(): return lax.ppermute(value, 'tp', [(0, 1), (1, 0)])]
    unnamed x40 -> x48, local copies, waits for them, and re-layouts: 5.75 us -> 7.62 us
    ppermute x15 -> x16, waiting for transfers between devices: 31.5 us -> 33.4 us  [shifted(): return lax.ppermute(value, 'seq', pairs)]
    ppermute x15 -> x16, starting transfers between devices: 57.8 us -> 56.6 us  [shifted(): return lax.ppermute(value, 'seq', pairs)]
  transfers between devices with their start and end apart: 25 -> 26, of which waited for: 8 -> 12; matrix products, arithmetic and copies ran while one was open for 7% -> 7% of each run, Pallas kernels for 8% -> 7%
where the time goes in v15:
time: 167 us; the launch traced here: 166 us
  starting transfers between devices  68.3 us (41%)
  waiting for transfers between devices  54.4 us (33%)
  Pallas kernels  15.8 us (9%)
  matrix products  13 us (8%)
  local copies, waits for them, and re-layouts  8.38 us (5%)
  other arithmetic  4.69 us (3%)
    ppermute x16, starting transfers between devices, shifted(): return lax.ppermute(value, 'seq', pairs)  56.6 us
    ppermute x16, waiting for transfers between devices, shifted(): return lax.ppermute(value, 'seq', pairs)  33.4 us
    ppermute x4, waiting for transfers between devices, swap_tp(): return lax.ppermute(value, 'tp', [(0, 1), (1, 0)])  20.2 us
    pallas_call x3, Pallas kernels, call(): pl.pallas_call(each_head(kernel), out_shape=outs, grid_spec=pltpu.Prefetc...  14.5 us
    ppermute x4, starting transfers between devices, swap_tp(): return lax.ppermute(value, 'tp', [(0, 1), (1, 0)])  9.69 us
    dot_general x8, matrix products, matmul_t(): return lax.dot_general(a, b, NT, preferred_element_type=F32)  8.45 us
    unnamed x48, local copies, waits for them, and re-layouts  7.62 us
    dot_general x8, matrix products, matmul(): return jnp.dot(a, b, preferred_element_type=F32)  4.55 us
  transfers between devices with their start and end apart: 26, of which 12 were waited for; matrix products, arithmetic and copies ran while one was open for 7% of the time, Pallas kernels for 7%

profile of v15, /device:TPU:24, one launch (start us, length us, event | category | flops | bytes accessed | tf_op | source)
XLA Modules:
  0.0 165.8 jit_solution(7618460508456531813)
XLA Ops:
  0.6 3.1 %collective-permute-start.1 = (bf16[128,2048]{1,0:T(8,128)(2,1)}, bf16[128,2048]{1,0:T(8,128)(2,1)S(1)}, u32[]{:S(2)}, u32[]{:S(2)}) collective-permute-start(bf16[128,2048]{1,0:T(8,128)(2,1)} %param.13), channel_id=1, source_target_pairs={{0,1},{1,0},{2,3},{3,2},{4,5},{5,4},{6,7},{7,6},{8,9},{9,8},{10,11... | collective-permute-start | bytes 1572872 | tf_op jit(solution)/shard_map/ppermute | solution.py:30
  3.8 0.7 copy-done.7
  4.5 1.3 normalize.1
  5.8 0.6 collective-permute-start
  6.4 2.6 %fusion.14 = bf16[1,128,512]{2,1,0:T(8,128)(2,1)S(1)} fusion(bf16[128,2048]{1,0:T(8,128)(2,1)} %param.13, bf16[512,2048]{1,0:T(8,128)(2,1)} %param.12), kind=kOutput, calls=%fused_computation.27 | convolution fusion | flops 268500992 | bytes 2752512 | tf_op jit(solution)/shard_map/dot_general | solution.py:301
  9.0 0.4 fusion.13
  9.5 0.5 fusion.10
  10.0 0.6 copy-done.11
  11.1 6.2 %collective-permute-done.1 = bf16[128,2048]{1,0:T(8,128)(2,1)S(1)} collective-permute-done((bf16[128,2048]{1,0:T(8,128)(2,1)}, bf16[128,2048]{1,0:T(8,128)(2,1)S(1)}, u32[]{:S(2)}, u32[]{:S(2)}) %collective-permute-start.1) | collective-permute-done | bytes 524320 | tf_op jit(solution)/shard_map/ppermute | solution.py:30
  17.3 10.1 %collective-permute-done = bf16[128,2048]{1,0:T(8,128)(2,1)S(1)} collective-permute-done((bf16[128,2048]{1,0:T(8,128)(2,1)S(1)}, bf16[128,2048]{1,0:T(8,128)(2,1)S(1)}, u32[]{:S(2)}, u32[]{:S(2)}) %collective-permute-start) | collective-permute-done | bytes 524320 | tf_op jit(solution)/shard_map/ppermute | solution.py:30
  27.3 0.5 fusion.12
  27.8 0.5 fusion.11
  28.3 0.5 fusion.15
  28.8 0.7 copy-done.13
  29.4 0.8 fusion.16
  30.3 3.5 %collective-permute-start.10 = (bf16[2,256,512]{2,1,0:T(8,128)(2,1)S(1)}, bf16[2,256,512]{2,1,0:T(8,128)(2,1)}, u32[]{:S(2)}, u32[]{:S(2)}) collective-permute-start(bf16[2,256,512]{2,1,0:T(8,128)(2,1)S(1)} %get-tuple-element.36.refs_0_.refs_1_), channel_id=1, source_target_pairs={{64,0},{66,2},{68,4},{70,6},{72,8},{74,10},{76,12},{78,14},{80,16}... | collective-permute-start | bytes 1572872 | tf_op jit(solution)/shard_map/ppermute | solution.py:26
  33.8 7.8 %collective-permute-start.9 = (bf16[2,256,512]{2,1,0:T(8,128)(2,1)S(1)}, bf16[2,256,512]{2,1,0:T(8,128)(2,1)}, u32[]{:S(2)}, u32[]{:S(2)}) collective-permute-start(bf16[2,256,512]{2,1,0:T(8,128)(2,1)S(1)} %get-tuple-element.36.refs_0_.refs_1_), channel_id=1, source_target_pairs={{4,0},{6,2},{8,4},{10,6},{12,8},{14,10},{16,12},{18,14},{20,16},{2... | collective-permute-start | bytes 1572872 | tf_op jit(solution)/shard_map/ppermute | solution.py:26
  41.6 1.3 collective-permute-start.3
  42.9 1.9 %collective-permute-start.2 = (bf16[2,256,512]{2,1,0:T(8,128)(2,1)S(1)}, bf16[2,256,512]{2,1,0:T(8,128)(2,1)}, u32[]{:S(2)}, u32[]{:S(2)}) collective-permute-start(bf16[2,256,512]{2,1,0:T(8,128)(2,1)S(1)} %get-tuple-element.37.refs_1_.refs_0_), channel_id=1, source_target_pairs={{0,4},{2,6},{4,8},{6,10},{8,12},{10,14},{12,16},{14,18},{16,20},{1... | collective-permute-start | bytes 1572872 | tf_op jit(solution)/shard_map/ppermute | solution.py:26
  44.9 5.2 %collective-permute-start.6 = (bf16[2,128,512]{2,1,0:T(8,128)(2,1)S(1)}, bf16[2,128,512]{2,1,0:T(8,128)(2,1)S(1)}, u32[]{:S(2)}, u32[]{:S(2)}) collective-permute-start(bf16[2,128,512]{2,1,0:T(8,128)(2,1)S(1)} %pad_maximum_fusion), channel_id=1, source_target_pairs={{0,16},{2,18},{4,20},{6,22},{8,24},{10,26},{12,28},{14,30},{16,32}... | collective-permute-start | bytes 786440 | tf_op jit(solution)/shard_map/ppermute | solution.py:26
  50.1 12.0 %collective-permute-done.9.refs_4_ = bf16[2,256,512]{2,1,0:T(8,128)(2,1)} collective-permute-done((bf16[2,256,512]{2,1,0:T(8,128)(2,1)S(1)}, bf16[2,256,512]{2,1,0:T(8,128)(2,1)}, u32[]{:S(2)}, u32[]{:S(2)}) %collective-permute-start.9) | collective-permute-done | bytes 524320 | tf_op jit(solution)/shard_map/ppermute | solution.py:26
  62.2 7.6 %collective-permute-start.11 = (bf16[2,256,512]{2,1,0:T(8,128)(2,1)}, bf16[2,256,512]{2,1,0:T(8,128)(2,1)}, u32[]{:S(2)}, u32[]{:S(2)}) collective-permute-start(bf16[2,256,512]{2,1,0:T(8,128)(2,1)} %collective-permute-done.9.refs_4_), channel_id=1, source_target_pairs={{4,0},{6,2},{8,4},{10,6},{12,8},{14,10},{16,12},{18,14},{20,16},{2... | collective-permute-start | bytes 1572872 | tf_op jit(solution)/shard_map/ppermute | solution.py:26
  69.8 1.3 collective-permute-done.3.refs_8_
  71.1 1.9 %collective-permute-start.4 = (bf16[2,256,512]{2,1,0:T(8,128)(2,1)}, bf16[2,256,512]{2,1,0:T(8,128)(2,1)S(1)}, u32[]{:S(2)}, u32[]{:S(2)}) collective-permute-start(bf16[2,256,512]{2,1,0:T(8,128)(2,1)} %collective-permute-done.2.refs_3_), channel_id=1, source_target_pairs={{0,4},{2,6},{4,8},{6,10},{8,12},{10,14},{12,16},{14,18},{16,20},{1... | collective-permute-start | bytes 1572872 | tf_op jit(solution)/shard_map/ppermute | solution.py:26
  73.0 1.3 collective-permute-start.13
  74.3 0.9 broadcast_select_fusion.1
  75.2 2.3 %broadcast_select_fusion = (bf16[2,256,512]{2,1,0:T(8,128)(2,1)}, bf16[2,256,512]{2,1,0:T(8,128)(2,1)}) fusion(bf16[2,256,512]{2,1,0:T(8,128)(2,1)S(1)} %get-tuple-element.36.refs_0_.refs_1_, bf16[2,256,512]{2,1,0:T(8,128)(2,1)} %collective-permute-done.10.refs_8_, pred[]{:T(512)S(6)} %eq.18, bf16[2,256,512]{2,1,0:T(8,128)(2,1)} %collective-permute-done.9.refs_4_, ...), kind=kLoop, calls=%fused_computation.37 | loop fusion | flops 524288 | bytes 2621442 | tf_op jit(solution)/shard_map/jit(_where)/select_n | solution.py:307
  77.9 8.5 %collective-permute-done.4.refs_4_ = bf16[2,256,512]{2,1,0:T(8,128)(2,1)S(1)} collective-permute-done((bf16[2,256,512]{2,1,0:T(8,128)(2,1)}, bf16[2,256,512]{2,1,0:T(8,128)(2,1)S(1)}, u32[]{:S(2)}, u32[]{:S(2)}) %collective-permute-start.4) | collective-permute-done | bytes 524320 | tf_op jit(solution)/shard_map/ppermute | solution.py:26
  86.4 0.8 slice.27
  87.3 0.8 copy-done.1
  88.1 1.9 %collective-permute-start.7 = (bf16[2,128,512]{2,1,0:T(8,128)(2,1)}, bf16[2,128,512]{2,1,0:T(8,128)(2,1)}, u32[]{:S(2)}, u32[]{:S(2)}) collective-permute-start(bf16[2,128,512]{2,1,0:T(8,128)(2,1)} %slice.27), channel_id=1, source_target_pairs={{0,8},{2,10},{4,12},{6,14},{8,16},{10,18},{12,20},{14,22},{16,24},... | collective-permute-start | bytes 786440 | tf_op jit(solution)/shard_map/ppermute | solution.py:26
  90.1 2.5 %collective-permute-start.16 = (bf16[2,256,512]{2,1,0:T(8,128)(2,1)}, bf16[2,256,512]{2,1,0:T(8,128)(2,1)S(1)}, u32[]{:S(2)}, u32[]{:S(2)}) collective-permute-start(bf16[2,256,512]{2,1,0:T(8,128)(2,1)} %collective-permute-done.10.refs_8_), channel_id=1, source_target_pairs={{64,0},{66,2},{68,4},{70,6},{72,8},{74,10},{76,12},{78,14},{80,16}... | collective-permute-start | bytes 1572872 | tf_op jit(solution)/shard_map/ppermute | solution.py:26
  92.6 6.0 %collective-permute-done.13.refs_9_ = bf16[2,256,512]{2,1,0:T(8,128)(2,1)} collective-permute-done((bf16[2,256,512]{2,1,0:T(8,128)(2,1)}, bf16[2,256,512]{2,1,0:T(8,128)(2,1)}, u32[]{:S(2)}, u32[]{:S(2)}) %collective-permute-start.13) | collective-permute-done | bytes 524320 | tf_op jit(solution)/shard_map/ppermute | solution.py:26
  98.6 3.5 %collective-permute-start.14 = (bf16[2,256,512]{2,1,0:T(8,128)(2,1)}, bf16[2,256,512]{2,1,0:T(8,128)(2,1)S(1)}, u32[]{:S(2)}, u32[]{:S(2)}) collective-permute-start(bf16[2,256,512]{2,1,0:T(8,128)(2,1)} %collective-permute-done.11.refs_5_), channel_id=1, source_target_pairs={{8,0},{10,2},{12,4},{14,6},{16,8},{18,10},{20,12},{22,14},{24,16},... | collective-permute-start | bytes 1572872 | tf_op jit(solution)/shard_map/ppermute | solution.py:26
  102.2 0.6 collective-permute-done.7.refs_5_
  102.8 1.0 copy-done.2
  103.8 1.0 copy-done.4
  104.9 6.6 %query_side.1 = (bf16[256,512]{1,0:T(8,128)(2,1)S(1)}, bf16[256,512]{1,0:T(8,128)(2,1)}, f32[4,2,256]{2,1,0:T(2,128)S(1)}) custom-call(s32[2]{0:T(128)S(1)} %pad_add_fusion.where_ref, bf16[2,256,512]{2,1,0:T(8,128)(2,1)S(1)} %get-tuple-element.36.refs_0_.refs_1_, bf16[2,256,512]{2,1,0:T(8,128)(2,1)S(1)} %get-tuple-element.37.refs_1_.refs_0_, ...), custom_call_target="tpu_custom_call" | custom-call | flops 163840 | bytes 65536 | tf_op jit(solution)/shard_map/query_side/pallas_call | solution.py:205
  111.4 0.7 copy-done.5
  112.6 3.1 %collective-permute-start.18 = (bf16[128,2048]{1,0:T(8,128)(2,1)S(1)}, bf16[128,2048]{1,0:T(8,128)(2,1)S(1)}, u32[]{:S(2)}, u32[]{:S(2)}) collective-permute-start(bf16[128,2048]{1,0:T(8,128)(2,1)S(1)} %convolution_convert_fusion), channel_id=1, source_target_pairs={{0,1},{1,0},{2,3},{3,2},{4,5},{5,4},{6,7},{7,6},{8,9},{9,8},{10,11... | collective-permute-start | bytes 1572872 | tf_op jit(solution)/shard_map/ppermute | solution.py:30
  115.7 3.8 %collective-permute-done.14.refs_6_ = bf16[2,256,512]{2,1,0:T(8,128)(2,1)S(1)} collective-permute-done((bf16[2,256,512]{2,1,0:T(8,128)(2,1)}, bf16[2,256,512]{2,1,0:T(8,128)(2,1)S(1)}, u32[]{:S(2)}, u32[]{:S(2)}) %collective-permute-start.14) | collective-permute-done | bytes 524320 | tf_op jit(solution)/shard_map/ppermute | solution.py:26
  119.5 7.1 %collective-permute-start.17 = (f32[4,2,256]{2,1,0:T(2,128)S(1)}, f32[4,2,256]{2,1,0:T(2,128)S(1)}, u32[]{:S(2)}, u32[]{:S(2)}) collective-permute-start(f32[4,2,256]{2,1,0:T(2,128)S(1)} %get-tuple-element.51.refs_2_), channel_id=1, source_target_pairs={{4,0},{6,2},{8,4},{10,6},{12,8},{14,10},{16,12},{18,14},{20,16},{2... | collective-permute-start | bytes 24584 | tf_op jit(solution)/shard_map/ppermute | solution.py:26
  126.6 1.3 collective-permute-start.22
  127.9 2.9 %collective-permute-start.24 = (f32[4,2,256]{2,1,0:T(2,128)S(1)}, f32[4,2,256]{2,1,0:T(2,128)S(1)}, u32[]{:S(2)}, u32[]{:S(2)}) collective-permute-start(f32[4,2,256]{2,1,0:T(2,128)S(1)} %get-tuple-element.51.refs_2_), channel_id=1, source_target_pairs={{128,0},{130,2},{132,4},{134,6},{136,8},{138,10},{140,12},{142,14}... | collective-permute-start | bytes 24584 | tf_op jit(solution)/shard_map/ppermute | solution.py:26
  130.8 1.9 %collective-permute-start.21 = (f32[4,2,256]{2,1,0:T(2,128)S(1)}, f32[4,2,256]{2,1,0:T(2,128)S(1)}, u32[]{:S(2)}, u32[]{:S(2)}) collective-permute-start(f32[4,2,256]{2,1,0:T(2,128)S(1)} %get-tuple-element.51.refs_2_), channel_id=1, source_target_pairs={{16,0},{18,2},{20,4},{22,6},{24,8},{26,10},{28,12},{30,14},{32,16}... | collective-permute-start | bytes 24584 | tf_op jit(solution)/shard_map/ppermute | solution.py:26
  132.7 5.0 %collective-permute-start.20 = (f32[4,2,256]{2,1,0:T(2,128)S(1)}, f32[4,2,256]{2,1,0:T(2,128)S(1)}, u32[]{:S(2)}, u32[]{:S(2)}) collective-permute-start(f32[4,2,256]{2,1,0:T(2,128)S(1)} %get-tuple-element.51.refs_2_), channel_id=1, source_target_pairs={{8,0},{10,2},{12,4},{14,6},{16,8},{18,10},{20,12},{22,14},{24,16},... | collective-permute-start | bytes 24584 | tf_op jit(solution)/shard_map/ppermute | solution.py:26
  137.8 1.6 collective-permute-start.23
  139.6 0.6 collective-permute-done.21.refs_13_
  140.2 0.5 collective-permute-done.20.refs_12_
  140.7 0.9 collective-permute-done.23.refs_14_
  141.6 4.0 %key_side.2 = bf16[2,128,512]{2,1,0:T(8,128)(2,1)S(1)} custom-call(s32[2]{0:T(128)S(1)} %pad_add_fusion.where_ref, bf16[2,256,512]{2,1,0:T(8,128)(2,1)S(1)} %get-tuple-element.37.refs_1_.refs_0_, bf16[2,256,512]{2,1,0:T(8,128)(2,1)S(1)} %get-tuple-element.36.refs_0_.refs_1_, f32[4,2,256]{2,1,0:T(2,128)S(1)} %get-tuple-element.51.refs_2_, ...), custom_call_target="tpu_custom_call" | custom-call | flops 81920 | bytes 65536 | tf_op jit(solution)/shard_map/key_side/pallas_call | solution.py:205
  145.6 0.8 fusion.24
  146.4 0.8 copy-done.12
  147.2 0.8 fusion.25
  148.1 0.8 fusion.6
  148.9 2.8 %collective-permute-start.25 = (bf16[128,2048]{1,0:T(8,128)(2,1)S(1)}, bf16[128,2048]{1,0:T(8,128)(2,1)S(1)}, u32[]{:S(2)}, u32[]{:S(2)}) collective-permute-start(bf16[128,2048]{1,0:T(8,128)(2,1)S(1)} %fusion.6), channel_id=1, source_target_pairs={{0,1},{1,0},{2,3},{3,2},{4,5},{5,4},{6,7},{7,6},{8,9},{9,8},{10,11... | collective-permute-start | bytes 1572872 | tf_op jit(solution)/shard_map/ppermute | solution.py:30
  151.7 4.0 %key_side.3 = bf16[2,128,512]{2,1,0:T(8,128)(2,1)S(1)} custom-call(s32[2]{0:T(128)S(1)} %pad_add_fusion.where_ref, bf16[2,256,512]{2,1,0:T(8,128)(2,1)S(1)} %get-tuple-element.37.refs_1_.refs_0_, bf16[2,256,512]{2,1,0:T(8,128)(2,1)S(1)} %get-tuple-element.36.refs_0_.refs_1_, f32[4,2,256]{2,1,0:T(2,128)S(1)} %get-tuple-element.51.refs_2_, ...), custom_call_target="tpu_custom_call" | custom-call | flops 81920 | bytes 65536 | tf_op jit(solution)/shard_map/key_side/pallas_call | solution.py:205
  155.7 0.8 fusion.22
  156.6 0.8 fusion.23
  157.5 0.7 copy-done.15
  158.3 1.4 fusion.5
  159.7 3.9 %collective-permute-done.25 = bf16[128,2048]{1,0:T(8,128)(2,1)S(1)} collective-permute-done((bf16[128,2048]{1,0:T(8,128)(2,1)S(1)}, bf16[128,2048]{1,0:T(8,128)(2,1)S(1)}, u32[]{:S(2)}, u32[]{:S(2)}) %collective-permute-start.25) | collective-permute-done | bytes 524320 | tf_op jit(solution)/shard_map/ppermute | solution.py:30
  163.6 1.0 fusion.17
  164.6 1.2 fusion.21
  (66 shorter events, 2.1 us)
Async XLA Ops:
  0.6 8.4 %copy-start = (bf16[2048,512]{1,0:T(8,128)(2,1)S(1)}, bf16[2048,512]{1,0:T(8,128)(2,1)}, u32[]{:S(2)}) copy-start(bf16[2048,512]{1,0:T(8,128)(2,1)} %param.9) | copy-start | bytes 6291460
  0.6 16.6 %collective-permute-start.1 = (bf16[128,2048]{1,0:T(8,128)(2,1)}, bf16[128,2048]{1,0:T(8,128)(2,1)S(1)}, u32[]{:S(2)}, u32[]{:S(2)}) collective-permute-start(bf16[128,2048]{1,0:T(8,128)(2,1)} %param.13), channel_id=1, source_target_pairs={{0,1},{1,0},{2,3},{3,2},{4,5},{5,4},{6,7},{7,6},{8,9},{9,8},{10,11... | collective-permute-start | bytes 1572872 | tf_op jit(solution)/shard_map/ppermute | solution.py:30
  3.8 0.7 copy-start.7
  5.8 3.7 %copy-start.9 = (bf16[2048,512]{1,0:T(8,128)(2,1)S(1)}, bf16[2048,512]{1,0:T(8,128)(2,1)}, u32[]{:S(2)}) copy-start(bf16[2048,512]{1,0:T(8,128)(2,1)} %param.11) | copy-start | bytes 6291460
  5.8 21.6 %collective-permute-start = (bf16[128,2048]{1,0:T(8,128)(2,1)S(1)}, bf16[128,2048]{1,0:T(8,128)(2,1)S(1)}, u32[]{:S(2)}, u32[]{:S(2)}) collective-permute-start(bf16[128,2048]{1,0:T(8,128)(2,1)S(1)} %get-tuple-element.33), channel_id=1, source_target_pairs={{0,1},{1,0},{2,3},{3,2},{4,5},{5,4},{6,7},{7,6},{8,9},{9,8},{10,11... | collective-permute-start | bytes 1572872 | tf_op jit(solution)/shard_map/ppermute | solution.py:30
  9.0 1.6 copy-start.11
  27.8 1.6 copy-start.13
  30.3 19.8 %collective-permute-start.10 = (bf16[2,256,512]{2,1,0:T(8,128)(2,1)S(1)}, bf16[2,256,512]{2,1,0:T(8,128)(2,1)}, u32[]{:S(2)}, u32[]{:S(2)}) collective-permute-start(bf16[2,256,512]{2,1,0:T(8,128)(2,1)S(1)} %get-tuple-element.36.refs_0_.refs_1_), channel_id=1, source_target_pairs={{64,0},{66,2},{68,4},{70,6},{72,8},{74,10},{76,12},{78,14},{80,16}... | collective-permute-start | bytes 1572872 | tf_op jit(solution)/shard_map/ppermute | solution.py:26
  33.8 28.4 %collective-permute-start.9 = (bf16[2,256,512]{2,1,0:T(8,128)(2,1)S(1)}, bf16[2,256,512]{2,1,0:T(8,128)(2,1)}, u32[]{:S(2)}, u32[]{:S(2)}) collective-permute-start(bf16[2,256,512]{2,1,0:T(8,128)(2,1)S(1)} %get-tuple-element.36.refs_0_.refs_1_), channel_id=1, source_target_pairs={{4,0},{6,2},{8,4},{10,6},{12,8},{14,10},{16,12},{18,14},{20,16},{2... | collective-permute-start | bytes 1572872 | tf_op jit(solution)/shard_map/ppermute | solution.py:26
  41.6 29.5 %collective-permute-start.3 = (bf16[2,256,512]{2,1,0:T(8,128)(2,1)S(1)}, bf16[2,256,512]{2,1,0:T(8,128)(2,1)}, u32[]{:S(2)}, u32[]{:S(2)}) collective-permute-start(bf16[2,256,512]{2,1,0:T(8,128)(2,1)S(1)} %get-tuple-element.37.refs_1_.refs_0_), channel_id=1, source_target_pairs={{0,64},{2,66},{4,68},{6,70},{8,72},{10,74},{12,76},{14,78},{16,80}... | collective-permute-start | bytes 1572872 | tf_op jit(solution)/shard_map/ppermute | solution.py:26
  42.9 28.2 %collective-permute-start.2 = (bf16[2,256,512]{2,1,0:T(8,128)(2,1)S(1)}, bf16[2,256,512]{2,1,0:T(8,128)(2,1)}, u32[]{:S(2)}, u32[]{:S(2)}) collective-permute-start(bf16[2,256,512]{2,1,0:T(8,128)(2,1)S(1)} %get-tuple-element.37.refs_1_.refs_0_), channel_id=1, source_target_pairs={{0,4},{2,6},{4,8},{6,10},{8,12},{10,14},{12,16},{14,18},{16,20},{1... | collective-permute-start | bytes 1572872 | tf_op jit(solution)/shard_map/ppermute | solution.py:26
  44.9 32.6 %collective-permute-start.6 = (bf16[2,128,512]{2,1,0:T(8,128)(2,1)S(1)}, bf16[2,128,512]{2,1,0:T(8,128)(2,1)S(1)}, u32[]{:S(2)}, u32[]{:S(2)}) collective-permute-start(bf16[2,128,512]{2,1,0:T(8,128)(2,1)S(1)} %pad_maximum_fusion), channel_id=1, source_target_pairs={{0,16},{2,18},{4,20},{6,22},{8,24},{10,26},{12,28},{14,30},{16,32}... | collective-permute-start | bytes 786440 | tf_op jit(solution)/shard_map/ppermute | solution.py:26
  62.2 27.9 %collective-permute-start.11 = (bf16[2,256,512]{2,1,0:T(8,128)(2,1)}, bf16[2,256,512]{2,1,0:T(8,128)(2,1)}, u32[]{:S(2)}, u32[]{:S(2)}) collective-permute-start(bf16[2,256,512]{2,1,0:T(8,128)(2,1)} %collective-permute-done.9.refs_4_), channel_id=1, source_target_pairs={{4,0},{6,2},{8,4},{10,6},{12,8},{14,10},{16,12},{18,14},{20,16},{2... | collective-permute-start | bytes 1572872 | tf_op jit(solution)/shard_map/ppermute | solution.py:26
  71.1 15.3 %collective-permute-start.4 = (bf16[2,256,512]{2,1,0:T(8,128)(2,1)}, bf16[2,256,512]{2,1,0:T(8,128)(2,1)S(1)}, u32[]{:S(2)}, u32[]{:S(2)}) collective-permute-start(bf16[2,256,512]{2,1,0:T(8,128)(2,1)} %collective-permute-done.2.refs_3_), channel_id=1, source_target_pairs={{0,4},{2,6},{4,8},{6,10},{8,12},{10,14},{12,16},{14,18},{16,20},{1... | collective-permute-start | bytes 1572872 | tf_op jit(solution)/shard_map/ppermute | solution.py:26
  73.0 25.6 %collective-permute-start.13 = (bf16[2,256,512]{2,1,0:T(8,128)(2,1)}, bf16[2,256,512]{2,1,0:T(8,128)(2,1)}, u32[]{:S(2)}, u32[]{:S(2)}) collective-permute-start(bf16[2,256,512]{2,1,0:T(8,128)(2,1)} %collective-permute-done.3.refs_8_), channel_id=1, source_target_pairs={{0,64},{2,66},{4,68},{6,70},{8,72},{10,74},{12,76},{14,78},{16,80}... | collective-permute-start | bytes 1572872 | tf_op jit(solution)/shard_map/ppermute | solution.py:26
  75.2 11.2 %collective-permute-start.5 = (bf16[2,256,512]{2,1,0:T(8,128)(2,1)S(1)}, bf16[2,256,512]{2,1,0:T(8,128)(2,1)S(1)}, u32[]{:S(2)}, u32[]{:S(2)}) collective-permute-start(bf16[2,256,512]{2,1,0:T(8,128)(2,1)S(1)} %get-tuple-element.67), channel_id=1, source_target_pairs={{0,2},{2,0},{4,6},{6,4},{8,10},{10,8},{12,14},{14,12},{16,18},{18,... | collective-permute-start | bytes 1572872 | tf_op jit(solution)/shard_map/ppermute | solution.py:308
  77.5 21.1 %collective-permute-start.12 = (bf16[2,256,512]{2,1,0:T(8,128)(2,1)}, bf16[2,256,512]{2,1,0:T(8,128)(2,1)}, u32[]{:S(2)}, u32[]{:S(2)}) collective-permute-start(bf16[2,256,512]{2,1,0:T(8,128)(2,1)} %get-tuple-element.65), channel_id=1, source_target_pairs={{0,2},{2,0},{4,6},{6,4},{8,10},{10,8},{12,14},{14,12},{16,18},{18,... | collective-permute-start | bytes 1572872 | tf_op jit(solution)/shard_map/ppermute | solution.py:308
  86.4 15.8 %collective-permute-start.8 = (bf16[2,256,512]{2,1,0:T(8,128)(2,1)}, bf16[2,256,512]{2,1,0:T(8,128)(2,1)}, u32[]{:S(2)}, u32[]{:S(2)}) collective-permute-start(bf16[2,256,512]{2,1,0:T(8,128)(2,1)} %get-tuple-element.66), channel_id=1, source_target_pairs={{0,32},{2,34},{4,36},{6,38},{8,40},{10,42},{12,44},{14,46},{16,48}... | collective-permute-start | bytes 1572872 | tf_op jit(solution)/shard_map/ppermute | solution.py:308
  86.4 0.9 copy-start.3
  87.3 0.8 copy-start.1
  88.1 14.7 %collective-permute-start.7 = (bf16[2,128,512]{2,1,0:T(8,128)(2,1)}, bf16[2,128,512]{2,1,0:T(8,128)(2,1)}, u32[]{:S(2)}, u32[]{:S(2)}) collective-permute-start(bf16[2,128,512]{2,1,0:T(8,128)(2,1)} %slice.27), channel_id=1, source_target_pairs={{0,8},{2,10},{4,12},{6,14},{8,16},{10,18},{12,20},{14,22},{16,24},... | collective-permute-start | bytes 786440 | tf_op jit(solution)/shard_map/ppermute | solution.py:26
  90.1 25.6 %collective-permute-start.16 = (bf16[2,256,512]{2,1,0:T(8,128)(2,1)}, bf16[2,256,512]{2,1,0:T(8,128)(2,1)S(1)}, u32[]{:S(2)}, u32[]{:S(2)}) collective-permute-start(bf16[2,256,512]{2,1,0:T(8,128)(2,1)} %collective-permute-done.10.refs_8_), channel_id=1, source_target_pairs={{64,0},{66,2},{68,4},{70,6},{72,8},{74,10},{76,12},{78,14},{80,16}... | collective-permute-start | bytes 1572872 | tf_op jit(solution)/shard_map/ppermute | solution.py:26
  98.6 17.1 %collective-permute-start.15 = (bf16[2,256,512]{2,1,0:T(8,128)(2,1)}, bf16[2,256,512]{2,1,0:T(8,128)(2,1)S(1)}, u32[]{:S(2)}, u32[]{:S(2)}) collective-permute-start(bf16[2,256,512]{2,1,0:T(8,128)(2,1)} %get-tuple-element.64), channel_id=1, source_target_pairs={{0,32},{2,34},{4,36},{6,38},{8,40},{10,42},{12,44},{14,46},{16,48}... | collective-permute-start | bytes 1572872 | tf_op jit(solution)/shard_map/ppermute | solution.py:308
  98.6 20.9 %collective-permute-start.14 = (bf16[2,256,512]{2,1,0:T(8,128)(2,1)}, bf16[2,256,512]{2,1,0:T(8,128)(2,1)S(1)}, u32[]{:S(2)}, u32[]{:S(2)}) collective-permute-start(bf16[2,256,512]{2,1,0:T(8,128)(2,1)} %collective-permute-done.11.refs_5_), channel_id=1, source_target_pairs={{8,0},{10,2},{12,4},{14,6},{16,8},{18,10},{20,12},{22,14},{24,16},... | collective-permute-start | bytes 1572872 | tf_op jit(solution)/shard_map/ppermute | solution.py:26
  102.8 1.0 copy-start.2
  103.8 1.0 copy-start.4
  104.9 7.3 %copy-start.14 = (bf16[512,2048]{1,0:T(8,128)(2,1)S(1)}, bf16[512,2048]{1,0:T(8,128)(2,1)}, u32[]{:S(2)}) copy-start(bf16[512,2048]{1,0:T(8,128)(2,1)} %param.12) | copy-start | bytes 6291460
  111.4 0.7 copy-start.5
  112.6 25.2 %collective-permute-start.18 = (bf16[128,2048]{1,0:T(8,128)(2,1)S(1)}, bf16[128,2048]{1,0:T(8,128)(2,1)S(1)}, u32[]{:S(2)}, u32[]{:S(2)}) collective-permute-start(bf16[128,2048]{1,0:T(8,128)(2,1)S(1)} %convolution_convert_fusion), channel_id=1, source_target_pairs={{0,1},{1,0},{2,3},{3,2},{4,5},{5,4},{6,7},{7,6},{8,9},{9,8},{10,11... | collective-permute-start | bytes 1572872 | tf_op jit(solution)/shard_map/ppermute | solution.py:30
  115.7 23.7 %copy-start.18 = (bf16[2,256,512]{2,1,0:T(8,128)(2,1)}, bf16[2,256,512]{2,1,0:T(8,128)(2,1)S(1)}, u32[]{:S(2)}) copy-start(bf16[2,256,512]{2,1,0:T(8,128)(2,1)S(1)} %collective-permute-done.16.refs_9_) | copy-start | bytes 1572868
  115.7 23.7 %copy-start.19 = (bf16[2,256,512]{2,1,0:T(8,128)(2,1)}, bf16[2,256,512]{2,1,0:T(8,128)(2,1)S(1)}, u32[]{:S(2)}) copy-start(bf16[2,256,512]{2,1,0:T(8,128)(2,1)S(1)} %collective-permute-done.15.refs_7_) | copy-start | bytes 1572868
  119.5 20.0 %copy-start.20 = (bf16[2,256,512]{2,1,0:T(8,128)(2,1)}, bf16[2,256,512]{2,1,0:T(8,128)(2,1)S(1)}, u32[]{:S(2)}) copy-start(bf16[2,256,512]{2,1,0:T(8,128)(2,1)S(1)} %collective-permute-done.14.refs_6_) | copy-start | bytes 1572868
  119.5 13.2 %collective-permute-start.17 = (f32[4,2,256]{2,1,0:T(2,128)S(1)}, f32[4,2,256]{2,1,0:T(2,128)S(1)}, u32[]{:S(2)}, u32[]{:S(2)}) collective-permute-start(f32[4,2,256]{2,1,0:T(2,128)S(1)} %get-tuple-element.51.refs_2_), channel_id=1, source_target_pairs={{4,0},{6,2},{8,4},{10,6},{12,8},{14,10},{16,12},{18,14},{20,16},{2... | collective-permute-start | bytes 24584 | tf_op jit(solution)/shard_map/ppermute | solution.py:26
  126.6 11.2 %collective-permute-start.22 = (f32[4,2,256]{2,1,0:T(2,128)S(1)}, f32[4,2,256]{2,1,0:T(2,128)S(1)}, u32[]{:S(2)}, u32[]{:S(2)}) collective-permute-start(f32[4,2,256]{2,1,0:T(2,128)S(1)} %get-tuple-element.51.refs_2_), channel_id=1, source_target_pairs={{64,0},{66,2},{68,4},{70,6},{72,8},{74,10},{76,12},{78,14},{80,16}... | collective-permute-start | bytes 24584 | tf_op jit(solution)/shard_map/ppermute | solution.py:26
  127.9 11.7 %collective-permute-start.24 = (f32[4,2,256]{2,1,0:T(2,128)S(1)}, f32[4,2,256]{2,1,0:T(2,128)S(1)}, u32[]{:S(2)}, u32[]{:S(2)}) collective-permute-start(f32[4,2,256]{2,1,0:T(2,128)S(1)} %get-tuple-element.51.refs_2_), channel_id=1, source_target_pairs={{128,0},{130,2},{132,4},{134,6},{136,8},{138,10},{140,12},{142,14}... | collective-permute-start | bytes 24584 | tf_op jit(solution)/shard_map/ppermute | solution.py:26
  130.8 9.5 %collective-permute-start.21 = (f32[4,2,256]{2,1,0:T(2,128)S(1)}, f32[4,2,256]{2,1,0:T(2,128)S(1)}, u32[]{:S(2)}, u32[]{:S(2)}) collective-permute-start(f32[4,2,256]{2,1,0:T(2,128)S(1)} %get-tuple-element.51.refs_2_), channel_id=1, source_target_pairs={{16,0},{18,2},{20,4},{22,6},{24,8},{26,10},{28,12},{30,14},{32,16}... | collective-permute-start | bytes 24584 | tf_op jit(solution)/shard_map/ppermute | solution.py:26
  132.7 8.0 %collective-permute-start.20 = (f32[4,2,256]{2,1,0:T(2,128)S(1)}, f32[4,2,256]{2,1,0:T(2,128)S(1)}, u32[]{:S(2)}, u32[]{:S(2)}) collective-permute-start(f32[4,2,256]{2,1,0:T(2,128)S(1)} %get-tuple-element.51.refs_2_), channel_id=1, source_target_pairs={{8,0},{10,2},{12,4},{14,6},{16,8},{18,10},{20,12},{22,14},{24,16},... | collective-permute-start | bytes 24584 | tf_op jit(solution)/shard_map/ppermute | solution.py:26
  137.8 1.7 %copy-start.21 = (bf16[128,2048]{1,0:T(8,128)(2,1)}, bf16[128,2048]{1,0:T(8,128)(2,1)S(1)}, u32[]{:S(2)}) copy-start(bf16[128,2048]{1,0:T(8,128)(2,1)S(1)} %collective-permute-done.18) | copy-start | bytes 1572868
  137.8 3.7 %collective-permute-start.23 = (f32[4,2,256]{2,1,0:T(2,128)S(1)}, f32[4,2,256]{2,1,0:T(2,128)S(1)}, u32[]{:S(2)}, u32[]{:S(2)}) collective-permute-start(f32[4,2,256]{2,1,0:T(2,128)S(1)} %bitcast.65), channel_id=1, source_target_pairs={{0,32},{2,34},{4,36},{6,38},{8,40},{10,42},{12,44},{14,46},{16,48}... | collective-permute-start | bytes 24584 | tf_op jit(solution)/shard_map/ppermute | solution.py:308
  139.5 2.1 %collective-permute-start.19 = (f32[4,2,256]{2,1,0:T(2,128)S(1)}, f32[4,2,256]{2,1,0:T(2,128)S(1)}, u32[]{:S(2)}, u32[]{:S(2)}) collective-permute-start(f32[4,2,256]{2,1,0:T(2,128)S(1)} %bitcast.64), channel_id=1, source_target_pairs={{0,2},{2,0},{4,6},{6,4},{8,10},{10,8},{12,14},{14,12},{16,18},{18,... | collective-permute-start | bytes 24584 | tf_op jit(solution)/shard_map/ppermute | solution.py:308
  139.6 6.0 %copy-start.10 = (bf16[2048,512]{1,0:T(8,128)(2,1)S(1)}, bf16[2048,512]{1,0:T(8,128)(2,1)}, u32[]{:S(2)}) copy-start(bf16[2048,512]{1,0:T(8,128)(2,1)} %param.11) | copy-start | bytes 6291460
  145.6 1.6 copy-start.12
  147.1 0.9 copy-start.23
  148.9 14.6 %collective-permute-start.25 = (bf16[128,2048]{1,0:T(8,128)(2,1)S(1)}, bf16[128,2048]{1,0:T(8,128)(2,1)S(1)}, u32[]{:S(2)}, u32[]{:S(2)}) collective-permute-start(bf16[128,2048]{1,0:T(8,128)(2,1)S(1)} %fusion.6), channel_id=1, source_target_pairs={{0,1},{1,0},{2,3},{3,2},{4,5},{5,4},{6,7},{7,6},{8,9},{9,8},{10,11... | collective-permute-start | bytes 1572872 | tf_op jit(solution)/shard_map/ppermute | solution.py:30
  155.7 1.7 %copy-start.22 = (bf16[128,2048]{1,0:T(8,128)(2,1)S(1)}, bf16[128,2048]{1,0:T(8,128)(2,1)}, u32[]{:S(2)}) copy-start(bf16[128,2048]{1,0:T(8,128)(2,1)} %copy-done.21) | copy-start | bytes 1572868
  156.5 1.0 copy-start.6
  156.5 1.7 %copy-start.15 = (bf16[512,2048]{1,0:T(8,128)(2,1)S(1)}, bf16[512,2048]{1,0:T(8,128)(2,1)}, u32[]{:S(2)}) copy-start(bf16[512,2048]{1,0:T(8,128)(2,1)} %param.12) | copy-start | bytes 6291460
  156.6 1.8 %copy-start.16 = (bf16[128,2048]{1,0:T(8,128)(2,1)S(1)}, bf16[128,2048]{1,0:T(8,128)(2,1)}, u32[]{:S(2)}) copy-start(bf16[128,2048]{1,0:T(8,128)(2,1)} %series_ref.1) | copy-start | bytes 1572868
  158.3 5.2 %copy-start.8 = (f32[2048]{0:T(1024)S(1)}, f32[2048]{0:T(1024)}, u32[]{:S(2)}) copy-start(f32[2048]{0:T(1024)} %param.8) | copy-start | bytes 24580
  159.7 4.9 %copy-start.17 = (bf16[128,2048]{1,0:T(8,128)(2,1)S(1)}, bf16[128,2048]{1,0:T(8,128)(2,1)}, u32[]{:S(2)}) copy-start(bf16[128,2048]{1,0:T(8,128)(2,1)} %param.13) | copy-start | bytes 1572868
